TPU v7x, 512 devices: a whole 4x8x8 slice. The times are simulated.
512 devices in a mesh: dp: 64 (over z_hi, x, y), tile: 8 (over z_lo, core).
Axes of the slice: x: 4, y: 8, z: 8 (z_hi: 2, z_lo: 4; z = z_hi * 4 + z_lo), core: 2. Of those that a mesh axis runs over, the one named last changes fastest.
Arguments:
- feats: bfloat16 [4096, 2048], P('dp'), may hold values from -11 to 11
- jitter: bfloat16 [4096, 2048], P('dp'), may hold values from -1.5 to 1.5
- mask_ids: int32 [4096, 2], P('dp'), may hold values from 0 to 31
- proj_weight: bfloat16 [2048, 4096], P('dp', 'tile'), may hold values from -0.125 to 0.125
Outputs:
- feats_grad: float32 [4096, 2048], P('dp', 'tile')
- diag_corr: float32 [4096], P('tile')
- cross_power: float32 [], replicated
All inputs are finite; a program needn't handle non-finite values.
Results may differ from a plain program's by a relative error of at most 0.02.
Values may be sent and summed in bfloat16 or wider, within the bound.
No kernel may reach another device: no remote copies, remote signals or barrier semaphores. Data moves between devices by JAX's collectives and lax.ppermute only.
A program may use at most 64 MiB of HBM per device.

v0:
```python
import jax
import jax.numpy as jnp
from jax import lax
from jax.sharding import PartitionSpec as P

EMB = 4096
GROUPS = 32


LAMBDA_OFF = 0.0051
NORM_EPS = 1e-05
LOSS_SCALE = 65536.0


def masked_views(feats, jitter, mask_ids):
    width = feats.shape[1]
    group_size = width // GROUPS
    channel_group = lax.broadcasted_iota(jnp.int32, (1, width), 1) // group_size
    keep_a = (channel_group != mask_ids[:, 0:1]).astype(jnp.float32)
    keep_b = (channel_group != mask_ids[:, 1:2]).astype(jnp.float32)
    values = feats.astype(jnp.float32)
    view_a = (values * keep_a).astype(jnp.bfloat16)
    view_b = (values * keep_b + jitter.astype(jnp.float32)).astype(jnp.bfloat16)
    return (view_a, view_b, keep_a, keep_b)


def contract_last(left, right):
    return lax.dot_general(
        left, right, (((1,), (1,)), ((), ())), preferred_element_type=jnp.float32
    )


def on_device(feats, jitter, mask_ids, proj_weight):
    view_a, view_b, keep_a, keep_b = masked_views(feats, jitter, mask_ids)
    rows = feats.shape[0]
    total = rows * lax.axis_size("dp")
    piece = lax.all_gather(proj_weight, "dp", axis=0, tiled=True)
    raw_a = jnp.dot(view_a, piece, preferred_element_type=jnp.float32)
    raw_b = jnp.dot(view_b, piece, preferred_element_type=jnp.float32)
    raw_a = raw_a.astype(jnp.bfloat16)
    raw_b = raw_b.astype(jnp.bfloat16)
    values_a = raw_a.astype(jnp.float32)
    values_b = raw_b.astype(jnp.float32)
    moment_sums = lax.psum(
        (
            jnp.sum(values_a, axis=0),
            jnp.sum(values_a * values_a, axis=0),
            jnp.sum(values_b, axis=0),
            jnp.sum(values_b * values_b, axis=0),
        ),
        "dp",
    )
    mean_a = moment_sums[0] / total
    mean_b = moment_sums[2] / total
    inv_a = lax.rsqrt(moment_sums[1] / total - mean_a * mean_a + NORM_EPS)
    inv_b = lax.rsqrt(moment_sums[3] / total - mean_b * mean_b + NORM_EPS)
    norm_a = ((values_a - mean_a) * inv_a).astype(jnp.bfloat16)
    norm_b = ((values_b - mean_b) * inv_b).astype(jnp.bfloat16)
    outgoing_a, outgoing_b = (norm_a, norm_b)
    gathered_a, gathered_b = (
        lax.all_gather(outgoing_a, "dp", axis=0, tiled=True),
        lax.all_gather(outgoing_b, "dp", axis=0, tiled=True),
    )
    whole_a, whole_b = (gathered_a, gathered_b)
    za = norm_a.astype(jnp.float32)
    zb = norm_b.astype(jnp.float32)
    diag_corr = jnp.sum(whole_a.astype(jnp.float32) * whole_b.astype(jnp.float32), axis=0) / total
    gram_a, gram_b = (
        lax.psum(contract_last(norm_a, whole_a).astype(jnp.bfloat16), "tile").astype(jnp.float32),
        lax.psum(contract_last(norm_b, whole_b).astype(jnp.bfloat16), "tile").astype(jnp.float32),
    )
    trace_part = jnp.sum(gram_a * gram_b)
    gram_bf_a = gram_a.astype(jnp.bfloat16)
    gram_bf_b = gram_b.astype(jnp.bfloat16)
    coeff = -2.0 * (1.0 - diag_corr) - 2.0 * LAMBDA_OFF * diag_corr
    factor = 2.0 * LAMBDA_OFF / (total * total)
    grad_na = zb * coeff / total + factor * jnp.dot(
        gram_bf_b, whole_a, preferred_element_type=jnp.float32
    )
    grad_nb = za * coeff / total + factor * jnp.dot(
        gram_bf_a, whole_b, preferred_element_type=jnp.float32
    )
    sums = lax.psum(
        (
            jnp.sum(grad_na, axis=0),
            jnp.sum(grad_na * za, axis=0),
            jnp.sum(grad_nb, axis=0),
            jnp.sum(grad_nb * zb, axis=0),
            trace_part,
        ),
        "dp",
    )
    dz_a = (inv_a * (grad_na - sums[0] / total - za * (sums[1] / total))).astype(jnp.bfloat16)
    dz_b = (inv_b * (grad_nb - sums[2] / total - zb * (sums[3] / total))).astype(jnp.bfloat16)
    cross_power = sums[4] / (total * total) / EMB
    piece = lax.all_gather(proj_weight, "dp", axis=0, tiled=True)
    combined = keep_a * contract_last(dz_a, piece) + keep_b * contract_last(dz_b, piece)
    feats_grad = LOSS_SCALE * lax.psum_scatter(
        combined.astype(jnp.bfloat16), "tile", scatter_dimension=1, tiled=True
    ).astype(jnp.float32)
    return (feats_grad, diag_corr, cross_power)


def solution(mesh):
    in_specs = (P("dp", None), P("dp", None), P("dp", None), P("dp", "tile"))
    out_specs = (P("dp", "tile"), P("tile"), P())
    return jax.shard_map(
        on_device, mesh=mesh, in_specs=in_specs, out_specs=out_specs, check_vma=False
    )
```

profile of v0, /device:TPU:1, one launch (start us, length us, event | category | flops | bytes accessed | tf_op | source)
XLA Modules:
  0.0 1042.4 jit_solution(3339325027411994053)
XLA Ops:
  7.2 0.0 all-gather.4.cloned.1.call-start
  7.2 0.7 all-gather.4.cloned.1.call-update
  7.9 0.0 all-gather.6.cloned.1.call-start
  8.0 0.8 slice_bitcast_fusion
  8.7 144.8 %all-gather.4.cloned.1.call-done = bf16[2048,512]{1,0:T(8,128)(2,1)} async-done(((bf16[32,512]{1,0:T(8,128)(2,1)}), bf16[2048,512]{1,0:T(8,128)(2,1)}) %all-gather.4.cloned.1.call-update) | async-done | bytes 2097168 | tf_op jit(solution)/shard_map/all_gather | solution.py:37
  153.5 2.2 multiply_reduce_fusion.3
  155.7 2.3 fusion.42
  158.0 189.4 %all-reduce.1 = (f32[512]{0:T(512)S(1)}, f32[512]{0:T(512)S(1)}, f32[512]{0:T(512)S(1)}, f32[512]{0:T(512)S(1)}) all-reduce(f32[512]{0:T(512)S(1)} %get-tuple-element.10, f32[512]{0:T(512)S(1)} %get-tuple-element.9, f32[512]{0:T(512)S(1)} %get-tuple-element.8, f32[512]{0:T(512)S(1)} %get-tuple-element.7), channel_id=1, replica_groups=mesh['dp'=64,'tile'=8] {'dp'}, use_global_device_ids=true, to_apply=%region_3.4 | all-reduce | flops 2048 | bytes 16384 | tf_op jit(solution)/shard_map/psum | solution.py:44
  347.4 0.6 multiply_convert_fusion
  348.1 0.0 all-gather.6.cloned.1.call-update
  348.1 0.0 all-gather.8.cloned.1.call-start
  348.2 0.6 multiply_convert_fusion.1
  348.8 0.0 copy-start.3
  348.8 0.0 all-gather.8.cloned.1.call-update
  348.8 0.0 all-reduce.5.cloned.1.call-start
  348.9 183.0 %all-gather.6.cloned.1.call-done = bf16[4096,512]{1,0:T(8,128)(2,1)} async-done(((bf16[64,512]{1,0:T(8,128)(2,1)}), bf16[4096,512]{1,0:T(8,128)(2,1)}) %all-gather.6.cloned.1.call-update) | async-done | bytes 4194320 | tf_op jit(solution)/shard_map/all_gather | solution.py:61
  531.9 4.4 convolution_convert_fusion
  536.3 152.4 %all-gather.8.cloned.1.call-done = bf16[4096,512]{1,0:T(8,128)(2,1)} async-done(((bf16[64,512]{1,0:T(8,128)(2,1)}), bf16[4096,512]{1,0:T(8,128)(2,1)}) %all-gather.8.cloned.1.call-update) | async-done | bytes 4194320 | tf_op jit(solution)/shard_map/all_gather | solution.py:62
  688.6 0.0 copy-done.3
  688.7 4.4 convolution_convert_fusion.1
  693.0 0.0 all-reduce.5.cloned.1.call-update
  693.1 0.0 copy-start.2
  693.1 0.0 reduce-scatter.2.cloned.1.call-start
  693.1 4.6 multiply_reduce_fusion
  697.7 0.6 multiply_subtract_fusion
  698.3 69.9 %all-reduce.5.cloned.1.call-done = (bf16[64,4096]{1,0:T(8,128)(2,1)}, bf16[64,4096]{1,0:T(8,128)(2,1)}) async-done(((bf16[64,4096]{1,0:T(8,128)(2,1)}, bf16[64,4096]{1,0:T(8,128)(2,1)}), (bf16[64,4096]{1,0:T(8,128)(2,1)}, bf16[64,4096]{1,0:T(8,128)(2,1)})) %all-reduce.5.cloned.1.call-update) | async-done | bytes 1048592 | tf_op jit(solution)/shard_map/psum | solution.py:70
  768.2 0.0 copy-start
  768.2 0.0 copy-start.4
  768.2 2.2 multiply_reduce_fusion.1
  770.4 0.0 copy-done.2
  770.4 0.0 copy-start.1
  770.4 3.4 fusion.40
  773.8 0.0 copy-done
  773.8 0.0 copy-done.4
  773.8 0.9 fusion.41
  774.7 201.0 %all-reduce = (f32[512]{0:T(512)S(1)}, f32[512]{0:T(512)S(1)}, f32[512]{0:T(512)S(1)}, f32[512]{0:T(512)S(1)}, f32[]{:T(128)}) all-reduce(f32[512]{0:T(512)S(1)} %get-tuple-element.6, f32[512]{0:T(512)S(1)} %get-tuple-element.5, f32[512]{0:T(512)S(1)} %get-tuple-element.4, ...), channel_id=1, replica_groups=mesh['dp'=64,'tile'=8] {'dp'}, use_global_device_ids=true, to_apply=%region_13.14 | all-reduce | flops 2049 | bytes 16392 | tf_op jit(solution)/shard_map/psum | solution.py:83
  975.7 0.0 copy-done.1
  975.7 0.8 convolution_select_fusion.1
  976.4 1.5 fusion.1
  977.9 0.0 reduce-scatter.2.cloned.1.call-update
  978.6 54.8 %reduce-scatter.2.cloned.1.call-done = bf16[64,256]{1,0:T(8,128)(2,1)} async-done(((bf16[64,2048]{1,0:T(8,128)(2,1)}), bf16[64,256]{1,0:T(8,128)(2,1)}) %reduce-scatter.2.cloned.1.call-update) | async-done | bytes 32784 | tf_op jit(solution)/shard_map/reduce_scatter | solution.py:98
  1033.4 1.4 convert_multiply_fusion.6
  (5 shorter events, 0.0 us)
Async XLA Ops:
  7.2 146.3 %all-gather.4.cloned.1.call-start = ((), (), s32[]{:S(2)}) async-start(), calls=%async_computation.1 | async-start | bytes 2129920 | tf_op jit(solution)/shard_map/all_gather | solution.py:37
  7.9 524.0 %all-gather.6.cloned.1.call-start = ((), (), s32[]{:S(2)}) async-start(), calls=%async_computation.2 | async-start | bytes 4259840 | tf_op jit(solution)/shard_map/all_gather | solution.py:61
  348.1 340.6 %all-gather.8.cloned.1.call-start = ((), (), s32[]{:S(2)}) async-start(), calls=%async_computation.3 | async-start | bytes 4259840 | tf_op jit(solution)/shard_map/all_gather | solution.py:62
  348.8 339.9 %copy-start.3 = (bf16[64,512]{1,0:T(8,128)(2,1)S(1)}, bf16[64,512]{1,0:T(8,128)(2,1)}, u32[]{:S(2)}) copy-start(bf16[64,512]{1,0:T(8,128)(2,1)} %multiply_convert_fusion.1) | copy-start | bytes 196612
  348.8 419.4 %all-reduce.5.cloned.1.call-start = ((), (), s32[]{:S(2)}) async-start(), calls=%async_computation.5 | async-start | bytes 2097152 | tf_op jit(solution)/shard_map/psum | solution.py:70
  693.1 77.4 %copy-start.2 = (bf16[64,512]{1,0:T(8,128)(2,1)S(1)}, bf16[64,512]{1,0:T(8,128)(2,1)}, u32[]{:S(2)}) copy-start(bf16[64,512]{1,0:T(8,128)(2,1)} %multiply_convert_fusion) | copy-start | bytes 196612
  693.1 340.3 %reduce-scatter.2.cloned.1.call-start = ((), (), s32[]{:S(2)}) async-start(), calls=%async_computation.4 | async-start | bytes 294912 | tf_op jit(solution)/shard_map/reduce_scatter | solution.py:98
  768.2 5.6 copy-start
  768.2 5.6 copy-start.4
  770.4 205.2 %copy-start.1 = (bf16[2048,512]{1,0:T(8,128)(2,1)S(1)}, bf16[2048,512]{1,0:T(8,128)(2,1)}, u32[]{:S(2)}) copy-start(bf16[2048,512]{1,0:T(8,128)(2,1)} %all-gather.4.cloned.1.call-done) | copy-start | bytes 6291460
Sparse Core Ops, SparseCore 0:
  12.5 140.9 all-gather.3
  348.2 183.6 all-gather.5
  536.4 152.2 all-gather.7
  693.2 74.9 all-reduce.4
  978.0 55.3 reduce-scatter.1
where the time goes:
time: 1040 us
  waiting for transfers between devices  606 us (58%)
  blocking collectives  390 us (38%)
  matrix products  19.7 us (2%)
  between operations  15.6 us (2%)
    psum x1, blocking collectives, on_device(): lax.psum((jnp.sum(grad_na, axis=0), jnp.sum(grad_na * za, axis=0), jnp.su...  201 us
    psum x1, blocking collectives, on_device(): lax.psum((jnp.sum(values_a, axis=0), jnp.sum(values_a * values_a, axis=0)...  189 us
    all_gather x1, waiting for transfers between devices, on_device(): lax.all_gather(outgoing_a, 'dp', axis=0, tiled=True)  183 us
    all_gather x1, waiting for transfers between devices, on_device(): lax.all_gather(outgoing_b, 'dp', axis=0, tiled=True)  152 us
    all_gather x1, waiting for transfers between devices, on_device(): piece = lax.all_gather(proj_weight, 'dp', axis=0, tiled=True)  145 us
    psum x1, waiting for transfers between devices, on_device(): lax.psum(contract_last(norm_b, whole_b).astype(jnp.bfloat16), 'tile')  69.9 us
    reduce_scatter x1, waiting for transfers between devices, on_device(): lax.psum_scatter(combined.astype(jnp.bfloat16), 'tile', scatter_dimension...  54.8 us
  transfers between devices with their start and end apart: 5, of which 5 were waited for; matrix products, arithmetic and copies ran while one was open for 1% of the time, Pallas kernels for 0%

commit v1 on v0

v1 whole, which is shorter than its diff:
```python
import jax
import jax.numpy as jnp
from jax import lax
from jax.sharding import Mesh
from jax.sharding import PartitionSpec as P

GROUPS = 32
LAMBDA_OFF = 0.0051
NORM_EPS = 1e-05
LOSS_SCALE = 65536.0

DP_SHAPE = (2, 4, 8)
TILE_SHAPE = (4, 2)
DP = ("zh", "x", "y")
ROWS = "y"
COLS = ("zh", "x")
TILE = ("zl", "c")
BF = jnp.bfloat16
F32 = jnp.float32


def masked_views(feats, jitter, mask_ids):
    width = feats.shape[1]
    group_size = width // GROUPS
    channel_group = lax.broadcasted_iota(jnp.int32, (1, width), 1) // group_size
    keep_a = (channel_group != mask_ids[:, 0:1]).astype(F32)
    keep_b = (channel_group != mask_ids[:, 1:2]).astype(F32)
    values = feats.astype(F32)
    view_a = (values * keep_a).astype(BF)
    view_b = (values * keep_b + jitter.astype(F32)).astype(BF)
    return view_a, view_b, keep_a, keep_b


def pieces(value, count):
    out = []
    for _ in range(count):
        part = lax.reduce_precision(value, 8, 7)
        out.append(part.astype(BF))
        value = value - part
    return out


def joined(rows):
    total = rows[..., 0, :].astype(F32)
    for i in range(1, rows.shape[-2]):
        total = total + rows[..., i, :].astype(F32)
    return total


def stack_rows(rows, count):
    rows = [jnp.reshape(r, (1, -1)) for r in rows]
    width = rows[0].shape[1]
    if len(rows) < count:
        rows.append(jnp.zeros((count - len(rows), width), BF))
    return jnp.concatenate(rows, axis=0)


def exchange(blocks, extra, axes):
    parts = blocks.shape[0]
    tail = jnp.broadcast_to(extra[None], (parts,) + extra.shape)
    got = lax.all_to_all(jnp.concatenate([blocks, tail], axis=1), axes, 0, 0, tiled=True)
    return got[:, : blocks.shape[1]], got[:, blocks.shape[1] :]


def swap_pairs():
    y_n = DP_SHAPE[2]
    cols_n = DP_SHAPE[0] * DP_SHAPE[1]
    tile_n = TILE_SHAPE[0] * TILE_SHAPE[1]
    where = lambda c, y, t: (c * y_n + y) * tile_n + t
    return [
        (where(c, y, t), where(t, y, c))
        for c in range(cols_n)
        for y in range(y_n)
        for t in range(tile_n)
    ]


def dot(a, b, ca, cb):
    return lax.dot_general(a, b, (((ca,), (cb,)), ((), ())), preferred_element_type=F32)


def on_device(feats, jitter, mask_ids, weight):
    view_a, view_b, keep_a, keep_b = masked_views(feats, jitter, mask_ids)
    rows, width = feats.shape
    kt = weight.shape[1]
    zh_n, x_n, y_n = DP_SHAPE
    cols_n = zh_n * x_n
    tile_n = TILE_SHAPE[0] * TILE_SHAPE[1]
    total = rows * cols_n * y_n
    block = rows * cols_n
    sub = kt // y_n
    all_axes = DP + TILE
    pairs = swap_pairs()

    piece = lax.all_gather(weight, "x", axis=0, tiled=True)
    piece = lax.all_gather(piece, "zh", axis=0, tiled=True)
    piece = lax.all_gather(piece, "y", axis=0, tiled=True)
    piece = piece.reshape(y_n, cols_n, -1, kt).swapaxes(0, 1).reshape(width, kt)

    raw = dot(jnp.concatenate([view_a, view_b], axis=0), piece, 1, 0).astype(BF)
    raw_a, raw_b = raw[:rows], raw[rows:]

    own_b = lax.ppermute(raw_b, all_axes, pairs)
    big_a = lax.all_gather(raw_a, "x", axis=0, tiled=True)
    big_a = lax.all_gather(big_a, "zh", axis=0, tiled=True).astype(F32)
    big_b = lax.all_gather(own_b, TILE, axis=0, tiled=True).astype(F32)

    part_mean_a = jnp.mean(big_a, axis=0)
    part_mean_b = jnp.mean(big_b, axis=0)
    mid_a = big_a - part_mean_a
    mid_b = big_b - part_mean_b
    square_a = jnp.sum(mid_a * mid_a, axis=0)
    square_b = jnp.sum(mid_b * mid_b, axis=0)
    cross = jnp.sum(mid_a * mid_b, axis=0)
    gram = dot(mid_a.astype(BF), mid_b.astype(BF), 0, 0).astype(BF)

    stats = [part_mean_a, square_a, part_mean_b, square_b, cross]
    stat_rows = stack_rows([p for s in stats for p in pieces(s, 3)], 16)
    got, got_stats = exchange(gram.reshape(y_n, sub, kt), stat_rows, ROWS)
    means_a, squares_a, means_b, squares_b, crosses = (
        joined(got_stats[:, 3 * i : 3 * i + 3]) for i in range(5)
    )

    def moments(means, squares):
        mean = jnp.mean(means, axis=0)
        off = means - mean
        var = (jnp.sum(squares, axis=0) + block * jnp.sum(off * off, axis=0)) / total
        return mean, off, lax.rsqrt(var + NORM_EPS)

    mean_a, off_a, inv_a = moments(means_a, squares_a)
    mean_b, off_b, inv_b = moments(means_b, squares_b)
    y_at = lax.axis_index("y")
    cols_at = lax.axis_index(COLS)
    tile_at = lax.axis_index(TILE)
    on_diag = (cols_at == tile_at).astype(F32)
    diag = (jnp.sum(crosses, axis=0) + block * jnp.sum(off_a * off_b, axis=0)) * (
        inv_a * inv_b / total
    )
    coeff = -2.0 * (1.0 - diag) - 2.0 * LAMBDA_OFF * diag

    start = y_at * sub
    off_a_sub = lax.dynamic_slice_in_dim(off_a, start, sub, 1)
    inv_a_sub = lax.dynamic_slice_in_dim(inv_a, start, sub, 0)
    corr = jnp.sum(got.astype(F32), axis=0) + block * lax.dot_general(
        off_a_sub,
        off_b,
        (((0,), (0,)), ((), ())),
        precision=lax.Precision.HIGHEST,
        preferred_element_type=F32,
    )
    corr = corr * (inv_a_sub[:, None] * inv_b[None, :] / total)
    k_of = lax.broadcasted_iota(jnp.int32, (sub, kt), 0) + start
    l_of = lax.broadcasted_iota(jnp.int32, (sub, kt), 1)
    here = (k_of == l_of) & (cols_at == tile_at)
    mix = jnp.where(here, coeff + 2.0 * LAMBDA_OFF * diag, 2.0 * LAMBDA_OFF * corr)
    mix = lax.all_gather(mix.astype(BF), ROWS, axis=0, tiled=True)

    mix32 = mix.astype(F32)
    k_of = lax.broadcasted_iota(jnp.int32, (kt, kt), 0)
    l_of = lax.broadcasted_iota(jnp.int32, (kt, kt), 1)
    here = (k_of == l_of) & (cols_at == tile_at)
    corr = jnp.where(here, diag, mix32 * (0.5 / LAMBDA_OFF))
    product = mix32 * corr
    second_a = jnp.sum(product, axis=1)
    second_b = jnp.sum(product, axis=0)
    power = jnp.sum(corr * corr, axis=1)
    norm_mean_a = block * jnp.sum(off_a, axis=0) * inv_a / total
    norm_mean_b = block * jnp.sum(off_b, axis=0) * inv_b / total
    first_a = jnp.sum(mix32 * norm_mean_b[None, :], axis=1)
    first_b = jnp.sum(mix32 * norm_mean_a[:, None], axis=0)

    norm_a = ((big_a - mean_a) * inv_a).astype(BF)
    norm_b = ((big_b - mean_b) * inv_b).astype(BF)
    grad_a = dot(norm_b, mix, 1, 1).astype(BF)
    grad_b = dot(norm_a, mix, 1, 0).astype(BF)

    tail_b = stack_rows(pieces(second_b, 3) + pieces(first_b, 2), 8)
    got_b, tail_b = exchange(grad_b.reshape(tile_n, rows, kt), tail_b, TILE)
    second_b = jnp.sum(joined(tail_b[:, 0:3]), axis=0)
    first_b = jnp.sum(joined(tail_b[:, 3:5]), axis=0)
    own_norm_b = ((own_b.astype(F32) - mean_b) * inv_b).astype(BF).astype(F32)
    grad_b = jnp.sum(got_b.astype(F32), axis=0)
    dz_b = (inv_b * (grad_b - first_b - own_norm_b * second_b)).astype(BF)
    dz_b = lax.ppermute(dz_b, all_axes, pairs)

    tail_a = stack_rows(
        pieces(second_a, 2) + pieces(power, 2) + pieces(diag * on_diag, 3) + pieces(first_a, 1), 8
    )
    got_a, tail_a = exchange(grad_a.reshape(cols_n, rows, kt), tail_a, COLS)
    second_a = jnp.sum(joined(tail_a[:, 0:2]), axis=0)
    power = jnp.sum(joined(tail_a[:, 2:4]))
    diag_corr = jnp.sum(joined(tail_a[:, 4:7]), axis=0)
    first_a = jnp.sum(joined(tail_a[:, 7:8]), axis=0)
    own_norm_a = ((raw_a.astype(F32) - mean_a) * inv_a).astype(BF).astype(F32)
    grad_a = jnp.sum(got_a.astype(F32), axis=0)
    dz_a = (inv_a * (grad_a - first_a - own_norm_a * second_a)).astype(BF)

    combined = keep_a * dot(dz_a, piece, 1, 1) + keep_b * dot(dz_b, piece, 1, 1)
    share = combined.astype(BF).reshape(rows, tile_n, width // tile_n).swapaxes(0, 1)
    power_rows = stack_rows(pieces(jnp.broadcast_to(power, (width // tile_n,)), 3), 8)
    got, power_rows = exchange(share, power_rows, TILE)
    feats_grad = (LOSS_SCALE / total) * jnp.sum(got.astype(F32), axis=0)
    cross_power = jnp.sum(joined(power_rows[:, 0:3])[:, 0]) / (kt * tile_n)
    return feats_grad, diag_corr, cross_power


def solution(mesh):
    fine = Mesh(mesh.devices.reshape(DP_SHAPE + TILE_SHAPE), DP + TILE)
    in_specs = (P(DP, None), P(DP, None), P(DP, None), P(DP, TILE))
    out_specs = (P(DP, TILE), P(TILE), P())
    return jax.shard_map(
        on_device, mesh=fine, in_specs=in_specs, out_specs=out_specs, check_vma=False
    )
```

time: 1040 us -> 279 us (0.27)
  waiting for transfers between devices: 606 us -> 87.8 us
  blocking collectives: 390 us -> 101 us
  starting transfers between devices: 0.2 us -> 41.9 us
  matrix products: 19.7 us -> 6.43 us
    all_gather x3 -> x1, waiting for transfers between devices: 480 us -> 44 us  [on_device(): piece = lax.all_gather(piece, 'y', axis=0, tiled=True)]
    psum x2 -> x0, blocking collectives: 390 us -> none  [the longest x1 201 us: on_device(): lax.psum((jnp.sum(grad_na, axis=0), jnp.sum(grad_na * za, axis=0), jnp.su...]
    all_gather x0 -> x6, blocking collectives: none -> 83.3 us  [the longest x1 20.8 us: on_device(): big_b = lax.all_gather(own_b, TILE, axis=0, tiled=True).astype(F32)]
    psum x1 -> x0, waiting for transfers between devices: 69.9 us -> none  [on_device(): lax.psum(contract_last(norm_b, whole_b).astype(jnp.bfloat16), 'tile')]
    reduce_scatter x1 -> x0, waiting for transfers between devices: 54.8 us -> none  [on_device(): lax.psum_scatter(combined.astype(jnp.bfloat16), 'tile', scatter_dimension...]
    all_to_all x0 -> x3, waiting for transfers between devices: none -> 40.2 us  [exchange(): lax.all_to_all(jnp.concatenate([blocks, tail], axis=1), axes, 0, 0, tiled...]
    all_to_all x0 -> x3, starting transfers between devices: none -> 26.4 us  [exchange(): lax.all_to_all(jnp.concatenate([blocks, tail], axis=1), axes, 0, 0, tiled...]
    all_to_all x0 -> x1, blocking collectives: none -> 17.6 us  [exchange(): lax.all_to_all(jnp.concatenate([blocks, tail], axis=1), axes, 0, 0, tiled...]
  transfers between devices with their start and end apart: 5 -> 6, of which waited for: 5 -> 6; matrix products, arithmetic and copies ran while one was open for 1% -> 2% of each run, Pallas kernels for 0% -> 0%
where the time goes in v1:
time: 279 us; the launch traced here: 278 us
  blocking collectives  101 us (36%)
  waiting for transfers between devices  87.8 us (31%)
  starting transfers between devices  41.9 us (15%)
  between operations  21.5 us (8%)
  other arithmetic  15.3 us (5%)
  matrix products  6.43 us (2%)
  local copies, waits for them, and re-layouts  3.97 us (1%)
    all_gather x1, waiting for transfers between devices, on_device(): piece = lax.all_gather(piece, 'y', axis=0, tiled=True)  44 us
    all_to_all x3, waiting for transfers between devices, exchange(): lax.all_to_all(jnp.concatenate([blocks, tail], axis=1), axes, 0, 0, tiled...  40.2 us
    all_to_all x3, starting transfers between devices, exchange(): lax.all_to_all(jnp.concatenate([blocks, tail], axis=1), axes, 0, 0, tiled...  26.4 us
    all_gather x1, blocking collectives, on_device(): big_b = lax.all_gather(own_b, TILE, axis=0, tiled=True).astype(F32)  20.8 us
    all_gather x1, blocking collectives, on_device(): mix = lax.all_gather(mix.astype(BF), ROWS, axis=0, tiled=True)  19.4 us
    all_to_all x1, blocking collectives, exchange(): lax.all_to_all(jnp.concatenate([blocks, tail], axis=1), axes, 0, 0, tiled...  17.6 us
    ppermute x1, starting transfers between devices, on_device(): own_b = lax.ppermute(raw_b, all_axes, pairs)  13.2 us
    all_gather x1, blocking collectives, on_device(): piece = lax.all_gather(piece, 'zh', axis=0, tiled=True)  12 us
  transfers between devices with their start and end apart: 6, of which 6 were waited for; matrix products, arithmetic and copies ran while one was open for 2% of the time, Pallas kernels for 0%

profile of v1, /device:TPU:1, one launch (start us, length us, event | category | flops | bytes accessed | tf_op | source)
XLA Modules:
  0.0 277.8 jit_solution(13339089672352820980)
XLA Ops:
  7.2 10.5 %all_gather.21 = bf16[128,512]{1,0:T(8,128)(2,1)S(1)} all-gather(bf16[32,512]{1,0:T(8,128)(2,1)} %param.7), channel_id=1, replica_groups=mesh['zh'=2,'x'=4,'y'=8,'zl'=4,'c'=2] {'x'}, dimensions={0}, use_global_device_ids=true | all-gather | bytes 163840 | tf_op jit(solution)/shard_map/all_gather | solution.py:95
  17.7 12.0 %all_gather.22 = bf16[256,512]{1,0:T(8,128)(2,1)} all-gather(bf16[128,512]{1,0:T(8,128)(2,1)S(1)} %all_gather.21), channel_id=1, replica_groups=mesh['zh'=2,'x'=4,'y'=8,'zl'=4,'c'=2] {'zh'}, dimensions={0}, use_global_device_ids=true | all-gather | bytes 393216 | tf_op jit(solution)/shard_map/all_gather | solution.py:96
  29.7 0.8 slice_bitcast_fusion
  30.5 1.3 fusion.27
  31.7 44.0 %all-gather.2.cloned.1.call-done = bf16[2048,512]{1,0:T(8,128)(2,1)} async-done(((bf16[256,512]{1,0:T(8,128)(2,1)}), bf16[2048,512]{1,0:T(8,128)(2,1)}) %all-gather.2.cloned.1.call-update) | async-done | bytes 2097168 | tf_op jit(solution)/shard_map/all_gather | solution.py:97
  75.7 1.8 copy.17
  77.6 0.5 convolution_convert_fusion.3
  78.1 10.3 %all_gather.24 = bf16[256,512]{1,0:T(8,128)(2,1)S(1)} all-gather(bf16[64,512]{1,0:T(8,128)(2,1)S(1)} %get-tuple-element.41), channel_id=1, replica_groups=mesh['zh'=2,'x'=4,'y'=8,'zl'=4,'c'=2] {'x'}, dimensions={0}, use_global_device_ids=true | all-gather | bytes 327680 | tf_op jit(solution)/shard_map/all_gather | solution.py:104
  88.4 10.3 %all_gather.25 = bf16[512,512]{1,0:T(8,128)(2,1)S(1)} all-gather(bf16[256,512]{1,0:T(8,128)(2,1)S(1)} %all_gather.24), channel_id=1, replica_groups=mesh['zh'=2,'x'=4,'y'=8,'zl'=4,'c'=2] {'zh'}, dimensions={0}, use_global_device_ids=true | all-gather | bytes 786432 | tf_op jit(solution)/shard_map/all_gather | solution.py:105
  98.7 0.1 convert_reduce_fusion.1
  98.8 13.2 %collective-permute-start = (bf16[64,512]{1,0:T(8,128)(2,1)S(1)}, bf16[64,512]{1,0:T(8,128)(2,1)S(1)}, u32[]{:S(2)}, u32[]{:S(2)}) collective-permute-start(bf16[64,512]{1,0:T(8,128)(2,1)S(1)} %get-tuple-element.40), channel_id=1, source_target_pairs={{0,0},{1,64},{2,128},{3,192},{4,256},{5,320},{6,384},{7,448},{8,8}... | collective-permute-start | bytes 196616 | tf_op jit(solution)/shard_map/ppermute | solution.py:103
  112.0 1.9 collective-permute-done
  114.0 20.8 %all_gather.26 = bf16[512,512]{1,0:T(8,128)(2,1)S(1)} all-gather(bf16[64,512]{1,0:T(8,128)(2,1)S(1)} %collective-permute-done), channel_id=1, replica_groups=mesh['zh'=2,'x'=4,'y'=8,'zl'=4,'c'=2] {'zl','c'}, dimensions={0}, use_global_device_ids=true | all-gather | bytes 589824 | tf_op jit(solution)/shard_map/all_gather | solution.py:106
  134.8 0.1 convert_reduce_fusion
  134.9 0.4 fusion.14
  135.3 1.3 convolution_convert_fusion.2
  136.6 0.1 concatenate.28
  136.7 1.9 pad_maximum_fusion
  138.6 4.2 %all-to-all-start = ((bf16[8,80,512]{2,1,0:T(8,128)(2,1)}), bf16[8,80,512]{2,1,0:T(8,128)(2,1)}, u32[]{:S(2)}, u32[]{:S(2)}) async-start(bf16[8,80,512]{2,1,0:T(8,128)(2,1)} %pad_maximum_fusion), calls=%async_computation | async-start | bytes 1310720 | tf_op jit(solution)/shard_map/all_to_all | solution.py:61
  142.9 20.8 %all-to-all-done = bf16[8,80,512]{2,1,0:T(8,128)(2,1)} async-done(((bf16[8,80,512]{2,1,0:T(8,128)(2,1)}), bf16[8,80,512]{2,1,0:T(8,128)(2,1)}, u32[]{:S(2)}, u32[]{:S(2)}) %all-to-all-start) | async-done | bytes 655392 | tf_op jit(solution)/shard_map/all_to_all | solution.py:61
  163.7 1.5 fusion.104
  165.2 1.0 fusion.106
  166.3 0.1 dynamic_slice.7
  166.4 1.1 convert_reduce_fusion.4
  167.5 0.4 fusion.11
  167.9 19.4 %all_gather.27 = bf16[512,512]{1,0:T(8,128)(2,1)S(1)} all-gather(bf16[64,512]{1,0:T(8,128)(2,1)S(1)} %fusion.11), channel_id=1, replica_groups=mesh['zh'=2,'x'=4,'y'=8,'zl'=4,'c'=2] {'y'}, dimensions={0}, use_global_device_ids=true | all-gather | bytes 589824 | tf_op jit(solution)/shard_map/all_gather | solution.py:156
  187.3 1.3 convolution_convert_fusion.1
  188.6 0.6 fusion.25
  189.4 1.9 pad_maximum_fusion.1
  191.3 8.9 %all-to-all-start.1 = ((bf16[8,72,512]{2,1,0:T(8,128)(2,1)}), bf16[8,72,512]{2,1,0:T(8,128)(2,1)S(1)}, u32[]{:S(2)}, u32[]{:S(2)}) async-start(bf16[8,72,512]{2,1,0:T(8,128)(2,1)} %pad_maximum_fusion.1), calls=%async_computation.1 | async-start | bytes 1179648 | tf_op jit(solution)/shard_map/all_to_all | solution.py:61
  200.2 1.5 convolution_convert_fusion
  201.7 0.9 pad_maximum_fusion.2
  202.6 9.0 %all-to-all-done.1 = bf16[8,72,512]{2,1,0:T(8,128)(2,1)S(1)} async-done(((bf16[8,72,512]{2,1,0:T(8,128)(2,1)}), bf16[8,72,512]{2,1,0:T(8,128)(2,1)S(1)}, u32[]{:S(2)}, u32[]{:S(2)}) %all-to-all-start.1) | async-done | bytes 589856 | tf_op jit(solution)/shard_map/all_to_all | solution.py:61
  211.6 13.4 %all-to-all-start.2 = ((bf16[8,72,512]{2,1,0:T(8,128)(2,1)}), bf16[8,72,512]{2,1,0:T(8,128)(2,1)}, u32[]{:S(2)}, u32[]{:S(2)}) async-start(bf16[8,72,512]{2,1,0:T(8,128)(2,1)} %pad_maximum_fusion.2), calls=%async_computation.2 | async-start | bytes 1179648 | tf_op jit(solution)/shard_map/all_to_all | solution.py:61
  225.0 0.7 fusion.71
  230.6 10.4 %all-to-all-done.2 = bf16[8,72,512]{2,1,0:T(8,128)(2,1)} async-done(((bf16[8,72,512]{2,1,0:T(8,128)(2,1)}), bf16[8,72,512]{2,1,0:T(8,128)(2,1)}, u32[]{:S(2)}, u32[]{:S(2)}) %all-to-all-start.2) | async-done | bytes 589856 | tf_op jit(solution)/shard_map/all_to_all | solution.py:61
  241.0 1.1 convert_reduce_fusion.2
  242.1 1.1 fusion.65
  243.3 2.2 collective-permute-start.1
  246.1 0.8 convolution_select_fusion.1
  246.9 0.7 maximum_maximum_fusion
  247.6 0.1 pad.1.clone
  247.7 1.7 collective-permute-done.1
  249.3 0.8 fusion.1
  250.1 0.1 pad_maximum_fusion.3
  250.2 17.6 %all_to_all.20 = bf16[8,72,256]{2,1,0:T(8,128)(2,1)S(1)} all-to-all(bf16[8,72,256]{2,1,0:T(8,128)(2,1)S(1)} %pad_maximum_fusion.3), channel_id=1, replica_groups=mesh['zh'=2,'x'=4,'y'=8,'zl'=4,'c'=2] {'zl','c'}, dimensions={0} | all-to-all | bytes 589824 | tf_op jit(solution)/shard_map/all_to_all | solution.py:61
  267.9 0.6 broadcast_multiply_fusion
  268.6 0.6 slice_reduce_fusion
  (41 shorter events, 0.6 us)
Async XLA Ops:
  7.2 68.6 %all-gather.2.cloned.1.call-start = ((), (), s32[]{:S(2)}) async-start(), calls=%async_computation.4 | async-start | bytes 2359296 | tf_op jit(solution)/shard_map/all_gather | solution.py:97
  98.8 15.2 %collective-permute-start = (bf16[64,512]{1,0:T(8,128)(2,1)S(1)}, bf16[64,512]{1,0:T(8,128)(2,1)S(1)}, u32[]{:S(2)}, u32[]{:S(2)}) collective-permute-start(bf16[64,512]{1,0:T(8,128)(2,1)S(1)} %get-tuple-element.40), channel_id=1, source_target_pairs={{0,0},{1,64},{2,128},{3,192},{4,256},{5,320},{6,384},{7,448},{8,8}... | collective-permute-start | bytes 196616 | tf_op jit(solution)/shard_map/ppermute | solution.py:103
  138.6 25.0 %all-to-all-start = ((bf16[8,80,512]{2,1,0:T(8,128)(2,1)}), bf16[8,80,512]{2,1,0:T(8,128)(2,1)}, u32[]{:S(2)}, u32[]{:S(2)}) async-start(bf16[8,80,512]{2,1,0:T(8,128)(2,1)} %pad_maximum_fusion), calls=%async_computation | async-start | bytes 1310720 | tf_op jit(solution)/shard_map/all_to_all | solution.py:61
  187.3 1.3 copy-start
  191.3 20.3 %all-to-all-start.1 = ((bf16[8,72,512]{2,1,0:T(8,128)(2,1)}), bf16[8,72,512]{2,1,0:T(8,128)(2,1)S(1)}, u32[]{:S(2)}, u32[]{:S(2)}) async-start(bf16[8,72,512]{2,1,0:T(8,128)(2,1)} %pad_maximum_fusion.1), calls=%async_computation.1 | async-start | bytes 1179648 | tf_op jit(solution)/shard_map/all_to_all | solution.py:61
  211.6 29.4 %all-to-all-start.2 = ((bf16[8,72,512]{2,1,0:T(8,128)(2,1)}), bf16[8,72,512]{2,1,0:T(8,128)(2,1)}, u32[]{:S(2)}, u32[]{:S(2)}) async-start(bf16[8,72,512]{2,1,0:T(8,128)(2,1)} %pad_maximum_fusion.2), calls=%async_computation.2 | async-start | bytes 1179648 | tf_op jit(solution)/shard_map/all_to_all | solution.py:61
  243.3 6.1 %collective-permute-start.1 = (bf16[64,512]{1,0:T(8,128)(2,1)S(1)}, bf16[64,512]{1,0:T(8,128)(2,1)S(1)}, u32[]{:S(2)}, u32[]{:S(2)}) collective-permute-start(bf16[64,512]{1,0:T(8,128)(2,1)S(1)} %multiply_convert_fusion), channel_id=1, source_target_pairs={{0,0},{1,64},{2,128},{3,192},{4,256},{5,320},{6,384},{7,448},{8,8}... | collective-permute-start | bytes 196616 | tf_op jit(solution)/shard_map/ppermute | solution.py:184
Sparse Core Ops, SparseCore 0:
  29.8 45.8 all-gather.1

commit v2 on v1

--- a/solution.py
+++ b/solution.py
@@ -60,6 +60,50 @@
     tail = jnp.broadcast_to(extra[None], (parts,) + extra.shape)
     got = lax.all_to_all(jnp.concatenate([blocks, tail], axis=1), axes, 0, 0, tiled=True)
     return got[:, : blocks.shape[1]], got[:, blocks.shape[1] :]
+
+
+def spread(value, axes):
+    parts = lax.axis_size(axes)
+    return lax.all_to_all(
+        jnp.broadcast_to(value[None], (parts,) + value.shape), axes, 0, 0, tiled=True
+    ).reshape((parts * value.shape[0],) + value.shape[1:])
+
+
+def pick(blocks, at, axis):
+    return lax.dynamic_index_in_dim(blocks, at, axis, keepdims=False)
+
+
+def fold_core(blocks, tail, counts):
+    at = lax.axis_index("c")
+    own_tail = [pieces(r, n) for r, n in zip(tail, counts)]
+    rows, width = blocks.shape[2:]
+    sent = pick(blocks, 1 - at, 1).astype(BF).reshape(-1, width)
+    sent = jnp.concatenate([sent, stack_rows([p for ps in own_tail for p in ps], 8)], axis=0)
+    got = lax.ppermute(sent, "c", [(0, 1), (1, 0)])
+    main = pick(blocks, at, 1) + got[: -8].reshape(-1, rows, width).astype(F32)
+    out, start = [], got.shape[0] - 8
+    for ps in own_tail:
+        theirs = joined(got[start : start + len(ps)])
+        out.append(joined(jnp.stack(ps)) + theirs)
+        start += len(ps)
+    return main, out
+
+
+def fold_line(blocks, tail, counts):
+    at = lax.axis_index("zl")
+    n = blocks.shape[0]
+    rows = blocks.shape[1]
+    tail_rows = stack_rows([p for r, k in zip(tail, counts) for p in pieces(r, k)], 8)
+    main, out = pick(blocks, at, 0), list(tail)
+    for step in range(1, n):
+        sent = jnp.concatenate([pick(blocks, at ^ step, 0).astype(BF), tail_rows], axis=0)
+        got = lax.ppermute(sent, "zl", [(i, i ^ step) for i in range(n)])
+        main = main + got[:rows].astype(F32)
+        start = rows
+        for i, k in enumerate(counts):
+            out[i] = out[i] + joined(got[start : start + k])
+            start += k
+    return main, out
 
 
 def swap_pairs():
@@ -92,17 +136,15 @@
     all_axes = DP + TILE
     pairs = swap_pairs()
 
-    piece = lax.all_gather(weight, "x", axis=0, tiled=True)
-    piece = lax.all_gather(piece, "zh", axis=0, tiled=True)
-    piece = lax.all_gather(piece, "y", axis=0, tiled=True)
-    piece = piece.reshape(y_n, cols_n, -1, kt).swapaxes(0, 1).reshape(width, kt)
+    piece = lax.all_gather(weight, "zh", axis=0, tiled=True)
+    piece = spread(spread(piece, "y"), "x")
+    piece = piece.reshape(x_n, y_n, zh_n, -1, kt).transpose(2, 0, 1, 3, 4).reshape(width, kt)
 
     raw = dot(jnp.concatenate([view_a, view_b], axis=0), piece, 1, 0).astype(BF)
     raw_a, raw_b = raw[:rows], raw[rows:]
 
     own_b = lax.ppermute(raw_b, all_axes, pairs)
-    big_a = lax.all_gather(raw_a, "x", axis=0, tiled=True)
-    big_a = lax.all_gather(big_a, "zh", axis=0, tiled=True).astype(F32)
+    big_a = spread(raw_a, COLS).astype(F32)
     big_b = lax.all_gather(own_b, TILE, axis=0, tiled=True).astype(F32)
 
     part_mean_a = jnp.mean(big_a, axis=0)
@@ -153,7 +195,7 @@
     l_of = lax.broadcasted_iota(jnp.int32, (sub, kt), 1)
     here = (k_of == l_of) & (cols_at == tile_at)
     mix = jnp.where(here, coeff + 2.0 * LAMBDA_OFF * diag, 2.0 * LAMBDA_OFF * corr)
-    mix = lax.all_gather(mix.astype(BF), ROWS, axis=0, tiled=True)
+    mix = spread(mix.astype(BF), ROWS)
 
     mix32 = mix.astype(F32)
     k_of = lax.broadcasted_iota(jnp.int32, (kt, kt), 0)
@@ -172,14 +214,13 @@
     norm_a = ((big_a - mean_a) * inv_a).astype(BF)
     norm_b = ((big_b - mean_b) * inv_b).astype(BF)
     grad_a = dot(norm_b, mix, 1, 1).astype(BF)
-    grad_b = dot(norm_a, mix, 1, 0).astype(BF)
-
-    tail_b = stack_rows(pieces(second_b, 3) + pieces(first_b, 2), 8)
-    got_b, tail_b = exchange(grad_b.reshape(tile_n, rows, kt), tail_b, TILE)
-    second_b = jnp.sum(joined(tail_b[:, 0:3]), axis=0)
-    first_b = jnp.sum(joined(tail_b[:, 3:5]), axis=0)
+    grad_b = dot(norm_a, mix, 1, 0)
+
+    grad_b, tail_b = fold_core(
+        grad_b.reshape(TILE_SHAPE + (rows, kt)), (second_b, first_b), (3, 2)
+    )
+    grad_b, (second_b, first_b) = fold_line(grad_b, tail_b, (3, 2))
     own_norm_b = ((own_b.astype(F32) - mean_b) * inv_b).astype(BF).astype(F32)
-    grad_b = jnp.sum(got_b.astype(F32), axis=0)
     dz_b = (inv_b * (grad_b - first_b - own_norm_b * second_b)).astype(BF)
     dz_b = lax.ppermute(dz_b, all_axes, pairs)
 
@@ -196,9 +237,9 @@
     dz_a = (inv_a * (grad_a - first_a - own_norm_a * second_a)).astype(BF)
 
     combined = keep_a * dot(dz_a, piece, 1, 1) + keep_b * dot(dz_b, piece, 1, 1)
-    share = combined.astype(BF).reshape(rows, tile_n, width // tile_n).swapaxes(0, 1)
-    power_rows = stack_rows(pieces(jnp.broadcast_to(power, (width // tile_n,)), 3), 8)
-    got, power_rows = exchange(share, power_rows, TILE)
+    share = combined.reshape((rows,) + TILE_SHAPE + (width // tile_n,)).transpose(1, 2, 0, 3)
+    share, (power,) = fold_core(share, (jnp.broadcast_to(power, (width // tile_n,)),), (3,))
+    got, power_rows = exchange(share.astype(BF), stack_rows(pieces(power, 3), 8), "zl")
     feats_grad = (LOSS_SCALE / total) * jnp.sum(got.astype(F32), axis=0)
     cross_power = jnp.sum(joined(power_rows[:, 0:3])[:, 0]) / (kt * tile_n)
     return feats_grad, diag_corr, cross_power

time: 279 us -> 247 us (0.89)
  blocking collectives: 101 us -> 68.7 us
  waiting for transfers between devices: 87.8 us -> 73.4 us
  local copies, waits for them, and re-layouts: 3.97 us -> 16.6 us
  between operations: 21.5 us -> 9.17 us
  starting transfers between devices: 41.9 us -> 51.2 us
  other arithmetic: 15.3 us -> 18.7 us
    all_gather x5 -> x1, blocking collectives: 62.5 us -> 11.8 us  [on_device(): piece = lax.all_gather(weight, 'zh', axis=0, tiled=True)]
    all_gather x1 -> x0, waiting for transfers between devices: 44 us -> none  [on_device(): piece = lax.all_gather(piece, 'y', axis=0, tiled=True)]
    all_to_all x0 -> x3, waiting for transfers between devices: none -> 38.4 us  [spread(): lax.all_to_all(jnp.broadcast_to(value[None], (parts,) + value.shape), axe...]
    all_to_all x0 -> x1, blocking collectives: none -> 21.4 us  [spread(): lax.all_to_all(jnp.broadcast_to(value[None], (parts,) + value.shape), axe...]
    all_to_all x3 -> x2, waiting for transfers between devices: 40.2 us -> 20.4 us  [exchange(): lax.all_to_all(jnp.concatenate([blocks, tail], axis=1), axes, 0, 0, tiled...]
    all_to_all x3 -> x2, starting transfers between devices: 26.4 us -> 9.55 us  [exchange(): lax.all_to_all(jnp.concatenate([blocks, tail], axis=1), axes, 0, 0, tiled...]
    all_to_all x0 -> x3, starting transfers between devices: none -> 15.5 us  [spread(): lax.all_to_all(jnp.broadcast_to(value[None], (parts,) + value.shape), axe...]
    ppermute x0 -> x5, starting transfers between devices: none -> 13.7 us  [the longest x3 9.38 us: fold_line(): got = lax.ppermute(sent, 'zl', [(i, i ^ step) for i in range(n)])]
  transfers between devices with their start and end apart: 6 -> 12, of which waited for: 6 -> 7; matrix products, arithmetic and copies ran while one was open for 2% -> 6% of each run, Pallas kernels for 0% -> 0%
where the time goes in v2:
time: 247 us; the launch traced here: 245 us
  waiting for transfers between devices  73.4 us (30%)
  blocking collectives  68.7 us (28%)
  starting transfers between devices  51.2 us (21%)
  other arithmetic  18.7 us (8%)
  local copies, waits for them, and re-layouts  16.6 us (7%)
  between operations  9.17 us (4%)
  matrix products  7.38 us (3%)
    all_to_all x3, waiting for transfers between devices, spread(): lax.all_to_all(jnp.broadcast_to(value[None], (parts,) + value.shape), axe...  38.4 us
    all_gather x1, blocking collectives, on_device(): big_b = lax.all_gather(own_b, TILE, axis=0, tiled=True).astype(F32)  24.1 us
    all_to_all x1, blocking collectives, spread(): lax.all_to_all(jnp.broadcast_to(value[None], (parts,) + value.shape), axe...  21.4 us
    all_to_all x2, waiting for transfers between devices, exchange(): lax.all_to_all(jnp.concatenate([blocks, tail], axis=1), axes, 0, 0, tiled...  20.4 us
    all_to_all x3, starting transfers between devices, spread(): lax.all_to_all(jnp.broadcast_to(value[None], (parts,) + value.shape), axe...  15.5 us
    all_gather x1, blocking collectives, on_device(): piece = lax.all_gather(weight, 'zh', axis=0, tiled=True)  11.8 us
    all_to_all x1, blocking collectives, exchange(): lax.all_to_all(jnp.concatenate([blocks, tail], axis=1), axes, 0, 0, tiled...  11.4 us
    ppermute x3, waiting for transfers between devices, fold_line(): got = lax.ppermute(sent, 'zl', [(i, i ^ step) for i in range(n)])  11.1 us
  transfers between devices with their start and end apart: 12, of which 7 were waited for; matrix products, arithmetic and copies ran while one was open for 6% of the time, Pallas kernels for 0%

profile of v2, /device:TPU:1, one launch (start us, length us, event | category | flops | bytes accessed | tf_op | source)
XLA Modules:
  0.0 245.1 jit_solution(4491066622135891763)
XLA Ops:
  0.6 11.8 %all_gather.6 = bf16[64,512]{1,0:T(8,128)(2,1)S(1)} all-gather(bf16[32,512]{1,0:T(8,128)(2,1)} %param.7), channel_id=1, replica_groups=mesh['zh'=2,'x'=4,'y'=8,'zl'=4,'c'=2] {'zh'}, dimensions={0}, use_global_device_ids=true | all-gather | bytes 98304 | tf_op jit(solution)/shard_map/all_gather | solution.py:139
  12.5 21.4 %all_to_all.35 = bf16[8,64,512]{2,1,0:T(8,128)(2,1)S(1)} all-to-all(bf16[8,64,512]{2,1,0:T(8,128)(2,1)S(1)} %broadcast_in_dim.34), channel_id=1, replica_groups=mesh['zh'=2,'x'=4,'y'=8,'zl'=4,'c'=2] {'y'}, dimensions={0} | all-to-all | bytes 1048576 | tf_op jit(solution)/shard_map/all_to_all | solution.py:67
  33.9 1.5 broadcast_in_dim.36
  35.4 4.1 %all-to-all-start.1 = ((bf16[4,512,512]{2,1,0:T(8,128)(2,1)}), bf16[4,512,512]{2,1,0:T(8,128)(2,1)S(1)}, u32[]{:S(2)}, u32[]{:S(2)}) async-start(bf16[4,512,512]{2,1,0:T(8,128)(2,1)} %broadcast_in_dim.36), calls=%async_computation.1 | async-start | bytes 4194304 | tf_op jit(solution)/shard_map/all_to_all | solution.py:67
  39.9 22.1 %all-to-all-done.1 = bf16[4,512,512]{2,1,0:T(8,128)(2,1)S(1)} async-done(((bf16[4,512,512]{2,1,0:T(8,128)(2,1)}), bf16[4,512,512]{2,1,0:T(8,128)(2,1)S(1)}, u32[]{:S(2)}, u32[]{:S(2)}) %all-to-all-start.1) | async-done | bytes 2097184 | tf_op jit(solution)/shard_map/all_to_all | solution.py:67
  61.9 1.3 copy-done
  63.3 1.7 copy.15
  65.5 0.8 broadcast_in_dim.37
  66.4 7.2 %all-to-all-start.2 = ((bf16[8,64,512]{2,1,0:T(8,128)(2,1)}), bf16[8,64,512]{2,1,0:T(8,128)(2,1)S(1)}, u32[]{:S(2)}, u32[]{:S(2)}) async-start(bf16[8,64,512]{2,1,0:T(8,128)(2,1)} %broadcast_in_dim.37), calls=%async_computation.2 | async-start | bytes 1048576 | tf_op jit(solution)/shard_map/all_to_all | solution.py:67
  73.6 8.8 %collective-permute-start = (bf16[64,512]{1,0:T(8,128)(2,1)S(1)}, bf16[64,512]{1,0:T(8,128)(2,1)S(1)}, u32[]{:S(2)}, u32[]{:S(2)}) collective-permute-start(bf16[64,512]{1,0:T(8,128)(2,1)S(1)} %get-tuple-element.51), channel_id=1, source_target_pairs={{0,0},{1,64},{2,128},{3,192},{4,256},{5,320},{6,384},{7,448},{8,8}... | collective-permute-start | bytes 196616 | tf_op jit(solution)/shard_map/ppermute | solution.py:146
  82.4 3.2 %collective-permute-done = bf16[64,512]{1,0:T(8,128)(2,1)S(1)} collective-permute-done((bf16[64,512]{1,0:T(8,128)(2,1)S(1)}, bf16[64,512]{1,0:T(8,128)(2,1)S(1)}, u32[]{:S(2)}, u32[]{:S(2)}) %collective-permute-start) | collective-permute-done | bytes 65568 | tf_op jit(solution)/shard_map/ppermute | solution.py:146
  86.2 24.1 %all_gather.7 = bf16[512,512]{1,0:T(8,128)(2,1)S(1)} all-gather(bf16[64,512]{1,0:T(8,128)(2,1)S(1)} %collective-permute-done), channel_id=1, replica_groups=mesh['zh'=2,'x'=4,'y'=8,'zl'=4,'c'=2] {'zl','c'}, dimensions={0}, use_global_device_ids=true | all-gather | bytes 589824 | tf_op jit(solution)/shard_map/all_gather | solution.py:148
  110.9 1.3 convolution_convert_fusion.1
  112.5 2.0 pad_maximum_fusion
  114.5 5.3 %all-to-all-start.3 = ((bf16[8,80,512]{2,1,0:T(8,128)(2,1)}), bf16[8,80,512]{2,1,0:T(8,128)(2,1)}, u32[]{:S(2)}, u32[]{:S(2)}) async-start(bf16[8,80,512]{2,1,0:T(8,128)(2,1)} %pad_maximum_fusion), calls=%async_computation.3 | async-start | bytes 1310720 | tf_op jit(solution)/shard_map/all_to_all | solution.py:61
  120.3 20.4 %all-to-all-done.3 = bf16[8,80,512]{2,1,0:T(8,128)(2,1)} async-done(((bf16[8,80,512]{2,1,0:T(8,128)(2,1)}), bf16[8,80,512]{2,1,0:T(8,128)(2,1)}, u32[]{:S(2)}, u32[]{:S(2)}) %all-to-all-start.3) | async-done | bytes 655392 | tf_op jit(solution)/shard_map/all_to_all | solution.py:61
  140.7 1.9 fusion.132
  142.6 1.1 fusion.134
  145.0 1.1 convert_reduce_fusion.2
  146.1 1.0 fusion.8
  147.1 0.8 broadcast_in_dim.41
  148.0 4.1 %all-to-all-start.4 = ((bf16[8,64,512]{2,1,0:T(8,128)(2,1)}), bf16[8,64,512]{2,1,0:T(8,128)(2,1)}, u32[]{:S(2)}, u32[]{:S(2)}) async-start(bf16[8,64,512]{2,1,0:T(8,128)(2,1)} %broadcast_in_dim.41), calls=%async_computation.4 | async-start | bytes 1048576 | tf_op jit(solution)/shard_map/all_to_all | solution.py:67
  152.8 0.9 multiply_convert_fusion
  153.8 16.3 %all-to-all-done.4 = bf16[8,64,512]{2,1,0:T(8,128)(2,1)} async-done(((bf16[8,64,512]{2,1,0:T(8,128)(2,1)}), bf16[8,64,512]{2,1,0:T(8,128)(2,1)}, u32[]{:S(2)}, u32[]{:S(2)}) %all-to-all-start.4) | async-done | bytes 524320 | tf_op jit(solution)/shard_map/all_to_all | solution.py:67
  170.1 1.8 fusion.19
  172.5 1.6 fusion.136
  174.1 1.0 copy-done.1
  175.2 1.4 concatenate.45
  176.6 2.4 collective-permute-start.1
  179.6 1.5 convolution_convert_fusion
  181.2 0.8 broadcast_in_dim.43
  182.0 0.9 pad_maximum_fusion.1
  182.8 4.2 %all-to-all-start.5 = ((bf16[8,72,512]{2,1,0:T(8,128)(2,1)}), bf16[8,72,512]{2,1,0:T(8,128)(2,1)}, u32[]{:S(2)}, u32[]{:S(2)}) async-start(bf16[8,72,512]{2,1,0:T(8,128)(2,1)} %pad_maximum_fusion.1), calls=%async_computation.5 | async-start | bytes 1179648 | tf_op jit(solution)/shard_map/all_to_all | solution.py:61
  187.2 0.8 fusion.101
  188.1 0.7 concatenate.48
  188.8 5.3 %collective-permute-start.4 = (bf16[72,512]{1,0:T(8,128)(2,1)S(1)}, bf16[72,512]{1,0:T(8,128)(2,1)S(1)}, u32[]{:S(2)}, u32[]{:S(2)}) collective-permute-start(bf16[72,512]{1,0:T(8,128)(2,1)S(1)} %concatenate.48), channel_id=1, source_target_pairs={{0,6},{2,4},{4,2},{6,0},{1,7},{3,5},{5,3},{7,1},{8,14},{10,12},{12... | collective-permute-start | bytes 221192 | tf_op jit(solution)/shard_map/ppermute | solution.py:100
  194.8 1.9 collective-permute-start.3
  197.5 2.2 collective-permute-start.2
  199.7 4.3 %collective-permute-done.4 = bf16[72,512]{1,0:T(8,128)(2,1)S(1)} collective-permute-done((bf16[72,512]{1,0:T(8,128)(2,1)S(1)}, bf16[72,512]{1,0:T(8,128)(2,1)S(1)}, u32[]{:S(2)}, u32[]{:S(2)}) %collective-permute-start.4) | collective-permute-done | bytes 73760 | tf_op jit(solution)/shard_map/ppermute | solution.py:100
  204.0 6.8 %collective-permute-done.3 = bf16[72,512]{1,0:T(8,128)(2,1)S(1)} collective-permute-done((bf16[72,512]{1,0:T(8,128)(2,1)S(1)}, bf16[72,512]{1,0:T(8,128)(2,1)S(1)}, u32[]{:S(2)}, u32[]{:S(2)}) %collective-permute-start.3) | collective-permute-done | bytes 73760 | tf_op jit(solution)/shard_map/ppermute | solution.py:100
  210.8 1.0 fusion.40
  211.8 3.6 %collective-permute-start.5 = (bf16[64,512]{1,0:T(8,128)(2,1)S(1)}, bf16[64,512]{1,0:T(8,128)(2,1)S(1)}, u32[]{:S(2)}, u32[]{:S(2)}) collective-permute-start(bf16[64,512]{1,0:T(8,128)(2,1)S(1)} %fusion.40), channel_id=1, source_target_pairs={{0,0},{1,64},{2,128},{3,192},{4,256},{5,320},{6,384},{7,448},{8,8}... | collective-permute-start | bytes 196616 | tf_op jit(solution)/shard_map/ppermute | solution.py:225
  215.5 1.1 convert_reduce_fusion.1
  216.6 2.3 fusion.67
  218.9 0.8 convolution_select_fusion.1
  224.6 0.8 fusion
  227.3 1.9 collective-permute-start.6
  230.7 11.4 %all_to_all.36 = bf16[4,72,256]{2,1,0:T(8,128)(2,1)S(1)} all-to-all(bf16[4,72,256]{2,1,0:T(8,128)(2,1)S(1)} %pad_maximum_fusion.2), channel_id=1, replica_groups=mesh['zh'=2,'x'=4,'y'=8,'zl'=4,'c'=2] {'zl'}, dimensions={0} | all-to-all | bytes 294912 | tf_op jit(solution)/shard_map/all_to_all | solution.py:61
  (133 shorter events, 11.1 us)
Async XLA Ops:
  35.4 4.2 %copy-start.28 = (s32[64,2]{0,1:T(2,128)S(1)}, s32[64,2]{0,1:T(2,128)}, u32[]{:S(2)}) copy-start(s32[64,2]{0,1:T(2,128)} %param.6) | copy-start | bytes 1540
  35.4 4.2 %copy-start.4 = (bf16[64,2048]{1,0:T(8,128)(2,1)S(1)}, bf16[64,2048]{1,0:T(8,128)(2,1)}, u32[]{:S(2)}) copy-start(bf16[64,2048]{1,0:T(8,128)(2,1)} %param.4) | copy-start | bytes 786436
  35.4 4.2 %copy-start.5 = (bf16[64,2048]{1,0:T(8,128)(2,1)S(1)}, bf16[64,2048]{1,0:T(8,128)(2,1)}, u32[]{:S(2)}) copy-start(bf16[64,2048]{1,0:T(8,128)(2,1)} %param.5) | copy-start | bytes 786436
  35.4 26.5 %all-to-all-start.1 = ((bf16[4,512,512]{2,1,0:T(8,128)(2,1)}), bf16[4,512,512]{2,1,0:T(8,128)(2,1)S(1)}, u32[]{:S(2)}, u32[]{:S(2)}) async-start(bf16[4,512,512]{2,1,0:T(8,128)(2,1)} %broadcast_in_dim.36), calls=%async_computation.1 | async-start | bytes 4194304 | tf_op jit(solution)/shard_map/all_to_all | solution.py:67
  39.6 25.5 %copy-start.24 = (s32[64]{0:T(128)}, s32[64]{0:T(128)S(1)}, u32[]{:S(2)}) copy-start(s32[64]{0:T(128)S(1)} %get-tuple-element.85) | copy-start | bytes 772
  39.6 25.5 %copy-start.26 = (s32[64]{0:T(128)}, s32[64]{0:T(128)S(1)}, u32[]{:S(2)}) copy-start(s32[64]{0:T(128)S(1)} %get-tuple-element.84) | copy-start | bytes 772
  61.9 1.4 copy-start
  66.4 44.1 %all-to-all-start.2 = ((bf16[8,64,512]{2,1,0:T(8,128)(2,1)}), bf16[8,64,512]{2,1,0:T(8,128)(2,1)S(1)}, u32[]{:S(2)}, u32[]{:S(2)}) async-start(bf16[8,64,512]{2,1,0:T(8,128)(2,1)} %broadcast_in_dim.37), calls=%async_computation.2 | async-start | bytes 1048576 | tf_op jit(solution)/shard_map/all_to_all | solution.py:67
  73.6 12.0 %collective-permute-start = (bf16[64,512]{1,0:T(8,128)(2,1)S(1)}, bf16[64,512]{1,0:T(8,128)(2,1)S(1)}, u32[]{:S(2)}, u32[]{:S(2)}) collective-permute-start(bf16[64,512]{1,0:T(8,128)(2,1)S(1)} %get-tuple-element.51), channel_id=1, source_target_pairs={{0,0},{1,64},{2,128},{3,192},{4,256},{5,320},{6,384},{7,448},{8,8}... | collective-permute-start | bytes 196616 | tf_op jit(solution)/shard_map/ppermute | solution.py:146
  85.6 0.6 copy-start.6
  114.5 26.2 %all-to-all-start.3 = ((bf16[8,80,512]{2,1,0:T(8,128)(2,1)}), bf16[8,80,512]{2,1,0:T(8,128)(2,1)}, u32[]{:S(2)}, u32[]{:S(2)}) async-start(bf16[8,80,512]{2,1,0:T(8,128)(2,1)} %pad_maximum_fusion), calls=%async_computation.3 | async-start | bytes 1310720 | tf_op jit(solution)/shard_map/all_to_all | solution.py:61
  142.6 11.2 %copy-start.14 = (f32[512]{0:T(512)}, f32[512]{0:T(512)S(1)}, u32[]{:S(2)}) copy-start(f32[512]{0:T(512)S(1)} %broadcast_multiply_fusion.2) | copy-start | bytes 6148
  143.7 28.2 %copy-start.8 = (f32[512]{0:T(512)}, f32[512]{0:T(512)S(1)}, u32[]{:S(2)}) copy-start(f32[512]{0:T(512)S(1)} %broadcast_multiply_fusion.3) | copy-start | bytes 6148
  144.9 8.9 %copy-start.17 = (f32[512]{0:T(512)}, f32[512]{0:T(512)S(1)}, u32[]{:S(2)}) copy-start(f32[512]{0:T(512)S(1)} %get-tuple-element.31) | copy-start | bytes 6148
  144.9 27.0 %copy-start.10 = (f32[512]{0:T(512)}, f32[512]{0:T(512)S(1)}, u32[]{:S(2)}) copy-start(f32[512]{0:T(512)S(1)} %get-tuple-element.30) | copy-start | bytes 6148
  144.9 7.2 %copy-start.19 = (f32[512]{0:T(512)S(1)}, f32[512]{0:T(512)}, u32[]{:S(2)}) copy-start(f32[512]{0:T(512)} %get-tuple-element.20) | copy-start | bytes 6148
  144.9 7.3 %copy-start.23 = (f32[512]{0:T(512)S(1)}, f32[512]{0:T(512)}, u32[]{:S(2)}) copy-start(f32[512]{0:T(512)} %get-tuple-element.28) | copy-start | bytes 6148
  148.0 22.1 %all-to-all-start.4 = ((bf16[8,64,512]{2,1,0:T(8,128)(2,1)}), bf16[8,64,512]{2,1,0:T(8,128)(2,1)}, u32[]{:S(2)}, u32[]{:S(2)}) async-start(bf16[8,64,512]{2,1,0:T(8,128)(2,1)} %broadcast_in_dim.41), calls=%async_computation.4 | async-start | bytes 1048576 | tf_op jit(solution)/shard_map/all_to_all | solution.py:67
  153.8 25.2 %copy-start.20 = (bf16[1,512]{1,0:T(2,128)(2,1)S(1)}, bf16[1,512]{1,0:T(2,128)(2,1)}, u32[]{:S(2)}) copy-start(bf16[1,512]{1,0:T(2,128)(2,1)} %get-tuple-element.60) | copy-start | bytes 3076
  153.8 25.2 %copy-start.21 = (bf16[1,512]{1,0:T(2,128)(2,1)S(1)}, bf16[1,512]{1,0:T(2,128)(2,1)}, u32[]{:S(2)}) copy-start(bf16[1,512]{1,0:T(2,128)(2,1)} %get-tuple-element.61) | copy-start | bytes 3076
  153.8 25.2 %copy-start.22 = (bf16[1,512]{1,0:T(2,128)(2,1)S(1)}, bf16[1,512]{1,0:T(2,128)(2,1)}, u32[]{:S(2)}) copy-start(bf16[1,512]{1,0:T(2,128)(2,1)} %get-tuple-element.62) | copy-start | bytes 3076
  170.1 9.6 %copy-start.15 = (f32[512]{0:T(512)S(1)}, f32[512]{0:T(512)}, u32[]{:S(2)}) copy-start(f32[512]{0:T(512)} %copy-done.14) | copy-start | bytes 6148
  170.1 9.6 %copy-start.18 = (f32[512]{0:T(512)S(1)}, f32[512]{0:T(512)}, u32[]{:S(2)}) copy-start(f32[512]{0:T(512)} %copy-done.17) | copy-start | bytes 6148
  171.9 0.6 copy-start.16
  171.9 3.3 %copy-start.12 = (f32[512]{0:T(512)}, f32[512]{0:T(512)S(1)}, u32[]{:S(2)}) copy-start(f32[512]{0:T(512)S(1)} %get-tuple-element.15) | copy-start | bytes 6148
  172.5 2.7 %copy-start.13 = (bf16[1,512]{1,0:T(2,128)(2,1)}, bf16[1,512]{1,0:T(2,128)(2,1)S(1)}, u32[]{:S(2)}) copy-start(bf16[1,512]{1,0:T(2,128)(2,1)S(1)} %get-tuple-element.55) | copy-start | bytes 3076
  174.1 1.0 copy-start.1
  175.2 4.4 %copy-start.7 = (bf16[3,512]{1,0:T(4,128)(2,1)}, bf16[3,512]{1,0:T(4,128)(2,1)S(1)}, u32[]{:S(2)}) copy-start(bf16[3,512]{1,0:T(4,128)(2,1)S(1)} %broadcast.496) | copy-start | bytes 9220
  176.6 10.5 %collective-permute-start.1 = (bf16[264,512]{1,0:T(8,128)(2,1)}, bf16[264,512]{1,0:T(8,128)(2,1)S(1)}, u32[]{:S(2)}, u32[]{:S(2)}) collective-permute-start(bf16[264,512]{1,0:T(8,128)(2,1)} %concatenate.45), channel_id=1, source_target_pairs={{0,1},{1,0},{2,3},{3,2},{4,5},{5,4},{6,7},{7,6},{8,9},{9,8},{10,11... | collective-permute-start | bytes 811016 | tf_op jit(solution)/shard_map/ppermute | solution.py:82
  181.2 5.9 %copy-start.2 = (f32[4,2,64,512]{3,2,1,0:T(8,128)S(1)}, f32[4,2,64,512]{3,2,1,0:T(8,128)}, u32[]{:S(2)}) copy-start(f32[4,2,64,512]{3,2,1,0:T(8,128)} %copy-done.1) | copy-start | bytes 3145732
  182.8 32.6 %all-to-all-start.5 = ((bf16[8,72,512]{2,1,0:T(8,128)(2,1)}), bf16[8,72,512]{2,1,0:T(8,128)(2,1)}, u32[]{:S(2)}, u32[]{:S(2)}) async-start(bf16[8,72,512]{2,1,0:T(8,128)(2,1)} %pad_maximum_fusion.1), calls=%async_computation.5 | async-start | bytes 1179648 | tf_op jit(solution)/shard_map/all_to_all | solution.py:61
  187.2 0.8 copy-start.3
  187.2 31.7 %copy-start.9 = (f32[512]{0:T(512)S(1)}, f32[512]{0:T(512)}, u32[]{:S(2)}) copy-start(f32[512]{0:T(512)} %copy-done.8) | copy-start | bytes 6148
  187.2 31.7 %copy-start.11 = (f32[512]{0:T(512)S(1)}, f32[512]{0:T(512)}, u32[]{:S(2)}) copy-start(f32[512]{0:T(512)} %copy-done.10) | copy-start | bytes 6148
  187.2 31.7 %copy-start.25 = (s32[64]{0:T(128)S(1)}, s32[64]{0:T(128)}, u32[]{:S(2)}) copy-start(s32[64]{0:T(128)} %copy-done.24) | copy-start | bytes 772
  188.8 15.2 %collective-permute-start.4 = (bf16[72,512]{1,0:T(8,128)(2,1)S(1)}, bf16[72,512]{1,0:T(8,128)(2,1)S(1)}, u32[]{:S(2)}, u32[]{:S(2)}) collective-permute-start(bf16[72,512]{1,0:T(8,128)(2,1)S(1)} %concatenate.48), channel_id=1, source_target_pairs={{0,6},{2,4},{4,2},{6,0},{1,7},{3,5},{5,3},{7,1},{8,14},{10,12},{12... | collective-permute-start | bytes 221192 | tf_op jit(solution)/shard_map/ppermute | solution.py:100
  194.8 16.0 %collective-permute-start.3 = (bf16[72,512]{1,0:T(8,128)(2,1)S(1)}, bf16[72,512]{1,0:T(8,128)(2,1)S(1)}, u32[]{:S(2)}, u32[]{:S(2)}) collective-permute-start(bf16[72,512]{1,0:T(8,128)(2,1)S(1)} %concatenate.47), channel_id=1, source_target_pairs={{0,4},{2,6},{4,0},{6,2},{1,5},{3,7},{5,1},{7,3},{8,12},{10,14},{12... | collective-permute-start | bytes 221192 | tf_op jit(solution)/shard_map/ppermute | solution.py:100
  197.4 27.1 %copy-start.27 = (s32[64]{0:T(128)S(1)}, s32[64]{0:T(128)}, u32[]{:S(2)}) copy-start(s32[64]{0:T(128)} %copy-done.26) | copy-start | bytes 772
  197.5 13.3 %collective-permute-start.2 = (bf16[72,512]{1,0:T(8,128)(2,1)S(1)}, bf16[72,512]{1,0:T(8,128)(2,1)S(1)}, u32[]{:S(2)}, u32[]{:S(2)}) collective-permute-start(bf16[72,512]{1,0:T(8,128)(2,1)S(1)} %concatenate.46), channel_id=1, source_target_pairs={{0,2},{2,0},{4,6},{6,4},{1,3},{3,1},{5,7},{7,5},{8,10},{10,8},{12,... | collective-permute-start | bytes 221192 | tf_op jit(solution)/shard_map/ppermute | solution.py:100
  211.8 12.8 %collective-permute-start.5 = (bf16[64,512]{1,0:T(8,128)(2,1)S(1)}, bf16[64,512]{1,0:T(8,128)(2,1)S(1)}, u32[]{:S(2)}, u32[]{:S(2)}) collective-permute-start(bf16[64,512]{1,0:T(8,128)(2,1)S(1)} %fusion.40), channel_id=1, source_target_pairs={{0,0},{1,64},{2,128},{3,192},{4,256},{5,320},{6,384},{7,448},{8,8}... | collective-permute-start | bytes 196616 | tf_op jit(solution)/shard_map/ppermute | solution.py:225
  227.3 3.2 %collective-permute-start.6 = (bf16[264,256]{1,0:T(8,128)(2,1)S(1)}, bf16[264,256]{1,0:T(8,128)(2,1)S(1)}, u32[]{:S(2)}, u32[]{:S(2)}) collective-permute-start(bf16[264,256]{1,0:T(8,128)(2,1)S(1)} %concatenate.49), channel_id=1, source_target_pairs={{0,1},{1,0},{2,3},{3,2},{4,5},{5,4},{6,7},{7,6},{8,9},{9,8},{10,11... | collective-permute-start | bytes 405512 | tf_op jit(solution)/shard_map/ppermute | solution.py:82

commit v3 on v2

--- a/solution.py
+++ b/solution.py
@@ -12,8 +12,8 @@
 DP_SHAPE = (2, 4, 8)
 TILE_SHAPE = (4, 2)
 DP = ("zh", "x", "y")
-ROWS = "y"
-COLS = ("zh", "x")
+ROWS = ("x", "zh")
+COLS = "y"
 TILE = ("zl", "c")
 BF = jnp.bfloat16
 F32 = jnp.float32
@@ -107,15 +107,11 @@
 
 
 def swap_pairs():
-    y_n = DP_SHAPE[2]
-    cols_n = DP_SHAPE[0] * DP_SHAPE[1]
-    tile_n = TILE_SHAPE[0] * TILE_SHAPE[1]
-    where = lambda c, y, t: (c * y_n + y) * tile_n + t
+    rows_n = DP_SHAPE[0] * DP_SHAPE[1]
+    n = DP_SHAPE[2]
+    where = lambda r, y, t: (r * n + y) * n + t
     return [
-        (where(c, y, t), where(t, y, c))
-        for c in range(cols_n)
-        for y in range(y_n)
-        for t in range(tile_n)
+        (where(r, y, t), where(r, t, y)) for r in range(rows_n) for y in range(n) for t in range(n)
     ]
 
 
@@ -128,11 +124,11 @@
     rows, width = feats.shape
     kt = weight.shape[1]
     zh_n, x_n, y_n = DP_SHAPE
-    cols_n = zh_n * x_n
+    rows_n = zh_n * x_n
     tile_n = TILE_SHAPE[0] * TILE_SHAPE[1]
-    total = rows * cols_n * y_n
-    block = rows * cols_n
-    sub = kt // y_n
+    total = rows * rows_n * y_n
+    block = rows * y_n
+    sub = kt // rows_n
     all_axes = DP + TILE
     pairs = swap_pairs()
 
@@ -158,7 +154,10 @@
 
     stats = [part_mean_a, square_a, part_mean_b, square_b, cross]
     stat_rows = stack_rows([p for s in stats for p in pieces(s, 3)], 16)
-    got, got_stats = exchange(gram.reshape(y_n, sub, kt), stat_rows, ROWS)
+    got, got_stats = exchange(gram.reshape(x_n, zh_n * sub, kt), stat_rows, "x")
+    got = jnp.sum(got.astype(F32), axis=0).astype(BF).reshape(zh_n, sub, kt)
+    got, got_stats = exchange(got, got_stats.reshape(-1, kt), "zh")
+    got_stats = got_stats.reshape(rows_n, 16, kt)
     means_a, squares_a, means_b, squares_b, crosses = (
         joined(got_stats[:, 3 * i : 3 * i + 3]) for i in range(5)
     )
@@ -171,7 +170,6 @@
 
     mean_a, off_a, inv_a = moments(means_a, squares_a)
     mean_b, off_b, inv_b = moments(means_b, squares_b)
-    y_at = lax.axis_index("y")
     cols_at = lax.axis_index(COLS)
     tile_at = lax.axis_index(TILE)
     on_diag = (cols_at == tile_at).astype(F32)
@@ -180,7 +178,7 @@
     )
     coeff = -2.0 * (1.0 - diag) - 2.0 * LAMBDA_OFF * diag
 
-    start = y_at * sub
+    start = lax.axis_index(ROWS) * sub
     off_a_sub = lax.dynamic_slice_in_dim(off_a, start, sub, 1)
     inv_a_sub = lax.dynamic_slice_in_dim(inv_a, start, sub, 0)
     corr = jnp.sum(got.astype(F32), axis=0) + block * lax.dot_general(
@@ -195,7 +193,7 @@
     l_of = lax.broadcasted_iota(jnp.int32, (sub, kt), 1)
     here = (k_of == l_of) & (cols_at == tile_at)
     mix = jnp.where(here, coeff + 2.0 * LAMBDA_OFF * diag, 2.0 * LAMBDA_OFF * corr)
-    mix = spread(mix.astype(BF), ROWS)
+    mix = spread(lax.all_gather(mix.astype(BF), "zh", axis=0, tiled=True), "x")
 
     mix32 = mix.astype(F32)
     k_of = lax.broadcasted_iota(jnp.int32, (kt, kt), 0)
@@ -227,7 +225,7 @@
     tail_a = stack_rows(
         pieces(second_a, 2) + pieces(power, 2) + pieces(diag * on_diag, 3) + pieces(first_a, 1), 8
     )
-    got_a, tail_a = exchange(grad_a.reshape(cols_n, rows, kt), tail_a, COLS)
+    got_a, tail_a = exchange(grad_a.reshape(y_n, rows, kt), tail_a, COLS)
     second_a = jnp.sum(joined(tail_a[:, 0:2]), axis=0)
     power = jnp.sum(joined(tail_a[:, 2:4]))
     diag_corr = jnp.sum(joined(tail_a[:, 4:7]), axis=0)

time: 247 us -> 237 us (0.960)
  waiting for transfers between devices: 73.4 us -> 46.1 us
  blocking collectives: 68.7 us -> 86.6 us
  starting transfers between devices: 51.2 us -> 55.9 us
  local copies, waits for them, and re-layouts: 16.6 us -> 12.7 us
    all_to_all x1 -> x2, blocking collectives: 11.4 us -> 25.2 us  [exchange(): lax.all_to_all(jnp.concatenate([blocks, tail], axis=1), axes, 0, 0, tiled...]
    all_to_all x2, waiting for transfers between devices: 20.4 us -> 6.89 us  [exchange(): lax.all_to_all(jnp.concatenate([blocks, tail], axis=1), axes, 0, 0, tiled...]
    all_to_all x3, waiting for transfers between devices: 38.4 us -> 27.4 us  [spread(): lax.all_to_all(jnp.broadcast_to(value[None], (parts,) + value.shape), axe...]
    all_gather x0 -> x1, blocking collectives: none -> 7.7 us  [on_device(): mix = spread(lax.all_gather(mix.astype(BF), 'zh', axis=0, tiled=True), 'x')]
    ppermute x3, waiting for transfers between devices: 11.1 us -> 4.47 us  [fold_line(): got = lax.ppermute(sent, 'zl', [(i, i ^ step) for i in range(n)])]
    ppermute x2, starting transfers between devices: 4.3 us -> 9.6 us  [fold_core(): got = lax.ppermute(sent, 'c', [(0, 1), (1, 0)])]
    ppermute x1, waiting for transfers between devices: 3.18 us -> 6.93 us  [on_device(): own_b = lax.ppermute(raw_b, all_axes, pairs)]
    all_gather x1, blocking collectives: 24.1 us -> 20.6 us  [on_device(): big_b = lax.all_gather(own_b, TILE, axis=0, tiled=True).astype(F32)]
where the time goes in v3:
time: 237 us; the launch traced here: 235 us
  blocking collectives  86.6 us (37%)
  starting transfers between devices  55.9 us (24%)
  waiting for transfers between devices  46.1 us (19%)
  other arithmetic  16.7 us (7%)
  local copies, waits for them, and re-layouts  12.7 us (5%)
  between operations  9.2 us (4%)
  matrix products  8.12 us (3%)
    all_to_all x3, waiting for transfers between devices, spread(): lax.all_to_all(jnp.broadcast_to(value[None], (parts,) + value.shape), axe...  27.4 us
    all_to_all x2, blocking collectives, exchange(): lax.all_to_all(jnp.concatenate([blocks, tail], axis=1), axes, 0, 0, tiled...  25.2 us
    all_to_all x1, blocking collectives, spread(): lax.all_to_all(jnp.broadcast_to(value[None], (parts,) + value.shape), axe...  21.4 us
    all_gather x1, blocking collectives, on_device(): big_b = lax.all_gather(own_b, TILE, axis=0, tiled=True).astype(F32)  20.6 us
    all_to_all x3, starting transfers between devices, spread(): lax.all_to_all(jnp.broadcast_to(value[None], (parts,) + value.shape), axe...  13.9 us
    all_to_all x2, starting transfers between devices, exchange(): lax.all_to_all(jnp.concatenate([blocks, tail], axis=1), axes, 0, 0, tiled...  12.6 us
    all_gather x1, blocking collectives, on_device(): piece = lax.all_gather(weight, 'zh', axis=0, tiled=True)  11.8 us
    ppermute x2, starting transfers between devices, fold_core(): got = lax.ppermute(sent, 'c', [(0, 1), (1, 0)])  9.6 us
  transfers between devices with their start and end apart: 12, of which 7 were waited for; matrix products, arithmetic and copies ran while one was open for 6% of the time, Pallas kernels for 0%

profile of v3, /device:TPU:1, one launch (start us, length us, event | category | flops | bytes accessed | tf_op | source)
XLA Modules:
  0.0 235.3 jit_solution(8993324243626547701)
XLA Ops:
  0.6 11.8 %all_gather.9 = bf16[64,512]{1,0:T(8,128)(2,1)S(1)} all-gather(bf16[32,512]{1,0:T(8,128)(2,1)} %param.7), channel_id=1, replica_groups=mesh['zh'=2,'x'=4,'y'=8,'zl'=4,'c'=2] {'zh'}, dimensions={0}, use_global_device_ids=true | all-gather | bytes 98304 | tf_op jit(solution)/shard_map/all_gather | solution.py:135
  12.5 21.4 %all_to_all.40 = bf16[8,64,512]{2,1,0:T(8,128)(2,1)S(1)} all-to-all(bf16[8,64,512]{2,1,0:T(8,128)(2,1)S(1)} %broadcast_in_dim.38), channel_id=1, replica_groups=mesh['zh'=2,'x'=4,'y'=8,'zl'=4,'c'=2] {'y'}, dimensions={0} | all-to-all | bytes 1048576 | tf_op jit(solution)/shard_map/all_to_all | solution.py:67
  33.9 1.5 broadcast_in_dim.40
  35.4 4.1 %all-to-all-start.1 = ((bf16[4,512,512]{2,1,0:T(8,128)(2,1)}), bf16[4,512,512]{2,1,0:T(8,128)(2,1)S(1)}, u32[]{:S(2)}, u32[]{:S(2)}) async-start(bf16[4,512,512]{2,1,0:T(8,128)(2,1)} %broadcast_in_dim.40), calls=%async_computation.1 | async-start | bytes 4194304 | tf_op jit(solution)/shard_map/all_to_all | solution.py:67
  39.9 22.1 %all-to-all-done.1 = bf16[4,512,512]{2,1,0:T(8,128)(2,1)S(1)} async-done(((bf16[4,512,512]{2,1,0:T(8,128)(2,1)}), bf16[4,512,512]{2,1,0:T(8,128)(2,1)S(1)}, u32[]{:S(2)}, u32[]{:S(2)}) %all-to-all-start.1) | async-done | bytes 2097184 | tf_op jit(solution)/shard_map/all_to_all | solution.py:67
  61.9 1.3 copy-done
  63.3 1.8 copy.34
  65.6 0.8 broadcast_in_dim.41
  66.4 5.7 %all-to-all-start.2 = ((bf16[8,64,512]{2,1,0:T(8,128)(2,1)}), bf16[8,64,512]{2,1,0:T(8,128)(2,1)S(1)}, u32[]{:S(2)}, u32[]{:S(2)}) async-start(bf16[8,64,512]{2,1,0:T(8,128)(2,1)} %broadcast_in_dim.41), calls=%async_computation.2 | async-start | bytes 1048576 | tf_op jit(solution)/shard_map/all_to_all | solution.py:67
  72.1 6.5 %collective-permute-start = (bf16[64,512]{1,0:T(8,128)(2,1)S(1)}, bf16[64,512]{1,0:T(8,128)(2,1)S(1)}, u32[]{:S(2)}, u32[]{:S(2)}) collective-permute-start(bf16[64,512]{1,0:T(8,128)(2,1)S(1)} %get-tuple-element.54), channel_id=1, source_target_pairs={{0,0},{1,8},{2,16},{3,24},{4,32},{5,40},{6,48},{7,56},{8,1},{9,9},... | collective-permute-start | bytes 196616 | tf_op jit(solution)/shard_map/ppermute | solution.py:142
  78.7 6.9 %collective-permute-done = bf16[64,512]{1,0:T(8,128)(2,1)S(1)} collective-permute-done((bf16[64,512]{1,0:T(8,128)(2,1)S(1)}, bf16[64,512]{1,0:T(8,128)(2,1)S(1)}, u32[]{:S(2)}, u32[]{:S(2)}) %collective-permute-start) | collective-permute-done | bytes 65568 | tf_op jit(solution)/shard_map/ppermute | solution.py:142
  85.6 20.6 %all_gather.10 = bf16[512,512]{1,0:T(8,128)(2,1)S(1)} all-gather(bf16[64,512]{1,0:T(8,128)(2,1)S(1)} %collective-permute-done), channel_id=1, replica_groups=mesh['zh'=2,'x'=4,'y'=8,'zl'=4,'c'=2] {'zl','c'}, dimensions={0}, use_global_device_ids=true | all-gather | bytes 589824 | tf_op jit(solution)/shard_map/all_gather | solution.py:144
  106.7 1.3 convolution_convert_fusion.1
  108.3 1.1 pad_maximum_fusion
  109.4 12.5 %all_to_all.41 = bf16[4,144,512]{2,1,0:T(8,128)(2,1)S(1)} all-to-all(bf16[4,144,512]{2,1,0:T(8,128)(2,1)S(1)} %pad_maximum_fusion), channel_id=1, replica_groups=mesh['zh'=2,'x'=4,'y'=8,'zl'=4,'c'=2] {'x'}, dimensions={0} | all-to-all | bytes 1179648 | tf_op jit(solution)/shard_map/all_to_all | solution.py:61
  122.1 0.7 pad_maximum_fusion.2
  122.8 6.5 %all-to-all-start.4 = ((bf16[2,128,512]{2,1,0:T(8,128)(2,1)}), bf16[2,128,512]{2,1,0:T(8,128)(2,1)S(1)}, u32[]{:S(2)}, u32[]{:S(2)}) async-start(bf16[2,128,512]{2,1,0:T(8,128)(2,1)} %pad_maximum_fusion.2), calls=%async_computation.4 | async-start | bytes 524288 | tf_op jit(solution)/shard_map/all_to_all | solution.py:61
  130.4 6.9 %all-to-all-done.4 = bf16[2,128,512]{2,1,0:T(8,128)(2,1)S(1)} async-done(((bf16[2,128,512]{2,1,0:T(8,128)(2,1)}), bf16[2,128,512]{2,1,0:T(8,128)(2,1)S(1)}, u32[]{:S(2)}, u32[]{:S(2)}) %all-to-all-start.4) | async-done | bytes 262176 | tf_op jit(solution)/shard_map/all_to_all | solution.py:61
  139.7 1.1 fusion.8
  140.8 7.7 %all_gather.11 = bf16[128,512]{1,0:T(8,128)(2,1)S(1)} all-gather(bf16[64,512]{1,0:T(8,128)(2,1)S(1)} %fusion.8), channel_id=1, replica_groups=mesh['zh'=2,'x'=4,'y'=8,'zl'=4,'c'=2] {'zh'}, dimensions={0}, use_global_device_ids=true | all-gather | bytes 196608 | tf_op jit(solution)/shard_map/all_gather | solution.py:196
  148.5 0.8 broadcast_in_dim.47
  149.3 4.1 %all-to-all-start.5 = ((bf16[4,128,512]{2,1,0:T(8,128)(2,1)}), bf16[4,128,512]{2,1,0:T(8,128)(2,1)}, u32[]{:S(2)}, u32[]{:S(2)}) async-start(bf16[4,128,512]{2,1,0:T(8,128)(2,1)} %broadcast_in_dim.47), calls=%async_computation.5 | async-start | bytes 1048576 | tf_op jit(solution)/shard_map/all_to_all | solution.py:67
  153.5 0.7 multiply_multiply_fusion
  154.2 0.9 multiply_convert_fusion
  155.2 5.3 %all-to-all-done.5 = bf16[4,128,512]{2,1,0:T(8,128)(2,1)} async-done(((bf16[4,128,512]{2,1,0:T(8,128)(2,1)}), bf16[4,128,512]{2,1,0:T(8,128)(2,1)}, u32[]{:S(2)}, u32[]{:S(2)}) %all-to-all-start.5) | async-done | bytes 524320 | tf_op jit(solution)/shard_map/all_to_all | solution.py:67
  160.5 1.8 fusion.19
  162.3 1.6 fusion.128
  164.0 1.0 copy-done.1
  165.0 1.4 concatenate.49
  166.4 7.7 %collective-permute-start.1 = (bf16[264,512]{1,0:T(8,128)(2,1)}, bf16[264,512]{1,0:T(8,128)(2,1)}, u32[]{:S(2)}, u32[]{:S(2)}) collective-permute-start(bf16[264,512]{1,0:T(8,128)(2,1)} %concatenate.49), channel_id=1, source_target_pairs={{0,1},{1,0},{2,3},{3,2},{4,5},{5,4},{6,7},{7,6},{8,9},{9,8},{10,11... | collective-permute-start | bytes 811016 | tf_op jit(solution)/shard_map/ppermute | solution.py:82
  174.2 1.5 convolution_convert_fusion
  175.7 0.9 pad_maximum_fusion.1
  176.6 6.1 %all-to-all-start.6 = ((bf16[8,72,512]{2,1,0:T(8,128)(2,1)}), bf16[8,72,512]{2,1,0:T(8,128)(2,1)}, u32[]{:S(2)}, u32[]{:S(2)}) async-start(bf16[8,72,512]{2,1,0:T(8,128)(2,1)} %pad_maximum_fusion.1), calls=%async_computation.6 | async-start | bytes 1179648 | tf_op jit(solution)/shard_map/all_to_all | solution.py:61
  182.7 1.0 slice.358
  183.7 1.0 fusion.92
  184.8 3.7 %collective-permute-start.4 = (bf16[72,512]{1,0:T(8,128)(2,1)S(1)}, bf16[72,512]{1,0:T(8,128)(2,1)S(1)}, u32[]{:S(2)}, u32[]{:S(2)}) collective-permute-start(bf16[72,512]{1,0:T(8,128)(2,1)S(1)} %concatenate.52), channel_id=1, source_target_pairs={{0,6},{2,4},{4,2},{6,0},{1,7},{3,5},{5,3},{7,1},{8,14},{10,12},{12... | collective-permute-start | bytes 221192 | tf_op jit(solution)/shard_map/ppermute | solution.py:100
  188.6 3.3 %collective-permute-start.3 = (bf16[72,512]{1,0:T(8,128)(2,1)S(1)}, bf16[72,512]{1,0:T(8,128)(2,1)S(1)}, u32[]{:S(2)}, u32[]{:S(2)}) collective-permute-start(bf16[72,512]{1,0:T(8,128)(2,1)S(1)} %concatenate.51), channel_id=1, source_target_pairs={{0,4},{2,6},{4,0},{6,2},{1,5},{3,7},{5,1},{7,3},{8,12},{10,14},{12... | collective-permute-start | bytes 221192 | tf_op jit(solution)/shard_map/ppermute | solution.py:100
  192.0 2.2 collective-permute-start.2
  194.2 2.9 %collective-permute-done.3 = bf16[72,512]{1,0:T(8,128)(2,1)S(1)} collective-permute-done((bf16[72,512]{1,0:T(8,128)(2,1)S(1)}, bf16[72,512]{1,0:T(8,128)(2,1)S(1)}, u32[]{:S(2)}, u32[]{:S(2)}) %collective-permute-start.3) | collective-permute-done | bytes 73760 | tf_op jit(solution)/shard_map/ppermute | solution.py:100
  197.2 1.5 collective-permute-done.2
  198.7 1.0 fusion.40
  199.7 4.0 %collective-permute-start.5 = (bf16[64,512]{1,0:T(8,128)(2,1)S(1)}, bf16[64,512]{1,0:T(8,128)(2,1)S(1)}, u32[]{:S(2)}, u32[]{:S(2)}) collective-permute-start(bf16[64,512]{1,0:T(8,128)(2,1)S(1)} %fusion.40), channel_id=1, source_target_pairs={{0,0},{1,8},{2,16},{3,24},{4,32},{5,40},{6,48},{7,56},{8,1},{9,9},... | collective-permute-start | bytes 196616 | tf_op jit(solution)/shard_map/ppermute | solution.py:223
  203.7 1.1 convert_reduce_fusion.1
  204.9 2.3 fusion.58
  207.1 1.4 convolution_select_fusion.1
  213.5 0.8 fusion
  216.2 1.9 collective-permute-start.6
  219.6 12.6 %all_to_all.42 = bf16[4,72,256]{2,1,0:T(8,128)(2,1)S(1)} all-to-all(bf16[4,72,256]{2,1,0:T(8,128)(2,1)S(1)} %pad_maximum_fusion.3), channel_id=1, replica_groups=mesh['zh'=2,'x'=4,'y'=8,'zl'=4,'c'=2] {'zl'}, dimensions={0} | all-to-all | bytes 294912 | tf_op jit(solution)/shard_map/all_to_all | solution.py:61
  (126 shorter events, 9.1 us)
Async XLA Ops:
  35.4 4.2 %copy-start.21 = (s32[64,2]{0,1:T(2,128)S(1)}, s32[64,2]{0,1:T(2,128)}, u32[]{:S(2)}) copy-start(s32[64,2]{0,1:T(2,128)} %param.6) | copy-start | bytes 1540
  35.4 4.2 %copy-start.4 = (bf16[64,2048]{1,0:T(8,128)(2,1)S(1)}, bf16[64,2048]{1,0:T(8,128)(2,1)}, u32[]{:S(2)}) copy-start(bf16[64,2048]{1,0:T(8,128)(2,1)} %param.4) | copy-start | bytes 786436
  35.4 4.2 %copy-start.5 = (bf16[64,2048]{1,0:T(8,128)(2,1)S(1)}, bf16[64,2048]{1,0:T(8,128)(2,1)}, u32[]{:S(2)}) copy-start(bf16[64,2048]{1,0:T(8,128)(2,1)} %param.5) | copy-start | bytes 786436
  35.4 26.5 %all-to-all-start.1 = ((bf16[4,512,512]{2,1,0:T(8,128)(2,1)}), bf16[4,512,512]{2,1,0:T(8,128)(2,1)S(1)}, u32[]{:S(2)}, u32[]{:S(2)}) async-start(bf16[4,512,512]{2,1,0:T(8,128)(2,1)} %broadcast_in_dim.40), calls=%async_computation.1 | async-start | bytes 4194304 | tf_op jit(solution)/shard_map/all_to_all | solution.py:67
  39.6 25.6 %copy-start.18 = (s32[64]{0:T(128)}, s32[64]{0:T(128)S(1)}, u32[]{:S(2)}) copy-start(s32[64]{0:T(128)S(1)} %get-tuple-element.88) | copy-start | bytes 772
  39.6 25.6 %copy-start.19 = (s32[64]{0:T(128)}, s32[64]{0:T(128)S(1)}, u32[]{:S(2)}) copy-start(s32[64]{0:T(128)S(1)} %get-tuple-element.87) | copy-start | bytes 772
  61.9 1.4 copy-start
  66.4 39.8 %all-to-all-start.2 = ((bf16[8,64,512]{2,1,0:T(8,128)(2,1)}), bf16[8,64,512]{2,1,0:T(8,128)(2,1)S(1)}, u32[]{:S(2)}, u32[]{:S(2)}) async-start(bf16[8,64,512]{2,1,0:T(8,128)(2,1)} %broadcast_in_dim.41), calls=%async_computation.2 | async-start | bytes 1048576 | tf_op jit(solution)/shard_map/all_to_all | solution.py:67
  72.1 13.5 %collective-permute-start = (bf16[64,512]{1,0:T(8,128)(2,1)S(1)}, bf16[64,512]{1,0:T(8,128)(2,1)S(1)}, u32[]{:S(2)}, u32[]{:S(2)}) collective-permute-start(bf16[64,512]{1,0:T(8,128)(2,1)S(1)} %get-tuple-element.54), channel_id=1, source_target_pairs={{0,0},{1,8},{2,16},{3,24},{4,32},{5,40},{6,48},{7,56},{8,1},{9,9},... | collective-permute-start | bytes 196616 | tf_op jit(solution)/shard_map/ppermute | solution.py:142
  85.6 22.4 %copy-start.6 = (bf16[64,512]{1,0:T(8,128)(2,1)}, bf16[64,512]{1,0:T(8,128)(2,1)S(1)}, u32[]{:S(2)}) copy-start(bf16[64,512]{1,0:T(8,128)(2,1)S(1)} %collective-permute-done) | copy-start | bytes 196612
  122.8 14.6 %all-to-all-start.4 = ((bf16[2,128,512]{2,1,0:T(8,128)(2,1)}), bf16[2,128,512]{2,1,0:T(8,128)(2,1)S(1)}, u32[]{:S(2)}, u32[]{:S(2)}) async-start(bf16[2,128,512]{2,1,0:T(8,128)(2,1)} %pad_maximum_fusion.2), calls=%async_computation.4 | async-start | bytes 524288 | tf_op jit(solution)/shard_map/all_to_all | solution.py:61
  137.6 3.1 %copy-start.9 = (f32[512]{0:T(512)}, f32[512]{0:T(512)S(1)}, u32[]{:S(2)}) copy-start(f32[512]{0:T(512)S(1)} %broadcast_multiply_fusion.2) | copy-start | bytes 6148
  139.0 0.6 copy-start.13
  139.0 1.8 copy-start.11
  139.0 25.0 %copy-start.8 = (f32[512]{0:T(512)}, f32[512]{0:T(512)S(1)}, u32[]{:S(2)}) copy-start(f32[512]{0:T(512)S(1)} %get-tuple-element.27) | copy-start | bytes 6148
  139.6 13.8 %copy-start.16 = (f32[512]{0:T(512)S(1)}, f32[512]{0:T(512)}, u32[]{:S(2)}) copy-start(f32[512]{0:T(512)} %get-tuple-element.17) | copy-start | bytes 6148
  139.7 13.8 %copy-start.17 = (f32[512]{0:T(512)S(1)}, f32[512]{0:T(512)}, u32[]{:S(2)}) copy-start(f32[512]{0:T(512)} %get-tuple-element.25) | copy-start | bytes 6148
  139.7 13.8 %copy-start.15 = (f32[512]{0:T(512)S(1)}, f32[512]{0:T(512)}, u32[]{:S(2)}) copy-start(f32[512]{0:T(512)} %get-tuple-element.14) | copy-start | bytes 6148
  139.7 20.8 %copy-start.14 = (f32[512]{0:T(512)S(1)}, f32[512]{0:T(512)}, u32[]{:S(2)}) copy-start(f32[512]{0:T(512)} %copy-done.13) | copy-start | bytes 6148
  149.3 11.1 %all-to-all-start.5 = ((bf16[4,128,512]{2,1,0:T(8,128)(2,1)}), bf16[4,128,512]{2,1,0:T(8,128)(2,1)}, u32[]{:S(2)}, u32[]{:S(2)}) async-start(bf16[4,128,512]{2,1,0:T(8,128)(2,1)} %broadcast_in_dim.47), calls=%async_computation.5 | async-start | bytes 1048576 | tf_op jit(solution)/shard_map/all_to_all | solution.py:67
  155.1 19.0 %copy-start.10 = (f32[512]{0:T(512)S(1)}, f32[512]{0:T(512)}, u32[]{:S(2)}) copy-start(f32[512]{0:T(512)} %copy-done.9) | copy-start | bytes 6148
  155.1 19.0 %copy-start.12 = (f32[512]{0:T(512)S(1)}, f32[512]{0:T(512)}, u32[]{:S(2)}) copy-start(f32[512]{0:T(512)} %copy-done.11) | copy-start | bytes 6148
  164.0 1.0 copy-start.1
  166.4 16.3 %collective-permute-start.1 = (bf16[264,512]{1,0:T(8,128)(2,1)}, bf16[264,512]{1,0:T(8,128)(2,1)}, u32[]{:S(2)}, u32[]{:S(2)}) collective-permute-start(bf16[264,512]{1,0:T(8,128)(2,1)} %concatenate.49), channel_id=1, source_target_pairs={{0,1},{1,0},{2,3},{3,2},{4,5},{5,4},{6,7},{7,6},{8,9},{9,8},{10,11... | collective-permute-start | bytes 811016 | tf_op jit(solution)/shard_map/ppermute | solution.py:82
  175.7 7.9 %copy-start.2 = (f32[4,2,64,512]{3,2,1,0:T(8,128)S(1)}, f32[4,2,64,512]{3,2,1,0:T(8,128)}, u32[]{:S(2)}) copy-start(f32[4,2,64,512]{3,2,1,0:T(8,128)} %copy-done.1) | copy-start | bytes 3145732
  176.6 22.1 %copy-start.7 = (bf16[64,512]{1,0:T(8,128)(2,1)S(1)}, bf16[64,512]{1,0:T(8,128)(2,1)}, u32[]{:S(2)}) copy-start(bf16[64,512]{1,0:T(8,128)(2,1)} %copy-done.6) | copy-start | bytes 196612
  176.6 27.1 %all-to-all-start.6 = ((bf16[8,72,512]{2,1,0:T(8,128)(2,1)}), bf16[8,72,512]{2,1,0:T(8,128)(2,1)}, u32[]{:S(2)}, u32[]{:S(2)}) async-start(bf16[8,72,512]{2,1,0:T(8,128)(2,1)} %pad_maximum_fusion.1), calls=%async_computation.6 | async-start | bytes 1179648 | tf_op jit(solution)/shard_map/all_to_all | solution.py:61
  183.7 1.0 copy-start.3
  184.8 9.4 %collective-permute-start.4 = (bf16[72,512]{1,0:T(8,128)(2,1)S(1)}, bf16[72,512]{1,0:T(8,128)(2,1)S(1)}, u32[]{:S(2)}, u32[]{:S(2)}) collective-permute-start(bf16[72,512]{1,0:T(8,128)(2,1)S(1)} %concatenate.52), channel_id=1, source_target_pairs={{0,6},{2,4},{4,2},{6,0},{1,7},{3,5},{5,3},{7,1},{8,14},{10,12},{12... | collective-permute-start | bytes 221192 | tf_op jit(solution)/shard_map/ppermute | solution.py:100
  188.6 8.5 %collective-permute-start.3 = (bf16[72,512]{1,0:T(8,128)(2,1)S(1)}, bf16[72,512]{1,0:T(8,128)(2,1)S(1)}, u32[]{:S(2)}, u32[]{:S(2)}) collective-permute-start(bf16[72,512]{1,0:T(8,128)(2,1)S(1)} %concatenate.51), channel_id=1, source_target_pairs={{0,4},{2,6},{4,0},{6,2},{1,5},{3,7},{5,1},{7,3},{8,12},{10,14},{12... | collective-permute-start | bytes 221192 | tf_op jit(solution)/shard_map/ppermute | solution.py:100
  192.0 21.5 %copy-start.20 = (s32[64]{0:T(128)S(1)}, s32[64]{0:T(128)}, u32[]{:S(2)}) copy-start(s32[64]{0:T(128)} %copy-done.19) | copy-start | bytes 772
  192.0 6.7 %collective-permute-start.2 = (bf16[72,512]{1,0:T(8,128)(2,1)S(1)}, bf16[72,512]{1,0:T(8,128)(2,1)S(1)}, u32[]{:S(2)}, u32[]{:S(2)}) collective-permute-start(bf16[72,512]{1,0:T(8,128)(2,1)S(1)} %concatenate.50), channel_id=1, source_target_pairs={{0,2},{2,0},{4,6},{6,4},{1,3},{3,1},{5,7},{7,5},{8,10},{10,8},{12,... | collective-permute-start | bytes 221192 | tf_op jit(solution)/shard_map/ppermute | solution.py:100
  199.7 13.8 %collective-permute-start.5 = (bf16[64,512]{1,0:T(8,128)(2,1)S(1)}, bf16[64,512]{1,0:T(8,128)(2,1)S(1)}, u32[]{:S(2)}, u32[]{:S(2)}) collective-permute-start(bf16[64,512]{1,0:T(8,128)(2,1)S(1)} %fusion.40), channel_id=1, source_target_pairs={{0,0},{1,8},{2,16},{3,24},{4,32},{5,40},{6,48},{7,56},{8,1},{9,9},... | collective-permute-start | bytes 196616 | tf_op jit(solution)/shard_map/ppermute | solution.py:223
  216.2 3.2 %collective-permute-start.6 = (bf16[264,256]{1,0:T(8,128)(2,1)S(1)}, bf16[264,256]{1,0:T(8,128)(2,1)S(1)}, u32[]{:S(2)}, u32[]{:S(2)}) collective-permute-start(bf16[264,256]{1,0:T(8,128)(2,1)S(1)} %concatenate.53), channel_id=1, source_target_pairs={{0,1},{1,0},{2,3},{3,2},{4,5},{5,4},{6,7},{7,6},{8,9},{9,8},{10,11... | collective-permute-start | bytes 405512 | tf_op jit(solution)/shard_map/ppermute | solution.py:82

commit v4 on v0

v4 whole, which is shorter than its diff:
```python
import jax
import jax.numpy as jnp
from jax import lax
from jax.experimental import pallas as pl
from jax.experimental.pallas import tpu as pltpu
from jax.sharding import Mesh
from jax.sharding import PartitionSpec as P

GROUPS = 32
LAMBDA_OFF = 0.0051
NORM_EPS = 1e-05
LOSS_SCALE = 65536.0
INTERPRET = False

DP_SHAPE = (2, 4, 8)
TILE_SHAPE = (4, 2)
DP = ("zh", "x", "y")
TILE = ("zl", "c")
BF = jnp.bfloat16
F32 = jnp.float32
FAR = 1 << 20


def masked_views(feats, jitter, mask_ids):
    width = feats.shape[1]
    group_size = width // GROUPS
    channel_group = lax.broadcasted_iota(jnp.int32, (1, width), 1) // group_size
    keep_a = (channel_group != mask_ids[:, 0:1]).astype(F32)
    keep_b = (channel_group != mask_ids[:, 1:2]).astype(F32)
    values = feats.astype(F32)
    view_a = (values * keep_a).astype(BF)
    view_b = (values * keep_b + jitter.astype(F32)).astype(BF)
    return jnp.concatenate([view_a, view_b], axis=0), keep_a, keep_b


def spread(value, axes):
    parts = lax.axis_size(axes)
    return lax.all_to_all(
        jnp.broadcast_to(value[None], (parts,) + value.shape), axes, 0, 0, tiled=True
    )


def shift(value, axis, step):
    n = lax.axis_size(axis)
    return lax.ppermute(value, axis, [(i, (i + step) % n) for i in range(n)])


def flip(value, axis, step):
    n = lax.axis_size(axis)
    return lax.ppermute(value, axis, [(i, i ^ step) for i in range(n)])


def swap_pairs():
    rows_n = DP_SHAPE[0] * DP_SHAPE[1]
    n = DP_SHAPE[2]
    where = lambda r, y, t: (r * n + y) * n + t
    return [
        (where(r, y, t), where(r, t, y)) for r in range(rows_n) for y in range(n) for t in range(n)
    ]


def dot(a, b, ca, cb, precision=None):
    return lax.dot_general(
        a, b, (((ca,), (cb,)), ((), ())), precision=precision, preferred_element_type=F32
    )


def exact(a, b, ca, cb):
    return dot(a, b, ca, cb, lax.Precision.HIGHEST)


def put_pieces(ref, at, value, count):
    for i in range(count):
        part = value.astype(BF).astype(F32)
        ref[at + i : at + i + 1, :] = part
        value = value - part
    return at + count


def joined(rows, at, count):
    total = rows[at : at + 1]
    for i in range(1, count):
        total = total + rows[at + i : at + i + 1]
    return total


def call(body, name, outs, args, scratch=()):
    specs = [
        pl.BlockSpec(memory_space=pltpu.SMEM if a.dtype == jnp.int32 and a.ndim == 1 else pltpu.VMEM)
        for a in args
    ]
    return pl.pallas_call(
        body,
        name=name,
        out_shape=[jax.ShapeDtypeStruct(s, d) for s, d in outs],
        in_specs=specs,
        out_specs=[pl.BlockSpec(memory_space=pltpu.VMEM) for _ in outs],
        scratch_shapes=[pltpu.VMEM(s, d) for s, d in scratch],
        interpret=INTERPRET,
    )(*args)


def project_body(at, view, own, back, ahead, far_low, far_high, piece, wide_a, raw_b):
    zh_n, x_n, y_n, rows, kt = piece.shape
    x = at[0]
    half = y_n // 2
    for zh in range(zh_n):
        piece[zh, x] = own[:, zh]
        piece[zh, lax.rem(x + x_n - 1, x_n)] = back[:, zh]
        piece[zh, lax.rem(x + 1, x_n)] = ahead[:, zh]
        far = lax.rem(x + 2, x_n)
        piece[zh, far, :half] = far_low[:, zh]
        piece[zh, far, half:] = far_high[:, zh]
    weight = piece[...].reshape(zh_n * x_n * y_n * rows, kt)
    raw = dot(view[...], weight, 1, 0).astype(BF)
    n = raw_b.shape[0]
    for i in range(wide_a.shape[0]):
        wide_a[i] = raw[:n]
    raw_b[...] = raw[n:]


def gram_body(at, big_a, pair0, pair1, pair2, pair3, big_b, out, tail):
    zl, c = at[1], at[2]
    parts, rows, kt = big_a.shape
    block = parts * rows
    for step, pair in enumerate((pair0, pair1, pair2, pair3)):
        big_b[(zl ^ step) * 2 + c] = pair[0]
        big_b[(zl ^ step) * 2 + (1 - c)] = pair[1]
    a = big_a[...].reshape(block, kt).astype(F32)
    b = big_b[...].reshape(block, kt).astype(F32)
    mean_a = jnp.sum(a, axis=0, keepdims=True) / block
    mean_b = jnp.sum(b, axis=0, keepdims=True) / block
    a = a - mean_a
    b = b - mean_b
    gram = dot(a.astype(BF), b.astype(BF), 0, 0).astype(BF)
    tail[...] = jnp.zeros_like(tail)
    pos = put_pieces(tail, 0, mean_a, 3)
    pos = put_pieces(tail, pos, jnp.sum(a * a, axis=0, keepdims=True), 3)
    pos = put_pieces(tail, pos, mean_b, 3)
    pos = put_pieces(tail, pos, jnp.sum(b * b, axis=0, keepdims=True), 3)
    put_pieces(tail, pos, jnp.sum(a * b, axis=0, keepdims=True), 3)
    x_n = out.shape[0]
    deep = out.shape[1] - 16
    rows_out = tail[...].astype(BF)
    for x in range(x_n):
        out[x, :deep] = gram[x * deep : (x + 1) * deep]
        out[x, deep:] = rows_out


def merge_body(got, out):
    x_n = got.shape[0]
    zh_n, deep, kt = out.shape
    sub = deep - 16 * x_n
    for zh in range(zh_n):
        total = got[0, zh * sub : (zh + 1) * sub].astype(F32)
        for x in range(1, x_n):
            total = total + got[x, zh * sub : (zh + 1) * sub].astype(F32)
        out[zh, :sub] = total.astype(BF)
        for x in range(x_n):
            out[zh, sub + 16 * x : sub + 16 * (x + 1)] = got[x, zh_n * sub :]


def mix_body(at, got, mix, stats, table, offs, *, block):
    zh_n, deep, kt = got.shape
    sub = mix.shape[0]
    sets = zh_n * ((deep - sub) // 16)
    total = block * sets
    raws = []
    for zh in range(zh_n):
        for x in range((deep - sub) // 16):
            rows = got[zh, sub + 16 * x : sub + 16 * (x + 1)].astype(F32)
            raws.append([joined(rows, 3 * i, 3) for i in range(5)])
    summed = [sum(r[i] for r in raws[1:]) + raws[0][i] for i in range(5)]
    mean_a, mean_b = summed[0] / sets, summed[2] / sets
    square_a, square_b, cross = summed[1], summed[3], summed[4]
    drift_a = jnp.zeros_like(mean_a)
    drift_b = jnp.zeros_like(mean_b)
    table[...] = jnp.zeros_like(table)
    for i, r in enumerate(raws):
        off_a, off_b = r[0] - mean_a, r[2] - mean_b
        square_a = square_a + block * off_a * off_a
        square_b = square_b + block * off_b * off_b
        cross = cross + block * off_a * off_b
        drift_a, drift_b = drift_a + off_a, drift_b + off_b
        table[i : i + 1, :] = off_a
        offs[i : i + 1, :] = block * off_b
    inv_a = lax.rsqrt(square_a / total + NORM_EPS)
    inv_b = lax.rsqrt(square_b / total + NORM_EPS)
    table[sets : sets + 1, :] = inv_a
    diag = cross * (inv_a * inv_b / total)
    coeff = -2.0 * (1.0 - diag) - 2.0 * LAMBDA_OFF * diag
    k_of = lax.broadcasted_iota(jnp.int32, (sub, kt), 0)
    l_of = lax.broadcasted_iota(jnp.int32, (sub, kt), 1)
    chosen = exact((k_of + at[3] == l_of).astype(F32), table[...], 1, 1)
    corr = got[0, :sub].astype(F32)
    for zh in range(1, zh_n):
        corr = corr + got[zh, :sub].astype(F32)
    corr = corr + exact(chosen[:, :sets], offs[...], 1, 0)
    corr = corr * (chosen[:, sets : sets + 1] * (inv_b / total))
    here = k_of + (at[3] + at[4]) == l_of
    mix[...] = jnp.where(
        here, coeff + 2.0 * LAMBDA_OFF * diag, 2.0 * LAMBDA_OFF * corr
    ).astype(BF)
    stats[0:1, :] = mean_a
    stats[1:2, :] = inv_a
    stats[2:3, :] = mean_b
    stats[3:4, :] = inv_b
    stats[4:5, :] = diag
    stats[5:6, :] = drift_a * inv_a / sets
    stats[6:7, :] = drift_b * inv_b / sets
    stats[7:8, :] = diag * (at[4] == 0).astype(F32)


def correlation(at, mix, stats):
    kt = mix.shape[0]
    k_of = lax.broadcasted_iota(jnp.int32, (kt, kt), 0)
    l_of = lax.broadcasted_iota(jnp.int32, (kt, kt), 1)
    return jnp.where(k_of + at[4] == l_of, stats[4:5, :], mix * (0.5 / LAMBDA_OFF))


def grad_b_body(at, mix4, big_a, stats, sent, kept, grads, tail):
    c = at[2]
    parts, rows, kt = big_a.shape
    line = parts // 2
    mix = mix4[...].reshape(kt, kt)
    wide = mix.astype(F32)
    norm_a = (big_a[...].reshape(parts * rows, kt).astype(F32) - stats[0:1, :]) * stats[1:2, :]
    grads[...] = dot(norm_a.astype(BF), mix, 1, 0).reshape(parts, rows, kt)
    for z in range(line):
        sent[z * rows : (z + 1) * rows] = grads[z * 2 + (1 - c)].astype(BF)
        kept[z * rows : (z + 1) * rows] = grads[z * 2 + c]
    second = jnp.sum(wide * correlation(at, wide, stats), axis=0, keepdims=True)
    first = exact(stats[...], wide, 1, 0)[5:6]
    tail[...] = jnp.zeros_like(tail)
    pos = put_pieces(tail, 0, second, 3)
    put_pieces(tail, pos, first, 2)
    sent[line * rows :] = tail[...].astype(BF)
    kept[line * rows :] = jnp.zeros_like(tail)
    kept[line * rows : line * rows + 1] = second
    kept[line * rows + 1 : line * rows + 2] = first


def grad_a_body(at, mix4, big_b, stats, out, tail):
    parts, rows, kt = big_b.shape
    mix = mix4[...].reshape(kt, kt)
    wide = mix.astype(F32)
    norm_b = (big_b[...].reshape(parts * rows, kt).astype(F32) - stats[2:3, :]) * stats[3:4, :]
    grad = dot(norm_b.astype(BF), mix, 1, 1).astype(BF)
    corr = correlation(at, wide, stats)
    ones = jnp.ones((8, kt), F32)
    pos = put_pieces(tail, 0, exact(ones, wide * corr, 1, 1)[0:1], 2)
    pos = put_pieces(tail, pos, exact(ones, corr * corr, 1, 1)[0:1], 2)
    pos = put_pieces(tail, pos, stats[7:8, :], 3)
    put_pieces(tail, pos, exact(stats[...], wide, 1, 1)[6:7], 1)
    rows_out = tail[...].astype(BF)
    for i in range(parts):
        out[i, :rows] = grad[i * rows : (i + 1) * rows]
        out[i, rows:] = rows_out


def core_body(at, kept, got, own, out1, out2, out3, total, tail):
    zl = at[1]
    rows = own.shape[0] - 8
    deep = kept.shape[0] - 8
    total[...] = kept[:deep] + got[:deep].astype(F32)
    theirs = got[deep:].astype(F32)
    second = kept[deep : deep + 1] + joined(theirs, 0, 3)
    first = kept[deep + 1 : deep + 2] + joined(theirs, 3, 2)
    tail[...] = jnp.zeros_like(tail)
    pos = put_pieces(tail, 0, second, 3)
    put_pieces(tail, pos, first, 2)
    rows_out = tail[...].astype(BF)
    start = lambda step: pl.ds(pl.multiple_of((zl ^ step) * rows, rows), rows)
    for step, out in enumerate((out1, out2, out3), 1):
        out[:rows] = total[start(step), :].astype(BF)
        out[rows:] = rows_out
    own[:rows] = total[start(0), :]
    own[rows:] = jnp.zeros_like(tail)
    own[rows : rows + 1] = second
    own[rows + 1 : rows + 2] = first


def dz_b_body(own, got1, got2, got3, raw_b, stats, out):
    rows = out.shape[0]
    grad = own[:rows]
    second, first = own[rows : rows + 1], own[rows + 1 : rows + 2]
    for got in (got1, got2, got3):
        grad = grad + got[:rows].astype(F32)
        theirs = got[rows:].astype(F32)
        second = second + joined(theirs, 0, 3)
        first = first + joined(theirs, 3, 2)
    inv = stats[3:4, :]
    norm = ((raw_b[...].astype(F32) - stats[2:3, :]) * inv).astype(BF).astype(F32)
    out[...] = (inv * (grad - first - norm * second)).astype(BF)


def back_a_body(got, raw_a, stats, keep, weight, out, diag_out, power_out):
    parts, deep, kt = got.shape
    rows = deep - 8
    grad = got[0, :rows].astype(F32)
    tails = [got[i, rows:].astype(F32) for i in range(parts)]
    for i in range(1, parts):
        grad = grad + got[i, :rows].astype(F32)
    gather = lambda pos, count: sum(
        (joined(t, pos, count) for t in tails[1:]), joined(tails[0], pos, count)
    )
    second, power, diag, first = gather(0, 2), gather(2, 2), gather(4, 3), gather(7, 1)
    inv = stats[1:2, :]
    norm = ((raw_a[...].astype(F32) - stats[0:1, :]) * inv).astype(BF).astype(F32)
    dz = (inv * (grad - first - norm * second)).astype(BF)
    width = keep.shape[1]
    out[...] = keep[...] * dot(dz, weight[...].reshape(width, kt), 1, 1)
    diag_out[...] = diag
    power_out[...] = jnp.broadcast_to(jnp.sum(power, axis=1, keepdims=True), power_out.shape)


def back_b_body(at, part, dz, keep, weight, power, sent, kept, blocks, tail):
    c = at[2]
    rows, width = part.shape
    parts, _, chunk = blocks.shape
    line = parts // 2
    both = part[...] + keep[...] * dot(dz[...], weight[...].reshape(width, dz.shape[1]), 1, 1)
    for i in range(parts):
        blocks[i] = both[:, i * chunk : (i + 1) * chunk]
    for z in range(line):
        sent[z * rows : (z + 1) * rows] = blocks[z * 2 + (1 - c)].astype(BF)
        kept[z * rows : (z + 1) * rows] = blocks[z * 2 + c]
    tail[...] = jnp.zeros_like(tail)
    put_pieces(tail, 0, power[...], 3)
    sent[line * rows :] = tail[...].astype(BF)
    kept[line * rows :] = tail[...]


def last_body(kept, got, out, tail):
    line, deep, chunk = out.shape
    rows = deep - 8
    theirs = got[line * rows :].astype(F32)
    power = joined(kept[line * rows :], 0, 3) + joined(theirs, 0, 3)
    tail[...] = jnp.zeros_like(tail)
    put_pieces(tail, 0, power, 3)
    rows_out = tail[...].astype(BF)
    for z in range(line):
        at = slice(z * rows, (z + 1) * rows)
        out[z, :rows] = (kept[at] + got[at].astype(F32)).astype(BF)
        out[z, rows:] = rows_out


def end_body(got, out, power_out, *, scale, features):
    line, deep, _ = got.shape
    rows = deep - 8
    total = got[0, :rows].astype(F32)
    power = joined(got[0, rows:].astype(F32), 0, 3)
    for z in range(1, line):
        total = total + got[z, :rows].astype(F32)
        power = power + joined(got[z, rows:].astype(F32), 0, 3)
    out[...] = scale * total
    power_out[...] = power / features


def on_device(feats, jitter, mask_ids, weight):
    rows, width = feats.shape
    w_rows, kt = weight.shape
    zh_n, x_n, y_n = DP_SHAPE
    zl_n, c_n = TILE_SHAPE
    rows_n = zh_n * x_n
    tile_n = zl_n * c_n
    total = rows * rows_n * y_n
    block = rows * y_n
    sub = kt // rows_n
    chunk = width // tile_n
    every = DP + TILE
    pairs = swap_pairs()

    y_at = lax.axis_index("y")
    tile_at = lax.axis_index(TILE)
    at = jnp.stack(
        [
            lax.axis_index("x"),
            lax.axis_index("zl"),
            lax.axis_index("c"),
            lax.axis_index(("x", "zh")) * sub,
            jnp.where(y_at == tile_at, 0, FAR),
        ]
    ).astype(jnp.int32)
    view, keep_a, keep_b = masked_views(feats, jitter, mask_ids)

    own = lax.all_gather(weight, "zh", axis=0, tiled=True)
    own = spread(own, "y").reshape(y_n, zh_n, w_rows, kt)
    half = y_n // 2
    back = shift(own, "x", 1)
    ahead = shift(own, "x", x_n - 1)
    far_low = shift(back[:half], "x", 1)
    far_high = shift(ahead[half:], "x", x_n - 1)
    piece, wide_a, raw_b = call(
        project_body,
        "project",
        [((zh_n, x_n, y_n, w_rows, kt), BF), ((y_n, rows, kt), BF), ((rows, kt), BF)],
        (at, view, own, back, ahead, far_low, far_high),
    )

    raw_a = wide_a[0]
    big_a = lax.all_to_all(wide_a, "y", 0, 0, tiled=True)
    own_b = lax.ppermute(raw_b, every, pairs)
    pair = jnp.stack([own_b, flip(own_b, "c", 1)])
    others = [flip(pair, "zl", step) for step in range(1, zl_n)]
    big_b, gram = call(
        gram_body,
        "gram",
        [((tile_n, rows, kt), BF), ((x_n, zh_n * sub + 16, kt), BF)],
        (at, big_a, pair, *others),
        [((16, kt), F32)],
    )

    got = lax.all_to_all(gram, "x", 0, 0, tiled=True)
    (got,) = call(merge_body, "merge", [((zh_n, sub + 16 * x_n, kt), BF)], (got,))
    got = lax.all_to_all(got, "zh", 0, 0, tiled=True)
    mix, stats = call(
        lambda *refs: mix_body(*refs, block=block),
        "mix",
        [((sub, kt), BF), ((8, kt), F32)],
        (at, got),
        [((16, kt), F32), ((rows_n, kt), F32)],
    )
    mix = spread(lax.all_gather(mix, "zh", axis=0, tiled=True), "x")

    line_rows = zl_n * rows + 8
    sent, kept = call(
        grad_b_body,
        "grad_b",
        [((line_rows, kt), BF), ((line_rows, kt), F32)],
        (at, mix, big_a, stats),
        [((tile_n, rows, kt), F32), ((8, kt), F32)],
    )
    got_b = flip(sent, "c", 1)
    (grad_a,) = call(
        grad_a_body, "grad_a", [((y_n, rows + 8, kt), BF)], (at, mix, big_b, stats), [((8, kt), F32)]
    )
    got_a = lax.all_to_all(grad_a, "y", 0, 0, tiled=True)
    own, *outs = call(
        core_body,
        "core",
        [((rows + 8, kt), F32)] + [((rows + 8, kt), BF)] * 3,
        (at, kept, got_b),
        [((zl_n * rows, kt), F32), ((8, kt), F32)],
    )
    gots = [flip(o, "zl", step) for step, o in enumerate(outs, 1)]
    (dz_b,) = call(dz_b_body, "dz_b", [((rows, kt), BF)], (own, *gots, own_b, stats))
    dz_b = lax.ppermute(dz_b, every, pairs)
    part, diag_corr, power = call(
        back_a_body,
        "back_a",
        [((rows, width), F32), ((1, kt), F32), ((1, chunk), F32)],
        (got_a, raw_a, stats, keep_a, piece),
    )
    sent, kept = call(
        back_b_body,
        "back_b",
        [((line_rows, chunk), BF), ((line_rows, chunk), F32)],
        (at, part, dz_b, keep_b, piece, power),
        [((tile_n, rows, chunk), F32), ((8, chunk), F32)],
    )
    (share,) = call(
        last_body,
        "last",
        [((zl_n, rows + 8, chunk), BF)],
        (kept, flip(sent, "c", 1)),
        [((8, chunk), F32)],
    )
    got = lax.all_to_all(share, "zl", 0, 0, tiled=True)
    feats_grad, cross_power = call(
        lambda *refs: end_body(*refs, scale=LOSS_SCALE / total, features=kt * tile_n),
        "end",
        [((rows, chunk), F32), ((1, chunk), F32)],
        (got,),
    )
    return feats_grad, diag_corr[0], cross_power[0, 0]


def solution(mesh):
    fine = Mesh(mesh.devices.reshape(DP_SHAPE + TILE_SHAPE), DP + TILE)
    in_specs = (P(DP, None), P(DP, None), P(DP, None), P(DP, TILE))
    out_specs = (P(DP, TILE), P(TILE), P())
    return jax.shard_map(
        on_device, mesh=fine, in_specs=in_specs, out_specs=out_specs, check_vma=False
    )
```

time: 1040 us -> 241 us (0.23)
  waiting for transfers between devices: 606 us -> 28.5 us
  blocking collectives: 390 us -> 93.1 us
  starting transfers between devices: 0.2 us -> 73 us
  Pallas kernels: 0 us -> 32.4 us
  matrix products: 19.7 us -> 0 us
  between operations: 15.6 us -> 0.96 us
    all_gather x3 -> x0, waiting for transfers between devices: 480 us -> none  [the longest x1 183 us: on_device(): lax.all_gather(outgoing_a, 'dp', axis=0, tiled=True)]
    psum x2 -> x0, blocking collectives: 390 us -> none  [the longest x1 201 us: on_device(): lax.psum((jnp.sum(grad_na, axis=0), jnp.sum(grad_na * za, axis=0), jnp.su...]
    all_to_all x0 -> x5, blocking collectives: none -> 73.2 us  [the longest x2 31.4 us: spread(): lax.all_to_all(jnp.broadcast_to(value[None], (parts,) + value.shape), axe...]
    psum x1 -> x0, waiting for transfers between devices: 69.9 us -> none  [on_device(): lax.psum(contract_last(norm_b, whole_b).astype(jnp.bfloat16), 'tile')]
    ppermute x0 -> x15, starting transfers between devices: none -> 62.4 us  [the longest x9 35.6 us: flip(): return lax.ppermute(value, axis, [(i, i ^ step) for i in range(n)])]
    reduce_scatter x1 -> x0, waiting for transfers between devices: 54.8 us -> none  [on_device(): lax.psum_scatter(combined.astype(jnp.bfloat16), 'tile', scatter_dimension...]
    pallas_call x0 -> x12, Pallas kernels: none -> 32.4 us  [call(): pl.pallas_call(body, name=name, out_shape=[jax.ShapeDtypeStruct(s, d) for...]
    ppermute x0 -> x15, waiting for transfers between devices: none -> 28.5 us  [the longest x9 13.3 us: flip(): return lax.ppermute(value, axis, [(i, i ^ step) for i in range(n)])]
  transfers between devices with their start and end apart: 5 -> 17, of which waited for: 5 -> 9; matrix products, arithmetic and copies ran while one was open for 1% -> 2% of each run, Pallas kernels for 0% -> 4%
where the time goes in v4:
time: 241 us; the launch traced here: 240 us
  blocking collectives  93.1 us (39%)
  starting transfers between devices  73 us (30%)
  Pallas kernels  32.4 us (13%)
  waiting for transfers between devices  28.5 us (12%)
  local copies, waits for them, and re-layouts  9.69 us (4%)
    ppermute x9, starting transfers between devices, flip(): return lax.ppermute(value, axis, [(i, i ^ step) for i in range(n)])  35.6 us
    pallas_call x12, Pallas kernels, call(): pl.pallas_call(body, name=name, out_shape=[jax.ShapeDtypeStruct(s, d) for...  32.4 us
    all_to_all x2, blocking collectives, spread(): lax.all_to_all(jnp.broadcast_to(value[None], (parts,) + value.shape), axe...  31.4 us
    all_to_all x1, blocking collectives, on_device(): got = lax.all_to_all(got, 'zh', 0, 0, tiled=True)  15.7 us
    ppermute x4, starting transfers between devices, shift(): return lax.ppermute(value, axis, [(i, (i + step) % n) for i in range(n)])  13.5 us
    ppermute x9, waiting for transfers between devices, flip(): return lax.ppermute(value, axis, [(i, i ^ step) for i in range(n)])  13.3 us
    all_to_all x1, blocking collectives, on_device(): got = lax.all_to_all(gram, 'x', 0, 0, tiled=True)  13.2 us
    all_to_all x1, blocking collectives, on_device(): got = lax.all_to_all(share, 'zl', 0, 0, tiled=True)  13 us
  transfers between devices with their start and end apart: 17, of which 9 were waited for; matrix products, arithmetic and copies ran while one was open for 2% of the time, Pallas kernels for 4%

profile of v4, /device:TPU:1, one launch (start us, length us, event | category | flops | bytes accessed | tf_op | source)
XLA Modules:
  0.0 239.8 jit_solution(17634951623441740339)
XLA Ops:
  0.7 12.0 %all_gather.6 = bf16[64,512]{1,0:T(8,128)(2,1)S(1)} all-gather(bf16[32,512]{1,0:T(8,128)(2,1)} %param.7), channel_id=1, replica_groups=mesh['zh'=2,'x'=4,'y'=8,'zl'=4,'c'=2] {'zh'}, dimensions={0}, use_global_device_ids=true | all-gather | bytes 98304 | tf_op jit(solution)/shard_map/all_gather | solution.py:387
  12.7 21.4 %all_to_all.35 = bf16[8,64,512]{2,1,0:T(8,128)(2,1)S(1)} all-to-all(bf16[8,64,512]{2,1,0:T(8,128)(2,1)S(1)} %broadcast_in_dim.4), channel_id=1, replica_groups=mesh['zh'=2,'x'=4,'y'=8,'zl'=4,'c'=2] {'y'}, dimensions={0} | all-to-all | bytes 1048576 | tf_op jit(solution)/shard_map/all_to_all | solution.py:38
  34.0 4.4 %collective-permute-start.1 = (bf16[8,2,32,512]{3,2,1,0:T(8,128)(2,1)S(1)}, bf16[8,2,32,512]{3,2,1,0:T(8,128)(2,1)S(1)}, u32[]{:S(2)}, u32[]{:S(2)}) collective-permute-start(bf16[8,2,32,512]{3,2,1,0:T(8,128)(2,1)S(1)} %bitcast.16), channel_id=1, source_target_pairs={{0,192},{64,0},{128,64},{192,128},{1,193},{65,1},{129,65},{193,129... | collective-permute-start | bytes 1572872 | tf_op jit(solution)/shard_map/ppermute | solution.py:45
  38.4 1.9 collective-permute-start
  41.1 4.8 %collective-permute-done.1.ahead = bf16[8,2,32,512]{3,2,1,0:T(8,128)(2,1)S(1)} collective-permute-done((bf16[8,2,32,512]{3,2,1,0:T(8,128)(2,1)S(1)}, bf16[8,2,32,512]{3,2,1,0:T(8,128)(2,1)S(1)}, u32[]{:S(2)}, u32[]{:S(2)}) %collective-permute-start.1) | collective-permute-done | bytes 524320 | tf_op jit(solution)/shard_map/ppermute | solution.py:45
  45.9 5.3 %collective-permute-start.3 = (bf16[4,2,32,512]{3,2,1,0:T(8,128)(2,1)S(1)}, bf16[4,2,32,512]{3,2,1,0:T(8,128)(2,1)S(1)}, u32[]{:S(2)}, u32[]{:S(2)}) collective-permute-start(bf16[4,2,32,512]{3,2,1,0:T(8,128)(2,1)S(1)} %slice.25), channel_id=1, source_target_pairs={{0,192},{64,0},{128,64},{192,128},{1,193},{65,1},{129,65},{193,129... | collective-permute-start | bytes 786440 | tf_op jit(solution)/shard_map/ppermute | solution.py:45
  51.3 1.9 collective-permute-start.2
  54.2 0.8 pad_maximum_fusion.view
  55.0 4.6 %collective-permute-done.2.far_low = bf16[4,2,32,512]{3,2,1,0:T(8,128)(2,1)S(1)} collective-permute-done((bf16[4,2,32,512]{3,2,1,0:T(8,128)(2,1)S(1)}, bf16[4,2,32,512]{3,2,1,0:T(8,128)(2,1)S(1)}, u32[]{:S(2)}, u32[]{:S(2)}) %collective-permute-start.2) | collective-permute-done | bytes 262176 | tf_op jit(solution)/shard_map/ppermute | solution.py:45
  60.4 3.4 %project.1 = (bf16[2,4,8,32,512]{4,3,2,1,0:T(8,128)(2,1)}, bf16[8,64,512]{2,1,0:T(8,128)(2,1)}, bf16[64,512]{1,0:T(8,128)(2,1)}) custom-call(s32[5]{0:T(128)} %stack.32.at.refs_0_, bf16[128,2048]{1,0:T(8,128)(2,1)} %pad_maximum_fusion.view, bf16[8,2,32,512]{3,2,1,0:T(8,128)(2,1)} %bitcast.18, bf16[8,2,32,512]{3,2,1,0:T(8,128)(2,1)} %copy-done.4, ...), custom_call_target="tpu_custom_call" | custom-call | tf_op jit(solution)/shard_map/project/pallas_call | solution.py:92
  63.8 5.7 %all-to-all-start.1 = ((bf16[8,64,512]{2,1,0:T(8,128)(2,1)}), bf16[8,64,512]{2,1,0:T(8,128)(2,1)S(1)}, u32[]{:S(2)}, u32[]{:S(2)}) async-start(bf16[8,64,512]{2,1,0:T(8,128)(2,1)} %get-tuple-element.23), calls=%async_computation.1 | async-start | bytes 1048576 | tf_op jit(solution)/shard_map/all_to_all | solution.py:402
  69.4 7.7 %collective-permute-start.4 = (bf16[64,512]{1,0:T(8,128)(2,1)}, bf16[64,512]{1,0:T(8,128)(2,1)S(1)}, u32[]{:S(2)}, u32[]{:S(2)}) collective-permute-start(bf16[64,512]{1,0:T(8,128)(2,1)} %get-tuple-element.24), channel_id=1, source_target_pairs={{0,0},{1,8},{2,16},{3,24},{4,32},{5,40},{6,48},{7,56},{8,1},{9,9},... | collective-permute-start | bytes 196616 | tf_op jit(solution)/shard_map/ppermute | solution.py:403
  77.1 5.7 %collective-permute-done.4.raw_b = bf16[64,512]{1,0:T(8,128)(2,1)S(1)} collective-permute-done((bf16[64,512]{1,0:T(8,128)(2,1)}, bf16[64,512]{1,0:T(8,128)(2,1)S(1)}, u32[]{:S(2)}, u32[]{:S(2)}) %collective-permute-start.4) | collective-permute-done | bytes 65568 | tf_op jit(solution)/shard_map/ppermute | solution.py:403
  82.9 1.9 collective-permute-start.5
  84.8 1.2 collective-permute-done.5
  86.0 11.5 %collective-permute-start.8 = (bf16[2,64,512]{2,1,0:T(8,128)(2,1)S(1)}, bf16[2,64,512]{2,1,0:T(8,128)(2,1)S(1)}, u32[]{:S(2)}, u32[]{:S(2)}) collective-permute-start(bf16[2,64,512]{2,1,0:T(8,128)(2,1)S(1)} %pad_maximum_fusion.1.pair0), channel_id=1, source_target_pairs={{0,6},{2,4},{4,2},{6,0},{1,7},{3,5},{5,3},{7,1},{8,14},{10,12},{12... | collective-permute-start | bytes 393224 | tf_op jit(solution)/shard_map/ppermute | solution.py:50
  97.5 1.9 collective-permute-start.7
  99.4 2.2 collective-permute-start.6
  101.7 6.3 %collective-permute-done.7.pair2 = bf16[2,64,512]{2,1,0:T(8,128)(2,1)S(1)} collective-permute-done((bf16[2,64,512]{2,1,0:T(8,128)(2,1)S(1)}, bf16[2,64,512]{2,1,0:T(8,128)(2,1)S(1)}, u32[]{:S(2)}, u32[]{:S(2)}) %collective-permute-start.7) | collective-permute-done | bytes 131104 | tf_op jit(solution)/shard_map/ppermute | solution.py:50
  110.2 3.0 %gram.1 = (bf16[8,64,512]{2,1,0:T(8,128)(2,1)}, bf16[4,144,512]{2,1,0:T(8,128)(2,1)}) custom-call(s32[5]{0:T(128)} %stack.32.at.refs_0_, bf16[8,64,512]{2,1,0:T(8,128)(2,1)} %copy-done, bf16[2,64,512]{2,1,0:T(8,128)(2,1)} %copy-done.5, bf16[2,64,512]{2,1,0:T(8,128)(2,1)} %copy-done.15, bf16[2,64,512]{2,1,0:T(8,128)(2,1)} %copy-done.14, ...), custom_call_target="tpu_custom_call" | custom-call | tf_op jit(solution)/shard_map/gram/pallas_call | solution.py:92
  113.2 13.2 %all_to_all.36.got = bf16[4,144,512]{2,1,0:T(8,128)(2,1)} all-to-all(bf16[4,144,512]{2,1,0:T(8,128)(2,1)} %get-tuple-element.25), channel_id=1, replica_groups=mesh['zh'=2,'x'=4,'y'=8,'zl'=4,'c'=2] {'x'}, dimensions={0} | all-to-all | bytes 1179648 | tf_op jit(solution)/shard_map/all_to_all | solution.py:414
  126.3 1.8 merge.1
  128.2 15.7 %all_to_all.37.refs_1_ = bf16[2,128,512]{2,1,0:T(8,128)(2,1)} all-to-all(bf16[2,128,512]{2,1,0:T(8,128)(2,1)} %merge.1), channel_id=1, replica_groups=mesh['zh'=2,'x'=4,'y'=8,'zl'=4,'c'=2] {'zh'}, dimensions={0} | all-to-all | bytes 524288 | tf_op jit(solution)/shard_map/all_to_all | solution.py:416
  143.8 2.3 mix.1
  146.1 7.9 %all_gather.7 = bf16[128,512]{1,0:T(8,128)(2,1)S(1)} all-gather(bf16[64,512]{1,0:T(8,128)(2,1)} %get-tuple-element.26), channel_id=1, replica_groups=mesh['zh'=2,'x'=4,'y'=8,'zl'=4,'c'=2] {'zh'}, dimensions={0}, use_global_device_ids=true | all-gather | bytes 196608 | tf_op jit(solution)/shard_map/all_gather | solution.py:424
  154.1 10.1 %all_to_all.38.mix4 = bf16[4,128,512]{2,1,0:T(8,128)(2,1)} all-to-all(bf16[4,128,512]{2,1,0:T(8,128)(2,1)S(1)} %broadcast_in_dim.5), channel_id=1, replica_groups=mesh['zh'=2,'x'=4,'y'=8,'zl'=4,'c'=2] {'x'}, dimensions={0} | all-to-all | bytes 1048576 | tf_op jit(solution)/shard_map/all_to_all | solution.py:38
  164.1 4.9 %grad_a.1 = bf16[8,72,512]{2,1,0:T(8,128)(2,1)} custom-call(s32[5]{0:T(128)} %stack.32.at.refs_0_, bf16[4,128,512]{2,1,0:T(8,128)(2,1)} %all_to_all.38.mix4, bf16[8,64,512]{2,1,0:T(8,128)(2,1)} %get-tuple-element.27.big_b, f32[8,512]{1,0:T(8,128)} %get-tuple-element.28.stats), custom_call_target="tpu_custom_call" | custom-call | tf_op jit(solution)/shard_map/grad_a/pallas_call | solution.py:92
  169.1 4.9 %all-to-all-start.5 = ((bf16[8,72,512]{2,1,0:T(8,128)(2,1)}), bf16[8,72,512]{2,1,0:T(8,128)(2,1)S(1)}, u32[]{:S(2)}, u32[]{:S(2)}) async-start(bf16[8,72,512]{2,1,0:T(8,128)(2,1)} %grad_a.1), calls=%async_computation.5 | async-start | bytes 1179648 | tf_op jit(solution)/shard_map/all_to_all | solution.py:438
  174.0 3.1 %grad_b.1 = (bf16[264,512]{1,0:T(8,128)(2,1)}, f32[264,512]{1,0:T(8,128)}) custom-call(s32[5]{0:T(128)} %stack.32.at.refs_0_, bf16[4,128,512]{2,1,0:T(8,128)(2,1)} %all_to_all.38.mix4, bf16[8,64,512]{2,1,0:T(8,128)(2,1)} %copy-done, f32[8,512]{1,0:T(8,128)} %get-tuple-element.28.stats), custom_call_target="tpu_custom_call" | custom-call | tf_op jit(solution)/shard_map/grad_b/pallas_call | solution.py:92
  177.1 6.9 %collective-permute-start.9 = (bf16[264,512]{1,0:T(8,128)(2,1)}, bf16[264,512]{1,0:T(8,128)(2,1)S(1)}, u32[]{:S(2)}, u32[]{:S(2)}) collective-permute-start(bf16[264,512]{1,0:T(8,128)(2,1)} %get-tuple-element.32), channel_id=1, source_target_pairs={{0,1},{1,0},{2,3},{3,2},{4,5},{5,4},{6,7},{7,6},{8,9},{9,8},{10,11... | collective-permute-start | bytes 811016 | tf_op jit(solution)/shard_map/ppermute | solution.py:50
  184.0 1.4 collective-permute-done.9.got
  186.0 2.0 core.1
  188.0 1.9 collective-permute-start.10
  189.9 3.4 %collective-permute-start.11 = (bf16[72,512]{1,0:T(8,128)(2,1)}, bf16[72,512]{1,0:T(8,128)(2,1)S(1)}, u32[]{:S(2)}, u32[]{:S(2)}) collective-permute-start(bf16[72,512]{1,0:T(8,128)(2,1)} %get-tuple-element.35), channel_id=1, source_target_pairs={{0,4},{2,6},{4,0},{6,2},{1,5},{3,7},{5,1},{7,3},{8,12},{10,14},{12... | collective-permute-start | bytes 221192 | tf_op jit(solution)/shard_map/ppermute | solution.py:50
  193.3 4.0 %collective-permute-start.12 = (bf16[72,512]{1,0:T(8,128)(2,1)}, bf16[72,512]{1,0:T(8,128)(2,1)S(1)}, u32[]{:S(2)}, u32[]{:S(2)}) collective-permute-start(bf16[72,512]{1,0:T(8,128)(2,1)} %get-tuple-element.36), channel_id=1, source_target_pairs={{0,6},{2,4},{4,2},{6,0},{1,7},{3,5},{5,3},{7,1},{8,14},{10,12},{12... | collective-permute-start | bytes 221192 | tf_op jit(solution)/shard_map/ppermute | solution.py:50
  197.3 1.1 compare_convert_fusion
  198.4 2.1 collective-permute-done.12.got3
  201.1 1.7 dz_b.1
  202.8 5.6 %collective-permute-start.13 = (bf16[64,512]{1,0:T(8,128)(2,1)}, bf16[64,512]{1,0:T(8,128)(2,1)S(1)}, u32[]{:S(2)}, u32[]{:S(2)}) collective-permute-start(bf16[64,512]{1,0:T(8,128)(2,1)} %dz_b.1), channel_id=1, source_target_pairs={{0,0},{1,8},{2,16},{3,24},{4,32},{5,40},{6,48},{7,56},{8,1},{9,9},... | collective-permute-start | bytes 196616 | tf_op jit(solution)/shard_map/ppermute | solution.py:448
  208.5 1.5 slice_bitcast_fusion.raw_a
  210.8 3.6 %back_a.1 = (f32[64,2048]{1,0:T(8,128)}, f32[1,512]{1,0:T(1,128)}, f32[1,256]{1,0:T(1,128)}) custom-call(bf16[8,72,512]{2,1,0:T(8,128)(2,1)} %copy-done.1, bf16[64,512]{1,0:T(8,128)(2,1)} %slice_bitcast_fusion.raw_a, f32[8,512]{1,0:T(8,128)} %get-tuple-element.28.stats, f32[64,2048]{1,0:T(8,128)} %get-tuple-element.46.keep, ...), custom_call_target="tpu_custom_call" | custom-call | tf_op jit(solution)/shard_map/back_a/pallas_call | solution.py:92
  214.9 3.4 %back_b.1 = (bf16[264,256]{1,0:T(8,128)(2,1)}, f32[264,256]{1,0:T(8,128)}) custom-call(s32[5]{0:T(128)} %stack.32.at.refs_0_, f32[64,2048]{1,0:T(8,128)} %get-tuple-element.30.part, bf16[64,512]{1,0:T(8,128)(2,1)} %copy-done.19, f32[64,2048]{1,0:T(8,128)} %get-tuple-element.45.keep, bf16[2,4,8,32,512]{4,3,2,1,0:T(8,128)(2,1)} %get-tuple-element.29.weight, ...), custom_call_target="tpu_custom_call" | custom-call | tf_op jit(solution)/shard_map/back_b/pallas_call | solution.py:92
  218.4 1.9 collective-permute-start.14
  220.3 1.5 collective-permute-done.14.got
  222.5 1.7 last.1
  224.1 13.0 %all_to_all.39.refs_0_ = bf16[4,72,256]{2,1,0:T(8,128)(2,1)} all-to-all(bf16[4,72,256]{2,1,0:T(8,128)(2,1)} %last.1), channel_id=1, replica_groups=mesh['zh'=2,'x'=4,'y'=8,'zl'=4,'c'=2] {'zl'}, dimensions={0} | all-to-all | bytes 294912 | tf_op jit(solution)/shard_map/all_to_all | solution.py:469
  237.1 1.6 end.1
  238.7 1.1 slice.23
  (58 shorter events, 8.2 us)
Async XLA Ops:
  0.6 52.6 %copy-start.8 = (bf16[64,2048]{1,0:T(8,128)(2,1)S(1)}, bf16[64,2048]{1,0:T(8,128)(2,1)}, u32[]{:S(2)}) copy-start(bf16[64,2048]{1,0:T(8,128)(2,1)} %param.5) | copy-start | bytes 786436
  0.6 52.6 %copy-start.7 = (bf16[64,2048]{1,0:T(8,128)(2,1)S(1)}, bf16[64,2048]{1,0:T(8,128)(2,1)}, u32[]{:S(2)}) copy-start(bf16[64,2048]{1,0:T(8,128)(2,1)} %param.4) | copy-start | bytes 786436
  34.0 25.6 %copy-start.2 = (bf16[8,64,512]{2,1,0:T(8,128)(2,1)}, bf16[8,64,512]{2,1,0:T(8,128)(2,1)S(1)}, u32[]{:S(2)}) copy-start(bf16[8,64,512]{2,1,0:T(8,128)(2,1)S(1)} %all_to_all.35) | copy-start | bytes 1572868
  34.0 11.9 %collective-permute-start.1 = (bf16[8,2,32,512]{3,2,1,0:T(8,128)(2,1)S(1)}, bf16[8,2,32,512]{3,2,1,0:T(8,128)(2,1)S(1)}, u32[]{:S(2)}, u32[]{:S(2)}) collective-permute-start(bf16[8,2,32,512]{3,2,1,0:T(8,128)(2,1)S(1)} %bitcast.16), channel_id=1, source_target_pairs={{0,192},{64,0},{128,64},{192,128},{1,193},{65,1},{129,65},{193,129... | collective-permute-start | bytes 1572872 | tf_op jit(solution)/shard_map/ppermute | solution.py:45
  38.4 12.9 %collective-permute-start = (bf16[8,2,32,512]{3,2,1,0:T(8,128)(2,1)S(1)}, bf16[8,2,32,512]{3,2,1,0:T(8,128)(2,1)S(1)}, u32[]{:S(2)}, u32[]{:S(2)}) collective-permute-start(bf16[8,2,32,512]{3,2,1,0:T(8,128)(2,1)S(1)} %bitcast.17), channel_id=1, source_target_pairs={{0,64},{64,128},{128,192},{192,0},{1,65},{65,129},{129,193},{193,1... | collective-permute-start | bytes 1572872 | tf_op jit(solution)/shard_map/ppermute | solution.py:45
  45.9 13.7 %copy-start.3 = (bf16[8,2,32,512]{3,2,1,0:T(8,128)(2,1)}, bf16[8,2,32,512]{3,2,1,0:T(8,128)(2,1)S(1)}, u32[]{:S(2)}) copy-start(bf16[8,2,32,512]{3,2,1,0:T(8,128)(2,1)S(1)} %collective-permute-done.1.ahead) | copy-start | bytes 1572868
  45.9 9.1 %collective-permute-start.3 = (bf16[4,2,32,512]{3,2,1,0:T(8,128)(2,1)S(1)}, bf16[4,2,32,512]{3,2,1,0:T(8,128)(2,1)S(1)}, u32[]{:S(2)}, u32[]{:S(2)}) collective-permute-start(bf16[4,2,32,512]{3,2,1,0:T(8,128)(2,1)S(1)} %slice.25), channel_id=1, source_target_pairs={{0,192},{64,0},{128,64},{192,128},{1,193},{65,1},{129,65},{193,129... | collective-permute-start | bytes 786440 | tf_op jit(solution)/shard_map/ppermute | solution.py:45
  51.3 8.4 %copy-start.4 = (bf16[8,2,32,512]{3,2,1,0:T(8,128)(2,1)}, bf16[8,2,32,512]{3,2,1,0:T(8,128)(2,1)S(1)}, u32[]{:S(2)}) copy-start(bf16[8,2,32,512]{3,2,1,0:T(8,128)(2,1)S(1)} %collective-permute-done.back) | copy-start | bytes 1572868
  51.3 8.3 %collective-permute-start.2 = (bf16[4,2,32,512]{3,2,1,0:T(8,128)(2,1)S(1)}, bf16[4,2,32,512]{3,2,1,0:T(8,128)(2,1)S(1)}, u32[]{:S(2)}, u32[]{:S(2)}) collective-permute-start(bf16[4,2,32,512]{3,2,1,0:T(8,128)(2,1)S(1)} %slice.24), channel_id=1, source_target_pairs={{0,64},{64,128},{128,192},{192,0},{1,65},{65,129},{129,193},{193,1... | collective-permute-start | bytes 786440 | tf_op jit(solution)/shard_map/ppermute | solution.py:45
  55.0 4.7 %copy-start.10 = (bf16[4,2,32,512]{3,2,1,0:T(8,128)(2,1)}, bf16[4,2,32,512]{3,2,1,0:T(8,128)(2,1)S(1)}, u32[]{:S(2)}) copy-start(bf16[4,2,32,512]{3,2,1,0:T(8,128)(2,1)S(1)} %collective-permute-done.3.far_high) | copy-start | bytes 786436
  59.7 0.7 copy-start.11
  63.8 45.0 %all-to-all-start.1 = ((bf16[8,64,512]{2,1,0:T(8,128)(2,1)}), bf16[8,64,512]{2,1,0:T(8,128)(2,1)S(1)}, u32[]{:S(2)}, u32[]{:S(2)}) async-start(bf16[8,64,512]{2,1,0:T(8,128)(2,1)} %get-tuple-element.23), calls=%async_computation.1 | async-start | bytes 1048576 | tf_op jit(solution)/shard_map/all_to_all | solution.py:402
  69.4 13.4 %collective-permute-start.4 = (bf16[64,512]{1,0:T(8,128)(2,1)}, bf16[64,512]{1,0:T(8,128)(2,1)S(1)}, u32[]{:S(2)}, u32[]{:S(2)}) collective-permute-start(bf16[64,512]{1,0:T(8,128)(2,1)} %get-tuple-element.24), channel_id=1, source_target_pairs={{0,0},{1,8},{2,16},{3,24},{4,32},{5,40},{6,48},{7,56},{8,1},{9,9},... | collective-permute-start | bytes 196616 | tf_op jit(solution)/shard_map/ppermute | solution.py:403
  82.9 71.2 %copy-start.9 = (bf16[64,512]{1,0:T(8,128)(2,1)}, bf16[64,512]{1,0:T(8,128)(2,1)S(1)}, u32[]{:S(2)}) copy-start(bf16[64,512]{1,0:T(8,128)(2,1)S(1)} %collective-permute-done.4.raw_b) | copy-start | bytes 196612
  82.9 3.1 %collective-permute-start.5 = (bf16[64,512]{1,0:T(8,128)(2,1)S(1)}, bf16[64,512]{1,0:T(8,128)(2,1)S(1)}, u32[]{:S(2)}, u32[]{:S(2)}) collective-permute-start(bf16[64,512]{1,0:T(8,128)(2,1)S(1)} %collective-permute-done.4.raw_b), channel_id=1, source_target_pairs={{0,1},{1,0},{2,3},{3,2},{4,5},{5,4},{6,7},{7,6},{8,9},{9,8},{10,11... | collective-permute-start | bytes 196616 | tf_op jit(solution)/shard_map/ppermute | solution.py:50
  86.0 22.7 %copy-start.5 = (bf16[2,64,512]{2,1,0:T(8,128)(2,1)}, bf16[2,64,512]{2,1,0:T(8,128)(2,1)S(1)}, u32[]{:S(2)}) copy-start(bf16[2,64,512]{2,1,0:T(8,128)(2,1)S(1)} %pad_maximum_fusion.1.pair0) | copy-start | bytes 393220
  86.0 15.6 %collective-permute-start.8 = (bf16[2,64,512]{2,1,0:T(8,128)(2,1)S(1)}, bf16[2,64,512]{2,1,0:T(8,128)(2,1)S(1)}, u32[]{:S(2)}, u32[]{:S(2)}) collective-permute-start(bf16[2,64,512]{2,1,0:T(8,128)(2,1)S(1)} %pad_maximum_fusion.1.pair0), channel_id=1, source_target_pairs={{0,6},{2,4},{4,2},{6,0},{1,7},{3,5},{5,3},{7,1},{8,14},{10,12},{12... | collective-permute-start | bytes 393224 | tf_op jit(solution)/shard_map/ppermute | solution.py:50
  97.5 10.4 %collective-permute-start.7 = (bf16[2,64,512]{2,1,0:T(8,128)(2,1)S(1)}, bf16[2,64,512]{2,1,0:T(8,128)(2,1)S(1)}, u32[]{:S(2)}, u32[]{:S(2)}) collective-permute-start(bf16[2,64,512]{2,1,0:T(8,128)(2,1)S(1)} %pad_maximum_fusion.1.pair0), channel_id=1, source_target_pairs={{0,4},{2,6},{4,0},{6,2},{1,5},{3,7},{5,1},{7,3},{8,12},{10,14},{12... | collective-permute-start | bytes 393224 | tf_op jit(solution)/shard_map/ppermute | solution.py:50
  99.4 9.3 %collective-permute-start.6 = (bf16[2,64,512]{2,1,0:T(8,128)(2,1)S(1)}, bf16[2,64,512]{2,1,0:T(8,128)(2,1)S(1)}, u32[]{:S(2)}, u32[]{:S(2)}) collective-permute-start(bf16[2,64,512]{2,1,0:T(8,128)(2,1)S(1)} %pad_maximum_fusion.1.pair0), channel_id=1, source_target_pairs={{0,2},{2,0},{4,6},{6,4},{1,3},{3,1},{5,7},{7,5},{8,10},{10,8},{12,... | collective-permute-start | bytes 393224 | tf_op jit(solution)/shard_map/ppermute | solution.py:50
  101.6 7.1 %copy-start.13 = (bf16[2,64,512]{2,1,0:T(8,128)(2,1)}, bf16[2,64,512]{2,1,0:T(8,128)(2,1)S(1)}, u32[]{:S(2)}) copy-start(bf16[2,64,512]{2,1,0:T(8,128)(2,1)S(1)} %collective-permute-done.8.pair3) | copy-start | bytes 393220
  107.9 0.9 copy-start.14
  108.8 0.6 copy-start.15
  109.4 0.8 copy-start
  169.1 40.9 %all-to-all-start.5 = ((bf16[8,72,512]{2,1,0:T(8,128)(2,1)}), bf16[8,72,512]{2,1,0:T(8,128)(2,1)S(1)}, u32[]{:S(2)}, u32[]{:S(2)}) async-start(bf16[8,72,512]{2,1,0:T(8,128)(2,1)} %grad_a.1), calls=%async_computation.5 | async-start | bytes 1179648 | tf_op jit(solution)/shard_map/all_to_all | solution.py:438
  177.1 8.3 %collective-permute-start.9 = (bf16[264,512]{1,0:T(8,128)(2,1)}, bf16[264,512]{1,0:T(8,128)(2,1)S(1)}, u32[]{:S(2)}, u32[]{:S(2)}) collective-permute-start(bf16[264,512]{1,0:T(8,128)(2,1)} %get-tuple-element.32), channel_id=1, source_target_pairs={{0,1},{1,0},{2,3},{3,2},{4,5},{5,4},{6,7},{7,6},{8,9},{9,8},{10,11... | collective-permute-start | bytes 811016 | tf_op jit(solution)/shard_map/ppermute | solution.py:50
  185.3 0.7 copy-start.6
  188.0 10.4 %collective-permute-start.10 = (bf16[72,512]{1,0:T(8,128)(2,1)}, bf16[72,512]{1,0:T(8,128)(2,1)S(1)}, u32[]{:S(2)}, u32[]{:S(2)}) collective-permute-start(bf16[72,512]{1,0:T(8,128)(2,1)} %get-tuple-element.34), channel_id=1, source_target_pairs={{0,2},{2,0},{4,6},{6,4},{1,3},{3,1},{5,7},{7,5},{8,10},{10,8},{12,... | collective-permute-start | bytes 221192 | tf_op jit(solution)/shard_map/ppermute | solution.py:50
  189.9 8.5 %collective-permute-start.11 = (bf16[72,512]{1,0:T(8,128)(2,1)}, bf16[72,512]{1,0:T(8,128)(2,1)S(1)}, u32[]{:S(2)}, u32[]{:S(2)}) collective-permute-start(bf16[72,512]{1,0:T(8,128)(2,1)} %get-tuple-element.35), channel_id=1, source_target_pairs={{0,4},{2,6},{4,0},{6,2},{1,5},{3,7},{5,1},{7,3},{8,12},{10,14},{12... | collective-permute-start | bytes 221192 | tf_op jit(solution)/shard_map/ppermute | solution.py:50
  193.3 7.2 %collective-permute-start.12 = (bf16[72,512]{1,0:T(8,128)(2,1)}, bf16[72,512]{1,0:T(8,128)(2,1)S(1)}, u32[]{:S(2)}, u32[]{:S(2)}) collective-permute-start(bf16[72,512]{1,0:T(8,128)(2,1)} %get-tuple-element.36), channel_id=1, source_target_pairs={{0,6},{2,4},{4,2},{6,0},{1,7},{3,5},{5,3},{7,1},{8,14},{10,12},{12... | collective-permute-start | bytes 221192 | tf_op jit(solution)/shard_map/ppermute | solution.py:50
  198.4 2.1 copy-start.16
  198.4 2.1 copy-start.17
  200.5 0.6 copy-start.18
  202.8 11.5 %collective-permute-start.13 = (bf16[64,512]{1,0:T(8,128)(2,1)}, bf16[64,512]{1,0:T(8,128)(2,1)S(1)}, u32[]{:S(2)}, u32[]{:S(2)}) collective-permute-start(bf16[64,512]{1,0:T(8,128)(2,1)} %dz_b.1), channel_id=1, source_target_pairs={{0,0},{1,8},{2,16},{3,24},{4,32},{5,40},{6,48},{7,56},{8,1},{9,9},... | collective-permute-start | bytes 196616 | tf_op jit(solution)/shard_map/ppermute | solution.py:448
  209.9 0.8 copy-start.1
  214.3 0.6 copy-start.19
  218.4 3.4 %collective-permute-start.14 = (bf16[264,256]{1,0:T(8,128)(2,1)}, bf16[264,256]{1,0:T(8,128)(2,1)S(1)}, u32[]{:S(2)}, u32[]{:S(2)}) collective-permute-start(bf16[264,256]{1,0:T(8,128)(2,1)} %get-tuple-element.39), channel_id=1, source_target_pairs={{0,1},{1,0},{2,3},{3,2},{4,5},{5,4},{6,7},{7,6},{8,9},{9,8},{10,11... | collective-permute-start | bytes 405512 | tf_op jit(solution)/shard_map/ppermute | solution.py:50
  221.8 0.7 copy-start.12

commit v5 on v4

v5 whole, which is shorter than its diff:
```python
import jax
import jax.numpy as jnp
from jax import lax
from jax.experimental import pallas as pl
from jax.experimental.pallas import tpu as pltpu
from jax.sharding import Mesh
from jax.sharding import PartitionSpec as P

GROUPS = 32
LAMBDA_OFF = 0.0051
NORM_EPS = 1e-05
LOSS_SCALE = 65536.0
INTERPRET = False

DP_SHAPE = (2, 4, 8)
TILE_SHAPE = (4, 2)
DP = ("zh", "x", "y")
TILE = ("zl", "c")
BF = jnp.bfloat16
F32 = jnp.float32
FAR = 1 << 20


def masked_views(feats, jitter, mask_ids):
    width = feats.shape[1]
    group_size = width // GROUPS
    channel_group = lax.broadcasted_iota(jnp.int32, (1, width), 1) // group_size
    keep_a = (channel_group != mask_ids[:, 0:1]).astype(F32)
    keep_b = (channel_group != mask_ids[:, 1:2]).astype(F32)
    values = feats.astype(F32)
    view_a = (values * keep_a).astype(BF)
    view_b = (values * keep_b + jitter.astype(F32)).astype(BF)
    return jnp.concatenate([view_a, view_b], axis=0), keep_a, keep_b


def spread(value, axes):
    parts = lax.axis_size(axes)
    return lax.all_to_all(
        jnp.broadcast_to(value[None], (parts,) + value.shape), axes, 0, 0, tiled=True
    )


def shift(value, axis, step):
    n = lax.axis_size(axis)
    return lax.ppermute(value, axis, [(i, (i + step) % n) for i in range(n)])


def flip(value, axis, step):
    n = lax.axis_size(axis)
    return lax.ppermute(value, axis, [(i, i ^ step) for i in range(n)])


def swap_pairs(other):
    zh_n, x_n, n = DP_SHAPE
    where = lambda zh, x, y, t: ((zh * x_n + x) * n + y) * n + t
    return [
        (where(zh, x, y, t), where(zh ^ other, x, t, y))
        for zh in range(zh_n)
        for x in range(x_n)
        for y in range(n)
        for t in range(n)
    ]


def dot(a, b, ca, cb, precision=None):
    return lax.dot_general(
        a, b, (((ca,), (cb,)), ((), ())), precision=precision, preferred_element_type=F32
    )


def exact(a, b, ca, cb):
    return dot(a, b, ca, cb, lax.Precision.HIGHEST)


def put_pieces(ref, at, value, count):
    for i in range(count):
        part = value.astype(BF).astype(F32)
        ref[at + i : at + i + 1, :] = part
        value = value - part
    return at + count


def joined(rows, at, count):
    total = rows[at : at + 1]
    for i in range(1, count):
        total = total + rows[at + i : at + i + 1]
    return total


def call(body, name, outs, args, scratch=()):
    specs = [
        pl.BlockSpec(memory_space=pltpu.SMEM if a.dtype == jnp.int32 and a.ndim == 1 else pltpu.VMEM)
        for a in args
    ]
    return pl.pallas_call(
        body,
        name=name,
        out_shape=[jax.ShapeDtypeStruct(s, d) for s, d in outs],
        in_specs=specs,
        out_specs=[pl.BlockSpec(memory_space=pltpu.VMEM) for _ in outs],
        scratch_shapes=[pltpu.VMEM(s, d) for s, d in scratch],
        interpret=INTERPRET,
    )(*args)


def project_body(at, view, own, back, ahead, far_low, far_high, piece, wide_a, same_b, other_b):
    zh_n, x_n, y_n, rows, kt = piece.shape
    x = at[0]
    half = y_n // 2
    for zh in range(zh_n):
        piece[zh, x] = own[:, zh]
        piece[zh, lax.rem(x + x_n - 1, x_n)] = back[:, zh]
        piece[zh, lax.rem(x + 1, x_n)] = ahead[:, zh]
        far = lax.rem(x + 2, x_n)
        piece[zh, far, :half] = far_low[:, zh]
        piece[zh, far, half:] = far_high[:, zh]
    weight = piece[...].reshape(zh_n * x_n * y_n * rows, kt)
    raw = dot(view[...], weight, 1, 0).astype(BF)
    n, half_kt = same_b.shape
    for i in range(wide_a.shape[0]):
        wide_a[i] = raw[:n]
    low, high = raw[n:, :half_kt], raw[n:, half_kt:]
    first = at[5] == 0
    same_b[...] = jnp.where(first, low, high)
    other_b[...] = jnp.where(first, high, low)


def gram_body(at, big_a, big_b, out, tail):
    parts, rows, kt = big_a.shape
    block = parts * rows
    kl = big_b.shape[2]
    a = big_a[...].reshape(block, kt).astype(F32)
    b = big_b[...].reshape(block, kl).astype(F32)
    mean_a = jnp.sum(a, axis=0, keepdims=True) / block
    mean_b = jnp.sum(b, axis=0, keepdims=True) / block
    a = a - mean_a
    b = b - mean_b
    gram = dot(a.astype(BF), b.astype(BF), 0, 0).astype(BF)
    square_a = jnp.sum(a * a, axis=0, keepdims=True)
    facing = jnp.where(at[5] == 0, a[:, :kl], a[:, kl:])
    tail[...] = jnp.zeros_like(tail)
    pos = 0
    for row in (
        mean_a[:, :kl],
        mean_a[:, kl:],
        square_a[:, :kl],
        square_a[:, kl:],
        mean_b,
        jnp.sum(b * b, axis=0, keepdims=True),
        jnp.sum(facing * b, axis=0, keepdims=True),
    ):
        pos = put_pieces(tail, pos, row, 3)
    deep = out.shape[1] - tail.shape[0]
    rows_out = tail[...].astype(BF)
    for x in range(out.shape[0]):
        out[x, :deep] = gram[x * deep : (x + 1) * deep]
        out[x, deep:] = rows_out


def mix_body(at, got, mix, stats_a, stats_b, table, offs, *, block):
    sets, deep, kl = got.shape
    sub = mix.shape[0]
    kt = stats_a.shape[1]
    total = block * sets
    raws = []
    for x in range(sets):
        rows = got[x, sub:].astype(F32)
        r = [joined(rows, 3 * i, 3) for i in range(7)]
        wide = lambda i: jnp.concatenate([r[i], r[i + 1]], axis=1)
        raws.append((wide(0), wide(2), r[4], r[5], r[6]))
    summed = [sum((r[i] for r in raws[1:]), raws[0][i]) for i in range(5)]
    mean_a, mean_b = summed[0] / sets, summed[2] / sets
    square_a, square_b, cross = summed[1], summed[3], summed[4]
    drift_a = jnp.zeros_like(mean_a)
    drift_b = jnp.zeros_like(mean_b)
    first = at[5] == 0
    facing = lambda row: jnp.where(first, row[:, :kl], row[:, kl:])
    table[...] = jnp.zeros_like(table)
    offs[...] = jnp.zeros_like(offs)
    for i, r in enumerate(raws):
        off_a, off_b = r[0] - mean_a, r[2] - mean_b
        square_a = square_a + block * off_a * off_a
        square_b = square_b + block * off_b * off_b
        cross = cross + block * facing(off_a) * off_b
        drift_a, drift_b = drift_a + off_a, drift_b + off_b
        table[i : i + 1, :] = off_a
        offs[i : i + 1, :] = block * off_b
    inv_a = lax.rsqrt(square_a / total + NORM_EPS)
    inv_b = lax.rsqrt(square_b / total + NORM_EPS)
    table[sets : sets + 1, :] = inv_a
    diag = cross * (facing(inv_a) * inv_b / total)
    coeff = -2.0 * (1.0 - diag) - 2.0 * LAMBDA_OFF * diag
    k_of = lax.broadcasted_iota(jnp.int32, (sub, kt), 0)
    l_of = lax.broadcasted_iota(jnp.int32, (sub, kt), 1)
    chosen = exact((k_of + at[3] == l_of).astype(F32), table[...], 1, 1)
    corr = got[0, :sub].astype(F32)
    for x in range(1, sets):
        corr = corr + got[x, :sub].astype(F32)
    corr = corr + exact(chosen, offs[...], 1, 0)
    corr = corr * (chosen[:, sets : sets + 1] * (inv_b / total))
    k_of = lax.broadcasted_iota(jnp.int32, (sub, kl), 0)
    l_of = lax.broadcasted_iota(jnp.int32, (sub, kl), 1)
    here = k_of + at[3] == l_of + at[4]
    mix[...] = jnp.where(
        here, coeff + 2.0 * LAMBDA_OFF * diag, 2.0 * LAMBDA_OFF * corr
    ).astype(BF)
    held = diag * (at[4] != FAR).astype(F32)
    none = jnp.zeros_like(held)
    stats_a[...] = jnp.zeros_like(stats_a)
    stats_b[...] = jnp.zeros_like(stats_b)
    stats_a[0:1, :] = mean_a
    stats_a[1:2, :] = inv_a
    stats_a[2:3, :] = drift_a * inv_a / sets
    stats_a[3:4, :kl] = jnp.where(first, held, none)
    stats_a[3:4, kl:] = jnp.where(first, none, held)
    stats_b[0:1, :] = mean_b
    stats_b[1:2, :] = inv_b
    stats_b[2:3, :] = drift_b * inv_b / sets
    stats_b[3:4, :] = diag


def correlation(at, mix, stats_b):
    k_of = lax.broadcasted_iota(jnp.int32, mix.shape, 0)
    l_of = lax.broadcasted_iota(jnp.int32, mix.shape, 1)
    return jnp.where(k_of == l_of + at[4], stats_b[3:4, :], mix * (0.5 / LAMBDA_OFF))


def grad_b_body(at, mix4, big_a, stats_a, stats_b, sent, kept, grads, tail):
    c = at[2]
    parts, rows, kl = grads.shape
    kt = big_a.shape[2]
    line = parts // 2
    mix = mix4[...].reshape(kt, kl)
    wide = mix.astype(F32)
    norm_a = (big_a[...].reshape(parts * rows, kt).astype(F32) - stats_a[0:1, :]) * stats_a[1:2, :]
    grads[...] = dot(norm_a.astype(BF), mix, 1, 0).reshape(parts, rows, kl)
    for z in range(line):
        sent[z * rows : (z + 1) * rows] = grads[z * 2 + (1 - c)].astype(BF)
        kept[z * rows : (z + 1) * rows] = grads[z * 2 + c]
    second = jnp.sum(wide * correlation(at, wide, stats_b), axis=0, keepdims=True)
    first = exact(stats_a[...], wide, 1, 0)[2:3]
    tail[...] = jnp.zeros_like(tail)
    pos = put_pieces(tail, 0, second, 3)
    put_pieces(tail, pos, first, 2)
    sent[line * rows :] = tail[...].astype(BF)
    kept[line * rows :] = jnp.zeros_like(tail)
    kept[line * rows : line * rows + 1] = second
    kept[line * rows + 1 : line * rows + 2] = first


def grad_a_body(at, mix4, big_b, stats_a, stats_b, out, tail):
    parts, deep, kt = out.shape
    rows = deep - 8
    kl = big_b.shape[2]
    mix = mix4[...].reshape(kt, kl)
    wide = mix.astype(F32)
    norm_b = (big_b[...].reshape(parts * rows, kl).astype(F32) - stats_b[0:1, :]) * stats_b[1:2, :]
    grad = dot(norm_b.astype(BF), mix, 1, 1).astype(BF)
    corr = correlation(at, wide, stats_b)
    ones = jnp.ones((8, kl), F32)
    pos = put_pieces(tail, 0, exact(ones, wide * corr, 1, 1)[0:1], 2)
    pos = put_pieces(tail, pos, exact(ones, corr * corr, 1, 1)[0:1], 2)
    pos = put_pieces(tail, pos, stats_a[3:4, :], 3)
    put_pieces(tail, pos, exact(stats_b[...], wide, 1, 1)[2:3], 1)
    rows_out = tail[...].astype(BF)
    for i in range(parts):
        out[i, :rows] = grad[i * rows : (i + 1) * rows]
        out[i, rows:] = rows_out


def core_body(at, kept, got, own, out1, out2, out3, total, tail):
    zl = at[1]
    rows = own.shape[0] - 8
    deep = kept.shape[0] - 8
    total[...] = kept[:deep] + got[:deep].astype(F32)
    theirs = got[deep:].astype(F32)
    second = kept[deep : deep + 1] + joined(theirs, 0, 3)
    first = kept[deep + 1 : deep + 2] + joined(theirs, 3, 2)
    tail[...] = jnp.zeros_like(tail)
    pos = put_pieces(tail, 0, second, 3)
    put_pieces(tail, pos, first, 2)
    rows_out = tail[...].astype(BF)
    start = lambda step: pl.ds(pl.multiple_of((zl ^ step) * rows, rows), rows)
    for step, out in enumerate((out1, out2, out3), 1):
        out[:rows] = total[start(step), :].astype(BF)
        out[rows:] = rows_out
    own[:rows] = total[start(0), :]
    own[rows:] = jnp.zeros_like(tail)
    own[rows : rows + 1] = second
    own[rows + 1 : rows + 2] = first


def dz_b_body(at, own, got1, got2, got3, raw_b, stats_b, same, other, both):
    deep = both.shape[0]
    rows = same.shape[0]
    grad = own[:deep]
    second, first = own[deep : deep + 1], own[deep + 1 : deep + 2]
    for got in (got1, got2, got3):
        grad = grad + got[:deep].astype(F32)
        theirs = got[deep:].astype(F32)
        second = second + joined(theirs, 0, 3)
        first = first + joined(theirs, 3, 2)
    inv = stats_b[1:2, :]
    norm = ((raw_b[...].astype(F32) - stats_b[0:1, :]) * inv).astype(BF).astype(F32)
    both = (inv * (grad - first - norm * second)).astype(BF)
    low = at[5] == 0
    same[...] = jnp.where(low, both[:rows], both[rows:])
    other[...] = jnp.where(low, both[rows:], both[:rows])


def back_a_body(got, raw_a, stats_a, keep, weight, out, diag_out, power_out):
    parts, deep, kt = got.shape
    rows = deep - 8
    grad = got[0, :rows].astype(F32)
    tails = [got[i, rows:].astype(F32) for i in range(parts)]
    for i in range(1, parts):
        grad = grad + got[i, :rows].astype(F32)
    gather = lambda pos, count: sum(
        (joined(t, pos, count) for t in tails[1:]), joined(tails[0], pos, count)
    )
    second, power, diag, first = gather(0, 2), gather(2, 2), gather(4, 3), gather(7, 1)
    inv = stats_a[1:2, :]
    norm = ((raw_a[...].astype(F32) - stats_a[0:1, :]) * inv).astype(BF).astype(F32)
    dz = (inv * (grad - first - norm * second)).astype(BF)
    width = keep.shape[1]
    out[...] = keep[...] * dot(dz, weight[...].reshape(width, kt), 1, 1)
    diag_out[...] = diag
    power_out[...] = jnp.broadcast_to(jnp.sum(power, axis=1, keepdims=True), power_out.shape)


def back_b_body(at, part, same, other, keep, weight, power, out, tail):
    rows, width = part.shape
    parts, _, chunk = out.shape
    low = at[5] == 0
    dz = jnp.concatenate(
        [jnp.where(low, same[...], other[...]), jnp.where(low, other[...], same[...])], axis=1
    )
    both = part[...] + keep[...] * dot(dz, weight[...].reshape(width, dz.shape[1]), 1, 1)
    both = both.astype(BF)
    tail[...] = jnp.zeros_like(tail)
    put_pieces(tail, 0, power[...], 3)
    rows_out = tail[...].astype(BF)
    for i in range(parts):
        out[i, :rows] = both[:, i * chunk : (i + 1) * chunk]
        out[i, rows:] = rows_out


def end_body(got, out, power_out, *, scale, features):
    line, deep, _ = got.shape
    rows = deep - 8
    total = got[0, :rows].astype(F32)
    power = joined(got[0, rows:].astype(F32), 0, 3)
    for z in range(1, line):
        total = total + got[z, :rows].astype(F32)
        power = power + joined(got[z, rows:].astype(F32), 0, 3)
    out[...] = scale * total
    power_out[...] = power / features


def on_device(feats, jitter, mask_ids, weight):
    rows, width = feats.shape
    w_rows, kt = weight.shape
    zh_n, x_n, y_n = DP_SHAPE
    zl_n, c_n = TILE_SHAPE
    tile_n = zl_n * c_n
    parts = y_n * zh_n
    block = rows * parts
    total = block * x_n
    sub = kt // x_n
    kl = kt // zh_n
    chunk = width // tile_n
    every = DP + TILE
    zh_at = lax.axis_index("zh")
    at = jnp.stack(
        [
            lax.axis_index("x"),
            lax.axis_index("zl"),
            lax.axis_index("c"),
            lax.axis_index("x") * sub,
            jnp.where(lax.axis_index("y") == lax.axis_index(TILE), zh_at * kl, FAR),
            zh_at,
        ]
    ).astype(jnp.int32)
    view, keep_a, keep_b = masked_views(feats, jitter, mask_ids)

    own = lax.all_gather(weight, "zh", axis=0, tiled=True)
    own = spread(own, "y").reshape(y_n, zh_n, w_rows, kt)
    half = y_n // 2
    back = shift(own, "x", 1)
    ahead = shift(own, "x", x_n - 1)
    far_low = shift(back[:half], "x", 1)
    far_high = shift(ahead[half:], "x", x_n - 1)
    piece, wide_a, same_b, other_b = call(
        project_body,
        "project",
        [
            ((zh_n, x_n, y_n, w_rows, kt), BF),
            ((parts, rows, kt), BF),
            ((rows, kl), BF),
            ((rows, kl), BF),
        ],
        (at, view, own, back, ahead, far_low, far_high),
    )

    raw_a = wide_a[0]
    big_a = lax.all_to_all(wide_a, ("y", "zh"), 0, 0, tiled=True)
    same_b = lax.ppermute(same_b, every, swap_pairs(0))
    other_b = lax.ppermute(other_b, every, swap_pairs(1))
    own_b = jnp.concatenate(
        [jnp.where(zh_at == 0, same_b, other_b), jnp.where(zh_at == 0, other_b, same_b)], axis=0
    )
    big_b = lax.all_gather(own_b, TILE, axis=0)
    (gram,) = call(
        gram_body, "gram", [((x_n, sub + 32, kl), BF)], (at, big_a, big_b), [((32, kl), F32)]
    )

    got = lax.all_to_all(gram, "x", 0, 0, tiled=True)
    mix, stats_a, stats_b = call(
        lambda *refs: mix_body(*refs, block=block),
        "mix",
        [((sub, kl), BF), ((8, kt), F32), ((8, kl), F32)],
        (at, got),
        [((8, kt), F32), ((8, kl), F32)],
    )
    mix = spread(mix, "x")

    b_rows = rows * zh_n
    line_rows = zl_n * b_rows + 8
    sent, kept = call(
        grad_b_body,
        "grad_b",
        [((line_rows, kl), BF), ((line_rows, kl), F32)],
        (at, mix, big_a, stats_a, stats_b),
        [((tile_n, b_rows, kl), F32), ((8, kl), F32)],
    )
    got_b = flip(sent, "c", 1)
    (grad_a,) = call(
        grad_a_body,
        "grad_a",
        [((parts, rows + 8, kt), BF)],
        (at, mix, big_b, stats_a, stats_b),
        [((8, kt), F32)],
    )
    got_a = lax.all_to_all(grad_a, ("y", "zh"), 0, 0, tiled=True)
    own, *outs = call(
        core_body,
        "core",
        [((b_rows + 8, kl), F32)] + [((b_rows + 8, kl), BF)] * 3,
        (at, kept, got_b),
        [((zl_n * b_rows, kl), F32), ((8, kl), F32)],
    )
    gots = [flip(o, "zl", step) for step, o in enumerate(outs, 1)]
    same_b, other_b = call(
        dz_b_body,
        "dz_b",
        [((rows, kl), BF), ((rows, kl), BF)],
        (at, own, *gots, own_b, stats_b),
        [((b_rows, kl), BF)],
    )
    same_b = lax.ppermute(same_b, every, swap_pairs(0))
    other_b = lax.ppermute(other_b, every, swap_pairs(1))
    part, diag_corr, power = call(
        back_a_body,
        "back_a",
        [((rows, width), F32), ((1, kt), F32), ((1, chunk), F32)],
        (got_a, raw_a, stats_a, keep_a, piece),
    )
    (share,) = call(
        back_b_body,
        "back_b",
        [((tile_n, rows + 8, chunk), BF)],
        (at, part, same_b, other_b, keep_b, piece, power),
        [((8, chunk), F32)],
    )
    got = lax.all_to_all(share, TILE, 0, 0, tiled=True)
    feats_grad, cross_power = call(
        lambda *refs: end_body(*refs, scale=LOSS_SCALE / total, features=kt * tile_n),
        "end",
        [((rows, chunk), F32), ((1, chunk), F32)],
        (got,),
    )
    return feats_grad, diag_corr[0], cross_power[0, 0]


def solution(mesh):
    fine = Mesh(mesh.devices.reshape(DP_SHAPE + TILE_SHAPE), DP + TILE)
    in_specs = (P(DP, None), P(DP, None), P(DP, None), P(DP, TILE))
    out_specs = (P(DP, TILE), P(TILE), P())
    return jax.shard_map(
        on_device, mesh=fine, in_specs=in_specs, out_specs=out_specs, check_vma=False
    )
```

time: 241 us -> 256 us (1.062)
  waiting for transfers between devices: 28.5 us -> 55.3 us
  starting transfers between devices: 73 us -> 69 us
  Pallas kernels: 32.4 us -> 28.6 us
  blocking collectives: 93.1 us -> 89.7 us
    ppermute x9 -> x4, starting transfers between devices: 35.6 us -> 13.5 us  [flip(): return lax.ppermute(value, axis, [(i, i ^ step) for i in range(n)])]
    ppermute x2 -> x4, waiting for transfers between devices: 5.72 us -> 21.2 us  [the longest x2 10.8 us: on_device(): same_b = lax.ppermute(same_b, every, swap_pairs(0))]
    ppermute x9 -> x4, waiting for transfers between devices: 13.3 us -> 23.9 us  [flip(): return lax.ppermute(value, axis, [(i, i ^ step) for i in range(n)])]
    ppermute x2 -> x4, starting transfers between devices: 13.3 us -> 23.1 us  [the longest x2 12.4 us: on_device(): other_b = lax.ppermute(other_b, every, swap_pairs(1))]
    all_to_all x2 -> x1, blocking collectives: 28.6 us -> 19.7 us  [on_device(): got = lax.all_to_all(share, TILE, 0, 0, tiled=True)]
    all_gather x1, blocking collectives: 7.9 us -> 16.5 us  [on_device(): big_b = lax.all_gather(own_b, TILE, axis=0)]
    all_to_all x2, starting transfers between devices: 10.6 us -> 18.8 us  [the longest x1 10.9 us: on_device(): big_a = lax.all_to_all(wide_a, ('y', 'zh'), 0, 0, tiled=True)]
    pallas_call x12 -> x10, Pallas kernels: 32.4 us -> 28.6 us  [call(): pl.pallas_call(body, name=name, out_shape=[jax.ShapeDtypeStruct(s, d) for...]
  transfers between devices with their start and end apart: 17 -> 14, of which waited for: 9 -> 7; matrix products, arithmetic and copies ran while one was open for 2% -> 2% of each run, Pallas kernels for 4% -> 4%
where the time goes in v5:
time: 256 us; the launch traced here: 255 us
  blocking collectives  89.7 us (35%)
  starting transfers between devices  69 us (27%)
  waiting for transfers between devices  55.3 us (22%)
  Pallas kernels  28.6 us (11%)
  local copies, waits for them, and re-layouts  8.9 us (3%)
    all_to_all x2, blocking collectives, spread(): lax.all_to_all(jnp.broadcast_to(value[None], (parts,) + value.shape), axe...  30.1 us
    pallas_call x10, Pallas kernels, call(): pl.pallas_call(body, name=name, out_shape=[jax.ShapeDtypeStruct(s, d) for...  28.6 us
    ppermute x4, waiting for transfers between devices, flip(): return lax.ppermute(value, axis, [(i, i ^ step) for i in range(n)])  23.9 us
    all_to_all x1, blocking collectives, on_device(): got = lax.all_to_all(share, TILE, 0, 0, tiled=True)  19.7 us
    all_gather x1, blocking collectives, on_device(): big_b = lax.all_gather(own_b, TILE, axis=0)  16.5 us
    ppermute x4, starting transfers between devices, shift(): return lax.ppermute(value, axis, [(i, (i + step) % n) for i in range(n)])  13.5 us
    ppermute x4, starting transfers between devices, flip(): return lax.ppermute(value, axis, [(i, i ^ step) for i in range(n)])  13.5 us
    ppermute x2, starting transfers between devices, on_device(): other_b = lax.ppermute(other_b, every, swap_pairs(1))  12.4 us
  transfers between devices with their start and end apart: 14, of which 7 were waited for; matrix products, arithmetic and copies ran while one was open for 2% of the time, Pallas kernels for 4%

profile of v5, /device:TPU:1, one launch (start us, length us, event | category | flops | bytes accessed | tf_op | source)
XLA Modules:
  0.0 254.7 jit_solution(7003185392878484768)
XLA Ops:
  0.6 11.8 %all_gather.9 = bf16[64,512]{1,0:T(8,128)(2,1)S(1)} all-gather(bf16[32,512]{1,0:T(8,128)(2,1)} %param.7), channel_id=1, replica_groups=mesh['zh'=2,'x'=4,'y'=8,'zl'=4,'c'=2] {'zh'}, dimensions={0}, use_global_device_ids=true | all-gather | bytes 98304 | tf_op jit(solution)/shard_map/all_gather | solution.py:386
  12.5 21.5 %all_to_all.30 = bf16[8,64,512]{2,1,0:T(8,128)(2,1)S(1)} all-to-all(bf16[8,64,512]{2,1,0:T(8,128)(2,1)S(1)} %broadcast_in_dim.4), channel_id=1, replica_groups=mesh['zh'=2,'x'=4,'y'=8,'zl'=4,'c'=2] {'y'}, dimensions={0} | all-to-all | bytes 1048576 | tf_op jit(solution)/shard_map/all_to_all | solution.py:38
  34.0 4.4 %collective-permute-start.1 = (bf16[8,2,32,512]{3,2,1,0:T(8,128)(2,1)S(1)}, bf16[8,2,32,512]{3,2,1,0:T(8,128)(2,1)S(1)}, u32[]{:S(2)}, u32[]{:S(2)}) collective-permute-start(bf16[8,2,32,512]{3,2,1,0:T(8,128)(2,1)S(1)} %bitcast.18), channel_id=1, source_target_pairs={{0,192},{64,0},{128,64},{192,128},{1,193},{65,1},{129,65},{193,129... | collective-permute-start | bytes 1572872 | tf_op jit(solution)/shard_map/ppermute | solution.py:45
  38.4 1.9 collective-permute-start
  40.4 5.5 %collective-permute-done.1.ahead = bf16[8,2,32,512]{3,2,1,0:T(8,128)(2,1)S(1)} collective-permute-done((bf16[8,2,32,512]{3,2,1,0:T(8,128)(2,1)S(1)}, bf16[8,2,32,512]{3,2,1,0:T(8,128)(2,1)S(1)}, u32[]{:S(2)}, u32[]{:S(2)}) %collective-permute-start.1) | collective-permute-done | bytes 524320 | tf_op jit(solution)/shard_map/ppermute | solution.py:45
  46.0 5.3 %collective-permute-start.3 = (bf16[4,2,32,512]{3,2,1,0:T(8,128)(2,1)S(1)}, bf16[4,2,32,512]{3,2,1,0:T(8,128)(2,1)S(1)}, u32[]{:S(2)}, u32[]{:S(2)}) collective-permute-start(bf16[4,2,32,512]{3,2,1,0:T(8,128)(2,1)S(1)} %slice.25), channel_id=1, source_target_pairs={{0,192},{64,0},{128,64},{192,128},{1,193},{65,1},{129,65},{193,129... | collective-permute-start | bytes 786440 | tf_op jit(solution)/shard_map/ppermute | solution.py:45
  51.3 1.9 collective-permute-start.2
  53.5 0.6 stack.27.at.refs_0_
  54.2 0.8 pad_maximum_fusion.view
  55.0 4.6 %collective-permute-done.2.far_low = bf16[4,2,32,512]{3,2,1,0:T(8,128)(2,1)S(1)} collective-permute-done((bf16[4,2,32,512]{3,2,1,0:T(8,128)(2,1)S(1)}, bf16[4,2,32,512]{3,2,1,0:T(8,128)(2,1)S(1)}, u32[]{:S(2)}, u32[]{:S(2)}) %collective-permute-start.2) | collective-permute-done | bytes 262176 | tf_op jit(solution)/shard_map/ppermute | solution.py:45
  59.7 0.7 copy-done.10
  60.3 3.7 %project.1 = (bf16[2,4,8,32,512]{4,3,2,1,0:T(8,128)(2,1)}, bf16[16,64,512]{2,1,0:T(8,128)(2,1)}, bf16[64,256]{1,0:T(8,128)(2,1)}, bf16[64,256]{1,0:T(8,128)(2,1)}) custom-call(s32[6]{0:T(128)} %stack.27.at.refs_0_, bf16[128,2048]{1,0:T(8,128)(2,1)} %pad_maximum_fusion.view, bf16[8,2,32,512]{3,2,1,0:T(8,128)(2,1)} %bitcast.20, ...), custom_call_target="tpu_custom_call" | custom-call | tf_op jit(solution)/shard_map/project/pallas_call | solution.py:95
  64.0 10.9 %all-to-all-start.1 = ((bf16[16,64,512]{2,1,0:T(8,128)(2,1)}), bf16[16,64,512]{2,1,0:T(8,128)(2,1)S(1)}, u32[]{:S(2)}, u32[]{:S(2)}) async-start(bf16[16,64,512]{2,1,0:T(8,128)(2,1)} %get-tuple-element.23), calls=%async_computation.1 | async-start | bytes 2097152 | tf_op jit(solution)/shard_map/all_to_all | solution.py:406
  74.9 7.8 %collective-permute-start.4 = (bf16[64,256]{1,0:T(8,128)(2,1)S(1)}, bf16[64,256]{1,0:T(8,128)(2,1)S(1)}, u32[]{:S(2)}, u32[]{:S(2)}) collective-permute-start(bf16[64,256]{1,0:T(8,128)(2,1)S(1)} %copy-done.18), channel_id=1, source_target_pairs={{0,0},{1,8},{2,16},{3,24},{4,32},{5,40},{6,48},{7,56},{8,1},{9,9},... | collective-permute-start | bytes 98312 | tf_op jit(solution)/shard_map/ppermute | solution.py:407
  82.7 6.7 %collective-permute-start.5 = (bf16[64,256]{1,0:T(8,128)(2,1)S(1)}, bf16[64,256]{1,0:T(8,128)(2,1)S(1)}, u32[]{:S(2)}, u32[]{:S(2)}) collective-permute-start(bf16[64,256]{1,0:T(8,128)(2,1)S(1)} %copy-done.17), channel_id=1, source_target_pairs={{0,256},{1,264},{2,272},{3,280},{4,288},{5,296},{6,304},{7,312},{8... | collective-permute-start | bytes 98312 | tf_op jit(solution)/shard_map/ppermute | solution.py:408
  89.5 10.8 %collective-permute-done.4 = bf16[64,256]{1,0:T(8,128)(2,1)S(1)} collective-permute-done((bf16[64,256]{1,0:T(8,128)(2,1)S(1)}, bf16[64,256]{1,0:T(8,128)(2,1)S(1)}, u32[]{:S(2)}, u32[]{:S(2)}) %collective-permute-start.4) | collective-permute-done | bytes 32800 | tf_op jit(solution)/shard_map/ppermute | solution.py:407
  100.2 10.4 %collective-permute-done.5 = bf16[64,256]{1,0:T(8,128)(2,1)S(1)} collective-permute-done((bf16[64,256]{1,0:T(8,128)(2,1)S(1)}, bf16[64,256]{1,0:T(8,128)(2,1)S(1)}, u32[]{:S(2)}, u32[]{:S(2)}) %collective-permute-start.5) | collective-permute-done | bytes 32800 | tf_op jit(solution)/shard_map/ppermute | solution.py:408
  110.7 16.5 %all-gather = bf16[1024,256]{1,0:T(8,128)(2,1)} all-gather(bf16[128,256]{1,0:T(8,128)(2,1)S(1)} %pad_maximum_fusion.1.raw_b), channel_id=2, replica_groups=mesh['zh'=2,'x'=4,'y'=8,'zl'=4,'c'=2] {'zl','c'}, dimensions={0}, use_global_device_ids=true | all-gather | bytes 589824 | tf_op jit(solution)/shard_map/all_gather | solution.py:412
  127.2 1.0 copy-done
  128.2 3.3 %gram.1 = bf16[4,160,256]{2,1,0:T(8,128)(2,1)} custom-call(s32[6]{0:T(128)} %stack.27.at.refs_0_, bf16[16,64,512]{2,1,0:T(8,128)(2,1)} %copy-done, bf16[8,128,256]{2,1,0:T(8,128)(2,1)} %bitcast.16), custom_call_target="tpu_custom_call" | custom-call | tf_op jit(solution)/shard_map/gram/pallas_call | solution.py:95
  131.6 11.5 %all_to_all.31.refs_1_ = bf16[4,160,256]{2,1,0:T(8,128)(2,1)} all-to-all(bf16[4,160,256]{2,1,0:T(8,128)(2,1)} %gram.1), channel_id=1, replica_groups=mesh['zh'=2,'x'=4,'y'=8,'zl'=4,'c'=2] {'x'}, dimensions={0} | all-to-all | bytes 655360 | tf_op jit(solution)/shard_map/all_to_all | solution.py:417
  143.1 2.4 mix.1
  145.4 0.9 broadcast_in_dim.5
  146.3 8.6 %all_to_all.32.mix4 = bf16[4,128,256]{2,1,0:T(8,128)(2,1)} all-to-all(bf16[4,128,256]{2,1,0:T(8,128)(2,1)S(1)} %broadcast_in_dim.5), channel_id=1, replica_groups=mesh['zh'=2,'x'=4,'y'=8,'zl'=4,'c'=2] {'x'}, dimensions={0} | all-to-all | bytes 524288 | tf_op jit(solution)/shard_map/all_to_all | solution.py:38
  154.9 3.8 %grad_a.1 = bf16[16,72,512]{2,1,0:T(8,128)(2,1)} custom-call(s32[6]{0:T(128)} %stack.27.at.refs_0_, bf16[4,128,256]{2,1,0:T(8,128)(2,1)} %all_to_all.32.mix4, bf16[8,128,256]{2,1,0:T(8,128)(2,1)} %bitcast.17, f32[8,512]{1,0:T(8,128)} %get-tuple-element.27.stats_a, f32[8,256]{1,0:T(8,128)} %get-tuple-element.28.stats_b), custom_call_target="tpu_custom_call" | custom-call | tf_op jit(solution)/shard_map/grad_a/pallas_call | solution.py:95
  158.7 7.9 %all-to-all-start.4 = ((bf16[16,72,512]{2,1,0:T(8,128)(2,1)}), bf16[16,72,512]{2,1,0:T(8,128)(2,1)S(1)}, u32[]{:S(2)}, u32[]{:S(2)}) async-start(bf16[16,72,512]{2,1,0:T(8,128)(2,1)} %grad_a.1), calls=%async_computation.4 | async-start | bytes 2359296 | tf_op jit(solution)/shard_map/all_to_all | solution.py:444
  166.6 2.9 %grad_b.1 = (bf16[520,256]{1,0:T(8,128)(2,1)}, f32[520,256]{1,0:T(8,128)}) custom-call(s32[6]{0:T(128)} %stack.27.at.refs_0_, bf16[4,128,256]{2,1,0:T(8,128)(2,1)} %all_to_all.32.mix4, bf16[16,64,512]{2,1,0:T(8,128)(2,1)} %copy-done, f32[8,512]{1,0:T(8,128)} %get-tuple-element.27.stats_a, f32[8,256]{1,0:T(8,128)} %get-tuple-element.28.stats_b), custom_call_target="tpu_custom_call" | custom-call | tf_op jit(solution)/shard_map/grad_b/pallas_call | solution.py:95
  169.6 4.3 %collective-permute-start.6 = (bf16[520,256]{1,0:T(8,128)(2,1)}, bf16[520,256]{1,0:T(8,128)(2,1)S(1)}, u32[]{:S(2)}, u32[]{:S(2)}) collective-permute-start(bf16[520,256]{1,0:T(8,128)(2,1)} %get-tuple-element.32), channel_id=1, source_target_pairs={{0,1},{1,0},{2,3},{3,2},{4,5},{5,4},{6,7},{7,6},{8,9},{9,8},{10,11... | collective-permute-start | bytes 798728 | tf_op jit(solution)/shard_map/ppermute | solution.py:50
  173.9 1.4 collective-permute-done.6.got
  175.2 0.7 copy-done.6
  175.9 1.9 core.1
  177.9 3.1 %collective-permute-start.7 = (bf16[136,256]{1,0:T(8,128)(2,1)}, bf16[136,256]{1,0:T(8,128)(2,1)S(1)}, u32[]{:S(2)}, u32[]{:S(2)}) collective-permute-start(bf16[136,256]{1,0:T(8,128)(2,1)} %get-tuple-element.34), channel_id=1, source_target_pairs={{0,2},{2,0},{4,6},{6,4},{1,3},{3,1},{5,7},{7,5},{8,10},{10,8},{12,... | collective-permute-start | bytes 208904 | tf_op jit(solution)/shard_map/ppermute | solution.py:50
  181.0 4.1 %collective-permute-start.8 = (bf16[136,256]{1,0:T(8,128)(2,1)}, bf16[136,256]{1,0:T(8,128)(2,1)S(1)}, u32[]{:S(2)}, u32[]{:S(2)}) collective-permute-start(bf16[136,256]{1,0:T(8,128)(2,1)} %get-tuple-element.35), channel_id=1, source_target_pairs={{0,4},{2,6},{4,0},{6,2},{1,5},{3,7},{5,1},{7,3},{8,12},{10,14},{12... | collective-permute-start | bytes 208904 | tf_op jit(solution)/shard_map/ppermute | solution.py:50
  185.0 2.1 collective-permute-start.9
  187.1 1.1 compare_convert_fusion
  188.3 15.3 %collective-permute-done.7.got1 = bf16[136,256]{1,0:T(8,128)(2,1)S(1)} collective-permute-done((bf16[136,256]{1,0:T(8,128)(2,1)}, bf16[136,256]{1,0:T(8,128)(2,1)S(1)}, u32[]{:S(2)}, u32[]{:S(2)}) %collective-permute-start.7) | collective-permute-done | bytes 69664 | tf_op jit(solution)/shard_map/ppermute | solution.py:50
  203.5 7.3 %collective-permute-done.8.got2 = bf16[136,256]{1,0:T(8,128)(2,1)S(1)} collective-permute-done((bf16[136,256]{1,0:T(8,128)(2,1)}, bf16[136,256]{1,0:T(8,128)(2,1)S(1)}, u32[]{:S(2)}, u32[]{:S(2)}) %collective-permute-start.8) | collective-permute-done | bytes 69664 | tf_op jit(solution)/shard_map/ppermute | solution.py:50
  210.8 0.6 copy-done.12
  211.5 1.7 dz_b.1
  213.2 2.9 %collective-permute-start.10 = (bf16[64,256]{1,0:T(8,128)(2,1)}, bf16[64,256]{1,0:T(8,128)(2,1)S(1)}, u32[]{:S(2)}, u32[]{:S(2)}) collective-permute-start(bf16[64,256]{1,0:T(8,128)(2,1)} %get-tuple-element.37), channel_id=1, source_target_pairs={{0,0},{1,8},{2,16},{3,24},{4,32},{5,40},{6,48},{7,56},{8,1},{9,9},... | collective-permute-start | bytes 98312 | tf_op jit(solution)/shard_map/ppermute | solution.py:460
  216.2 5.7 %collective-permute-start.11 = (bf16[64,256]{1,0:T(8,128)(2,1)}, bf16[64,256]{1,0:T(8,128)(2,1)S(1)}, u32[]{:S(2)}, u32[]{:S(2)}) collective-permute-start(bf16[64,256]{1,0:T(8,128)(2,1)} %get-tuple-element.38), channel_id=1, source_target_pairs={{0,256},{1,264},{2,272},{3,280},{4,288},{5,296},{6,304},{7,312},{8... | collective-permute-start | bytes 98312 | tf_op jit(solution)/shard_map/ppermute | solution.py:461
  221.9 1.5 slice_bitcast_fusion.raw_a
  223.4 1.0 copy-done.1
  224.4 3.7 %back_a.1 = (f32[64,2048]{1,0:T(8,128)}, f32[1,512]{1,0:T(1,128)}, f32[1,256]{1,0:T(1,128)}) custom-call(bf16[16,72,512]{2,1,0:T(8,128)(2,1)} %copy-done.1, bf16[64,512]{1,0:T(8,128)(2,1)} %slice_bitcast_fusion.raw_a, f32[8,512]{1,0:T(8,128)} %get-tuple-element.27.stats_a, f32[64,2048]{1,0:T(8,128)} %get-tuple-element.48.keep, ...), custom_call_target="tpu_custom_call" | custom-call | tf_op jit(solution)/shard_map/back_a/pallas_call | solution.py:95
  228.7 3.5 %back_b.1 = bf16[8,72,256]{2,1,0:T(8,128)(2,1)} custom-call(s32[6]{0:T(128)} %stack.27.at.refs_0_, f32[64,2048]{1,0:T(8,128)} %get-tuple-element.30.part, bf16[64,256]{1,0:T(8,128)(2,1)} %copy-done.14, bf16[64,256]{1,0:T(8,128)(2,1)} %copy-done.15, f32[64,2048]{1,0:T(8,128)} %get-tuple-element.47.keep, bf16[2,4,8,32,512]{4,3,2,1,0:T(8,128)(2,1)} %get-tuple-element.29.weight, ...), custom_call_target="tpu_custom_call" | custom-call | tf_op jit(solution)/shard_map/back_b/pallas_call | solution.py:95
  232.2 19.7 %all_to_all.33.refs_0_ = bf16[8,72,256]{2,1,0:T(8,128)(2,1)} all-to-all(bf16[8,72,256]{2,1,0:T(8,128)(2,1)} %back_b.1), channel_id=1, replica_groups=mesh['zh'=2,'x'=4,'y'=8,'zl'=4,'c'=2] {'zl','c'}, dimensions={0} | all-to-all | bytes 589824 | tf_op jit(solution)/shard_map/all_to_all | solution.py:475
  251.9 1.6 end.1
  253.5 1.2 slice.23
  (48 shorter events, 1.0 us)
Async XLA Ops:
  0.6 39.7 %copy-start.16 = (s32[64,2]{0,1:T(2,128)S(1)}, s32[64,2]{0,1:T(2,128)}, u32[]{:S(2)}) copy-start(s32[64,2]{0,1:T(2,128)} %param.6) | copy-start | bytes 1540
  12.5 40.7 %copy-start.7 = (bf16[64,2048]{1,0:T(8,128)(2,1)S(1)}, bf16[64,2048]{1,0:T(8,128)(2,1)}, u32[]{:S(2)}) copy-start(bf16[64,2048]{1,0:T(8,128)(2,1)} %param.4) | copy-start | bytes 786436
  12.5 40.7 %copy-start.8 = (bf16[64,2048]{1,0:T(8,128)(2,1)S(1)}, bf16[64,2048]{1,0:T(8,128)(2,1)}, u32[]{:S(2)}) copy-start(bf16[64,2048]{1,0:T(8,128)(2,1)} %param.5) | copy-start | bytes 786436
  34.0 21.0 %copy-start.2 = (bf16[8,64,512]{2,1,0:T(8,128)(2,1)}, bf16[8,64,512]{2,1,0:T(8,128)(2,1)S(1)}, u32[]{:S(2)}) copy-start(bf16[8,64,512]{2,1,0:T(8,128)(2,1)S(1)} %all_to_all.30) | copy-start | bytes 1572868
  34.0 11.9 %collective-permute-start.1 = (bf16[8,2,32,512]{3,2,1,0:T(8,128)(2,1)S(1)}, bf16[8,2,32,512]{3,2,1,0:T(8,128)(2,1)S(1)}, u32[]{:S(2)}, u32[]{:S(2)}) collective-permute-start(bf16[8,2,32,512]{3,2,1,0:T(8,128)(2,1)S(1)} %bitcast.18), channel_id=1, source_target_pairs={{0,192},{64,0},{128,64},{192,128},{1,193},{65,1},{129,65},{193,129... | collective-permute-start | bytes 1572872 | tf_op jit(solution)/shard_map/ppermute | solution.py:45
  38.4 12.9 %collective-permute-start = (bf16[8,2,32,512]{3,2,1,0:T(8,128)(2,1)S(1)}, bf16[8,2,32,512]{3,2,1,0:T(8,128)(2,1)S(1)}, u32[]{:S(2)}, u32[]{:S(2)}) collective-permute-start(bf16[8,2,32,512]{3,2,1,0:T(8,128)(2,1)S(1)} %bitcast.19), channel_id=1, source_target_pairs={{0,64},{64,128},{128,192},{192,0},{1,65},{65,129},{129,193},{193,1... | collective-permute-start | bytes 1572872 | tf_op jit(solution)/shard_map/ppermute | solution.py:45
  45.9 9.1 %copy-start.3 = (bf16[8,2,32,512]{3,2,1,0:T(8,128)(2,1)}, bf16[8,2,32,512]{3,2,1,0:T(8,128)(2,1)S(1)}, u32[]{:S(2)}) copy-start(bf16[8,2,32,512]{3,2,1,0:T(8,128)(2,1)S(1)} %collective-permute-done.1.ahead) | copy-start | bytes 1572868
  46.0 9.1 %collective-permute-start.3 = (bf16[4,2,32,512]{3,2,1,0:T(8,128)(2,1)S(1)}, bf16[4,2,32,512]{3,2,1,0:T(8,128)(2,1)S(1)}, u32[]{:S(2)}, u32[]{:S(2)}) collective-permute-start(bf16[4,2,32,512]{3,2,1,0:T(8,128)(2,1)S(1)} %slice.25), channel_id=1, source_target_pairs={{0,192},{64,0},{128,64},{192,128},{1,193},{65,1},{129,65},{193,129... | collective-permute-start | bytes 786440 | tf_op jit(solution)/shard_map/ppermute | solution.py:45
  51.3 3.7 %copy-start.4 = (bf16[8,2,32,512]{3,2,1,0:T(8,128)(2,1)}, bf16[8,2,32,512]{3,2,1,0:T(8,128)(2,1)S(1)}, u32[]{:S(2)}) copy-start(bf16[8,2,32,512]{3,2,1,0:T(8,128)(2,1)S(1)} %collective-permute-done.back) | copy-start | bytes 1572868
  51.3 8.3 %collective-permute-start.2 = (bf16[4,2,32,512]{3,2,1,0:T(8,128)(2,1)S(1)}, bf16[4,2,32,512]{3,2,1,0:T(8,128)(2,1)S(1)}, u32[]{:S(2)}, u32[]{:S(2)}) collective-permute-start(bf16[4,2,32,512]{3,2,1,0:T(8,128)(2,1)S(1)} %slice.24), channel_id=1, source_target_pairs={{0,64},{64,128},{128,192},{192,0},{1,65},{65,129},{129,193},{193,1... | collective-permute-start | bytes 786440 | tf_op jit(solution)/shard_map/ppermute | solution.py:45
  55.0 4.6 %copy-start.9 = (bf16[4,2,32,512]{3,2,1,0:T(8,128)(2,1)}, bf16[4,2,32,512]{3,2,1,0:T(8,128)(2,1)S(1)}, u32[]{:S(2)}) copy-start(bf16[4,2,32,512]{3,2,1,0:T(8,128)(2,1)S(1)} %collective-permute-done.3.far_high) | copy-start | bytes 786436
  59.7 0.7 copy-start.10
  64.0 10.9 %copy-start.18 = (bf16[64,256]{1,0:T(8,128)(2,1)S(1)}, bf16[64,256]{1,0:T(8,128)(2,1)}, u32[]{:S(2)}) copy-start(bf16[64,256]{1,0:T(8,128)(2,1)} %get-tuple-element.24) | copy-start | bytes 98308
  64.0 18.7 %copy-start.17 = (bf16[64,256]{1,0:T(8,128)(2,1)S(1)}, bf16[64,256]{1,0:T(8,128)(2,1)}, u32[]{:S(2)}) copy-start(bf16[64,256]{1,0:T(8,128)(2,1)} %get-tuple-element.25) | copy-start | bytes 98308
  64.0 63.2 %all-to-all-start.1 = ((bf16[16,64,512]{2,1,0:T(8,128)(2,1)}), bf16[16,64,512]{2,1,0:T(8,128)(2,1)S(1)}, u32[]{:S(2)}, u32[]{:S(2)}) async-start(bf16[16,64,512]{2,1,0:T(8,128)(2,1)} %get-tuple-element.23), calls=%async_computation.1 | async-start | bytes 2097152 | tf_op jit(solution)/shard_map/all_to_all | solution.py:406
  74.9 25.3 %collective-permute-start.4 = (bf16[64,256]{1,0:T(8,128)(2,1)S(1)}, bf16[64,256]{1,0:T(8,128)(2,1)S(1)}, u32[]{:S(2)}, u32[]{:S(2)}) collective-permute-start(bf16[64,256]{1,0:T(8,128)(2,1)S(1)} %copy-done.18), channel_id=1, source_target_pairs={{0,0},{1,8},{2,16},{3,24},{4,32},{5,40},{6,48},{7,56},{8,1},{9,9},... | collective-permute-start | bytes 98312 | tf_op jit(solution)/shard_map/ppermute | solution.py:407
  82.7 27.9 %collective-permute-start.5 = (bf16[64,256]{1,0:T(8,128)(2,1)S(1)}, bf16[64,256]{1,0:T(8,128)(2,1)S(1)}, u32[]{:S(2)}, u32[]{:S(2)}) collective-permute-start(bf16[64,256]{1,0:T(8,128)(2,1)S(1)} %copy-done.17), channel_id=1, source_target_pairs={{0,256},{1,264},{2,272},{3,280},{4,288},{5,296},{6,304},{7,312},{8... | collective-permute-start | bytes 98312 | tf_op jit(solution)/shard_map/ppermute | solution.py:408
  110.7 20.9 %copy-start.5 = (bf16[128,256]{1,0:T(8,128)(2,1)}, bf16[128,256]{1,0:T(8,128)(2,1)S(1)}, u32[]{:S(2)}) copy-start(bf16[128,256]{1,0:T(8,128)(2,1)S(1)} %pad_maximum_fusion.1.raw_b) | copy-start | bytes 196612
  127.2 1.0 copy-start
  158.7 64.6 %all-to-all-start.4 = ((bf16[16,72,512]{2,1,0:T(8,128)(2,1)}), bf16[16,72,512]{2,1,0:T(8,128)(2,1)S(1)}, u32[]{:S(2)}, u32[]{:S(2)}) async-start(bf16[16,72,512]{2,1,0:T(8,128)(2,1)} %grad_a.1), calls=%async_computation.4 | async-start | bytes 2359296 | tf_op jit(solution)/shard_map/all_to_all | solution.py:444
  169.6 5.6 %collective-permute-start.6 = (bf16[520,256]{1,0:T(8,128)(2,1)}, bf16[520,256]{1,0:T(8,128)(2,1)S(1)}, u32[]{:S(2)}, u32[]{:S(2)}) collective-permute-start(bf16[520,256]{1,0:T(8,128)(2,1)} %get-tuple-element.32), channel_id=1, source_target_pairs={{0,1},{1,0},{2,3},{3,2},{4,5},{5,4},{6,7},{7,6},{8,9},{9,8},{10,11... | collective-permute-start | bytes 798728 | tf_op jit(solution)/shard_map/ppermute | solution.py:50
  175.2 0.7 copy-start.6
  177.9 25.6 %collective-permute-start.7 = (bf16[136,256]{1,0:T(8,128)(2,1)}, bf16[136,256]{1,0:T(8,128)(2,1)S(1)}, u32[]{:S(2)}, u32[]{:S(2)}) collective-permute-start(bf16[136,256]{1,0:T(8,128)(2,1)} %get-tuple-element.34), channel_id=1, source_target_pairs={{0,2},{2,0},{4,6},{6,4},{1,3},{3,1},{5,7},{7,5},{8,10},{10,8},{12,... | collective-permute-start | bytes 208904 | tf_op jit(solution)/shard_map/ppermute | solution.py:50
  181.0 29.9 %collective-permute-start.8 = (bf16[136,256]{1,0:T(8,128)(2,1)}, bf16[136,256]{1,0:T(8,128)(2,1)S(1)}, u32[]{:S(2)}, u32[]{:S(2)}) collective-permute-start(bf16[136,256]{1,0:T(8,128)(2,1)} %get-tuple-element.35), channel_id=1, source_target_pairs={{0,4},{2,6},{4,0},{6,2},{1,5},{3,7},{5,1},{7,3},{8,12},{10,14},{12... | collective-permute-start | bytes 208904 | tf_op jit(solution)/shard_map/ppermute | solution.py:50
  185.0 25.8 %collective-permute-start.9 = (bf16[136,256]{1,0:T(8,128)(2,1)}, bf16[136,256]{1,0:T(8,128)(2,1)S(1)}, u32[]{:S(2)}, u32[]{:S(2)}) collective-permute-start(bf16[136,256]{1,0:T(8,128)(2,1)} %get-tuple-element.36), channel_id=1, source_target_pairs={{0,6},{2,4},{4,2},{6,0},{1,7},{3,5},{5,3},{7,1},{8,14},{10,12},{12... | collective-permute-start | bytes 208904 | tf_op jit(solution)/shard_map/ppermute | solution.py:50
  203.5 7.3 %copy-start.11 = (bf16[136,256]{1,0:T(8,128)(2,1)}, bf16[136,256]{1,0:T(8,128)(2,1)S(1)}, u32[]{:S(2)}) copy-start(bf16[136,256]{1,0:T(8,128)(2,1)S(1)} %collective-permute-done.7.got1) | copy-start | bytes 208900
  210.8 0.6 copy-start.12
  210.8 0.6 copy-start.13
  213.2 14.9 %collective-permute-start.10 = (bf16[64,256]{1,0:T(8,128)(2,1)}, bf16[64,256]{1,0:T(8,128)(2,1)S(1)}, u32[]{:S(2)}, u32[]{:S(2)}) collective-permute-start(bf16[64,256]{1,0:T(8,128)(2,1)} %get-tuple-element.37), channel_id=1, source_target_pairs={{0,0},{1,8},{2,16},{3,24},{4,32},{5,40},{6,48},{7,56},{8,1},{9,9},... | collective-permute-start | bytes 98312 | tf_op jit(solution)/shard_map/ppermute | solution.py:460
  216.2 11.9 %collective-permute-start.11 = (bf16[64,256]{1,0:T(8,128)(2,1)}, bf16[64,256]{1,0:T(8,128)(2,1)S(1)}, u32[]{:S(2)}, u32[]{:S(2)}) collective-permute-start(bf16[64,256]{1,0:T(8,128)(2,1)} %get-tuple-element.38), channel_id=1, source_target_pairs={{0,256},{1,264},{2,272},{3,280},{4,288},{5,296},{6,304},{7,312},{8... | collective-permute-start | bytes 98312 | tf_op jit(solution)/shard_map/ppermute | solution.py:461
  223.4 1.0 copy-start.1
  228.1 0.6 copy-start.14
  228.1 0.6 copy-start.15

commit v6 on v5

--- a/solution.py
+++ b/solution.py
@@ -103,7 +103,9 @@
     )(*args)
 
 
-def project_body(at, view, own, back, ahead, far_low, far_high, piece, wide_a, same_b, other_b):
+def project_body(
+    at, view, view2, own, back, ahead, far_low, far_high, piece, wide_a, raw_a, half_b
+):
     zh_n, x_n, y_n, rows, kt = piece.shape
     x = at[0]
     half = y_n // 2
@@ -116,13 +118,19 @@
         piece[zh, far, half:] = far_high[:, zh]
     weight = piece[...].reshape(zh_n * x_n * y_n * rows, kt)
     raw = dot(view[...], weight, 1, 0).astype(BF)
-    n, half_kt = same_b.shape
+    raw2 = dot(view2[...], weight, 1, 0).astype(BF)
+    n, kt = raw_a.shape
+    kl = kt // zh_n
+    low = at[5] == 0
+    raw_a[...] = raw[:n]
+    low_a, high_a = jnp.where(low, raw[:n], raw2[:n]), jnp.where(low, raw2[:n], raw[:n])
     for i in range(wide_a.shape[0]):
-        wide_a[i] = raw[:n]
-    low, high = raw[n:, :half_kt], raw[n:, half_kt:]
-    first = at[5] == 0
-    same_b[...] = jnp.where(first, low, high)
-    other_b[...] = jnp.where(first, high, low)
+        wide_a[i, :n] = low_a
+        wide_a[i, n:] = high_a
+    mine = jnp.where(low, raw[n:, :kl], raw[n:, kl:])
+    theirs = jnp.where(low, raw2[n:, :kl], raw2[n:, kl:])
+    half_b[:n] = jnp.where(low, mine, theirs)
+    half_b[n:] = jnp.where(low, theirs, mine)
 
 
 def gram_body(at, big_a, big_b, out, tail):
@@ -308,16 +316,31 @@
     other[...] = jnp.where(low, both[rows:], both[:rows])
 
 
-def back_a_body(got, raw_a, stats_a, keep, weight, out, diag_out, power_out):
-    parts, deep, kt = got.shape
-    rows = deep - 8
-    grad = got[0, :rows].astype(F32)
-    tails = [got[i, rows:].astype(F32) for i in range(parts)]
+def sum_a_body(at, got, sent, kept, tail):
+    parts, deep, _ = got.shape
+    both = deep - 8
+    rows = both // 2
+    grad = got[0, :both].astype(F32)
+    tails = [got[i, both:].astype(F32) for i in range(parts)]
     for i in range(1, parts):
-        grad = grad + got[i, :rows].astype(F32)
-    gather = lambda pos, count: sum(
-        (joined(t, pos, count) for t in tails[1:]), joined(tails[0], pos, count)
-    )
+        grad = grad + got[i, :both].astype(F32)
+    pos, start = 0, 0
+    for count in (2, 2, 3, 1):
+        row = sum((joined(t, start, count) for t in tails[1:]), joined(tails[0], start, count))
+        start += count
+        pos = put_pieces(tail, pos, row, count)
+    low = at[5] == 0
+    sent[:rows] = jnp.where(low, grad[rows:], grad[:rows]).astype(BF)
+    sent[rows:] = tail[...].astype(BF)
+    kept[:rows] = jnp.where(low, grad[:rows], grad[rows:])
+    kept[rows:] = tail[...]
+
+
+def back_a_body(kept, got, raw_a, stats_a, keep, weight, out, diag_out, power_out):
+    rows, kt = raw_a.shape
+    grad = kept[:rows] + got[:rows].astype(F32)
+    mine, theirs = kept[rows:], got[rows:].astype(F32)
+    gather = lambda pos, count: joined(mine, pos, count) + joined(theirs, pos, count)
     second, power, diag, first = gather(0, 2), gather(2, 2), gather(4, 3), gather(7, 1)
     inv = stats_a[1:2, :]
     norm = ((raw_a[...].astype(F32) - stats_a[0:1, :]) * inv).astype(BF).astype(F32)
@@ -382,6 +405,7 @@
         ]
     ).astype(jnp.int32)
     view, keep_a, keep_b = masked_views(feats, jitter, mask_ids)
+    view2 = flip(view, "zh", 1)
 
     own = lax.all_gather(weight, "zh", axis=0, tiled=True)
     own = spread(own, "y").reshape(y_n, zh_n, w_rows, kt)
@@ -390,25 +414,20 @@
     ahead = shift(own, "x", x_n - 1)
     far_low = shift(back[:half], "x", 1)
     far_high = shift(ahead[half:], "x", x_n - 1)
-    piece, wide_a, same_b, other_b = call(
+    piece, wide_a, raw_a, half_b = call(
         project_body,
         "project",
         [
             ((zh_n, x_n, y_n, w_rows, kt), BF),
-            ((parts, rows, kt), BF),
-            ((rows, kl), BF),
-            ((rows, kl), BF),
+            ((y_n, zh_n * rows, kt), BF),
+            ((rows, kt), BF),
+            ((zh_n * rows, kl), BF),
         ],
-        (at, view, own, back, ahead, far_low, far_high),
-    )
-
-    raw_a = wide_a[0]
-    big_a = lax.all_to_all(wide_a, ("y", "zh"), 0, 0, tiled=True)
-    same_b = lax.ppermute(same_b, every, swap_pairs(0))
-    other_b = lax.ppermute(other_b, every, swap_pairs(1))
-    own_b = jnp.concatenate(
-        [jnp.where(zh_at == 0, same_b, other_b), jnp.where(zh_at == 0, other_b, same_b)], axis=0
-    )
+        (at, view, view2, own, back, ahead, far_low, far_high),
+    )
+
+    big_a = lax.all_to_all(wide_a, "y", 0, 0, tiled=True)
+    own_b = lax.ppermute(half_b, every, swap_pairs(0))
     big_b = lax.all_gather(own_b, TILE, axis=0)
     (gram,) = call(
         gram_body, "gram", [((x_n, sub + 32, kl), BF)], (at, big_a, big_b), [((32, kl), F32)]
@@ -437,11 +456,19 @@
     (grad_a,) = call(
         grad_a_body,
         "grad_a",
-        [((parts, rows + 8, kt), BF)],
+        [((y_n, zh_n * rows + 8, kt), BF)],
         (at, mix, big_b, stats_a, stats_b),
         [((8, kt), F32)],
     )
-    got_a = lax.all_to_all(grad_a, ("y", "zh"), 0, 0, tiled=True)
+    got_a = lax.all_to_all(grad_a, "y", 0, 0, tiled=True)
+    sent_a, kept_a = call(
+        sum_a_body,
+        "sum_a",
+        [((rows + 8, kt), BF), ((rows + 8, kt), F32)],
+        (at, got_a),
+        [((8, kt), F32)],
+    )
+    got_a = flip(sent_a, "zh", 1)
     own, *outs = call(
         core_body,
         "core",
@@ -463,7 +490,7 @@
         back_a_body,
         "back_a",
         [((rows, width), F32), ((1, kt), F32), ((1, chunk), F32)],
-        (got_a, raw_a, stats_a, keep_a, piece),
+        (kept_a, got_a, raw_a, stats_a, keep_a, piece),
     )
     (share,) = call(
         back_b_body,

time: 256 us -> 249 us (0.973)
  blocking collectives: 89.7 us -> 74.1 us
  starting transfers between devices: 69 us -> 81.7 us
  waiting for transfers between devices: 55.3 us -> 48.5 us
    all_to_all x2 -> x1, blocking collectives: 30.1 us -> 8.59 us  [spread(): lax.all_to_all(jnp.broadcast_to(value[None], (parts,) + value.shape), axe...]
    all_to_all x2 -> x3, waiting for transfers between devices: 0.01 us -> 15.9 us  [the longest x1 15.9 us: spread(): lax.all_to_all(jnp.broadcast_to(value[None], (parts,) + value.shape), axe...]
    ppermute x0 -> x1, waiting for transfers between devices: none -> 14.6 us  [on_device(): own_b = lax.ppermute(half_b, every, swap_pairs(0))]
    ppermute x0 -> x1, starting transfers between devices: none -> 11 us  [on_device(): own_b = lax.ppermute(half_b, every, swap_pairs(0))]
    ppermute x2 -> x1, waiting for transfers between devices: 10.8 us -> 0.01 us  [on_device(): same_b = lax.ppermute(same_b, every, swap_pairs(0))]
    ppermute x2 -> x1, waiting for transfers between devices: 10.4 us -> 0.01 us  [on_device(): other_b = lax.ppermute(other_b, every, swap_pairs(1))]
    ppermute x4 -> x6, starting transfers between devices: 13.5 us -> 23.5 us  [flip(): return lax.ppermute(value, axis, [(i, i ^ step) for i in range(n)])]
    ppermute x4 -> x6, waiting for transfers between devices: 23.9 us -> 14.3 us  [flip(): return lax.ppermute(value, axis, [(i, i ^ step) for i in range(n)])]
  transfers between devices with their start and end apart: 14 -> 16, of which waited for: 7 -> 8; matrix products, arithmetic and copies ran while one was open for 2% -> 1% of each run, Pallas kernels for 4% -> 5%
where the time goes in v6:
time: 249 us; the launch traced here: 246 us
  starting transfers between devices  81.7 us (33%)
  blocking collectives  74.1 us (30%)
  waiting for transfers between devices  48.5 us (19%)
  Pallas kernels  30.5 us (12%)
  local copies, waits for them, and re-layouts  8.85 us (4%)
    pallas_call x11, Pallas kernels, call(): pl.pallas_call(body, name=name, out_shape=[jax.ShapeDtypeStruct(s, d) for...  30.5 us
    all_gather x1, blocking collectives, on_device(): big_b = lax.all_gather(own_b, TILE, axis=0)  25.3 us
    ppermute x6, starting transfers between devices, flip(): return lax.ppermute(value, axis, [(i, i ^ step) for i in range(n)])  23.5 us
    all_to_all x1, blocking collectives, on_device(): got = lax.all_to_all(share, TILE, 0, 0, tiled=True)  17.3 us
    all_to_all x1, waiting for transfers between devices, spread(): lax.all_to_all(jnp.broadcast_to(value[None], (parts,) + value.shape), axe...  15.9 us
    ppermute x1, waiting for transfers between devices, on_device(): own_b = lax.ppermute(half_b, every, swap_pairs(0))  14.6 us
    ppermute x6, waiting for transfers between devices, flip(): return lax.ppermute(value, axis, [(i, i ^ step) for i in range(n)])  14.3 us
    ppermute x4, starting transfers between devices, shift(): return lax.ppermute(value, axis, [(i, (i + step) % n) for i in range(n)])  12.8 us
  transfers between devices with their start and end apart: 16, of which 8 were waited for; matrix products, arithmetic and copies ran while one was open for 1% of the time, Pallas kernels for 5%

profile of v6, /device:TPU:1, one launch (start us, length us, event | category | flops | bytes accessed | tf_op | source)
XLA Modules:
  0.0 246.1 jit_solution(10942209417167852337)
XLA Ops:
  0.7 12.0 %all_gather.9 = bf16[64,512]{1,0:T(8,128)(2,1)S(1)} all-gather(bf16[32,512]{1,0:T(8,128)(2,1)} %param.7), channel_id=1, replica_groups=mesh['zh'=2,'x'=4,'y'=8,'zl'=4,'c'=2] {'zh'}, dimensions={0}, use_global_device_ids=true | all-gather | bytes 98304 | tf_op jit(solution)/shard_map/all_gather | solution.py:410
  12.6 0.8 broadcast_in_dim.4
  13.5 6.8 %all-to-all-start = ((bf16[8,64,512]{2,1,0:T(8,128)(2,1)}), bf16[8,64,512]{2,1,0:T(8,128)(2,1)S(1)}, u32[]{:S(2)}, u32[]{:S(2)}) async-start(bf16[8,64,512]{2,1,0:T(8,128)(2,1)} %broadcast_in_dim.4), calls=%async_computation | async-start | bytes 1048576 | tf_op jit(solution)/shard_map/all_to_all | solution.py:38
  20.3 15.9 %all-to-all-done = bf16[8,64,512]{2,1,0:T(8,128)(2,1)S(1)} async-done(((bf16[8,64,512]{2,1,0:T(8,128)(2,1)}), bf16[8,64,512]{2,1,0:T(8,128)(2,1)S(1)}, u32[]{:S(2)}, u32[]{:S(2)}) %all-to-all-start) | async-done | bytes 524320 | tf_op jit(solution)/shard_map/all_to_all | solution.py:38
  36.2 4.4 %collective-permute-start.2 = (bf16[8,2,32,512]{3,2,1,0:T(8,128)(2,1)S(1)}, bf16[8,2,32,512]{3,2,1,0:T(8,128)(2,1)S(1)}, u32[]{:S(2)}, u32[]{:S(2)}) collective-permute-start(bf16[8,2,32,512]{3,2,1,0:T(8,128)(2,1)S(1)} %bitcast.16), channel_id=1, source_target_pairs={{0,192},{64,0},{128,64},{192,128},{1,193},{65,1},{129,65},{193,129... | collective-permute-start | bytes 1572872 | tf_op jit(solution)/shard_map/ppermute | solution.py:45
  40.6 1.9 collective-permute-start.1
  42.8 7.3 %collective-permute-start = (bf16[128,2048]{1,0:T(8,128)(2,1)S(1)}, bf16[128,2048]{1,0:T(8,128)(2,1)S(1)}, u32[]{:S(2)}, u32[]{:S(2)}) collective-permute-start(bf16[128,2048]{1,0:T(8,128)(2,1)S(1)} %pad_maximum_fusion.view), channel_id=1, source_target_pairs={{0,256},{256,0},{1,257},{257,1},{2,258},{258,2},{3,259},{259,3},{4... | collective-permute-start | bytes 1572872 | tf_op jit(solution)/shard_map/ppermute | solution.py:50
  50.2 4.6 %collective-permute-start.4 = (bf16[4,2,32,512]{3,2,1,0:T(8,128)(2,1)S(1)}, bf16[4,2,32,512]{3,2,1,0:T(8,128)(2,1)S(1)}, u32[]{:S(2)}, u32[]{:S(2)}) collective-permute-start(bf16[4,2,32,512]{3,2,1,0:T(8,128)(2,1)S(1)} %slice.21), channel_id=1, source_target_pairs={{0,192},{64,0},{128,64},{192,128},{1,193},{65,1},{129,65},{193,129... | collective-permute-start | bytes 786440 | tf_op jit(solution)/shard_map/ppermute | solution.py:45
  54.9 1.9 collective-permute-start.3
  57.5 2.0 collective-permute-done.view2
  59.5 3.7 %collective-permute-done.3.far_low = bf16[4,2,32,512]{3,2,1,0:T(8,128)(2,1)S(1)} collective-permute-done((bf16[4,2,32,512]{3,2,1,0:T(8,128)(2,1)S(1)}, bf16[4,2,32,512]{3,2,1,0:T(8,128)(2,1)S(1)}, u32[]{:S(2)}, u32[]{:S(2)}) %collective-permute-start.3) | collective-permute-done | bytes 262176 | tf_op jit(solution)/shard_map/ppermute | solution.py:45
  63.2 0.7 copy-done.12
  63.9 3.7 %project.1 = (bf16[2,4,8,32,512]{4,3,2,1,0:T(8,128)(2,1)}, bf16[8,128,512]{2,1,0:T(8,128)(2,1)}, bf16[64,512]{1,0:T(8,128)(2,1)}, bf16[128,256]{1,0:T(8,128)(2,1)}) custom-call(s32[6]{0:T(128)} %stack.27.at.refs_0_, bf16[128,2048]{1,0:T(8,128)(2,1)} %copy-done.3, bf16[128,2048]{1,0:T(8,128)(2,1)} %copy-done.6, bf16[8,2,32,512]{3,2,1,0:T(8,128)(2,1)} %bitcast.18, ...), custom_call_target="tpu_custom_call" | custom-call | tf_op jit(solution)/shard_map/project/pallas_call | solution.py:95
  67.7 3.7 %all-to-all-start.1 = ((bf16[8,128,512]{2,1,0:T(8,128)(2,1)}), bf16[8,128,512]{2,1,0:T(8,128)(2,1)S(1)}, u32[]{:S(2)}, u32[]{:S(2)}) async-start(bf16[8,128,512]{2,1,0:T(8,128)(2,1)} %get-tuple-element.25), calls=%async_computation.1 | async-start | bytes 2097152 | tf_op jit(solution)/shard_map/all_to_all | solution.py:429
  71.4 11.0 %collective-permute-start.5 = (bf16[128,256]{1,0:T(8,128)(2,1)S(1)}, bf16[128,256]{1,0:T(8,128)(2,1)S(1)}, u32[]{:S(2)}, u32[]{:S(2)}) collective-permute-start(bf16[128,256]{1,0:T(8,128)(2,1)S(1)} %copy-done.20), channel_id=1, source_target_pairs={{0,0},{1,8},{2,16},{3,24},{4,32},{5,40},{6,48},{7,56},{8,1},{9,9},... | collective-permute-start | bytes 196616 | tf_op jit(solution)/shard_map/ppermute | solution.py:430
  82.4 14.6 %collective-permute-done.5.raw_b = bf16[128,256]{1,0:T(8,128)(2,1)S(1)} collective-permute-done((bf16[128,256]{1,0:T(8,128)(2,1)S(1)}, bf16[128,256]{1,0:T(8,128)(2,1)S(1)}, u32[]{:S(2)}, u32[]{:S(2)}) %collective-permute-start.5) | collective-permute-done | bytes 65568 | tf_op jit(solution)/shard_map/ppermute | solution.py:430
  97.0 25.3 %all-gather = bf16[1024,256]{1,0:T(8,128)(2,1)} all-gather(bf16[128,256]{1,0:T(8,128)(2,1)S(1)} %collective-permute-done.5.raw_b), channel_id=2, replica_groups=mesh['zh'=2,'x'=4,'y'=8,'zl'=4,'c'=2] {'zl','c'}, dimensions={0}, use_global_device_ids=true | all-gather | bytes 589824 | tf_op jit(solution)/shard_map/all_gather | solution.py:431
  122.3 1.0 copy-done
  123.3 3.3 %gram.1 = bf16[4,160,256]{2,1,0:T(8,128)(2,1)} custom-call(s32[6]{0:T(128)} %stack.27.at.refs_0_, bf16[8,128,512]{2,1,0:T(8,128)(2,1)} %copy-done, bf16[8,128,256]{2,1,0:T(8,128)(2,1)} %bitcast.14), custom_call_target="tpu_custom_call" | custom-call | tf_op jit(solution)/shard_map/gram/pallas_call | solution.py:95
  126.6 11.0 %all_to_all.30.refs_1_ = bf16[4,160,256]{2,1,0:T(8,128)(2,1)} all-to-all(bf16[4,160,256]{2,1,0:T(8,128)(2,1)} %gram.1), channel_id=1, replica_groups=mesh['zh'=2,'x'=4,'y'=8,'zl'=4,'c'=2] {'x'}, dimensions={0} | all-to-all | bytes 655360 | tf_op jit(solution)/shard_map/all_to_all | solution.py:436
  137.6 2.4 mix.1
  140.0 0.9 broadcast_in_dim.5
  140.9 8.6 %all_to_all.31.mix4 = bf16[4,128,256]{2,1,0:T(8,128)(2,1)} all-to-all(bf16[4,128,256]{2,1,0:T(8,128)(2,1)S(1)} %broadcast_in_dim.5), channel_id=1, replica_groups=mesh['zh'=2,'x'=4,'y'=8,'zl'=4,'c'=2] {'x'}, dimensions={0} | all-to-all | bytes 524288 | tf_op jit(solution)/shard_map/all_to_all | solution.py:38
  149.5 3.8 %grad_a.1 = bf16[8,136,512]{2,1,0:T(8,128)(2,1)} custom-call(s32[6]{0:T(128)} %stack.27.at.refs_0_, bf16[4,128,256]{2,1,0:T(8,128)(2,1)} %all_to_all.31.mix4, bf16[8,128,256]{2,1,0:T(8,128)(2,1)} %bitcast.15, f32[8,512]{1,0:T(8,128)} %get-tuple-element.28.stats_a, f32[8,256]{1,0:T(8,128)} %get-tuple-element.29.stats_b), custom_call_target="tpu_custom_call" | custom-call | tf_op jit(solution)/shard_map/grad_a/pallas_call | solution.py:95
  153.2 11.5 %all-to-all-start.4 = ((bf16[8,136,512]{2,1,0:T(8,128)(2,1)}), bf16[8,136,512]{2,1,0:T(8,128)(2,1)S(1)}, u32[]{:S(2)}, u32[]{:S(2)}) async-start(bf16[8,136,512]{2,1,0:T(8,128)(2,1)} %grad_a.1), calls=%async_computation.4 | async-start | bytes 2228224 | tf_op jit(solution)/shard_map/all_to_all | solution.py:463
  164.8 2.9 %grad_b.1 = (bf16[520,256]{1,0:T(8,128)(2,1)}, f32[520,256]{1,0:T(8,128)}) custom-call(s32[6]{0:T(128)} %stack.27.at.refs_0_, bf16[4,128,256]{2,1,0:T(8,128)(2,1)} %all_to_all.31.mix4, bf16[8,128,512]{2,1,0:T(8,128)(2,1)} %copy-done, f32[8,512]{1,0:T(8,128)} %get-tuple-element.28.stats_a, f32[8,256]{1,0:T(8,128)} %get-tuple-element.29.stats_b), custom_call_target="tpu_custom_call" | custom-call | tf_op jit(solution)/shard_map/grad_b/pallas_call | solution.py:95
  167.7 4.8 %collective-permute-start.7 = (bf16[520,256]{1,0:T(8,128)(2,1)}, bf16[520,256]{1,0:T(8,128)(2,1)S(1)}, u32[]{:S(2)}, u32[]{:S(2)}) collective-permute-start(bf16[520,256]{1,0:T(8,128)(2,1)} %get-tuple-element.36), channel_id=1, source_target_pairs={{0,1},{1,0},{2,3},{3,2},{4,5},{5,4},{6,7},{7,6},{8,9},{9,8},{10,11... | collective-permute-start | bytes 798728 | tf_op jit(solution)/shard_map/ppermute | solution.py:50
  172.4 1.4 collective-permute-done.7.got
  173.8 0.7 copy-done.7
  174.5 2.0 core.1
  176.4 3.1 %collective-permute-start.8 = (bf16[136,256]{1,0:T(8,128)(2,1)}, bf16[136,256]{1,0:T(8,128)(2,1)S(1)}, u32[]{:S(2)}, u32[]{:S(2)}) collective-permute-start(bf16[136,256]{1,0:T(8,128)(2,1)} %get-tuple-element.38), channel_id=1, source_target_pairs={{0,2},{2,0},{4,6},{6,4},{1,3},{3,1},{5,7},{7,5},{8,10},{10,8},{12,... | collective-permute-start | bytes 208904 | tf_op jit(solution)/shard_map/ppermute | solution.py:50
  179.6 4.1 %collective-permute-start.9 = (bf16[136,256]{1,0:T(8,128)(2,1)}, bf16[136,256]{1,0:T(8,128)(2,1)S(1)}, u32[]{:S(2)}, u32[]{:S(2)}) collective-permute-start(bf16[136,256]{1,0:T(8,128)(2,1)} %get-tuple-element.39), channel_id=1, source_target_pairs={{0,4},{2,6},{4,0},{6,2},{1,5},{3,7},{5,1},{7,3},{8,12},{10,14},{12... | collective-permute-start | bytes 208904 | tf_op jit(solution)/shard_map/ppermute | solution.py:50
  183.7 2.0 collective-permute-start.10
  185.8 2.1 collective-permute-done.9.got2
  187.8 2.9 %collective-permute-done.10.got3 = bf16[136,256]{1,0:T(8,128)(2,1)S(1)} collective-permute-done((bf16[136,256]{1,0:T(8,128)(2,1)}, bf16[136,256]{1,0:T(8,128)(2,1)S(1)}, u32[]{:S(2)}, u32[]{:S(2)}) %collective-permute-start.10) | collective-permute-done | bytes 69664 | tf_op jit(solution)/shard_map/ppermute | solution.py:50
  191.4 1.7 dz_b.1
  193.1 5.6 %collective-permute-start.11 = (bf16[64,256]{1,0:T(8,128)(2,1)}, bf16[64,256]{1,0:T(8,128)(2,1)S(1)}, u32[]{:S(2)}, u32[]{:S(2)}) collective-permute-start(bf16[64,256]{1,0:T(8,128)(2,1)} %get-tuple-element.41), channel_id=1, source_target_pairs={{0,0},{1,8},{2,16},{3,24},{4,32},{5,40},{6,48},{7,56},{8,1},{9,9},... | collective-permute-start | bytes 98312 | tf_op jit(solution)/shard_map/ppermute | solution.py:487
  198.7 6.7 %collective-permute-start.12 = (bf16[64,256]{1,0:T(8,128)(2,1)}, bf16[64,256]{1,0:T(8,128)(2,1)S(1)}, u32[]{:S(2)}, u32[]{:S(2)}) collective-permute-start(bf16[64,256]{1,0:T(8,128)(2,1)} %get-tuple-element.42), channel_id=1, source_target_pairs={{0,256},{1,264},{2,272},{3,280},{4,288},{5,296},{6,304},{7,312},{8... | collective-permute-start | bytes 98312 | tf_op jit(solution)/shard_map/ppermute | solution.py:488
  205.5 1.0 copy-done.1
  206.4 2.2 sum_a.1
  208.6 2.2 collective-permute-start.6
  210.8 1.1 compare_convert_fusion
  212.0 5.9 %collective-permute-done.6.got = bf16[72,512]{1,0:T(8,128)(2,1)S(1)} collective-permute-done((bf16[72,512]{1,0:T(8,128)(2,1)}, bf16[72,512]{1,0:T(8,128)(2,1)S(1)}, u32[]{:S(2)}, u32[]{:S(2)}) %collective-permute-start.6) | collective-permute-done | bytes 73760 | tf_op jit(solution)/shard_map/ppermute | solution.py:50
  218.5 3.5 %back_a.1 = (f32[64,2048]{1,0:T(8,128)}, f32[1,512]{1,0:T(1,128)}, f32[1,256]{1,0:T(1,128)}) custom-call(f32[72,512]{1,0:T(8,128)} %get-tuple-element.30.kept, bf16[72,512]{1,0:T(8,128)(2,1)} %copy-done.13, bf16[64,512]{1,0:T(8,128)(2,1)} %get-tuple-element.32.raw_a, f32[8,512]{1,0:T(8,128)} %get-tuple-element.28.stats_a, ...), custom_call_target="tpu_custom_call" | custom-call | tf_op jit(solution)/shard_map/back_a/pallas_call | solution.py:95
  222.6 3.4 %back_b.1 = bf16[8,72,256]{2,1,0:T(8,128)(2,1)} custom-call(s32[6]{0:T(128)} %stack.27.at.refs_0_, f32[64,2048]{1,0:T(8,128)} %get-tuple-element.34.part, bf16[64,256]{1,0:T(8,128)(2,1)} %copy-done.17, bf16[64,256]{1,0:T(8,128)(2,1)} %copy-done.18, f32[64,2048]{1,0:T(8,128)} %get-tuple-element.49.keep, bf16[2,4,8,32,512]{4,3,2,1,0:T(8,128)(2,1)} %get-tuple-element.33.weight, ...), custom_call_target="tpu_custom_call" | custom-call | tf_op jit(solution)/shard_map/back_b/pallas_call | solution.py:95
  226.0 17.3 %all_to_all.32.refs_0_ = bf16[8,72,256]{2,1,0:T(8,128)(2,1)} all-to-all(bf16[8,72,256]{2,1,0:T(8,128)(2,1)} %back_b.1), channel_id=1, replica_groups=mesh['zh'=2,'x'=4,'y'=8,'zl'=4,'c'=2] {'zl','c'}, dimensions={0} | all-to-all | bytes 589824 | tf_op jit(solution)/shard_map/all_to_all | solution.py:502
  243.3 1.6 end.1
  244.9 1.2 slice.19
  (53 shorter events, 2.9 us)
Async XLA Ops:
  0.6 19.7 %copy-start.19 = (s32[64,2]{0,1:T(2,128)S(1)}, s32[64,2]{0,1:T(2,128)}, u32[]{:S(2)}) copy-start(s32[64,2]{0,1:T(2,128)} %param.6) | copy-start | bytes 1540
  0.6 41.9 %copy-start.9 = (bf16[64,2048]{1,0:T(8,128)(2,1)S(1)}, bf16[64,2048]{1,0:T(8,128)(2,1)}, u32[]{:S(2)}) copy-start(bf16[64,2048]{1,0:T(8,128)(2,1)} %param.5) | copy-start | bytes 786436
  0.7 41.9 %copy-start.8 = (bf16[64,2048]{1,0:T(8,128)(2,1)S(1)}, bf16[64,2048]{1,0:T(8,128)(2,1)}, u32[]{:S(2)}) copy-start(bf16[64,2048]{1,0:T(8,128)(2,1)} %param.4) | copy-start | bytes 786436
  13.5 22.7 %all-to-all-start = ((bf16[8,64,512]{2,1,0:T(8,128)(2,1)}), bf16[8,64,512]{2,1,0:T(8,128)(2,1)S(1)}, u32[]{:S(2)}, u32[]{:S(2)}) async-start(bf16[8,64,512]{2,1,0:T(8,128)(2,1)} %broadcast_in_dim.4), calls=%async_computation | async-start | bytes 1048576 | tf_op jit(solution)/shard_map/all_to_all | solution.py:38
  36.2 14.0 %copy-start.2 = (bf16[8,64,512]{2,1,0:T(8,128)(2,1)}, bf16[8,64,512]{2,1,0:T(8,128)(2,1)S(1)}, u32[]{:S(2)}) copy-start(bf16[8,64,512]{2,1,0:T(8,128)(2,1)S(1)} %all-to-all-done) | copy-start | bytes 1572868
  36.2 14.0 %collective-permute-start.2 = (bf16[8,2,32,512]{3,2,1,0:T(8,128)(2,1)S(1)}, bf16[8,2,32,512]{3,2,1,0:T(8,128)(2,1)S(1)}, u32[]{:S(2)}, u32[]{:S(2)}) collective-permute-start(bf16[8,2,32,512]{3,2,1,0:T(8,128)(2,1)S(1)} %bitcast.16), channel_id=1, source_target_pairs={{0,192},{64,0},{128,64},{192,128},{1,193},{65,1},{129,65},{193,129... | collective-permute-start | bytes 1572872 | tf_op jit(solution)/shard_map/ppermute | solution.py:45
  40.6 14.2 %collective-permute-start.1 = (bf16[8,2,32,512]{3,2,1,0:T(8,128)(2,1)S(1)}, bf16[8,2,32,512]{3,2,1,0:T(8,128)(2,1)S(1)}, u32[]{:S(2)}, u32[]{:S(2)}) collective-permute-start(bf16[8,2,32,512]{3,2,1,0:T(8,128)(2,1)S(1)} %bitcast.17), channel_id=1, source_target_pairs={{0,64},{64,128},{128,192},{192,0},{1,65},{65,129},{129,193},{193,1... | collective-permute-start | bytes 1572872 | tf_op jit(solution)/shard_map/ppermute | solution.py:45
  42.8 20.4 %copy-start.3 = (bf16[128,2048]{1,0:T(8,128)(2,1)}, bf16[128,2048]{1,0:T(8,128)(2,1)S(1)}, u32[]{:S(2)}) copy-start(bf16[128,2048]{1,0:T(8,128)(2,1)S(1)} %pad_maximum_fusion.view) | copy-start | bytes 1572868
  42.8 16.7 %collective-permute-start = (bf16[128,2048]{1,0:T(8,128)(2,1)S(1)}, bf16[128,2048]{1,0:T(8,128)(2,1)S(1)}, u32[]{:S(2)}, u32[]{:S(2)}) collective-permute-start(bf16[128,2048]{1,0:T(8,128)(2,1)S(1)} %pad_maximum_fusion.view), channel_id=1, source_target_pairs={{0,256},{256,0},{1,257},{257,1},{2,258},{258,2},{3,259},{259,3},{4... | collective-permute-start | bytes 1572872 | tf_op jit(solution)/shard_map/ppermute | solution.py:50
  50.2 13.0 %copy-start.4 = (bf16[8,2,32,512]{3,2,1,0:T(8,128)(2,1)}, bf16[8,2,32,512]{3,2,1,0:T(8,128)(2,1)S(1)}, u32[]{:S(2)}) copy-start(bf16[8,2,32,512]{3,2,1,0:T(8,128)(2,1)S(1)} %collective-permute-done.2.ahead) | copy-start | bytes 1572868
  50.2 9.3 %collective-permute-start.4 = (bf16[4,2,32,512]{3,2,1,0:T(8,128)(2,1)S(1)}, bf16[4,2,32,512]{3,2,1,0:T(8,128)(2,1)S(1)}, u32[]{:S(2)}, u32[]{:S(2)}) collective-permute-start(bf16[4,2,32,512]{3,2,1,0:T(8,128)(2,1)S(1)} %slice.21), channel_id=1, source_target_pairs={{0,192},{64,0},{128,64},{192,128},{1,193},{65,1},{129,65},{193,129... | collective-permute-start | bytes 786440 | tf_op jit(solution)/shard_map/ppermute | solution.py:45
  54.8 8.4 %copy-start.5 = (bf16[8,2,32,512]{3,2,1,0:T(8,128)(2,1)}, bf16[8,2,32,512]{3,2,1,0:T(8,128)(2,1)S(1)}, u32[]{:S(2)}) copy-start(bf16[8,2,32,512]{3,2,1,0:T(8,128)(2,1)S(1)} %collective-permute-done.1.back) | copy-start | bytes 1572868
  54.9 8.3 %collective-permute-start.3 = (bf16[4,2,32,512]{3,2,1,0:T(8,128)(2,1)S(1)}, bf16[4,2,32,512]{3,2,1,0:T(8,128)(2,1)S(1)}, u32[]{:S(2)}, u32[]{:S(2)}) collective-permute-start(bf16[4,2,32,512]{3,2,1,0:T(8,128)(2,1)S(1)} %slice.20), channel_id=1, source_target_pairs={{0,64},{64,128},{128,192},{192,0},{1,65},{65,129},{129,193},{193,1... | collective-permute-start | bytes 786440 | tf_op jit(solution)/shard_map/ppermute | solution.py:45
  59.5 3.7 %copy-start.6 = (bf16[128,2048]{1,0:T(8,128)(2,1)}, bf16[128,2048]{1,0:T(8,128)(2,1)S(1)}, u32[]{:S(2)}) copy-start(bf16[128,2048]{1,0:T(8,128)(2,1)S(1)} %collective-permute-done.view2) | copy-start | bytes 1572868
  59.5 3.7 %copy-start.11 = (bf16[4,2,32,512]{3,2,1,0:T(8,128)(2,1)}, bf16[4,2,32,512]{3,2,1,0:T(8,128)(2,1)S(1)}, u32[]{:S(2)}) copy-start(bf16[4,2,32,512]{3,2,1,0:T(8,128)(2,1)S(1)} %collective-permute-done.4.far_high) | copy-start | bytes 786436
  63.2 0.7 copy-start.12
  67.7 3.7 %copy-start.20 = (bf16[128,256]{1,0:T(8,128)(2,1)S(1)}, bf16[128,256]{1,0:T(8,128)(2,1)}, u32[]{:S(2)}) copy-start(bf16[128,256]{1,0:T(8,128)(2,1)} %get-tuple-element.26) | copy-start | bytes 196612
  67.7 54.6 %all-to-all-start.1 = ((bf16[8,128,512]{2,1,0:T(8,128)(2,1)}), bf16[8,128,512]{2,1,0:T(8,128)(2,1)S(1)}, u32[]{:S(2)}, u32[]{:S(2)}) async-start(bf16[8,128,512]{2,1,0:T(8,128)(2,1)} %get-tuple-element.25), calls=%async_computation.1 | async-start | bytes 2097152 | tf_op jit(solution)/shard_map/all_to_all | solution.py:429
  71.4 25.7 %collective-permute-start.5 = (bf16[128,256]{1,0:T(8,128)(2,1)S(1)}, bf16[128,256]{1,0:T(8,128)(2,1)S(1)}, u32[]{:S(2)}, u32[]{:S(2)}) collective-permute-start(bf16[128,256]{1,0:T(8,128)(2,1)S(1)} %copy-done.20), channel_id=1, source_target_pairs={{0,0},{1,8},{2,16},{3,24},{4,32},{5,40},{6,48},{7,56},{8,1},{9,9},... | collective-permute-start | bytes 196616 | tf_op jit(solution)/shard_map/ppermute | solution.py:430
  97.0 29.6 %copy-start.10 = (bf16[128,256]{1,0:T(8,128)(2,1)}, bf16[128,256]{1,0:T(8,128)(2,1)S(1)}, u32[]{:S(2)}) copy-start(bf16[128,256]{1,0:T(8,128)(2,1)S(1)} %collective-permute-done.5.raw_b) | copy-start | bytes 196612
  122.3 1.0 copy-start
  153.2 52.2 %all-to-all-start.4 = ((bf16[8,136,512]{2,1,0:T(8,128)(2,1)}), bf16[8,136,512]{2,1,0:T(8,128)(2,1)S(1)}, u32[]{:S(2)}, u32[]{:S(2)}) async-start(bf16[8,136,512]{2,1,0:T(8,128)(2,1)} %grad_a.1), calls=%async_computation.4 | async-start | bytes 2228224 | tf_op jit(solution)/shard_map/all_to_all | solution.py:463
  167.7 6.1 %collective-permute-start.7 = (bf16[520,256]{1,0:T(8,128)(2,1)}, bf16[520,256]{1,0:T(8,128)(2,1)S(1)}, u32[]{:S(2)}, u32[]{:S(2)}) collective-permute-start(bf16[520,256]{1,0:T(8,128)(2,1)} %get-tuple-element.36), channel_id=1, source_target_pairs={{0,1},{1,0},{2,3},{3,2},{4,5},{5,4},{6,7},{7,6},{8,9},{9,8},{10,11... | collective-permute-start | bytes 798728 | tf_op jit(solution)/shard_map/ppermute | solution.py:50
  173.8 0.7 copy-start.7
  176.4 9.3 %collective-permute-start.8 = (bf16[136,256]{1,0:T(8,128)(2,1)}, bf16[136,256]{1,0:T(8,128)(2,1)S(1)}, u32[]{:S(2)}, u32[]{:S(2)}) collective-permute-start(bf16[136,256]{1,0:T(8,128)(2,1)} %get-tuple-element.38), channel_id=1, source_target_pairs={{0,2},{2,0},{4,6},{6,4},{1,3},{3,1},{5,7},{7,5},{8,10},{10,8},{12,... | collective-permute-start | bytes 208904 | tf_op jit(solution)/shard_map/ppermute | solution.py:50
  179.6 8.2 %collective-permute-start.9 = (bf16[136,256]{1,0:T(8,128)(2,1)}, bf16[136,256]{1,0:T(8,128)(2,1)S(1)}, u32[]{:S(2)}, u32[]{:S(2)}) collective-permute-start(bf16[136,256]{1,0:T(8,128)(2,1)} %get-tuple-element.39), channel_id=1, source_target_pairs={{0,4},{2,6},{4,0},{6,2},{1,5},{3,7},{5,1},{7,3},{8,12},{10,14},{12... | collective-permute-start | bytes 208904 | tf_op jit(solution)/shard_map/ppermute | solution.py:50
  183.7 7.1 %collective-permute-start.10 = (bf16[136,256]{1,0:T(8,128)(2,1)}, bf16[136,256]{1,0:T(8,128)(2,1)S(1)}, u32[]{:S(2)}, u32[]{:S(2)}) collective-permute-start(bf16[136,256]{1,0:T(8,128)(2,1)} %get-tuple-element.40), channel_id=1, source_target_pairs={{0,6},{2,4},{4,2},{6,0},{1,7},{3,5},{5,3},{7,1},{8,14},{10,12},{12... | collective-permute-start | bytes 208904 | tf_op jit(solution)/shard_map/ppermute | solution.py:50
  185.7 5.0 %copy-start.14 = (bf16[136,256]{1,0:T(8,128)(2,1)}, bf16[136,256]{1,0:T(8,128)(2,1)S(1)}, u32[]{:S(2)}) copy-start(bf16[136,256]{1,0:T(8,128)(2,1)S(1)} %collective-permute-done.8.got1) | copy-start | bytes 208900
  187.8 2.9 %copy-start.15 = (bf16[136,256]{1,0:T(8,128)(2,1)}, bf16[136,256]{1,0:T(8,128)(2,1)S(1)}, u32[]{:S(2)}) copy-start(bf16[136,256]{1,0:T(8,128)(2,1)S(1)} %collective-permute-done.9.got2) | copy-start | bytes 208900
  190.7 0.6 copy-start.16
  193.1 28.9 %collective-permute-start.11 = (bf16[64,256]{1,0:T(8,128)(2,1)}, bf16[64,256]{1,0:T(8,128)(2,1)S(1)}, u32[]{:S(2)}, u32[]{:S(2)}) collective-permute-start(bf16[64,256]{1,0:T(8,128)(2,1)} %get-tuple-element.41), channel_id=1, source_target_pairs={{0,0},{1,8},{2,16},{3,24},{4,32},{5,40},{6,48},{7,56},{8,1},{9,9},... | collective-permute-start | bytes 98312 | tf_op jit(solution)/shard_map/ppermute | solution.py:487
  198.7 23.2 %collective-permute-start.12 = (bf16[64,256]{1,0:T(8,128)(2,1)}, bf16[64,256]{1,0:T(8,128)(2,1)S(1)}, u32[]{:S(2)}, u32[]{:S(2)}) collective-permute-start(bf16[64,256]{1,0:T(8,128)(2,1)} %get-tuple-element.42), channel_id=1, source_target_pairs={{0,256},{1,264},{2,272},{3,280},{4,288},{5,296},{6,304},{7,312},{8... | collective-permute-start | bytes 98312 | tf_op jit(solution)/shard_map/ppermute | solution.py:488
  205.5 1.0 copy-start.1
  208.6 9.2 %collective-permute-start.6 = (bf16[72,512]{1,0:T(8,128)(2,1)}, bf16[72,512]{1,0:T(8,128)(2,1)S(1)}, u32[]{:S(2)}, u32[]{:S(2)}) collective-permute-start(bf16[72,512]{1,0:T(8,128)(2,1)} %get-tuple-element.31), channel_id=1, source_target_pairs={{0,256},{256,0},{1,257},{257,1},{2,258},{258,2},{3,259},{259,3},{4... | collective-permute-start | bytes 221192 | tf_op jit(solution)/shard_map/ppermute | solution.py:50
  217.8 0.6 copy-start.13
  222.0 0.6 copy-start.17
  222.0 0.6 copy-start.18

commit v7 on v4

--- a/solution.py
+++ b/solution.py
@@ -119,13 +119,9 @@
     raw_b[...] = raw[n:]
 
 
-def gram_body(at, big_a, pair0, pair1, pair2, pair3, big_b, out, tail):
-    zl, c = at[1], at[2]
+def gram_body(big_a, big_b, out, tail):
     parts, rows, kt = big_a.shape
     block = parts * rows
-    for step, pair in enumerate((pair0, pair1, pair2, pair3)):
-        big_b[(zl ^ step) * 2 + c] = pair[0]
-        big_b[(zl ^ step) * 2 + (1 - c)] = pair[1]
     a = big_a[...].reshape(block, kt).astype(F32)
     b = big_b[...].reshape(block, kt).astype(F32)
     mean_a = jnp.sum(a, axis=0, keepdims=True) / block
@@ -139,37 +135,21 @@
     pos = put_pieces(tail, pos, mean_b, 3)
     pos = put_pieces(tail, pos, jnp.sum(b * b, axis=0, keepdims=True), 3)
     put_pieces(tail, pos, jnp.sum(a * b, axis=0, keepdims=True), 3)
-    x_n = out.shape[0]
     deep = out.shape[1] - 16
     rows_out = tail[...].astype(BF)
-    for x in range(x_n):
-        out[x, :deep] = gram[x * deep : (x + 1) * deep]
-        out[x, deep:] = rows_out
-
-
-def merge_body(got, out):
-    x_n = got.shape[0]
-    zh_n, deep, kt = out.shape
-    sub = deep - 16 * x_n
-    for zh in range(zh_n):
-        total = got[0, zh * sub : (zh + 1) * sub].astype(F32)
-        for x in range(1, x_n):
-            total = total + got[x, zh * sub : (zh + 1) * sub].astype(F32)
-        out[zh, :sub] = total.astype(BF)
-        for x in range(x_n):
-            out[zh, sub + 16 * x : sub + 16 * (x + 1)] = got[x, zh_n * sub :]
+    for i in range(out.shape[0]):
+        out[i, :deep] = gram[i * deep : (i + 1) * deep]
+        out[i, deep:] = rows_out
 
 
 def mix_body(at, got, mix, stats, table, offs, *, block):
-    zh_n, deep, kt = got.shape
+    sets, deep, kt = got.shape
     sub = mix.shape[0]
-    sets = zh_n * ((deep - sub) // 16)
     total = block * sets
     raws = []
-    for zh in range(zh_n):
-        for x in range((deep - sub) // 16):
-            rows = got[zh, sub + 16 * x : sub + 16 * (x + 1)].astype(F32)
-            raws.append([joined(rows, 3 * i, 3) for i in range(5)])
+    for i in range(sets):
+        rows = got[i, sub:].astype(F32)
+        raws.append([joined(rows, 3 * j, 3) for j in range(5)])
     summed = [sum(r[i] for r in raws[1:]) + raws[0][i] for i in range(5)]
     mean_a, mean_b = summed[0] / sets, summed[2] / sets
     square_a, square_b, cross = summed[1], summed[3], summed[4]
@@ -193,8 +173,8 @@
     l_of = lax.broadcasted_iota(jnp.int32, (sub, kt), 1)
     chosen = exact((k_of + at[3] == l_of).astype(F32), table[...], 1, 1)
     corr = got[0, :sub].astype(F32)
-    for zh in range(1, zh_n):
-        corr = corr + got[zh, :sub].astype(F32)
+    for i in range(1, sets):
+        corr = corr + got[i, :sub].astype(F32)
     corr = corr + exact(chosen[:, :sets], offs[...], 1, 0)
     corr = corr * (chosen[:, sets : sets + 1] * (inv_b / total))
     here = k_of + (at[3] + at[4]) == l_of
@@ -211,6 +191,14 @@
     stats[7:8, :] = diag * (at[4] == 0).astype(F32)
 
 
+def thirds(value):
+    out = []
+    for _ in range(3):
+        out.append(value.astype(BF))
+        value = value - out[-1].astype(F32)
+    return out
+
+
 def correlation(at, mix, stats):
     kt = mix.shape[0]
     k_of = lax.broadcasted_iota(jnp.int32, (kt, kt), 0)
@@ -230,7 +218,7 @@
         sent[z * rows : (z + 1) * rows] = grads[z * 2 + (1 - c)].astype(BF)
         kept[z * rows : (z + 1) * rows] = grads[z * 2 + c]
     second = jnp.sum(wide * correlation(at, wide, stats), axis=0, keepdims=True)
-    first = exact(stats[...], wide, 1, 0)[5:6]
+    first = sum(dot(p, mix, 1, 0) for p in thirds(stats[...]))[5:6]
     tail[...] = jnp.zeros_like(tail)
     pos = put_pieces(tail, 0, second, 3)
     put_pieces(tail, pos, first, 2)
@@ -246,12 +234,19 @@
     wide = mix.astype(F32)
     norm_b = (big_b[...].reshape(parts * rows, kt).astype(F32) - stats[2:3, :]) * stats[3:4, :]
     grad = dot(norm_b.astype(BF), mix, 1, 1).astype(BF)
-    corr = correlation(at, wide, stats)
-    ones = jnp.ones((8, kt), F32)
-    pos = put_pieces(tail, 0, exact(ones, wide * corr, 1, 1)[0:1], 2)
-    pos = put_pieces(tail, pos, exact(ones, corr * corr, 1, 1)[0:1], 2)
-    pos = put_pieces(tail, pos, stats[7:8, :], 3)
-    put_pieces(tail, pos, exact(stats[...], wide, 1, 1)[6:7], 1)
+    k_of = lax.broadcasted_iota(jnp.int32, (kt, kt), 0)
+    l_of = lax.broadcasted_iota(jnp.int32, (kt, kt), 1)
+    square = jnp.where(k_of + at[4] == l_of, 0.0, wide * wide)
+    ones = jnp.ones((8, kt), BF)
+    square = sum(dot(ones, p, 1, 1) for p in thirds(square)[:2])[0:1]
+    diag = stats[7:8, :]
+    on = (at[4] == 0).astype(F32)
+    coeff = -2.0 * (on - diag) - 2.0 * LAMBDA_OFF * diag
+    centre = (coeff + 2.0 * LAMBDA_OFF * diag).astype(BF).astype(F32)
+    pos = put_pieces(tail, 0, square * (0.5 / LAMBDA_OFF) + centre * diag, 2)
+    pos = put_pieces(tail, pos, square * (0.25 / LAMBDA_OFF**2) + diag * diag, 2)
+    pos = put_pieces(tail, pos, diag, 3)
+    put_pieces(tail, pos, sum(dot(p, mix, 1, 1) for p in thirds(stats[...]))[6:7], 1)
     rows_out = tail[...].astype(BF)
     for i in range(parts):
         out[i, :rows] = grad[i * rows : (i + 1) * rows]
@@ -314,35 +309,17 @@
     power_out[...] = jnp.broadcast_to(jnp.sum(power, axis=1, keepdims=True), power_out.shape)
 
 
-def back_b_body(at, part, dz, keep, weight, power, sent, kept, blocks, tail):
-    c = at[2]
+def back_b_body(part, dz, keep, weight, power, out, tail):
     rows, width = part.shape
-    parts, _, chunk = blocks.shape
-    line = parts // 2
+    parts, _, chunk = out.shape
     both = part[...] + keep[...] * dot(dz[...], weight[...].reshape(width, dz.shape[1]), 1, 1)
-    for i in range(parts):
-        blocks[i] = both[:, i * chunk : (i + 1) * chunk]
-    for z in range(line):
-        sent[z * rows : (z + 1) * rows] = blocks[z * 2 + (1 - c)].astype(BF)
-        kept[z * rows : (z + 1) * rows] = blocks[z * 2 + c]
+    both = both.astype(BF)
     tail[...] = jnp.zeros_like(tail)
     put_pieces(tail, 0, power[...], 3)
-    sent[line * rows :] = tail[...].astype(BF)
-    kept[line * rows :] = tail[...]
-
-
-def last_body(kept, got, out, tail):
-    line, deep, chunk = out.shape
-    rows = deep - 8
-    theirs = got[line * rows :].astype(F32)
-    power = joined(kept[line * rows :], 0, 3) + joined(theirs, 0, 3)
-    tail[...] = jnp.zeros_like(tail)
-    put_pieces(tail, 0, power, 3)
     rows_out = tail[...].astype(BF)
-    for z in range(line):
-        at = slice(z * rows, (z + 1) * rows)
-        out[z, :rows] = (kept[at] + got[at].astype(F32)).astype(BF)
-        out[z, rows:] = rows_out
+    for i in range(parts):
+        out[i, :rows] = both[:, i * chunk : (i + 1) * chunk]
+        out[i, rows:] = rows_out
 
 
 def end_body(got, out, power_out, *, scale, features):
@@ -384,8 +361,7 @@
     ).astype(jnp.int32)
     view, keep_a, keep_b = masked_views(feats, jitter, mask_ids)
 
-    own = lax.all_gather(weight, "zh", axis=0, tiled=True)
-    own = spread(own, "y").reshape(y_n, zh_n, w_rows, kt)
+    own = spread(weight, ("y", "zh")).reshape(y_n, zh_n, w_rows, kt)
     half = y_n // 2
     back = shift(own, "x", 1)
     ahead = shift(own, "x", x_n - 1)
@@ -401,19 +377,12 @@
     raw_a = wide_a[0]
     big_a = lax.all_to_all(wide_a, "y", 0, 0, tiled=True)
     own_b = lax.ppermute(raw_b, every, pairs)
-    pair = jnp.stack([own_b, flip(own_b, "c", 1)])
-    others = [flip(pair, "zl", step) for step in range(1, zl_n)]
-    big_b, gram = call(
-        gram_body,
-        "gram",
-        [((tile_n, rows, kt), BF), ((x_n, zh_n * sub + 16, kt), BF)],
-        (at, big_a, pair, *others),
-        [((16, kt), F32)],
-    )
-
-    got = lax.all_to_all(gram, "x", 0, 0, tiled=True)
-    (got,) = call(merge_body, "merge", [((zh_n, sub + 16 * x_n, kt), BF)], (got,))
-    got = lax.all_to_all(got, "zh", 0, 0, tiled=True)
+    big_b = lax.all_gather(own_b, TILE, axis=0)
+    (gram,) = call(
+        gram_body, "gram", [((rows_n, sub + 16, kt), BF)], (big_a, big_b), [((16, kt), F32)]
+    )
+
+    got = lax.all_to_all(gram, ("x", "zh"), 0, 0, tiled=True)
     mix, stats = call(
         lambda *refs: mix_body(*refs, block=block),
         "mix",
@@ -452,21 +421,14 @@
         [((rows, width), F32), ((1, kt), F32), ((1, chunk), F32)],
         (got_a, raw_a, stats, keep_a, piece),
     )
-    sent, kept = call(
+    (share,) = call(
         back_b_body,
         "back_b",
-        [((line_rows, chunk), BF), ((line_rows, chunk), F32)],
-        (at, part, dz_b, keep_b, piece, power),
-        [((tile_n, rows, chunk), F32), ((8, chunk), F32)],
-    )
-    (share,) = call(
-        last_body,
-        "last",
-        [((zl_n, rows + 8, chunk), BF)],
-        (kept, flip(sent, "c", 1)),
+        [((tile_n, rows + 8, chunk), BF)],
+        (part, dz_b, keep_b, piece, power),
         [((8, chunk), F32)],
     )
-    got = lax.all_to_all(share, "zl", 0, 0, tiled=True)
+    got = lax.all_to_all(share, TILE, 0, 0, tiled=True)
     feats_grad, cross_power = call(
         lambda *refs: end_body(*refs, scale=LOSS_SCALE / total, features=kt * tile_n),
         "end",

time: 241 us -> 235 us (0.975)
  blocking collectives: 93.1 us -> 120 us
  starting transfers between devices: 73 us -> 53.6 us
  waiting for transfers between devices: 28.5 us -> 20.7 us
  Pallas kernels: 32.4 us -> 27.4 us
    ppermute x9 -> x4, starting transfers between devices: 35.6 us -> 16.5 us  [flip(): return lax.ppermute(value, axis, [(i, i ^ step) for i in range(n)])]
    all_to_all x2, blocking collectives: 31.4 us -> 47 us  [spread(): lax.all_to_all(jnp.broadcast_to(value[None], (parts,) + value.shape), axe...]
    all_gather x1, blocking collectives: 12 us -> 23.2 us  [on_device(): big_b = lax.all_gather(own_b, TILE, axis=0)]
    ppermute x9 -> x4, waiting for transfers between devices: 13.3 us -> 4.36 us  [flip(): return lax.ppermute(value, axis, [(i, i ^ step) for i in range(n)])]
    pallas_call x12 -> x10, Pallas kernels: 32.4 us -> 27.4 us  [call(): pl.pallas_call(body, name=name, out_shape=[jax.ShapeDtypeStruct(s, d) for...]
    unnamed x40 -> x30, local copies, waits for them, and re-layouts: 5.59 us -> 4.31 us
    all_to_all x3 -> x2, blocking collectives: 41.8 us -> 41.4 us  [the longest x1 23.5 us: on_device(): got = lax.all_to_all(gram, ('x', 'zh'), 0, 0, tiled=True)]
  transfers between devices with their start and end apart: 17 -> 12, of which waited for: 9 -> 6; matrix products, arithmetic and copies ran while one was open for 2% -> 2% of each run, Pallas kernels for 4% -> 4%
where the time goes in v7:
time: 235 us; the launch traced here: 234 us
  blocking collectives  120 us (51%)
  starting transfers between devices  53.6 us (23%)
  Pallas kernels  27.4 us (12%)
  waiting for transfers between devices  20.7 us (9%)
  local copies, waits for them, and re-layouts  9.28 us (4%)
    all_to_all x2, blocking collectives, spread(): lax.all_to_all(jnp.broadcast_to(value[None], (parts,) + value.shape), axe...  47 us
    pallas_call x10, Pallas kernels, call(): pl.pallas_call(body, name=name, out_shape=[jax.ShapeDtypeStruct(s, d) for...  27.4 us
    all_to_all x1, blocking collectives, on_device(): got = lax.all_to_all(gram, ('x', 'zh'), 0, 0, tiled=True)  23.5 us
    all_gather x1, blocking collectives, on_device(): big_b = lax.all_gather(own_b, TILE, axis=0)  23.2 us
    all_to_all x1, blocking collectives, on_device(): got = lax.all_to_all(share, TILE, 0, 0, tiled=True)  17.9 us
    ppermute x4, starting transfers between devices, flip(): return lax.ppermute(value, axis, [(i, i ^ step) for i in range(n)])  16.5 us
    ppermute x4, starting transfers between devices, shift(): return lax.ppermute(value, axis, [(i, (i + step) % n) for i in range(n)])  13.5 us
    ppermute x4, waiting for transfers between devices, shift(): return lax.ppermute(value, axis, [(i, (i + step) % n) for i in range(n)])  11.7 us
  transfers between devices with their start and end apart: 12, of which 6 were waited for; matrix products, arithmetic and copies ran while one was open for 2% of the time, Pallas kernels for 4%

profile of v7, /device:TPU:1, one launch (start us, length us, event | category | flops | bytes accessed | tf_op | source)
XLA Modules:
  0.0 233.5 jit_solution(7950188182454830772)
XLA Ops:
  0.7 0.9 broadcast_in_dim.4
  1.5 37.0 %all_to_all.30 = bf16[16,32,512]{2,1,0:T(8,128)(2,1)S(1)} all-to-all(bf16[16,32,512]{2,1,0:T(8,128)(2,1)S(1)} %broadcast_in_dim.4), channel_id=1, replica_groups=mesh['zh'=2,'x'=4,'y'=8,'zl'=4,'c'=2] {'y','zh'}, dimensions={0} | all-to-all | bytes 1048576 | tf_op jit(solution)/shard_map/all_to_all | solution.py:38
  38.5 4.4 %collective-permute-start.1 = (bf16[8,2,32,512]{3,2,1,0:T(8,128)(2,1)S(1)}, bf16[8,2,32,512]{3,2,1,0:T(8,128)(2,1)S(1)}, u32[]{:S(2)}, u32[]{:S(2)}) collective-permute-start(bf16[8,2,32,512]{3,2,1,0:T(8,128)(2,1)S(1)} %bitcast.17), channel_id=1, source_target_pairs={{0,192},{64,0},{128,64},{192,128},{1,193},{65,1},{129,65},{193,129... | collective-permute-start | bytes 1572872 | tf_op jit(solution)/shard_map/ppermute | solution.py:45
  42.9 1.9 collective-permute-start
  44.8 0.8 slice_bitcast_fusion.2
  45.6 7.1 %collective-permute-done.1.ahead = bf16[8,2,32,512]{3,2,1,0:T(8,128)(2,1)S(1)} collective-permute-done((bf16[8,2,32,512]{3,2,1,0:T(8,128)(2,1)S(1)}, bf16[8,2,32,512]{3,2,1,0:T(8,128)(2,1)S(1)}, u32[]{:S(2)}, u32[]{:S(2)}) %collective-permute-start.1) | collective-permute-done | bytes 524320 | tf_op jit(solution)/shard_map/ppermute | solution.py:45
  52.7 5.3 %collective-permute-start.3 = (bf16[4,2,32,512]{3,2,1,0:T(8,128)(2,1)S(1)}, bf16[4,2,32,512]{3,2,1,0:T(8,128)(2,1)S(1)}, u32[]{:S(2)}, u32[]{:S(2)}) collective-permute-start(bf16[4,2,32,512]{3,2,1,0:T(8,128)(2,1)S(1)} %slice.25), channel_id=1, source_target_pairs={{0,192},{64,0},{128,64},{192,128},{1,193},{65,1},{129,65},{193,129... | collective-permute-start | bytes 786440 | tf_op jit(solution)/shard_map/ppermute | solution.py:45
  58.1 1.9 collective-permute-start.2
  60.0 0.3 fusion
  60.3 0.7 stack.23.at.refs_0_
  61.0 0.8 pad_maximum_fusion.view
  61.8 4.6 %collective-permute-done.2.far_low = bf16[4,2,32,512]{3,2,1,0:T(8,128)(2,1)S(1)} collective-permute-done((bf16[4,2,32,512]{3,2,1,0:T(8,128)(2,1)S(1)}, bf16[4,2,32,512]{3,2,1,0:T(8,128)(2,1)S(1)}, u32[]{:S(2)}, u32[]{:S(2)}) %collective-permute-start.2) | collective-permute-done | bytes 262176 | tf_op jit(solution)/shard_map/ppermute | solution.py:45
  66.4 0.7 copy-done.10
  67.1 3.5 %project.1 = (bf16[2,4,8,32,512]{4,3,2,1,0:T(8,128)(2,1)}, bf16[8,64,512]{2,1,0:T(8,128)(2,1)}, bf16[64,512]{1,0:T(8,128)(2,1)}) custom-call(s32[5]{0:T(128)} %stack.23.at.refs_0_, bf16[128,2048]{1,0:T(8,128)(2,1)} %pad_maximum_fusion.view, bf16[8,2,32,512]{3,2,1,0:T(8,128)(2,1)} %bitcast.19, bf16[8,2,32,512]{3,2,1,0:T(8,128)(2,1)} %copy-done.4, ...), custom_call_target="tpu_custom_call" | custom-call | tf_op jit(solution)/shard_map/project/pallas_call | solution.py:92
  70.6 6.1 %all-to-all-start.1 = ((bf16[8,64,512]{2,1,0:T(8,128)(2,1)}), bf16[8,64,512]{2,1,0:T(8,128)(2,1)S(1)}, u32[]{:S(2)}, u32[]{:S(2)}) async-start(bf16[8,64,512]{2,1,0:T(8,128)(2,1)} %get-tuple-element.19), calls=%async_computation.1 | async-start | bytes 1048576 | tf_op jit(solution)/shard_map/all_to_all | solution.py:378
  76.7 7.5 %collective-permute-start.4 = (bf16[64,512]{1,0:T(8,128)(2,1)}, bf16[64,512]{1,0:T(8,128)(2,1)S(1)}, u32[]{:S(2)}, u32[]{:S(2)}) collective-permute-start(bf16[64,512]{1,0:T(8,128)(2,1)} %get-tuple-element.20), channel_id=1, source_target_pairs={{0,0},{1,8},{2,16},{3,24},{4,32},{5,40},{6,48},{7,56},{8,1},{9,9},... | collective-permute-start | bytes 196616 | tf_op jit(solution)/shard_map/ppermute | solution.py:379
  84.2 4.7 %collective-permute-done.4.raw_b = bf16[64,512]{1,0:T(8,128)(2,1)S(1)} collective-permute-done((bf16[64,512]{1,0:T(8,128)(2,1)}, bf16[64,512]{1,0:T(8,128)(2,1)S(1)}, u32[]{:S(2)}, u32[]{:S(2)}) %collective-permute-start.4) | collective-permute-done | bytes 65568 | tf_op jit(solution)/shard_map/ppermute | solution.py:379
  88.8 23.2 %all-gather = bf16[512,512]{1,0:T(8,128)(2,1)} all-gather(bf16[64,512]{1,0:T(8,128)(2,1)S(1)} %collective-permute-done.4.raw_b), channel_id=2, replica_groups=mesh['zh'=2,'x'=4,'y'=8,'zl'=4,'c'=2] {'zl','c'}, dimensions={0}, use_global_device_ids=true | all-gather | bytes 589824 | tf_op jit(solution)/shard_map/all_gather | solution.py:380
  112.0 0.8 copy-done
  112.8 3.0 %gram.1 = bf16[8,80,512]{2,1,0:T(8,128)(2,1)} custom-call(bf16[8,64,512]{2,1,0:T(8,128)(2,1)} %copy-done, bf16[8,64,512]{2,1,0:T(8,128)(2,1)} %bitcast.15), custom_call_target="tpu_custom_call" | custom-call | tf_op jit(solution)/shard_map/gram/pallas_call | solution.py:92
  115.8 23.5 %all_to_all.31.refs_1_ = bf16[8,80,512]{2,1,0:T(8,128)(2,1)} all-to-all(bf16[8,80,512]{2,1,0:T(8,128)(2,1)} %gram.1), channel_id=1, replica_groups=mesh['zh'=2,'x'=4,'y'=8,'zl'=4,'c'=2] {'x','zh'}, dimensions={0} | all-to-all | bytes 1310720 | tf_op jit(solution)/shard_map/all_to_all | solution.py:385
  139.3 2.4 %mix.1 = (bf16[64,512]{1,0:T(8,128)(2,1)}, f32[8,512]{1,0:T(8,128)}) custom-call(s32[5]{0:T(128)} %stack.23.at.refs_0_, bf16[8,80,512]{2,1,0:T(8,128)(2,1)} %all_to_all.31.refs_1_), custom_call_target="tpu_custom_call" | custom-call | tf_op jit(solution)/shard_map/mix/pallas_call | solution.py:92
  141.8 7.9 %all_gather.11 = bf16[128,512]{1,0:T(8,128)(2,1)S(1)} all-gather(bf16[64,512]{1,0:T(8,128)(2,1)} %get-tuple-element.21), channel_id=1, replica_groups=mesh['zh'=2,'x'=4,'y'=8,'zl'=4,'c'=2] {'zh'}, dimensions={0}, use_global_device_ids=true | all-gather | bytes 196608 | tf_op jit(solution)/shard_map/all_gather | solution.py:393
  149.7 10.0 %all_to_all.32.mix4 = bf16[4,128,512]{2,1,0:T(8,128)(2,1)} all-to-all(bf16[4,128,512]{2,1,0:T(8,128)(2,1)S(1)} %broadcast_in_dim.5), channel_id=1, replica_groups=mesh['zh'=2,'x'=4,'y'=8,'zl'=4,'c'=2] {'x'}, dimensions={0} | all-to-all | bytes 1048576 | tf_op jit(solution)/shard_map/all_to_all | solution.py:38
  159.7 3.3 %grad_a.1 = bf16[8,72,512]{2,1,0:T(8,128)(2,1)} custom-call(s32[5]{0:T(128)} %stack.23.at.refs_0_, bf16[4,128,512]{2,1,0:T(8,128)(2,1)} %all_to_all.32.mix4, bf16[8,64,512]{2,1,0:T(8,128)(2,1)} %bitcast.16, f32[8,512]{1,0:T(8,128)} %get-tuple-element.22.stats), custom_call_target="tpu_custom_call" | custom-call | tf_op jit(solution)/shard_map/grad_a/pallas_call | solution.py:92
  163.0 4.7 %all-to-all-start.4 = ((bf16[8,72,512]{2,1,0:T(8,128)(2,1)}), bf16[8,72,512]{2,1,0:T(8,128)(2,1)S(1)}, u32[]{:S(2)}, u32[]{:S(2)}) async-start(bf16[8,72,512]{2,1,0:T(8,128)(2,1)} %grad_a.1), calls=%async_computation.4 | async-start | bytes 1179648 | tf_op jit(solution)/shard_map/all_to_all | solution.py:407
  167.8 2.9 %grad_b.1 = (bf16[264,512]{1,0:T(8,128)(2,1)}, f32[264,512]{1,0:T(8,128)}) custom-call(s32[5]{0:T(128)} %stack.23.at.refs_0_, bf16[4,128,512]{2,1,0:T(8,128)(2,1)} %all_to_all.32.mix4, bf16[8,64,512]{2,1,0:T(8,128)(2,1)} %copy-done, f32[8,512]{1,0:T(8,128)} %get-tuple-element.22.stats), custom_call_target="tpu_custom_call" | custom-call | tf_op jit(solution)/shard_map/grad_b/pallas_call | solution.py:92
  170.7 6.2 %collective-permute-start.5 = (bf16[264,512]{1,0:T(8,128)(2,1)}, bf16[264,512]{1,0:T(8,128)(2,1)S(1)}, u32[]{:S(2)}, u32[]{:S(2)}) collective-permute-start(bf16[264,512]{1,0:T(8,128)(2,1)} %get-tuple-element.26), channel_id=1, source_target_pairs={{0,1},{1,0},{2,3},{3,2},{4,5},{5,4},{6,7},{7,6},{8,9},{9,8},{10,11... | collective-permute-start | bytes 811016 | tf_op jit(solution)/shard_map/ppermute | solution.py:50
  176.9 1.4 collective-permute-done.5.got
  178.3 0.7 copy-done.5
  179.0 2.0 core.1
  181.0 4.3 %collective-permute-start.6 = (bf16[72,512]{1,0:T(8,128)(2,1)}, bf16[72,512]{1,0:T(8,128)(2,1)S(1)}, u32[]{:S(2)}, u32[]{:S(2)}) collective-permute-start(bf16[72,512]{1,0:T(8,128)(2,1)} %get-tuple-element.28), channel_id=1, source_target_pairs={{0,2},{2,0},{4,6},{6,4},{1,3},{3,1},{5,7},{7,5},{8,10},{10,8},{12,... | collective-permute-start | bytes 221192 | tf_op jit(solution)/shard_map/ppermute | solution.py:50
  185.3 2.9 %collective-permute-start.7 = (bf16[72,512]{1,0:T(8,128)(2,1)}, bf16[72,512]{1,0:T(8,128)(2,1)S(1)}, u32[]{:S(2)}, u32[]{:S(2)}) collective-permute-start(bf16[72,512]{1,0:T(8,128)(2,1)} %get-tuple-element.29), channel_id=1, source_target_pairs={{0,4},{2,6},{4,0},{6,2},{1,5},{3,7},{5,1},{7,3},{8,12},{10,14},{12... | collective-permute-start | bytes 221192 | tf_op jit(solution)/shard_map/ppermute | solution.py:50
  188.2 3.1 %collective-permute-start.8 = (bf16[72,512]{1,0:T(8,128)(2,1)}, bf16[72,512]{1,0:T(8,128)(2,1)S(1)}, u32[]{:S(2)}, u32[]{:S(2)}) collective-permute-start(bf16[72,512]{1,0:T(8,128)(2,1)} %get-tuple-element.30), channel_id=1, source_target_pairs={{0,6},{2,4},{4,2},{6,0},{1,7},{3,5},{5,3},{7,1},{8,14},{10,12},{12... | collective-permute-start | bytes 221192 | tf_op jit(solution)/shard_map/ppermute | solution.py:50
  191.3 1.1 compare_convert_fusion
  192.4 1.5 collective-permute-done.7.got2
  193.8 1.5 collective-permute-done.8.got3
  195.4 0.6 copy-done.13
  196.0 1.7 dz_b.1
  197.7 5.3 %collective-permute-start.9 = (bf16[64,512]{1,0:T(8,128)(2,1)}, bf16[64,512]{1,0:T(8,128)(2,1)S(1)}, u32[]{:S(2)}, u32[]{:S(2)}) collective-permute-start(bf16[64,512]{1,0:T(8,128)(2,1)} %dz_b.1), channel_id=1, source_target_pairs={{0,0},{1,8},{2,16},{3,24},{4,32},{5,40},{6,48},{7,56},{8,1},{9,9},... | collective-permute-start | bytes 196616 | tf_op jit(solution)/shard_map/ppermute | solution.py:417
  203.0 1.5 slice_bitcast_fusion.raw_a
  204.5 0.8 copy-done.1
  205.3 3.5 %back_a.1 = (f32[64,2048]{1,0:T(8,128)}, f32[1,512]{1,0:T(1,128)}, f32[1,256]{1,0:T(1,128)}) custom-call(bf16[8,72,512]{2,1,0:T(8,128)(2,1)} %copy-done.1, bf16[64,512]{1,0:T(8,128)(2,1)} %slice_bitcast_fusion.raw_a, f32[8,512]{1,0:T(8,128)} %get-tuple-element.22.stats, f32[64,2048]{1,0:T(8,128)} %get-tuple-element.38.keep, ...), custom_call_target="tpu_custom_call" | custom-call | tf_op jit(solution)/shard_map/back_a/pallas_call | solution.py:92
  208.9 0.6 copy-done.14
  209.5 3.3 %back_b.1 = bf16[8,72,256]{2,1,0:T(8,128)(2,1)} custom-call(f32[64,2048]{1,0:T(8,128)} %get-tuple-element.24.part, bf16[64,512]{1,0:T(8,128)(2,1)} %copy-done.14, f32[64,2048]{1,0:T(8,128)} %get-tuple-element.37.keep, bf16[2,4,8,32,512]{4,3,2,1,0:T(8,128)(2,1)} %get-tuple-element.23.weight, f32[1,256]{1,0:T(1,128)} %get-tuple-element.31.power), custom_call_target="tpu_custom_call" | custom-call | tf_op jit(solution)/shard_map/back_b/pallas_call | solution.py:92
  212.8 17.9 %all_to_all.33.refs_0_ = bf16[8,72,256]{2,1,0:T(8,128)(2,1)} all-to-all(bf16[8,72,256]{2,1,0:T(8,128)(2,1)} %back_b.1), channel_id=1, replica_groups=mesh['zh'=2,'x'=4,'y'=8,'zl'=4,'c'=2] {'zl','c'}, dimensions={0} | all-to-all | bytes 589824 | tf_op jit(solution)/shard_map/all_to_all | solution.py:431
  230.8 1.6 end.1
  232.4 1.1 slice.23
  (34 shorter events, 0.1 us)
Async XLA Ops:
  0.6 59.4 %copy-start.7 = (bf16[64,2048]{1,0:T(8,128)(2,1)S(1)}, bf16[64,2048]{1,0:T(8,128)(2,1)}, u32[]{:S(2)}) copy-start(bf16[64,2048]{1,0:T(8,128)(2,1)} %param.5) | copy-start | bytes 786436
  0.6 59.4 %copy-start.6 = (bf16[64,2048]{1,0:T(8,128)(2,1)S(1)}, bf16[64,2048]{1,0:T(8,128)(2,1)}, u32[]{:S(2)}) copy-start(bf16[64,2048]{1,0:T(8,128)(2,1)} %param.4) | copy-start | bytes 786436
  38.5 27.9 %copy-start.2 = (bf16[16,32,512]{2,1,0:T(8,128)(2,1)}, bf16[16,32,512]{2,1,0:T(8,128)(2,1)S(1)}, u32[]{:S(2)}) copy-start(bf16[16,32,512]{2,1,0:T(8,128)(2,1)S(1)} %all_to_all.30) | copy-start | bytes 1572868
  38.5 14.2 %collective-permute-start.1 = (bf16[8,2,32,512]{3,2,1,0:T(8,128)(2,1)S(1)}, bf16[8,2,32,512]{3,2,1,0:T(8,128)(2,1)S(1)}, u32[]{:S(2)}, u32[]{:S(2)}) collective-permute-start(bf16[8,2,32,512]{3,2,1,0:T(8,128)(2,1)S(1)} %bitcast.17), channel_id=1, source_target_pairs={{0,192},{64,0},{128,64},{192,128},{1,193},{65,1},{129,65},{193,129... | collective-permute-start | bytes 1572872 | tf_op jit(solution)/shard_map/ppermute | solution.py:45
  42.9 15.1 %collective-permute-start = (bf16[8,2,32,512]{3,2,1,0:T(8,128)(2,1)S(1)}, bf16[8,2,32,512]{3,2,1,0:T(8,128)(2,1)S(1)}, u32[]{:S(2)}, u32[]{:S(2)}) collective-permute-start(bf16[8,2,32,512]{3,2,1,0:T(8,128)(2,1)S(1)} %bitcast.18), channel_id=1, source_target_pairs={{0,64},{64,128},{128,192},{192,0},{1,65},{65,129},{129,193},{193,1... | collective-permute-start | bytes 1572872 | tf_op jit(solution)/shard_map/ppermute | solution.py:45
  52.7 13.7 %copy-start.3 = (bf16[8,2,32,512]{3,2,1,0:T(8,128)(2,1)}, bf16[8,2,32,512]{3,2,1,0:T(8,128)(2,1)S(1)}, u32[]{:S(2)}) copy-start(bf16[8,2,32,512]{3,2,1,0:T(8,128)(2,1)S(1)} %collective-permute-done.1.ahead) | copy-start | bytes 1572868
  52.7 9.1 %collective-permute-start.3 = (bf16[4,2,32,512]{3,2,1,0:T(8,128)(2,1)S(1)}, bf16[4,2,32,512]{3,2,1,0:T(8,128)(2,1)S(1)}, u32[]{:S(2)}, u32[]{:S(2)}) collective-permute-start(bf16[4,2,32,512]{3,2,1,0:T(8,128)(2,1)S(1)} %slice.25), channel_id=1, source_target_pairs={{0,192},{64,0},{128,64},{192,128},{1,193},{65,1},{129,65},{193,129... | collective-permute-start | bytes 786440 | tf_op jit(solution)/shard_map/ppermute | solution.py:45
  58.0 8.4 %copy-start.4 = (bf16[8,2,32,512]{3,2,1,0:T(8,128)(2,1)}, bf16[8,2,32,512]{3,2,1,0:T(8,128)(2,1)S(1)}, u32[]{:S(2)}) copy-start(bf16[8,2,32,512]{3,2,1,0:T(8,128)(2,1)S(1)} %collective-permute-done.back) | copy-start | bytes 1572868
  58.1 8.3 %collective-permute-start.2 = (bf16[4,2,32,512]{3,2,1,0:T(8,128)(2,1)S(1)}, bf16[4,2,32,512]{3,2,1,0:T(8,128)(2,1)S(1)}, u32[]{:S(2)}, u32[]{:S(2)}) collective-permute-start(bf16[4,2,32,512]{3,2,1,0:T(8,128)(2,1)S(1)} %slice.24), channel_id=1, source_target_pairs={{0,64},{64,128},{128,192},{192,0},{1,65},{65,129},{129,193},{193,1... | collective-permute-start | bytes 786440 | tf_op jit(solution)/shard_map/ppermute | solution.py:45
  61.8 4.6 %copy-start.9 = (bf16[4,2,32,512]{3,2,1,0:T(8,128)(2,1)}, bf16[4,2,32,512]{3,2,1,0:T(8,128)(2,1)S(1)}, u32[]{:S(2)}) copy-start(bf16[4,2,32,512]{3,2,1,0:T(8,128)(2,1)S(1)} %collective-permute-done.3.far_high) | copy-start | bytes 786436
  66.4 0.7 copy-start.10
  70.6 41.4 %all-to-all-start.1 = ((bf16[8,64,512]{2,1,0:T(8,128)(2,1)}), bf16[8,64,512]{2,1,0:T(8,128)(2,1)S(1)}, u32[]{:S(2)}, u32[]{:S(2)}) async-start(bf16[8,64,512]{2,1,0:T(8,128)(2,1)} %get-tuple-element.19), calls=%async_computation.1 | async-start | bytes 1048576 | tf_op jit(solution)/shard_map/all_to_all | solution.py:378
  76.7 12.2 %collective-permute-start.4 = (bf16[64,512]{1,0:T(8,128)(2,1)}, bf16[64,512]{1,0:T(8,128)(2,1)S(1)}, u32[]{:S(2)}, u32[]{:S(2)}) collective-permute-start(bf16[64,512]{1,0:T(8,128)(2,1)} %get-tuple-element.20), channel_id=1, source_target_pairs={{0,0},{1,8},{2,16},{3,24},{4,32},{5,40},{6,48},{7,56},{8,1},{9,9},... | collective-permute-start | bytes 196616 | tf_op jit(solution)/shard_map/ppermute | solution.py:379
  88.8 52.9 %copy-start.8 = (bf16[64,512]{1,0:T(8,128)(2,1)}, bf16[64,512]{1,0:T(8,128)(2,1)S(1)}, u32[]{:S(2)}) copy-start(bf16[64,512]{1,0:T(8,128)(2,1)S(1)} %collective-permute-done.4.raw_b) | copy-start | bytes 196612
  112.0 0.8 copy-start
  163.0 41.5 %all-to-all-start.4 = ((bf16[8,72,512]{2,1,0:T(8,128)(2,1)}), bf16[8,72,512]{2,1,0:T(8,128)(2,1)S(1)}, u32[]{:S(2)}, u32[]{:S(2)}) async-start(bf16[8,72,512]{2,1,0:T(8,128)(2,1)} %grad_a.1), calls=%async_computation.4 | async-start | bytes 1179648 | tf_op jit(solution)/shard_map/all_to_all | solution.py:407
  170.7 7.6 %collective-permute-start.5 = (bf16[264,512]{1,0:T(8,128)(2,1)}, bf16[264,512]{1,0:T(8,128)(2,1)S(1)}, u32[]{:S(2)}, u32[]{:S(2)}) collective-permute-start(bf16[264,512]{1,0:T(8,128)(2,1)} %get-tuple-element.26), channel_id=1, source_target_pairs={{0,1},{1,0},{2,3},{3,2},{4,5},{5,4},{6,7},{7,6},{8,9},{9,8},{10,11... | collective-permute-start | bytes 811016 | tf_op jit(solution)/shard_map/ppermute | solution.py:50
  178.3 0.7 copy-start.5
  181.0 11.4 %collective-permute-start.6 = (bf16[72,512]{1,0:T(8,128)(2,1)}, bf16[72,512]{1,0:T(8,128)(2,1)S(1)}, u32[]{:S(2)}, u32[]{:S(2)}) collective-permute-start(bf16[72,512]{1,0:T(8,128)(2,1)} %get-tuple-element.28), channel_id=1, source_target_pairs={{0,2},{2,0},{4,6},{6,4},{1,3},{3,1},{5,7},{7,5},{8,10},{10,8},{12,... | collective-permute-start | bytes 221192 | tf_op jit(solution)/shard_map/ppermute | solution.py:50
  185.3 8.6 %collective-permute-start.7 = (bf16[72,512]{1,0:T(8,128)(2,1)}, bf16[72,512]{1,0:T(8,128)(2,1)S(1)}, u32[]{:S(2)}, u32[]{:S(2)}) collective-permute-start(bf16[72,512]{1,0:T(8,128)(2,1)} %get-tuple-element.29), channel_id=1, source_target_pairs={{0,4},{2,6},{4,0},{6,2},{1,5},{3,7},{5,1},{7,3},{8,12},{10,14},{12... | collective-permute-start | bytes 221192 | tf_op jit(solution)/shard_map/ppermute | solution.py:50
  188.2 7.2 %collective-permute-start.8 = (bf16[72,512]{1,0:T(8,128)(2,1)}, bf16[72,512]{1,0:T(8,128)(2,1)S(1)}, u32[]{:S(2)}, u32[]{:S(2)}) collective-permute-start(bf16[72,512]{1,0:T(8,128)(2,1)} %get-tuple-element.30), channel_id=1, source_target_pairs={{0,6},{2,4},{4,2},{6,0},{1,7},{3,5},{5,3},{7,1},{8,14},{10,12},{12... | collective-permute-start | bytes 221192 | tf_op jit(solution)/shard_map/ppermute | solution.py:50
  192.4 3.0 %copy-start.11 = (bf16[72,512]{1,0:T(8,128)(2,1)}, bf16[72,512]{1,0:T(8,128)(2,1)S(1)}, u32[]{:S(2)}) copy-start(bf16[72,512]{1,0:T(8,128)(2,1)S(1)} %collective-permute-done.6.got1) | copy-start | bytes 221188
  193.8 1.5 copy-start.12
  195.4 0.6 copy-start.13
  197.7 11.1 %collective-permute-start.9 = (bf16[64,512]{1,0:T(8,128)(2,1)}, bf16[64,512]{1,0:T(8,128)(2,1)S(1)}, u32[]{:S(2)}, u32[]{:S(2)}) collective-permute-start(bf16[64,512]{1,0:T(8,128)(2,1)} %dz_b.1), channel_id=1, source_target_pairs={{0,0},{1,8},{2,16},{3,24},{4,32},{5,40},{6,48},{7,56},{8,1},{9,9},... | collective-permute-start | bytes 196616 | tf_op jit(solution)/shard_map/ppermute | solution.py:417
  204.5 0.8 copy-start.1
  208.9 0.6 copy-start.14

commit v8 on v7

--- a/solution.py
+++ b/solution.py
@@ -94,23 +94,28 @@
         name=name,
         out_shape=[jax.ShapeDtypeStruct(s, d) for s, d in outs],
         in_specs=specs,
-        out_specs=[pl.BlockSpec(memory_space=pltpu.VMEM) for _ in outs],
+        out_specs=[
+            pl.BlockSpec(memory_space=pltpu.SMEM if s == (1, 1) else pltpu.VMEM) for s, _ in outs
+        ],
         scratch_shapes=[pltpu.VMEM(s, d) for s, d in scratch],
         interpret=INTERPRET,
     )(*args)
 
 
-def project_body(at, view, own, back, ahead, far_low, far_high, piece, wide_a, raw_b):
+def project_body(at, view, own, back, ahead, far_low, far_high, right, piece, wide_a, raw_b):
     zh_n, x_n, y_n, rows, kt = piece.shape
     x = at[0]
     half = y_n // 2
+    left = kt // 2
+    after, before, far = lax.rem(x + 1, x_n), lax.rem(x + x_n - 1, x_n), lax.rem(x + 2, x_n)
     for zh in range(zh_n):
-        piece[zh, x] = own[:, zh]
-        piece[zh, lax.rem(x + x_n - 1, x_n)] = back[:, zh]
-        piece[zh, lax.rem(x + 1, x_n)] = ahead[:, zh]
-        far = lax.rem(x + 2, x_n)
-        piece[zh, far, :half] = far_low[:, zh]
-        piece[zh, far, half:] = far_high[:, zh]
+        piece[zh, x, :, :, :left] = own[:, zh]
+        piece[zh, before, :, :, :left] = back[:, zh]
+        piece[zh, after, :, :, :left] = ahead[:, zh]
+        piece[zh, far, :half, :, :left] = far_low[:, zh]
+        piece[zh, far, half:, :, :left] = far_high[:, zh]
+        for step in range(x_n):
+            piece[zh, x ^ step, :, :, left:] = right[:, step, zh]
     weight = piece[...].reshape(zh_n * x_n * y_n * rows, kt)
     raw = dot(view[...], weight, 1, 0).astype(BF)
     n = raw_b.shape[0]
@@ -331,7 +336,7 @@
         total = total + got[z, :rows].astype(F32)
         power = power + joined(got[z, rows:].astype(F32), 0, 3)
     out[...] = scale * total
-    power_out[...] = power / features
+    power_out[0, 0] = jnp.max(power[:, :128]) / features
 
 
 def on_device(feats, jitter, mask_ids, weight):
@@ -361,7 +366,11 @@
     ).astype(jnp.int32)
     view, keep_a, keep_b = masked_views(feats, jitter, mask_ids)
 
-    own = spread(weight, ("y", "zh")).reshape(y_n, zh_n, w_rows, kt)
+    own = lax.all_gather(weight, "zh", axis=0)
+    right = own[:, :, kt // 2 :]
+    right = jnp.stack([right] + [flip(right, "x", step) for step in range(1, x_n)])
+    own = spread(own[:, :, : kt // 2], "y").reshape(y_n, zh_n, w_rows, kt // 2)
+    right = spread(right, "y").reshape(y_n, x_n, zh_n, w_rows, kt // 2)
     half = y_n // 2
     back = shift(own, "x", 1)
     ahead = shift(own, "x", x_n - 1)
@@ -371,7 +380,7 @@
         project_body,
         "project",
         [((zh_n, x_n, y_n, w_rows, kt), BF), ((y_n, rows, kt), BF), ((rows, kt), BF)],
-        (at, view, own, back, ahead, far_low, far_high),
+        (at, view, own, back, ahead, far_low, far_high, right),
     )
 
     raw_a = wide_a[0]
@@ -432,10 +441,10 @@
     feats_grad, cross_power = call(
         lambda *refs: end_body(*refs, scale=LOSS_SCALE / total, features=kt * tile_n),
         "end",
-        [((rows, chunk), F32), ((1, chunk), F32)],
+        [((rows, chunk), F32), ((1, 1), F32)],
         (got,),
     )
-    return feats_grad, diag_corr[0], cross_power[0, 0]
+    return feats_grad, diag_corr.reshape(kt), cross_power.reshape(())
 
 
 def solution(mesh):

time: 235 us -> 235 us (level)
  blocking collectives: 120 us -> 94.4 us
  starting transfers between devices: 53.6 us -> 73.9 us
  waiting for transfers between devices: 20.7 us -> 26.4 us
    all_to_all x2 -> x1, blocking collectives: 47 us -> 10 us  [spread(): lax.all_to_all(jnp.broadcast_to(value[None], (parts,) + value.shape), axe...]
    all_to_all x0 -> x2, starting transfers between devices: none -> 13.6 us  [spread(): lax.all_to_all(jnp.broadcast_to(value[None], (parts,) + value.shape), axe...]
    all_gather x0 -> x1, blocking collectives: none -> 11.8 us  [on_device(): own = lax.all_gather(weight, 'zh', axis=0)]
    ppermute x4 -> x7, starting transfers between devices: 16.5 us -> 28.1 us  [flip(): return lax.ppermute(value, axis, [(i, i ^ step) for i in range(n)])]
    all_to_all x0 -> x2, waiting for transfers between devices: none -> 6.87 us  [spread(): lax.all_to_all(jnp.broadcast_to(value[None], (parts,) + value.shape), axe...]
    ppermute x4, waiting for transfers between devices: 11.7 us -> 6.25 us  [shift(): return lax.ppermute(value, axis, [(i, (i + step) % n) for i in range(n)])]
    ppermute x4 -> x7, waiting for transfers between devices: 4.36 us -> 7.56 us  [flip(): return lax.ppermute(value, axis, [(i, i ^ step) for i in range(n)])]
    ppermute x4, starting transfers between devices: 13.5 us -> 10.6 us  [shift(): return lax.ppermute(value, axis, [(i, (i + step) % n) for i in range(n)])]
  transfers between devices with their start and end apart: 12 -> 17, of which waited for: 6 -> 9; matrix products, arithmetic and copies ran while one was open for 2% -> 2% of each run, Pallas kernels for 4% -> 4%
where the time goes in v8:
time: 235 us; the launch traced here: 234 us
  blocking collectives  94.4 us (40%)
  starting transfers between devices  73.9 us (31%)
  Pallas kernels  27.3 us (12%)
  waiting for transfers between devices  26.4 us (11%)
  local copies, waits for them, and re-layouts  8.69 us (4%)
    ppermute x7, starting transfers between devices, flip(): return lax.ppermute(value, axis, [(i, i ^ step) for i in range(n)])  28.1 us
    pallas_call x10, Pallas kernels, call(): pl.pallas_call(body, name=name, out_shape=[jax.ShapeDtypeStruct(s, d) for...  27.3 us
    all_to_all x1, blocking collectives, on_device(): got = lax.all_to_all(gram, ('x', 'zh'), 0, 0, tiled=True)  24.5 us
    all_gather x1, blocking collectives, on_device(): big_b = lax.all_gather(own_b, TILE, axis=0)  22.2 us
    all_to_all x1, blocking collectives, on_device(): got = lax.all_to_all(share, TILE, 0, 0, tiled=True)  17.9 us
    all_to_all x2, starting transfers between devices, spread(): lax.all_to_all(jnp.broadcast_to(value[None], (parts,) + value.shape), axe...  13.6 us
    all_gather x1, blocking collectives, on_device(): own = lax.all_gather(weight, 'zh', axis=0)  11.8 us
    ppermute x4, starting transfers between devices, shift(): return lax.ppermute(value, axis, [(i, (i + step) % n) for i in range(n)])  10.6 us
  transfers between devices with their start and end apart: 17, of which 9 were waited for; matrix products, arithmetic and copies ran while one was open for 2% of the time, Pallas kernels for 4%

profile of v8, /device:TPU:1, one launch (start us, length us, event | category | flops | bytes accessed | tf_op | source)
XLA Modules:
  0.0 233.9 jit_solution(3015172333695094458)
XLA Ops:
  0.6 11.8 %all-gather = bf16[64,512]{1,0:T(8,128)(2,1)S(1)} all-gather(bf16[32,512]{1,0:T(8,128)(2,1)} %param.7), channel_id=2, replica_groups=mesh['zh'=2,'x'=4,'y'=8,'zl'=4,'c'=2] {'zh'}, dimensions={0}, use_global_device_ids=true | all-gather | bytes 98304 | tf_op jit(solution)/shard_map/all_gather | solution.py:369
  13.2 7.0 %all-to-all-start = ((bf16[8,2,32,256]{3,2,1,0:T(8,128)(2,1)}), bf16[8,2,32,256]{3,2,1,0:T(8,128)(2,1)S(1)}, u32[]{:S(2)}, u32[]{:S(2)}) async-start(bf16[8,2,32,256]{3,2,1,0:T(8,128)(2,1)} %broadcast_in_dim.6), calls=%async_computation | async-start | bytes 524288 | tf_op jit(solution)/shard_map/all_to_all | solution.py:38
  20.2 4.6 %collective-permute-start.5 = (bf16[2,32,256]{2,1,0:T(8,128)(2,1)S(1)}, bf16[2,32,256]{2,1,0:T(8,128)(2,1)S(1)}, u32[]{:S(2)}, u32[]{:S(2)}) collective-permute-start(bf16[2,32,256]{2,1,0:T(8,128)(2,1)S(1)} %get-tuple-element.38), channel_id=1, source_target_pairs={{0,128},{64,192},{128,0},{192,64},{1,129},{65,193},{129,1},{193,65... | collective-permute-start | bytes 98312 | tf_op jit(solution)/shard_map/ppermute | solution.py:50
  24.8 2.2 collective-permute-start.4
  27.0 2.5 %collective-permute-start.6 = (bf16[2,32,256]{2,1,0:T(8,128)(2,1)S(1)}, bf16[2,32,256]{2,1,0:T(8,128)(2,1)S(1)}, u32[]{:S(2)}, u32[]{:S(2)}) collective-permute-start(bf16[2,32,256]{2,1,0:T(8,128)(2,1)S(1)} %get-tuple-element.38), channel_id=1, source_target_pairs={{0,192},{64,128},{128,64},{192,0},{1,193},{65,129},{129,65},{193,1... | collective-permute-start | bytes 98312 | tf_op jit(solution)/shard_map/ppermute | solution.py:50
  29.6 3.3 %collective-permute-done.6 = bf16[2,32,256]{2,1,0:T(8,128)(2,1)S(1)} collective-permute-done((bf16[2,32,256]{2,1,0:T(8,128)(2,1)S(1)}, bf16[2,32,256]{2,1,0:T(8,128)(2,1)S(1)}, u32[]{:S(2)}, u32[]{:S(2)}) %collective-permute-start.6) | collective-permute-done | bytes 32800 | tf_op jit(solution)/shard_map/ppermute | solution.py:50
  33.0 1.1 broadcast_in_dim.7
  34.1 6.6 %all-to-all-start.1 = ((bf16[8,4,2,32,256]{4,3,2,1,0:T(8,128)(2,1)}), bf16[8,4,2,32,256]{4,3,2,1,0:T(8,128)(2,1)S(1)}, u32[]{:S(2)}, u32[]{:S(2)}) async-start(bf16[8,4,2,32,256]{4,3,2,1,0:T(8,128)(2,1)} %broadcast_in_dim.7), calls=%async_computation.1 | async-start | bytes 2097152 | tf_op jit(solution)/shard_map/all_to_all | solution.py:38
  41.4 2.5 %collective-permute-start.1 = (bf16[8,2,32,256]{3,2,1,0:T(8,128)(2,1)S(1)}, bf16[8,2,32,256]{3,2,1,0:T(8,128)(2,1)S(1)}, u32[]{:S(2)}, u32[]{:S(2)}) collective-permute-start(bf16[8,2,32,256]{3,2,1,0:T(8,128)(2,1)S(1)} %all-to-all-done.own), channel_id=1, source_target_pairs={{0,192},{64,0},{128,64},{192,128},{1,193},{65,1},{129,65},{193,129... | collective-permute-start | bytes 786440 | tf_op jit(solution)/shard_map/ppermute | solution.py:45
  43.9 2.8 %collective-permute-start = (bf16[8,2,32,256]{3,2,1,0:T(8,128)(2,1)S(1)}, bf16[8,2,32,256]{3,2,1,0:T(8,128)(2,1)S(1)}, u32[]{:S(2)}, u32[]{:S(2)}) collective-permute-start(bf16[8,2,32,256]{3,2,1,0:T(8,128)(2,1)S(1)} %all-to-all-done.own), channel_id=1, source_target_pairs={{0,64},{64,128},{128,192},{192,0},{1,65},{65,129},{129,193},{193,1... | collective-permute-start | bytes 786440 | tf_op jit(solution)/shard_map/ppermute | solution.py:45
  47.0 1.8 collective-permute-done.1.ahead
  48.9 3.4 %collective-permute-start.3 = (bf16[4,2,32,256]{3,2,1,0:T(8,128)(2,1)S(1)}, bf16[4,2,32,256]{3,2,1,0:T(8,128)(2,1)S(1)}, u32[]{:S(2)}, u32[]{:S(2)}) collective-permute-start(bf16[4,2,32,256]{3,2,1,0:T(8,128)(2,1)S(1)} %slice.30), channel_id=1, source_target_pairs={{0,192},{64,0},{128,64},{192,128},{1,193},{65,1},{129,65},{193,129... | collective-permute-start | bytes 393224 | tf_op jit(solution)/shard_map/ppermute | solution.py:45
  52.3 1.9 collective-permute-start.2
  54.2 0.9 pad_maximum_fusion.view
  55.1 4.4 %collective-permute-done.2.far_low = bf16[4,2,32,256]{3,2,1,0:T(8,128)(2,1)S(1)} collective-permute-done((bf16[4,2,32,256]{3,2,1,0:T(8,128)(2,1)S(1)}, bf16[4,2,32,256]{3,2,1,0:T(8,128)(2,1)S(1)}, u32[]{:S(2)}, u32[]{:S(2)}) %collective-permute-start.2) | collective-permute-done | bytes 131104 | tf_op jit(solution)/shard_map/ppermute | solution.py:45
  59.5 6.9 %all-to-all-done.1.right = bf16[8,4,2,32,256]{4,3,2,1,0:T(8,128)(2,1)S(1)} async-done(((bf16[8,4,2,32,256]{4,3,2,1,0:T(8,128)(2,1)}), bf16[8,4,2,32,256]{4,3,2,1,0:T(8,128)(2,1)S(1)}, u32[]{:S(2)}, u32[]{:S(2)}) %all-to-all-start.1) | async-done | bytes 1048608 | tf_op jit(solution)/shard_map/all_to_all | solution.py:38
  66.4 1.0 copy-done.1
  67.4 3.4 %project.1 = (bf16[2,4,8,32,512]{4,3,2,1,0:T(8,128)(2,1)}, bf16[8,64,512]{2,1,0:T(8,128)(2,1)}, bf16[64,512]{1,0:T(8,128)(2,1)}) custom-call(s32[5]{0:T(128)} %stack.38.at.refs_0_, bf16[128,2048]{1,0:T(8,128)(2,1)} %pad_maximum_fusion.view, bf16[8,2,32,256]{3,2,1,0:T(8,128)(2,1)} %copy-done.3, bf16[8,2,32,256]{3,2,1,0:T(8,128)(2,1)} %copy-done.5, ...), custom_call_target="tpu_custom_call" | custom-call | tf_op jit(solution)/shard_map/project/pallas_call | solution.py:92
  70.7 3.5 %all-to-all-start.2 = ((bf16[8,64,512]{2,1,0:T(8,128)(2,1)}), bf16[8,64,512]{2,1,0:T(8,128)(2,1)S(1)}, u32[]{:S(2)}, u32[]{:S(2)}) async-start(bf16[8,64,512]{2,1,0:T(8,128)(2,1)} %get-tuple-element.19), calls=%async_computation.2 | async-start | bytes 1048576 | tf_op jit(solution)/shard_map/all_to_all | solution.py:387
  74.2 7.5 %collective-permute-start.7 = (bf16[64,512]{1,0:T(8,128)(2,1)}, bf16[64,512]{1,0:T(8,128)(2,1)S(1)}, u32[]{:S(2)}, u32[]{:S(2)}) collective-permute-start(bf16[64,512]{1,0:T(8,128)(2,1)} %get-tuple-element.20), channel_id=1, source_target_pairs={{0,0},{1,8},{2,16},{3,24},{4,32},{5,40},{6,48},{7,56},{8,1},{9,9},... | collective-permute-start | bytes 196616 | tf_op jit(solution)/shard_map/ppermute | solution.py:388
  81.7 5.7 %collective-permute-done.7.raw_b = bf16[64,512]{1,0:T(8,128)(2,1)S(1)} collective-permute-done((bf16[64,512]{1,0:T(8,128)(2,1)}, bf16[64,512]{1,0:T(8,128)(2,1)S(1)}, u32[]{:S(2)}, u32[]{:S(2)}) %collective-permute-start.7) | collective-permute-done | bytes 65568 | tf_op jit(solution)/shard_map/ppermute | solution.py:388
  87.5 22.2 %all-gather.1 = bf16[512,512]{1,0:T(8,128)(2,1)} all-gather(bf16[64,512]{1,0:T(8,128)(2,1)S(1)} %collective-permute-done.7.raw_b), channel_id=3, replica_groups=mesh['zh'=2,'x'=4,'y'=8,'zl'=4,'c'=2] {'zl','c'}, dimensions={0}, use_global_device_ids=true | all-gather | bytes 589824 | tf_op jit(solution)/shard_map/all_gather | solution.py:389
  109.6 0.8 copy-done
  110.5 3.0 %gram.1 = bf16[8,80,512]{2,1,0:T(8,128)(2,1)} custom-call(bf16[8,64,512]{2,1,0:T(8,128)(2,1)} %copy-done, bf16[8,64,512]{2,1,0:T(8,128)(2,1)} %bitcast.20), custom_call_target="tpu_custom_call" | custom-call | tf_op jit(solution)/shard_map/gram/pallas_call | solution.py:92
  113.5 24.5 %all_to_all.35.refs_1_ = bf16[8,80,512]{2,1,0:T(8,128)(2,1)} all-to-all(bf16[8,80,512]{2,1,0:T(8,128)(2,1)} %gram.1), channel_id=1, replica_groups=mesh['zh'=2,'x'=4,'y'=8,'zl'=4,'c'=2] {'x','zh'}, dimensions={0} | all-to-all | bytes 1310720 | tf_op jit(solution)/shard_map/all_to_all | solution.py:394
  138.0 2.4 %mix.1 = (bf16[64,512]{1,0:T(8,128)(2,1)}, f32[8,512]{1,0:T(8,128)}) custom-call(s32[5]{0:T(128)} %stack.38.at.refs_0_, bf16[8,80,512]{2,1,0:T(8,128)(2,1)} %all_to_all.35.refs_1_), custom_call_target="tpu_custom_call" | custom-call | tf_op jit(solution)/shard_map/mix/pallas_call | solution.py:92
  140.4 7.9 %all_gather.19 = bf16[128,512]{1,0:T(8,128)(2,1)S(1)} all-gather(bf16[64,512]{1,0:T(8,128)(2,1)} %get-tuple-element.21), channel_id=1, replica_groups=mesh['zh'=2,'x'=4,'y'=8,'zl'=4,'c'=2] {'zh'}, dimensions={0}, use_global_device_ids=true | all-gather | bytes 196608 | tf_op jit(solution)/shard_map/all_gather | solution.py:402
  148.4 10.0 %all_to_all.36.mix4 = bf16[4,128,512]{2,1,0:T(8,128)(2,1)} all-to-all(bf16[4,128,512]{2,1,0:T(8,128)(2,1)S(1)} %broadcast_in_dim.8), channel_id=1, replica_groups=mesh['zh'=2,'x'=4,'y'=8,'zl'=4,'c'=2] {'x'}, dimensions={0} | all-to-all | bytes 1048576 | tf_op jit(solution)/shard_map/all_to_all | solution.py:38
  158.4 3.3 %grad_a.1 = bf16[8,72,512]{2,1,0:T(8,128)(2,1)} custom-call(s32[5]{0:T(128)} %stack.38.at.refs_0_, bf16[4,128,512]{2,1,0:T(8,128)(2,1)} %all_to_all.36.mix4, bf16[8,64,512]{2,1,0:T(8,128)(2,1)} %bitcast.21, f32[8,512]{1,0:T(8,128)} %get-tuple-element.22.stats), custom_call_target="tpu_custom_call" | custom-call | tf_op jit(solution)/shard_map/grad_a/pallas_call | solution.py:92
  161.7 5.4 %all-to-all-start.5 = ((bf16[8,72,512]{2,1,0:T(8,128)(2,1)}), bf16[8,72,512]{2,1,0:T(8,128)(2,1)S(1)}, u32[]{:S(2)}, u32[]{:S(2)}) async-start(bf16[8,72,512]{2,1,0:T(8,128)(2,1)} %grad_a.1), calls=%async_computation.5 | async-start | bytes 1179648 | tf_op jit(solution)/shard_map/all_to_all | solution.py:416
  167.1 2.9 %grad_b.1 = (bf16[264,512]{1,0:T(8,128)(2,1)}, f32[264,512]{1,0:T(8,128)}) custom-call(s32[5]{0:T(128)} %stack.38.at.refs_0_, bf16[4,128,512]{2,1,0:T(8,128)(2,1)} %all_to_all.36.mix4, bf16[8,64,512]{2,1,0:T(8,128)(2,1)} %copy-done, f32[8,512]{1,0:T(8,128)} %get-tuple-element.22.stats), custom_call_target="tpu_custom_call" | custom-call | tf_op jit(solution)/shard_map/grad_b/pallas_call | solution.py:92
  170.0 7.9 %collective-permute-start.8 = (bf16[264,512]{1,0:T(8,128)(2,1)}, bf16[264,512]{1,0:T(8,128)(2,1)S(1)}, u32[]{:S(2)}, u32[]{:S(2)}) collective-permute-start(bf16[264,512]{1,0:T(8,128)(2,1)} %get-tuple-element.26), channel_id=1, source_target_pairs={{0,1},{1,0},{2,3},{3,2},{4,5},{5,4},{6,7},{7,6},{8,9},{9,8},{10,11... | collective-permute-start | bytes 811016 | tf_op jit(solution)/shard_map/ppermute | solution.py:50
  178.0 1.4 collective-permute-done.8.got
  180.0 2.0 core.1
  182.0 4.9 %collective-permute-start.9 = (bf16[72,512]{1,0:T(8,128)(2,1)}, bf16[72,512]{1,0:T(8,128)(2,1)S(1)}, u32[]{:S(2)}, u32[]{:S(2)}) collective-permute-start(bf16[72,512]{1,0:T(8,128)(2,1)} %get-tuple-element.28), channel_id=1, source_target_pairs={{0,2},{2,0},{4,6},{6,4},{1,3},{3,1},{5,7},{7,5},{8,10},{10,8},{12,... | collective-permute-start | bytes 221192 | tf_op jit(solution)/shard_map/ppermute | solution.py:50
  187.0 2.7 %collective-permute-start.10 = (bf16[72,512]{1,0:T(8,128)(2,1)}, bf16[72,512]{1,0:T(8,128)(2,1)S(1)}, u32[]{:S(2)}, u32[]{:S(2)}) collective-permute-start(bf16[72,512]{1,0:T(8,128)(2,1)} %get-tuple-element.29), channel_id=1, source_target_pairs={{0,4},{2,6},{4,0},{6,2},{1,5},{3,7},{5,1},{7,3},{8,12},{10,14},{12... | collective-permute-start | bytes 221192 | tf_op jit(solution)/shard_map/ppermute | solution.py:50
  189.6 3.2 %collective-permute-start.11 = (bf16[72,512]{1,0:T(8,128)(2,1)}, bf16[72,512]{1,0:T(8,128)(2,1)S(1)}, u32[]{:S(2)}, u32[]{:S(2)}) collective-permute-start(bf16[72,512]{1,0:T(8,128)(2,1)} %get-tuple-element.30), channel_id=1, source_target_pairs={{0,6},{2,4},{4,2},{6,0},{1,7},{3,5},{5,3},{7,1},{8,14},{10,12},{12... | collective-permute-start | bytes 221192 | tf_op jit(solution)/shard_map/ppermute | solution.py:50
  192.9 1.2 compare_convert_fusion
  194.0 1.4 collective-permute-done.10.got2
  195.5 1.4 collective-permute-done.11.got3
  197.5 1.7 dz_b.1
  199.2 5.3 %collective-permute-start.12 = (bf16[64,512]{1,0:T(8,128)(2,1)}, bf16[64,512]{1,0:T(8,128)(2,1)S(1)}, u32[]{:S(2)}, u32[]{:S(2)}) collective-permute-start(bf16[64,512]{1,0:T(8,128)(2,1)} %dz_b.1), channel_id=1, source_target_pairs={{0,0},{1,8},{2,16},{3,24},{4,32},{5,40},{6,48},{7,56},{8,1},{9,9},... | collective-permute-start | bytes 196616 | tf_op jit(solution)/shard_map/ppermute | solution.py:426
  204.5 1.5 slice_bitcast_fusion.raw_a
  206.0 0.8 copy-done.2
  206.8 3.5 %back_a.1 = (f32[64,2048]{1,0:T(8,128)}, f32[1,512]{1,0:T(1,128)}, f32[1,256]{1,0:T(1,128)}) custom-call(bf16[8,72,512]{2,1,0:T(8,128)(2,1)} %copy-done.2, bf16[64,512]{1,0:T(8,128)(2,1)} %slice_bitcast_fusion.raw_a, f32[8,512]{1,0:T(8,128)} %get-tuple-element.22.stats, f32[64,2048]{1,0:T(8,128)} %get-tuple-element.41.keep, ...), custom_call_target="tpu_custom_call" | custom-call | tf_op jit(solution)/shard_map/back_a/pallas_call | solution.py:92
  211.0 3.4 %back_b.1 = bf16[8,72,256]{2,1,0:T(8,128)(2,1)} custom-call(f32[64,2048]{1,0:T(8,128)} %get-tuple-element.24.part, bf16[64,512]{1,0:T(8,128)(2,1)} %copy-done.15, f32[64,2048]{1,0:T(8,128)} %get-tuple-element.40.keep, bf16[2,4,8,32,512]{4,3,2,1,0:T(8,128)(2,1)} %get-tuple-element.23.weight, f32[1,256]{1,0:T(1,128)} %get-tuple-element.31.power), custom_call_target="tpu_custom_call" | custom-call | tf_op jit(solution)/shard_map/back_b/pallas_call | solution.py:92
  214.3 17.9 %all_to_all.37.refs_0_ = bf16[8,72,256]{2,1,0:T(8,128)(2,1)} all-to-all(bf16[8,72,256]{2,1,0:T(8,128)(2,1)} %back_b.1), channel_id=1, replica_groups=mesh['zh'=2,'x'=4,'y'=8,'zl'=4,'c'=2] {'zl','c'}, dimensions={0} | all-to-all | bytes 589824 | tf_op jit(solution)/shard_map/all_to_all | solution.py:440
  232.3 1.6 end.1
  (50 shorter events, 3.9 us)
Async XLA Ops:
  13.2 28.2 %copy-start.16 = (s32[64,2]{0,1:T(2,128)S(1)}, s32[64,2]{0,1:T(2,128)}, u32[]{:S(2)}) copy-start(s32[64,2]{0,1:T(2,128)} %param.6) | copy-start | bytes 1540
  13.2 33.5 %copy-start.7 = (bf16[64,2048]{1,0:T(8,128)(2,1)S(1)}, bf16[64,2048]{1,0:T(8,128)(2,1)}, u32[]{:S(2)}) copy-start(bf16[64,2048]{1,0:T(8,128)(2,1)} %param.4) | copy-start | bytes 786436
  13.2 33.5 %copy-start.8 = (bf16[64,2048]{1,0:T(8,128)(2,1)S(1)}, bf16[64,2048]{1,0:T(8,128)(2,1)}, u32[]{:S(2)}) copy-start(bf16[64,2048]{1,0:T(8,128)(2,1)} %param.5) | copy-start | bytes 786436
  13.2 19.7 %all-to-all-start = ((bf16[8,2,32,256]{3,2,1,0:T(8,128)(2,1)}), bf16[8,2,32,256]{3,2,1,0:T(8,128)(2,1)S(1)}, u32[]{:S(2)}, u32[]{:S(2)}) async-start(bf16[8,2,32,256]{3,2,1,0:T(8,128)(2,1)} %broadcast_in_dim.6), calls=%async_computation | async-start | bytes 524288 | tf_op jit(solution)/shard_map/all_to_all | solution.py:38
  20.2 9.4 %collective-permute-start.5 = (bf16[2,32,256]{2,1,0:T(8,128)(2,1)S(1)}, bf16[2,32,256]{2,1,0:T(8,128)(2,1)S(1)}, u32[]{:S(2)}, u32[]{:S(2)}) collective-permute-start(bf16[2,32,256]{2,1,0:T(8,128)(2,1)S(1)} %get-tuple-element.38), channel_id=1, source_target_pairs={{0,128},{64,192},{128,0},{192,64},{1,129},{65,193},{129,1},{193,65... | collective-permute-start | bytes 98312 | tf_op jit(solution)/shard_map/ppermute | solution.py:50
  24.8 4.8 %collective-permute-start.4 = (bf16[2,32,256]{2,1,0:T(8,128)(2,1)S(1)}, bf16[2,32,256]{2,1,0:T(8,128)(2,1)S(1)}, u32[]{:S(2)}, u32[]{:S(2)}) collective-permute-start(bf16[2,32,256]{2,1,0:T(8,128)(2,1)S(1)} %get-tuple-element.38), channel_id=1, source_target_pairs={{0,64},{64,0},{128,192},{192,128},{1,65},{65,1},{129,193},{193,129... | collective-permute-start | bytes 98312 | tf_op jit(solution)/shard_map/ppermute | solution.py:50
  27.0 5.9 %collective-permute-start.6 = (bf16[2,32,256]{2,1,0:T(8,128)(2,1)S(1)}, bf16[2,32,256]{2,1,0:T(8,128)(2,1)S(1)}, u32[]{:S(2)}, u32[]{:S(2)}) collective-permute-start(bf16[2,32,256]{2,1,0:T(8,128)(2,1)S(1)} %get-tuple-element.38), channel_id=1, source_target_pairs={{0,192},{64,128},{128,64},{192,0},{1,193},{65,129},{129,65},{193,1... | collective-permute-start | bytes 98312 | tf_op jit(solution)/shard_map/ppermute | solution.py:50
  32.9 14.1 %copy-start.3 = (bf16[8,2,32,256]{3,2,1,0:T(8,128)(2,1)}, bf16[8,2,32,256]{3,2,1,0:T(8,128)(2,1)S(1)}, u32[]{:S(2)}) copy-start(bf16[8,2,32,256]{3,2,1,0:T(8,128)(2,1)S(1)} %all-to-all-done.own) | copy-start | bytes 786436
  34.1 32.3 %all-to-all-start.1 = ((bf16[8,4,2,32,256]{4,3,2,1,0:T(8,128)(2,1)}), bf16[8,4,2,32,256]{4,3,2,1,0:T(8,128)(2,1)S(1)}, u32[]{:S(2)}, u32[]{:S(2)}) async-start(bf16[8,4,2,32,256]{4,3,2,1,0:T(8,128)(2,1)} %broadcast_in_dim.7), calls=%async_computation.1 | async-start | bytes 2097152 | tf_op jit(solution)/shard_map/all_to_all | solution.py:38
  41.4 7.4 %collective-permute-start.1 = (bf16[8,2,32,256]{3,2,1,0:T(8,128)(2,1)S(1)}, bf16[8,2,32,256]{3,2,1,0:T(8,128)(2,1)S(1)}, u32[]{:S(2)}, u32[]{:S(2)}) collective-permute-start(bf16[8,2,32,256]{3,2,1,0:T(8,128)(2,1)S(1)} %all-to-all-done.own), channel_id=1, source_target_pairs={{0,192},{64,0},{128,64},{192,128},{1,193},{65,1},{129,65},{193,129... | collective-permute-start | bytes 786440 | tf_op jit(solution)/shard_map/ppermute | solution.py:45
  43.9 8.3 %collective-permute-start = (bf16[8,2,32,256]{3,2,1,0:T(8,128)(2,1)S(1)}, bf16[8,2,32,256]{3,2,1,0:T(8,128)(2,1)S(1)}, u32[]{:S(2)}, u32[]{:S(2)}) collective-permute-start(bf16[8,2,32,256]{3,2,1,0:T(8,128)(2,1)S(1)} %all-to-all-done.own), channel_id=1, source_target_pairs={{0,64},{64,128},{128,192},{192,0},{1,65},{65,129},{129,193},{193,1... | collective-permute-start | bytes 786440 | tf_op jit(solution)/shard_map/ppermute | solution.py:45
  48.8 17.5 %copy-start.4 = (bf16[8,2,32,256]{3,2,1,0:T(8,128)(2,1)}, bf16[8,2,32,256]{3,2,1,0:T(8,128)(2,1)S(1)}, u32[]{:S(2)}) copy-start(bf16[8,2,32,256]{3,2,1,0:T(8,128)(2,1)S(1)} %collective-permute-done.1.ahead) | copy-start | bytes 786436
  48.9 6.2 %collective-permute-start.3 = (bf16[4,2,32,256]{3,2,1,0:T(8,128)(2,1)S(1)}, bf16[4,2,32,256]{3,2,1,0:T(8,128)(2,1)S(1)}, u32[]{:S(2)}, u32[]{:S(2)}) collective-permute-start(bf16[4,2,32,256]{3,2,1,0:T(8,128)(2,1)S(1)} %slice.30), channel_id=1, source_target_pairs={{0,192},{64,0},{128,64},{192,128},{1,193},{65,1},{129,65},{193,129... | collective-permute-start | bytes 393224 | tf_op jit(solution)/shard_map/ppermute | solution.py:45
  52.3 14.1 %copy-start.5 = (bf16[8,2,32,256]{3,2,1,0:T(8,128)(2,1)}, bf16[8,2,32,256]{3,2,1,0:T(8,128)(2,1)S(1)}, u32[]{:S(2)}) copy-start(bf16[8,2,32,256]{3,2,1,0:T(8,128)(2,1)S(1)} %collective-permute-done.back) | copy-start | bytes 786436
  52.3 7.2 %collective-permute-start.2 = (bf16[4,2,32,256]{3,2,1,0:T(8,128)(2,1)S(1)}, bf16[4,2,32,256]{3,2,1,0:T(8,128)(2,1)S(1)}, u32[]{:S(2)}, u32[]{:S(2)}) collective-permute-start(bf16[4,2,32,256]{3,2,1,0:T(8,128)(2,1)S(1)} %slice.29), channel_id=1, source_target_pairs={{0,64},{64,128},{128,192},{192,0},{1,65},{65,129},{129,193},{193,1... | collective-permute-start | bytes 393224 | tf_op jit(solution)/shard_map/ppermute | solution.py:45
  55.1 11.3 %copy-start.10 = (bf16[4,2,32,256]{3,2,1,0:T(8,128)(2,1)}, bf16[4,2,32,256]{3,2,1,0:T(8,128)(2,1)S(1)}, u32[]{:S(2)}) copy-start(bf16[4,2,32,256]{3,2,1,0:T(8,128)(2,1)S(1)} %collective-permute-done.3.far_high) | copy-start | bytes 393220
  59.5 6.9 %copy-start.11 = (bf16[4,2,32,256]{3,2,1,0:T(8,128)(2,1)}, bf16[4,2,32,256]{3,2,1,0:T(8,128)(2,1)S(1)}, u32[]{:S(2)}) copy-start(bf16[4,2,32,256]{3,2,1,0:T(8,128)(2,1)S(1)} %collective-permute-done.2.far_low) | copy-start | bytes 393220
  66.4 1.0 copy-start.1
  70.7 38.9 %all-to-all-start.2 = ((bf16[8,64,512]{2,1,0:T(8,128)(2,1)}), bf16[8,64,512]{2,1,0:T(8,128)(2,1)S(1)}, u32[]{:S(2)}, u32[]{:S(2)}) async-start(bf16[8,64,512]{2,1,0:T(8,128)(2,1)} %get-tuple-element.19), calls=%async_computation.2 | async-start | bytes 1048576 | tf_op jit(solution)/shard_map/all_to_all | solution.py:387
  74.2 13.2 %collective-permute-start.7 = (bf16[64,512]{1,0:T(8,128)(2,1)}, bf16[64,512]{1,0:T(8,128)(2,1)S(1)}, u32[]{:S(2)}, u32[]{:S(2)}) collective-permute-start(bf16[64,512]{1,0:T(8,128)(2,1)} %get-tuple-element.20), channel_id=1, source_target_pairs={{0,0},{1,8},{2,16},{3,24},{4,32},{5,40},{6,48},{7,56},{8,1},{9,9},... | collective-permute-start | bytes 196616 | tf_op jit(solution)/shard_map/ppermute | solution.py:388
  87.5 53.0 %copy-start.9 = (bf16[64,512]{1,0:T(8,128)(2,1)}, bf16[64,512]{1,0:T(8,128)(2,1)S(1)}, u32[]{:S(2)}) copy-start(bf16[64,512]{1,0:T(8,128)(2,1)S(1)} %collective-permute-done.7.raw_b) | copy-start | bytes 196612
  109.6 0.8 copy-start
  161.7 44.2 %all-to-all-start.5 = ((bf16[8,72,512]{2,1,0:T(8,128)(2,1)}), bf16[8,72,512]{2,1,0:T(8,128)(2,1)S(1)}, u32[]{:S(2)}, u32[]{:S(2)}) async-start(bf16[8,72,512]{2,1,0:T(8,128)(2,1)} %grad_a.1), calls=%async_computation.5 | async-start | bytes 1179648 | tf_op jit(solution)/shard_map/all_to_all | solution.py:416
  170.0 9.3 %collective-permute-start.8 = (bf16[264,512]{1,0:T(8,128)(2,1)}, bf16[264,512]{1,0:T(8,128)(2,1)S(1)}, u32[]{:S(2)}, u32[]{:S(2)}) collective-permute-start(bf16[264,512]{1,0:T(8,128)(2,1)} %get-tuple-element.26), channel_id=1, source_target_pairs={{0,1},{1,0},{2,3},{3,2},{4,5},{5,4},{6,7},{7,6},{8,9},{9,8},{10,11... | collective-permute-start | bytes 811016 | tf_op jit(solution)/shard_map/ppermute | solution.py:50
  179.3 0.7 copy-start.6
  182.0 12.0 %collective-permute-start.9 = (bf16[72,512]{1,0:T(8,128)(2,1)}, bf16[72,512]{1,0:T(8,128)(2,1)S(1)}, u32[]{:S(2)}, u32[]{:S(2)}) collective-permute-start(bf16[72,512]{1,0:T(8,128)(2,1)} %get-tuple-element.28), channel_id=1, source_target_pairs={{0,2},{2,0},{4,6},{6,4},{1,3},{3,1},{5,7},{7,5},{8,10},{10,8},{12,... | collective-permute-start | bytes 221192 | tf_op jit(solution)/shard_map/ppermute | solution.py:50
  187.0 8.5 %collective-permute-start.10 = (bf16[72,512]{1,0:T(8,128)(2,1)}, bf16[72,512]{1,0:T(8,128)(2,1)S(1)}, u32[]{:S(2)}, u32[]{:S(2)}) collective-permute-start(bf16[72,512]{1,0:T(8,128)(2,1)} %get-tuple-element.29), channel_id=1, source_target_pairs={{0,4},{2,6},{4,0},{6,2},{1,5},{3,7},{5,1},{7,3},{8,12},{10,14},{12... | collective-permute-start | bytes 221192 | tf_op jit(solution)/shard_map/ppermute | solution.py:50
  189.6 7.2 %collective-permute-start.11 = (bf16[72,512]{1,0:T(8,128)(2,1)}, bf16[72,512]{1,0:T(8,128)(2,1)S(1)}, u32[]{:S(2)}, u32[]{:S(2)}) collective-permute-start(bf16[72,512]{1,0:T(8,128)(2,1)} %get-tuple-element.30), channel_id=1, source_target_pairs={{0,6},{2,4},{4,2},{6,0},{1,7},{3,5},{5,3},{7,1},{8,14},{10,12},{12... | collective-permute-start | bytes 221192 | tf_op jit(solution)/shard_map/ppermute | solution.py:50
  194.0 2.8 %copy-start.12 = (bf16[72,512]{1,0:T(8,128)(2,1)}, bf16[72,512]{1,0:T(8,128)(2,1)S(1)}, u32[]{:S(2)}) copy-start(bf16[72,512]{1,0:T(8,128)(2,1)S(1)} %collective-permute-done.9.got1) | copy-start | bytes 221188
  195.5 1.4 copy-start.13
  196.8 0.6 copy-start.14
  199.2 11.1 %collective-permute-start.12 = (bf16[64,512]{1,0:T(8,128)(2,1)}, bf16[64,512]{1,0:T(8,128)(2,1)S(1)}, u32[]{:S(2)}, u32[]{:S(2)}) collective-permute-start(bf16[64,512]{1,0:T(8,128)(2,1)} %dz_b.1), channel_id=1, source_target_pairs={{0,0},{1,8},{2,16},{3,24},{4,32},{5,40},{6,48},{7,56},{8,1},{9,9},... | collective-permute-start | bytes 196616 | tf_op jit(solution)/shard_map/ppermute | solution.py:426
  206.0 0.8 copy-start.2
  210.3 0.6 copy-start.15

commit v9 on v7

--- a/solution.py
+++ b/solution.py
@@ -94,7 +94,9 @@
         name=name,
         out_shape=[jax.ShapeDtypeStruct(s, d) for s, d in outs],
         in_specs=specs,
-        out_specs=[pl.BlockSpec(memory_space=pltpu.VMEM) for _ in outs],
+        out_specs=[
+            pl.BlockSpec(memory_space=pltpu.SMEM if s == (1, 1) else pltpu.VMEM) for s, _ in outs
+        ],
         scratch_shapes=[pltpu.VMEM(s, d) for s, d in scratch],
         interpret=INTERPRET,
     )(*args)
@@ -104,11 +106,11 @@
     zh_n, x_n, y_n, rows, kt = piece.shape
     x = at[0]
     half = y_n // 2
+    after, before, far = lax.rem(x + 1, x_n), lax.rem(x + x_n - 1, x_n), lax.rem(x + 2, x_n)
     for zh in range(zh_n):
         piece[zh, x] = own[:, zh]
-        piece[zh, lax.rem(x + x_n - 1, x_n)] = back[:, zh]
-        piece[zh, lax.rem(x + 1, x_n)] = ahead[:, zh]
-        far = lax.rem(x + 2, x_n)
+        piece[zh, before] = back[:, zh]
+        piece[zh, after] = ahead[:, zh]
         piece[zh, far, :half] = far_low[:, zh]
         piece[zh, far, half:] = far_high[:, zh]
     weight = piece[...].reshape(zh_n * x_n * y_n * rows, kt)
@@ -142,14 +144,28 @@
         out[i, deep:] = rows_out
 
 
-def mix_body(at, got, mix, stats, table, offs, *, block):
-    sets, deep, kt = got.shape
-    sub = mix.shape[0]
+def merge_body(got, out):
+    x_n, deep, _ = got.shape
+    sub = deep - 16
+    total = got[0, :sub].astype(F32)
+    for x in range(1, x_n):
+        total = total + got[x, :sub].astype(F32)
+    out[:sub] = total.astype(BF)
+    for x in range(x_n):
+        out[sub + 16 * x : sub + 16 * (x + 1)] = got[x, sub:]
+
+
+def mix_body(at, mine, theirs, mix, stats, table, offs, *, block):
+    sub, kt = mix.shape
+    each = (mine.shape[0] - sub) // 16
+    sets = 2 * each
     total = block * sets
+    low = at[5] == 0
+    own, other = mine[sub:].astype(F32), theirs[sub:].astype(F32)
     raws = []
-    for i in range(sets):
-        rows = got[i, sub:].astype(F32)
-        raws.append([joined(rows, 3 * j, 3) for j in range(5)])
+    for tails in (jnp.where(low, own, other), jnp.where(low, other, own)):
+        for i in range(each):
+            raws.append([joined(tails, 16 * i + 3 * j, 3) for j in range(5)])
     summed = [sum(r[i] for r in raws[1:]) + raws[0][i] for i in range(5)]
     mean_a, mean_b = summed[0] / sets, summed[2] / sets
     square_a, square_b, cross = summed[1], summed[3], summed[4]
@@ -172,9 +188,7 @@
     k_of = lax.broadcasted_iota(jnp.int32, (sub, kt), 0)
     l_of = lax.broadcasted_iota(jnp.int32, (sub, kt), 1)
     chosen = exact((k_of + at[3] == l_of).astype(F32), table[...], 1, 1)
-    corr = got[0, :sub].astype(F32)
-    for i in range(1, sets):
-        corr = corr + got[i, :sub].astype(F32)
+    corr = mine[:sub].astype(F32) + theirs[:sub].astype(F32)
     corr = corr + exact(chosen[:, :sets], offs[...], 1, 0)
     corr = corr * (chosen[:, sets : sets + 1] * (inv_b / total))
     here = k_of + (at[3] + at[4]) == l_of
@@ -331,7 +345,7 @@
         total = total + got[z, :rows].astype(F32)
         power = power + joined(got[z, rows:].astype(F32), 0, 3)
     out[...] = scale * total
-    power_out[...] = power / features
+    power_out[0, 0] = jnp.max(power[:, :128]) / features
 
 
 def on_device(feats, jitter, mask_ids, weight):
@@ -343,7 +357,7 @@
     tile_n = zl_n * c_n
     total = rows * rows_n * y_n
     block = rows * y_n
-    sub = kt // rows_n
+    sub = kt // x_n
     chunk = width // tile_n
     every = DP + TILE
     pairs = swap_pairs()
@@ -355,13 +369,15 @@
             lax.axis_index("x"),
             lax.axis_index("zl"),
             lax.axis_index("c"),
-            lax.axis_index(("x", "zh")) * sub,
+            lax.axis_index("x") * sub,
             jnp.where(y_at == tile_at, 0, FAR),
+            lax.axis_index("zh"),
         ]
     ).astype(jnp.int32)
     view, keep_a, keep_b = masked_views(feats, jitter, mask_ids)
 
-    own = spread(weight, ("y", "zh")).reshape(y_n, zh_n, w_rows, kt)
+    own = lax.all_gather(weight, "zh", axis=0, tiled=True)
+    own = spread(own, "y").reshape(y_n, zh_n, w_rows, kt)
     half = y_n // 2
     back = shift(own, "x", 1)
     ahead = shift(own, "x", x_n - 1)
@@ -379,18 +395,19 @@
     own_b = lax.ppermute(raw_b, every, pairs)
     big_b = lax.all_gather(own_b, TILE, axis=0)
     (gram,) = call(
-        gram_body, "gram", [((rows_n, sub + 16, kt), BF)], (big_a, big_b), [((16, kt), F32)]
-    )
-
-    got = lax.all_to_all(gram, ("x", "zh"), 0, 0, tiled=True)
+        gram_body, "gram", [((x_n, sub + 16, kt), BF)], (big_a, big_b), [((16, kt), F32)]
+    )
+
+    got = lax.all_to_all(gram, "x", 0, 0, tiled=True)
+    (got,) = call(merge_body, "merge", [((sub + 16 * x_n, kt), BF)], (got,))
     mix, stats = call(
         lambda *refs: mix_body(*refs, block=block),
         "mix",
         [((sub, kt), BF), ((8, kt), F32)],
-        (at, got),
+        (at, got, flip(got, "zh", 1)),
         [((16, kt), F32), ((rows_n, kt), F32)],
     )
-    mix = spread(lax.all_gather(mix, "zh", axis=0, tiled=True), "x")
+    mix = spread(mix, "x")
 
     line_rows = zl_n * rows + 8
     sent, kept = call(
@@ -432,10 +449,10 @@
     feats_grad, cross_power = call(
         lambda *refs: end_body(*refs, scale=LOSS_SCALE / total, features=kt * tile_n),
         "end",
-        [((rows, chunk), F32), ((1, chunk), F32)],
+        [((rows, chunk), F32), ((1, 1), F32)],
         (got,),
     )
-    return feats_grad, diag_corr[0], cross_power[0, 0]
+    return feats_grad, diag_corr.reshape(kt), cross_power.reshape(())
 
 
 def solution(mesh):

time: 235 us -> 227 us (0.966)
  blocking collectives: 120 us -> 97.8 us
  starting transfers between devices: 53.6 us -> 62 us
  waiting for transfers between devices: 20.7 us -> 24.6 us
    all_to_all x2, blocking collectives: 47 us -> 31.4 us  [spread(): lax.all_to_all(jnp.broadcast_to(value[None], (parts,) + value.shape), axe...]
    all_to_all x1, blocking collectives: 23.5 us -> 14.4 us  [on_device(): got = lax.all_to_all(gram, 'x', 0, 0, tiled=True)]
    ppermute x4 -> x5, starting transfers between devices: 16.5 us -> 22.1 us  [flip(): return lax.ppermute(value, axis, [(i, i ^ step) for i in range(n)])]
    ppermute x4 -> x5, waiting for transfers between devices: 4.36 us -> 9.38 us  [flip(): return lax.ppermute(value, axis, [(i, i ^ step) for i in range(n)])]
    all_gather x1, blocking collectives: 7.9 us -> 12 us  [on_device(): own = lax.all_gather(weight, 'zh', axis=0, tiled=True)]
    all_to_all x1, starting transfers between devices: 4.74 us -> 7.4 us  [on_device(): got_a = lax.all_to_all(grad_a, 'y', 0, 0, tiled=True)]
    pallas_call x10 -> x11, Pallas kernels: 27.4 us -> 29.7 us  [call(): pl.pallas_call(body, name=name, out_shape=[jax.ShapeDtypeStruct(s, d) for...]
    unnamed x30 -> x32, local copies, waits for them, and re-layouts: 4.31 us -> 5 us
  transfers between devices with their start and end apart: 12 -> 13, of which waited for: 6 -> 7; matrix products, arithmetic and copies ran while one was open for 2% -> 2% of each run, Pallas kernels for 4% -> 5%
where the time goes in v9:
time: 227 us; the launch traced here: 226 us
  blocking collectives  97.8 us (43%)
  starting transfers between devices  62 us (27%)
  Pallas kernels  29.7 us (13%)
  waiting for transfers between devices  24.6 us (11%)
  local copies, waits for them, and re-layouts  8.87 us (4%)
    all_to_all x2, blocking collectives, spread(): lax.all_to_all(jnp.broadcast_to(value[None], (parts,) + value.shape), axe...  31.4 us
    pallas_call x11, Pallas kernels, call(): pl.pallas_call(body, name=name, out_shape=[jax.ShapeDtypeStruct(s, d) for...  29.7 us
    all_gather x1, blocking collectives, on_device(): big_b = lax.all_gather(own_b, TILE, axis=0)  22.2 us
    ppermute x5, starting transfers between devices, flip(): return lax.ppermute(value, axis, [(i, i ^ step) for i in range(n)])  22.1 us
    all_to_all x1, blocking collectives, on_device(): got = lax.all_to_all(share, TILE, 0, 0, tiled=True)  17.9 us
    all_to_all x1, blocking collectives, on_device(): got = lax.all_to_all(gram, 'x', 0, 0, tiled=True)  14.4 us
    ppermute x4, starting transfers between devices, shift(): return lax.ppermute(value, axis, [(i, (i + step) % n) for i in range(n)])  13.5 us
    all_gather x1, blocking collectives, on_device(): own = lax.all_gather(weight, 'zh', axis=0, tiled=True)  12 us
  transfers between devices with their start and end apart: 13, of which 7 were waited for; matrix products, arithmetic and copies ran while one was open for 2% of the time, Pallas kernels for 5%

profile of v9, /device:TPU:1, one launch (start us, length us, event | category | flops | bytes accessed | tf_op | source)
XLA Modules:
  0.0 226.1 jit_solution(11513281786906002083)
XLA Ops:
  0.7 12.0 %all_gather.9 = bf16[64,512]{1,0:T(8,128)(2,1)S(1)} all-gather(bf16[32,512]{1,0:T(8,128)(2,1)} %param.7), channel_id=1, replica_groups=mesh['zh'=2,'x'=4,'y'=8,'zl'=4,'c'=2] {'zh'}, dimensions={0}, use_global_device_ids=true | all-gather | bytes 98304 | tf_op jit(solution)/shard_map/all_gather | solution.py:379
  12.7 21.4 %all_to_all.30 = bf16[8,64,512]{2,1,0:T(8,128)(2,1)S(1)} all-to-all(bf16[8,64,512]{2,1,0:T(8,128)(2,1)S(1)} %broadcast_in_dim.4), channel_id=1, replica_groups=mesh['zh'=2,'x'=4,'y'=8,'zl'=4,'c'=2] {'y'}, dimensions={0} | all-to-all | bytes 1048576 | tf_op jit(solution)/shard_map/all_to_all | solution.py:38
  34.0 4.4 %collective-permute-start.1 = (bf16[8,2,32,512]{3,2,1,0:T(8,128)(2,1)S(1)}, bf16[8,2,32,512]{3,2,1,0:T(8,128)(2,1)S(1)}, u32[]{:S(2)}, u32[]{:S(2)}) collective-permute-start(bf16[8,2,32,512]{3,2,1,0:T(8,128)(2,1)S(1)} %bitcast.18), channel_id=1, source_target_pairs={{0,192},{64,0},{128,64},{192,128},{1,193},{65,1},{129,65},{193,129... | collective-permute-start | bytes 1572872 | tf_op jit(solution)/shard_map/ppermute | solution.py:45
  38.4 1.9 collective-permute-start
  40.4 0.8 slice_bitcast_fusion.2
  41.1 4.8 %collective-permute-done.1.ahead = bf16[8,2,32,512]{3,2,1,0:T(8,128)(2,1)S(1)} collective-permute-done((bf16[8,2,32,512]{3,2,1,0:T(8,128)(2,1)S(1)}, bf16[8,2,32,512]{3,2,1,0:T(8,128)(2,1)S(1)}, u32[]{:S(2)}, u32[]{:S(2)}) %collective-permute-start.1) | collective-permute-done | bytes 524320 | tf_op jit(solution)/shard_map/ppermute | solution.py:45
  45.9 5.3 %collective-permute-start.3 = (bf16[4,2,32,512]{3,2,1,0:T(8,128)(2,1)S(1)}, bf16[4,2,32,512]{3,2,1,0:T(8,128)(2,1)S(1)}, u32[]{:S(2)}, u32[]{:S(2)}) collective-permute-start(bf16[4,2,32,512]{3,2,1,0:T(8,128)(2,1)S(1)} %slice.21), channel_id=1, source_target_pairs={{0,192},{64,0},{128,64},{192,128},{1,193},{65,1},{129,65},{193,129... | collective-permute-start | bytes 786440 | tf_op jit(solution)/shard_map/ppermute | solution.py:45
  51.3 1.9 collective-permute-start.2
  54.2 0.8 pad_maximum_fusion.view
  55.0 4.6 %collective-permute-done.2.far_low = bf16[4,2,32,512]{3,2,1,0:T(8,128)(2,1)S(1)} collective-permute-done((bf16[4,2,32,512]{3,2,1,0:T(8,128)(2,1)S(1)}, bf16[4,2,32,512]{3,2,1,0:T(8,128)(2,1)S(1)}, u32[]{:S(2)}, u32[]{:S(2)}) %collective-permute-start.2) | collective-permute-done | bytes 262176 | tf_op jit(solution)/shard_map/ppermute | solution.py:45
  59.7 0.7 copy-done.10
  60.4 3.5 %project.1 = (bf16[2,4,8,32,512]{4,3,2,1,0:T(8,128)(2,1)}, bf16[8,64,512]{2,1,0:T(8,128)(2,1)}, bf16[64,512]{1,0:T(8,128)(2,1)}) custom-call(s32[6]{0:T(128)} %stack.27.at.refs_0_, bf16[128,2048]{1,0:T(8,128)(2,1)} %pad_maximum_fusion.view, bf16[8,2,32,512]{3,2,1,0:T(8,128)(2,1)} %bitcast.20, bf16[8,2,32,512]{3,2,1,0:T(8,128)(2,1)} %copy-done.4, ...), custom_call_target="tpu_custom_call" | custom-call | tf_op jit(solution)/shard_map/project/pallas_call | solution.py:92
  63.8 5.7 %all-to-all-start.1 = ((bf16[8,64,512]{2,1,0:T(8,128)(2,1)}), bf16[8,64,512]{2,1,0:T(8,128)(2,1)S(1)}, u32[]{:S(2)}, u32[]{:S(2)}) async-start(bf16[8,64,512]{2,1,0:T(8,128)(2,1)} %get-tuple-element.19), calls=%async_computation.1 | async-start | bytes 1048576 | tf_op jit(solution)/shard_map/all_to_all | solution.py:394
  69.5 7.7 %collective-permute-start.4 = (bf16[64,512]{1,0:T(8,128)(2,1)}, bf16[64,512]{1,0:T(8,128)(2,1)S(1)}, u32[]{:S(2)}, u32[]{:S(2)}) collective-permute-start(bf16[64,512]{1,0:T(8,128)(2,1)} %get-tuple-element.20), channel_id=1, source_target_pairs={{0,0},{1,8},{2,16},{3,24},{4,32},{5,40},{6,48},{7,56},{8,1},{9,9},... | collective-permute-start | bytes 196616 | tf_op jit(solution)/shard_map/ppermute | solution.py:395
  77.2 5.7 %collective-permute-done.4.raw_b = bf16[64,512]{1,0:T(8,128)(2,1)S(1)} collective-permute-done((bf16[64,512]{1,0:T(8,128)(2,1)}, bf16[64,512]{1,0:T(8,128)(2,1)S(1)}, u32[]{:S(2)}, u32[]{:S(2)}) %collective-permute-start.4) | collective-permute-done | bytes 65568 | tf_op jit(solution)/shard_map/ppermute | solution.py:395
  82.9 22.2 %all-gather = bf16[512,512]{1,0:T(8,128)(2,1)} all-gather(bf16[64,512]{1,0:T(8,128)(2,1)S(1)} %collective-permute-done.4.raw_b), channel_id=2, replica_groups=mesh['zh'=2,'x'=4,'y'=8,'zl'=4,'c'=2] {'zl','c'}, dimensions={0}, use_global_device_ids=true | all-gather | bytes 589824 | tf_op jit(solution)/shard_map/all_gather | solution.py:396
  105.1 0.8 copy-done
  105.9 3.0 %gram.1 = bf16[4,144,512]{2,1,0:T(8,128)(2,1)} custom-call(bf16[8,64,512]{2,1,0:T(8,128)(2,1)} %copy-done, bf16[8,64,512]{2,1,0:T(8,128)(2,1)} %bitcast.16), custom_call_target="tpu_custom_call" | custom-call | tf_op jit(solution)/shard_map/gram/pallas_call | solution.py:92
  108.9 14.4 %all_to_all.31.got = bf16[4,144,512]{2,1,0:T(8,128)(2,1)} all-to-all(bf16[4,144,512]{2,1,0:T(8,128)(2,1)} %gram.1), channel_id=1, replica_groups=mesh['zh'=2,'x'=4,'y'=8,'zl'=4,'c'=2] {'x'}, dimensions={0} | all-to-all | bytes 1179648 | tf_op jit(solution)/shard_map/all_to_all | solution.py:401
  123.3 1.8 merge.1.refs_1_
  125.1 7.0 %collective-permute-start.5 = (bf16[192,512]{1,0:T(8,128)(2,1)}, bf16[192,512]{1,0:T(8,128)(2,1)S(1)}, u32[]{:S(2)}, u32[]{:S(2)}) collective-permute-start(bf16[192,512]{1,0:T(8,128)(2,1)} %merge.1.refs_1_), channel_id=1, source_target_pairs={{0,256},{256,0},{1,257},{257,1},{2,258},{258,2},{3,259},{259,3},{4... | collective-permute-start | bytes 589832 | tf_op jit(solution)/shard_map/ppermute | solution.py:50
  132.1 4.4 %collective-permute-done.5.refs_2_ = bf16[192,512]{1,0:T(8,128)(2,1)S(1)} collective-permute-done((bf16[192,512]{1,0:T(8,128)(2,1)}, bf16[192,512]{1,0:T(8,128)(2,1)S(1)}, u32[]{:S(2)}, u32[]{:S(2)}) %collective-permute-start.5) | collective-permute-done | bytes 196640 | tf_op jit(solution)/shard_map/ppermute | solution.py:50
  136.5 0.7 copy-done.11
  137.2 2.9 %mix.1 = (bf16[128,512]{1,0:T(8,128)(2,1)}, f32[8,512]{1,0:T(8,128)}) custom-call(s32[6]{0:T(128)} %stack.27.at.refs_0_, bf16[192,512]{1,0:T(8,128)(2,1)} %merge.1.refs_1_, bf16[192,512]{1,0:T(8,128)(2,1)} %copy-done.11), custom_call_target="tpu_custom_call" | custom-call | tf_op jit(solution)/shard_map/mix/pallas_call | solution.py:92
  140.1 0.9 broadcast_in_dim.5
  141.0 10.0 %all_to_all.32.mix4 = bf16[4,128,512]{2,1,0:T(8,128)(2,1)} all-to-all(bf16[4,128,512]{2,1,0:T(8,128)(2,1)S(1)} %broadcast_in_dim.5), channel_id=1, replica_groups=mesh['zh'=2,'x'=4,'y'=8,'zl'=4,'c'=2] {'x'}, dimensions={0} | all-to-all | bytes 1048576 | tf_op jit(solution)/shard_map/all_to_all | solution.py:38
  151.1 3.3 %grad_a.1 = bf16[8,72,512]{2,1,0:T(8,128)(2,1)} custom-call(s32[6]{0:T(128)} %stack.27.at.refs_0_, bf16[4,128,512]{2,1,0:T(8,128)(2,1)} %all_to_all.32.mix4, bf16[8,64,512]{2,1,0:T(8,128)(2,1)} %bitcast.17, f32[8,512]{1,0:T(8,128)} %get-tuple-element.22.stats), custom_call_target="tpu_custom_call" | custom-call | tf_op jit(solution)/shard_map/grad_a/pallas_call | solution.py:92
  154.4 7.4 %all-to-all-start.4 = ((bf16[8,72,512]{2,1,0:T(8,128)(2,1)}), bf16[8,72,512]{2,1,0:T(8,128)(2,1)S(1)}, u32[]{:S(2)}, u32[]{:S(2)}) async-start(bf16[8,72,512]{2,1,0:T(8,128)(2,1)} %grad_a.1), calls=%async_computation.4 | async-start | bytes 1179648 | tf_op jit(solution)/shard_map/all_to_all | solution.py:424
  161.8 3.0 %grad_b.1 = (bf16[264,512]{1,0:T(8,128)(2,1)}, f32[264,512]{1,0:T(8,128)}) custom-call(s32[6]{0:T(128)} %stack.27.at.refs_0_, bf16[4,128,512]{2,1,0:T(8,128)(2,1)} %all_to_all.32.mix4, bf16[8,64,512]{2,1,0:T(8,128)(2,1)} %copy-done, f32[8,512]{1,0:T(8,128)} %get-tuple-element.22.stats), custom_call_target="tpu_custom_call" | custom-call | tf_op jit(solution)/shard_map/grad_b/pallas_call | solution.py:92
  164.8 5.7 %collective-permute-start.6 = (bf16[264,512]{1,0:T(8,128)(2,1)}, bf16[264,512]{1,0:T(8,128)(2,1)S(1)}, u32[]{:S(2)}, u32[]{:S(2)}) collective-permute-start(bf16[264,512]{1,0:T(8,128)(2,1)} %get-tuple-element.26), channel_id=1, source_target_pairs={{0,1},{1,0},{2,3},{3,2},{4,5},{5,4},{6,7},{7,6},{8,9},{9,8},{10,11... | collective-permute-start | bytes 811016 | tf_op jit(solution)/shard_map/ppermute | solution.py:50
  170.4 1.4 collective-permute-done.6.got
  171.8 0.7 copy-done.5
  172.5 2.0 core.1
  174.5 3.0 %collective-permute-start.7 = (bf16[72,512]{1,0:T(8,128)(2,1)}, bf16[72,512]{1,0:T(8,128)(2,1)S(1)}, u32[]{:S(2)}, u32[]{:S(2)}) collective-permute-start(bf16[72,512]{1,0:T(8,128)(2,1)} %get-tuple-element.28), channel_id=1, source_target_pairs={{0,2},{2,0},{4,6},{6,4},{1,3},{3,1},{5,7},{7,5},{8,10},{10,8},{12,... | collective-permute-start | bytes 221192 | tf_op jit(solution)/shard_map/ppermute | solution.py:50
  177.5 4.0 %collective-permute-start.8 = (bf16[72,512]{1,0:T(8,128)(2,1)}, bf16[72,512]{1,0:T(8,128)(2,1)S(1)}, u32[]{:S(2)}, u32[]{:S(2)}) collective-permute-start(bf16[72,512]{1,0:T(8,128)(2,1)} %get-tuple-element.29), channel_id=1, source_target_pairs={{0,4},{2,6},{4,0},{6,2},{1,5},{3,7},{5,1},{7,3},{8,12},{10,14},{12... | collective-permute-start | bytes 221192 | tf_op jit(solution)/shard_map/ppermute | solution.py:50
  181.5 2.4 %collective-permute-start.9 = (bf16[72,512]{1,0:T(8,128)(2,1)}, bf16[72,512]{1,0:T(8,128)(2,1)S(1)}, u32[]{:S(2)}, u32[]{:S(2)}) collective-permute-start(bf16[72,512]{1,0:T(8,128)(2,1)} %get-tuple-element.30), channel_id=1, source_target_pairs={{0,6},{2,4},{4,2},{6,0},{1,7},{3,5},{5,3},{7,1},{8,14},{10,12},{12... | collective-permute-start | bytes 221192 | tf_op jit(solution)/shard_map/ppermute | solution.py:50
  183.9 1.1 compare_convert_fusion
  185.0 1.0 collective-permute-done.8.got2
  186.0 2.6 %collective-permute-done.9.got3 = bf16[72,512]{1,0:T(8,128)(2,1)S(1)} collective-permute-done((bf16[72,512]{1,0:T(8,128)(2,1)}, bf16[72,512]{1,0:T(8,128)(2,1)S(1)}, u32[]{:S(2)}, u32[]{:S(2)}) %collective-permute-start.9) | collective-permute-done | bytes 73760 | tf_op jit(solution)/shard_map/ppermute | solution.py:50
  188.7 0.6 copy-done.14
  189.3 1.7 dz_b.1
  191.0 5.6 %collective-permute-start.10 = (bf16[64,512]{1,0:T(8,128)(2,1)}, bf16[64,512]{1,0:T(8,128)(2,1)S(1)}, u32[]{:S(2)}, u32[]{:S(2)}) collective-permute-start(bf16[64,512]{1,0:T(8,128)(2,1)} %dz_b.1), channel_id=1, source_target_pairs={{0,0},{1,8},{2,16},{3,24},{4,32},{5,40},{6,48},{7,56},{8,1},{9,9},... | collective-permute-start | bytes 196616 | tf_op jit(solution)/shard_map/ppermute | solution.py:434
  196.7 1.5 slice_bitcast_fusion.raw_a
  198.1 0.8 copy-done.1
  199.0 3.5 %back_a.1 = (f32[64,2048]{1,0:T(8,128)}, f32[1,512]{1,0:T(1,128)}, f32[1,256]{1,0:T(1,128)}) custom-call(bf16[8,72,512]{2,1,0:T(8,128)(2,1)} %copy-done.1, bf16[64,512]{1,0:T(8,128)(2,1)} %slice_bitcast_fusion.raw_a, f32[8,512]{1,0:T(8,128)} %get-tuple-element.22.stats, f32[64,2048]{1,0:T(8,128)} %get-tuple-element.38.keep, ...), custom_call_target="tpu_custom_call" | custom-call | tf_op jit(solution)/shard_map/back_a/pallas_call | solution.py:92
  203.2 3.4 %back_b.1 = bf16[8,72,256]{2,1,0:T(8,128)(2,1)} custom-call(f32[64,2048]{1,0:T(8,128)} %get-tuple-element.24.part, bf16[64,512]{1,0:T(8,128)(2,1)} %copy-done.15, f32[64,2048]{1,0:T(8,128)} %get-tuple-element.37.keep, bf16[2,4,8,32,512]{4,3,2,1,0:T(8,128)(2,1)} %get-tuple-element.23.weight, f32[1,256]{1,0:T(1,128)} %get-tuple-element.31.power), custom_call_target="tpu_custom_call" | custom-call | tf_op jit(solution)/shard_map/back_b/pallas_call | solution.py:92
  206.5 17.9 %all_to_all.33.refs_0_ = bf16[8,72,256]{2,1,0:T(8,128)(2,1)} all-to-all(bf16[8,72,256]{2,1,0:T(8,128)(2,1)} %back_b.1), channel_id=1, replica_groups=mesh['zh'=2,'x'=4,'y'=8,'zl'=4,'c'=2] {'zl','c'}, dimensions={0} | all-to-all | bytes 589824 | tf_op jit(solution)/shard_map/all_to_all | solution.py:448
  224.4 1.6 end.1
  (38 shorter events, 1.6 us)
Async XLA Ops:
  0.6 52.6 %copy-start.7 = (bf16[64,2048]{1,0:T(8,128)(2,1)S(1)}, bf16[64,2048]{1,0:T(8,128)(2,1)}, u32[]{:S(2)}) copy-start(bf16[64,2048]{1,0:T(8,128)(2,1)} %param.5) | copy-start | bytes 786436
  0.6 52.6 %copy-start.6 = (bf16[64,2048]{1,0:T(8,128)(2,1)S(1)}, bf16[64,2048]{1,0:T(8,128)(2,1)}, u32[]{:S(2)}) copy-start(bf16[64,2048]{1,0:T(8,128)(2,1)} %param.4) | copy-start | bytes 786436
  34.0 25.6 %copy-start.2 = (bf16[8,64,512]{2,1,0:T(8,128)(2,1)}, bf16[8,64,512]{2,1,0:T(8,128)(2,1)S(1)}, u32[]{:S(2)}) copy-start(bf16[8,64,512]{2,1,0:T(8,128)(2,1)S(1)} %all_to_all.30) | copy-start | bytes 1572868
  34.0 11.9 %collective-permute-start.1 = (bf16[8,2,32,512]{3,2,1,0:T(8,128)(2,1)S(1)}, bf16[8,2,32,512]{3,2,1,0:T(8,128)(2,1)S(1)}, u32[]{:S(2)}, u32[]{:S(2)}) collective-permute-start(bf16[8,2,32,512]{3,2,1,0:T(8,128)(2,1)S(1)} %bitcast.18), channel_id=1, source_target_pairs={{0,192},{64,0},{128,64},{192,128},{1,193},{65,1},{129,65},{193,129... | collective-permute-start | bytes 1572872 | tf_op jit(solution)/shard_map/ppermute | solution.py:45
  38.4 12.9 %collective-permute-start = (bf16[8,2,32,512]{3,2,1,0:T(8,128)(2,1)S(1)}, bf16[8,2,32,512]{3,2,1,0:T(8,128)(2,1)S(1)}, u32[]{:S(2)}, u32[]{:S(2)}) collective-permute-start(bf16[8,2,32,512]{3,2,1,0:T(8,128)(2,1)S(1)} %bitcast.19), channel_id=1, source_target_pairs={{0,64},{64,128},{128,192},{192,0},{1,65},{65,129},{129,193},{193,1... | collective-permute-start | bytes 1572872 | tf_op jit(solution)/shard_map/ppermute | solution.py:45
  45.9 13.7 %copy-start.3 = (bf16[8,2,32,512]{3,2,1,0:T(8,128)(2,1)}, bf16[8,2,32,512]{3,2,1,0:T(8,128)(2,1)S(1)}, u32[]{:S(2)}) copy-start(bf16[8,2,32,512]{3,2,1,0:T(8,128)(2,1)S(1)} %collective-permute-done.1.ahead) | copy-start | bytes 1572868
  45.9 9.1 %collective-permute-start.3 = (bf16[4,2,32,512]{3,2,1,0:T(8,128)(2,1)S(1)}, bf16[4,2,32,512]{3,2,1,0:T(8,128)(2,1)S(1)}, u32[]{:S(2)}, u32[]{:S(2)}) collective-permute-start(bf16[4,2,32,512]{3,2,1,0:T(8,128)(2,1)S(1)} %slice.21), channel_id=1, source_target_pairs={{0,192},{64,0},{128,64},{192,128},{1,193},{65,1},{129,65},{193,129... | collective-permute-start | bytes 786440 | tf_op jit(solution)/shard_map/ppermute | solution.py:45
  51.3 8.4 %copy-start.4 = (bf16[8,2,32,512]{3,2,1,0:T(8,128)(2,1)}, bf16[8,2,32,512]{3,2,1,0:T(8,128)(2,1)S(1)}, u32[]{:S(2)}) copy-start(bf16[8,2,32,512]{3,2,1,0:T(8,128)(2,1)S(1)} %collective-permute-done.back) | copy-start | bytes 1572868
  51.3 8.3 %collective-permute-start.2 = (bf16[4,2,32,512]{3,2,1,0:T(8,128)(2,1)S(1)}, bf16[4,2,32,512]{3,2,1,0:T(8,128)(2,1)S(1)}, u32[]{:S(2)}, u32[]{:S(2)}) collective-permute-start(bf16[4,2,32,512]{3,2,1,0:T(8,128)(2,1)S(1)} %slice.20), channel_id=1, source_target_pairs={{0,64},{64,128},{128,192},{192,0},{1,65},{65,129},{129,193},{193,1... | collective-permute-start | bytes 786440 | tf_op jit(solution)/shard_map/ppermute | solution.py:45
  55.0 4.7 %copy-start.9 = (bf16[4,2,32,512]{3,2,1,0:T(8,128)(2,1)}, bf16[4,2,32,512]{3,2,1,0:T(8,128)(2,1)S(1)}, u32[]{:S(2)}) copy-start(bf16[4,2,32,512]{3,2,1,0:T(8,128)(2,1)S(1)} %collective-permute-done.3.far_high) | copy-start | bytes 786436
  59.7 0.7 copy-start.10
  63.8 41.3 %all-to-all-start.1 = ((bf16[8,64,512]{2,1,0:T(8,128)(2,1)}), bf16[8,64,512]{2,1,0:T(8,128)(2,1)S(1)}, u32[]{:S(2)}, u32[]{:S(2)}) async-start(bf16[8,64,512]{2,1,0:T(8,128)(2,1)} %get-tuple-element.19), calls=%async_computation.1 | async-start | bytes 1048576 | tf_op jit(solution)/shard_map/all_to_all | solution.py:394
  69.5 13.4 %collective-permute-start.4 = (bf16[64,512]{1,0:T(8,128)(2,1)}, bf16[64,512]{1,0:T(8,128)(2,1)S(1)}, u32[]{:S(2)}, u32[]{:S(2)}) collective-permute-start(bf16[64,512]{1,0:T(8,128)(2,1)} %get-tuple-element.20), channel_id=1, source_target_pairs={{0,0},{1,8},{2,16},{3,24},{4,32},{5,40},{6,48},{7,56},{8,1},{9,9},... | collective-permute-start | bytes 196616 | tf_op jit(solution)/shard_map/ppermute | solution.py:395
  82.9 42.2 %copy-start.8 = (bf16[64,512]{1,0:T(8,128)(2,1)}, bf16[64,512]{1,0:T(8,128)(2,1)S(1)}, u32[]{:S(2)}) copy-start(bf16[64,512]{1,0:T(8,128)(2,1)S(1)} %collective-permute-done.4.raw_b) | copy-start | bytes 196612
  105.1 0.8 copy-start
  125.1 11.4 %collective-permute-start.5 = (bf16[192,512]{1,0:T(8,128)(2,1)}, bf16[192,512]{1,0:T(8,128)(2,1)S(1)}, u32[]{:S(2)}, u32[]{:S(2)}) collective-permute-start(bf16[192,512]{1,0:T(8,128)(2,1)} %merge.1.refs_1_), channel_id=1, source_target_pairs={{0,256},{256,0},{1,257},{257,1},{2,258},{258,2},{3,259},{259,3},{4... | collective-permute-start | bytes 589832 | tf_op jit(solution)/shard_map/ppermute | solution.py:50
  136.5 0.7 copy-start.11
  154.4 43.8 %all-to-all-start.4 = ((bf16[8,72,512]{2,1,0:T(8,128)(2,1)}), bf16[8,72,512]{2,1,0:T(8,128)(2,1)S(1)}, u32[]{:S(2)}, u32[]{:S(2)}) async-start(bf16[8,72,512]{2,1,0:T(8,128)(2,1)} %grad_a.1), calls=%async_computation.4 | async-start | bytes 1179648 | tf_op jit(solution)/shard_map/all_to_all | solution.py:424
  164.8 7.0 %collective-permute-start.6 = (bf16[264,512]{1,0:T(8,128)(2,1)}, bf16[264,512]{1,0:T(8,128)(2,1)S(1)}, u32[]{:S(2)}, u32[]{:S(2)}) collective-permute-start(bf16[264,512]{1,0:T(8,128)(2,1)} %get-tuple-element.26), channel_id=1, source_target_pairs={{0,1},{1,0},{2,3},{3,2},{4,5},{5,4},{6,7},{7,6},{8,9},{9,8},{10,11... | collective-permute-start | bytes 811016 | tf_op jit(solution)/shard_map/ppermute | solution.py:50
  171.8 0.7 copy-start.5
  174.5 10.5 %collective-permute-start.7 = (bf16[72,512]{1,0:T(8,128)(2,1)}, bf16[72,512]{1,0:T(8,128)(2,1)S(1)}, u32[]{:S(2)}, u32[]{:S(2)}) collective-permute-start(bf16[72,512]{1,0:T(8,128)(2,1)} %get-tuple-element.28), channel_id=1, source_target_pairs={{0,2},{2,0},{4,6},{6,4},{1,3},{3,1},{5,7},{7,5},{8,10},{10,8},{12,... | collective-permute-start | bytes 221192 | tf_op jit(solution)/shard_map/ppermute | solution.py:50
  177.5 8.5 %collective-permute-start.8 = (bf16[72,512]{1,0:T(8,128)(2,1)}, bf16[72,512]{1,0:T(8,128)(2,1)S(1)}, u32[]{:S(2)}, u32[]{:S(2)}) collective-permute-start(bf16[72,512]{1,0:T(8,128)(2,1)} %get-tuple-element.29), channel_id=1, source_target_pairs={{0,4},{2,6},{4,0},{6,2},{1,5},{3,7},{5,1},{7,3},{8,12},{10,14},{12... | collective-permute-start | bytes 221192 | tf_op jit(solution)/shard_map/ppermute | solution.py:50
  181.5 7.2 %collective-permute-start.9 = (bf16[72,512]{1,0:T(8,128)(2,1)}, bf16[72,512]{1,0:T(8,128)(2,1)S(1)}, u32[]{:S(2)}, u32[]{:S(2)}) collective-permute-start(bf16[72,512]{1,0:T(8,128)(2,1)} %get-tuple-element.30), channel_id=1, source_target_pairs={{0,6},{2,4},{4,2},{6,0},{1,7},{3,5},{5,3},{7,1},{8,14},{10,12},{12... | collective-permute-start | bytes 221192 | tf_op jit(solution)/shard_map/ppermute | solution.py:50
  185.0 3.6 %copy-start.12 = (bf16[72,512]{1,0:T(8,128)(2,1)}, bf16[72,512]{1,0:T(8,128)(2,1)S(1)}, u32[]{:S(2)}) copy-start(bf16[72,512]{1,0:T(8,128)(2,1)S(1)} %collective-permute-done.7.got1) | copy-start | bytes 221188
  186.0 2.6 %copy-start.13 = (bf16[72,512]{1,0:T(8,128)(2,1)}, bf16[72,512]{1,0:T(8,128)(2,1)S(1)}, u32[]{:S(2)}) copy-start(bf16[72,512]{1,0:T(8,128)(2,1)S(1)} %collective-permute-done.8.got2) | copy-start | bytes 221188
  188.6 0.6 copy-start.14
  191.0 11.5 %collective-permute-start.10 = (bf16[64,512]{1,0:T(8,128)(2,1)}, bf16[64,512]{1,0:T(8,128)(2,1)S(1)}, u32[]{:S(2)}, u32[]{:S(2)}) collective-permute-start(bf16[64,512]{1,0:T(8,128)(2,1)} %dz_b.1), channel_id=1, source_target_pairs={{0,0},{1,8},{2,16},{3,24},{4,32},{5,40},{6,48},{7,56},{8,1},{9,9},... | collective-permute-start | bytes 196616 | tf_op jit(solution)/shard_map/ppermute | solution.py:434
  198.1 0.8 copy-start.1
  202.5 0.6 copy-start.15

commit v10 on v9

--- a/solution.py
+++ b/solution.py
@@ -102,7 +102,7 @@
     )(*args)
 
 
-def project_body(at, view, own, back, ahead, far_low, far_high, piece, wide_a, raw_b):
+def project_b_body(at, view, own, back, ahead, far_low, far_high, piece, raw_b):
     zh_n, x_n, y_n, rows, kt = piece.shape
     x = at[0]
     half = y_n // 2
@@ -114,11 +114,15 @@
         piece[zh, far, :half] = far_low[:, zh]
         piece[zh, far, half:] = far_high[:, zh]
     weight = piece[...].reshape(zh_n * x_n * y_n * rows, kt)
-    raw = dot(view[...], weight, 1, 0).astype(BF)
-    n = raw_b.shape[0]
+    raw_b[...] = dot(view[raw_b.shape[0] :], weight, 1, 0).astype(BF)
+
+
+def project_a_body(view, weight, wide_a, raw_a):
+    n, kt = raw_a.shape
+    raw = dot(view[:n], weight[...].reshape(view.shape[1], kt), 1, 0).astype(BF)
+    raw_a[...] = raw
     for i in range(wide_a.shape[0]):
-        wide_a[i] = raw[:n]
-    raw_b[...] = raw[n:]
+        wide_a[i] = raw
 
 
 def gram_body(big_a, big_b, out, tail):
@@ -220,7 +224,7 @@
     return jnp.where(k_of + at[4] == l_of, stats[4:5, :], mix * (0.5 / LAMBDA_OFF))
 
 
-def grad_b_body(at, mix4, big_a, stats, sent, kept, grads, tail):
+def grad_b_body(at, mix4, big_a, stats, sent, kept, stats_out, grads, tail):
     c = at[2]
     parts, rows, kt = big_a.shape
     line = parts // 2
@@ -231,6 +235,7 @@
     for z in range(line):
         sent[z * rows : (z + 1) * rows] = grads[z * 2 + (1 - c)].astype(BF)
         kept[z * rows : (z + 1) * rows] = grads[z * 2 + c]
+    stats_out[...] = stats[...]
     second = jnp.sum(wide * correlation(at, wide, stats), axis=0, keepdims=True)
     first = sum(dot(p, mix, 1, 0) for p in thirds(stats[...]))[5:6]
     tail[...] = jnp.zeros_like(tail)
@@ -383,16 +388,22 @@
     ahead = shift(own, "x", x_n - 1)
     far_low = shift(back[:half], "x", 1)
     far_high = shift(ahead[half:], "x", x_n - 1)
-    piece, wide_a, raw_b = call(
-        project_body,
-        "project",
-        [((zh_n, x_n, y_n, w_rows, kt), BF), ((y_n, rows, kt), BF), ((rows, kt), BF)],
+    piece, raw_b = call(
+        project_b_body,
+        "project_b",
+        [((zh_n, x_n, y_n, w_rows, kt), BF), ((rows, kt), BF)],
         (at, view, own, back, ahead, far_low, far_high),
     )
 
-    raw_a = wide_a[0]
+    own_b = lax.ppermute(raw_b, every, pairs)
+    wide_a, raw_a = call(
+        project_a_body,
+        "project_a",
+        [((y_n, rows, kt), BF), ((rows, kt), BF)],
+        (view, piece),
+    )
+    own_b, wide_a = lax.optimization_barrier((own_b, wide_a))
     big_a = lax.all_to_all(wide_a, "y", 0, 0, tiled=True)
-    own_b = lax.ppermute(raw_b, every, pairs)
     big_b = lax.all_gather(own_b, TILE, axis=0)
     (gram,) = call(
         gram_body, "gram", [((x_n, sub + 16, kt), BF)], (big_a, big_b), [((16, kt), F32)]
@@ -410,17 +421,18 @@
     mix = spread(mix, "x")
 
     line_rows = zl_n * rows + 8
-    sent, kept = call(
+    sent, kept, stats_a = call(
         grad_b_body,
         "grad_b",
-        [((line_rows, kt), BF), ((line_rows, kt), F32)],
+        [((line_rows, kt), BF), ((line_rows, kt), F32), ((8, kt), F32)],
         (at, mix, big_a, stats),
         [((tile_n, rows, kt), F32), ((8, kt), F32)],
     )
     got_b = flip(sent, "c", 1)
     (grad_a,) = call(
-        grad_a_body, "grad_a", [((y_n, rows + 8, kt), BF)], (at, mix, big_b, stats), [((8, kt), F32)]
-    )
+        grad_a_body, "grad_a", [((y_n, rows + 8, kt), BF)], (at, mix, big_b, stats_a), [((8, kt), F32)]
+    )
+    got_b, grad_a = lax.optimization_barrier((got_b, grad_a))
     got_a = lax.all_to_all(grad_a, "y", 0, 0, tiled=True)
     own, *outs = call(
         core_body,

time: 227 us -> 221 us (0.974)
  waiting for transfers between devices: 24.6 us -> 17.8 us
  blocking collectives: 97.8 us -> 94.5 us
  starting transfers between devices: 62 us -> 65.1 us
  Pallas kernels: 29.7 us -> 32.5 us
    ppermute x1, waiting for transfers between devices: 5.72 us -> 0.01 us  [on_device(): own_b = lax.ppermute(raw_b, every, pairs)]
    all_gather x1, blocking collectives: 22.2 us -> 18.8 us  [on_device(): big_b = lax.all_gather(own_b, TILE, axis=0)]
    pallas_call x11 -> x12, Pallas kernels: 29.7 us -> 32.5 us  [call(): pl.pallas_call(body, name=name, out_shape=[jax.ShapeDtypeStruct(s, d) for...]
  transfers between devices with their start and end apart: 13 -> 13, of which waited for: 7 -> 5; matrix products, arithmetic and copies ran while one was open for 2% -> 2% of each run, Pallas kernels for 5% -> 6%
where the time goes in v10:
time: 221 us; the launch traced here: 220 us
  blocking collectives  94.5 us (43%)
  starting transfers between devices  65.1 us (29%)
  Pallas kernels  32.5 us (15%)
  waiting for transfers between devices  17.8 us (8%)
  local copies, waits for them, and re-layouts  6.66 us (3%)
    pallas_call x12, Pallas kernels, call(): pl.pallas_call(body, name=name, out_shape=[jax.ShapeDtypeStruct(s, d) for...  32.5 us
    all_to_all x2, blocking collectives, spread(): lax.all_to_all(jnp.broadcast_to(value[None], (parts,) + value.shape), axe...  31.4 us
    ppermute x5, starting transfers between devices, flip(): return lax.ppermute(value, axis, [(i, i ^ step) for i in range(n)])  23.6 us
    all_gather x1, blocking collectives, on_device(): big_b = lax.all_gather(own_b, TILE, axis=0)  18.8 us
    all_to_all x1, blocking collectives, on_device(): got = lax.all_to_all(share, TILE, 0, 0, tiled=True)  17.9 us
    all_to_all x1, blocking collectives, on_device(): got = lax.all_to_all(gram, 'x', 0, 0, tiled=True)  14.4 us
    ppermute x4, starting transfers between devices, shift(): return lax.ppermute(value, axis, [(i, (i + step) % n) for i in range(n)])  13.5 us
    all_gather x1, blocking collectives, on_device(): own = lax.all_gather(weight, 'zh', axis=0, tiled=True)  12 us
  transfers between devices with their start and end apart: 13, of which 5 were waited for; matrix products, arithmetic and copies ran while one was open for 2% of the time, Pallas kernels for 6%

profile of v10, /device:TPU:1, one launch (start us, length us, event | category | flops | bytes accessed | tf_op | source)
XLA Modules:
  0.0 219.7 jit_solution(9652635431194988615)
XLA Ops:
  0.7 12.0 %all_gather.9 = bf16[64,512]{1,0:T(8,128)(2,1)S(1)} all-gather(bf16[32,512]{1,0:T(8,128)(2,1)} %param.7), channel_id=1, replica_groups=mesh['zh'=2,'x'=4,'y'=8,'zl'=4,'c'=2] {'zh'}, dimensions={0}, use_global_device_ids=true | all-gather | bytes 98304 | tf_op jit(solution)/shard_map/all_gather | solution.py:384
  12.7 21.4 %all_to_all.30 = bf16[8,64,512]{2,1,0:T(8,128)(2,1)S(1)} all-to-all(bf16[8,64,512]{2,1,0:T(8,128)(2,1)S(1)} %broadcast_in_dim.4), channel_id=1, replica_groups=mesh['zh'=2,'x'=4,'y'=8,'zl'=4,'c'=2] {'y'}, dimensions={0} | all-to-all | bytes 1048576 | tf_op jit(solution)/shard_map/all_to_all | solution.py:38
  34.0 4.4 %collective-permute-start.1 = (bf16[8,2,32,512]{3,2,1,0:T(8,128)(2,1)S(1)}, bf16[8,2,32,512]{3,2,1,0:T(8,128)(2,1)S(1)}, u32[]{:S(2)}, u32[]{:S(2)}) collective-permute-start(bf16[8,2,32,512]{3,2,1,0:T(8,128)(2,1)S(1)} %bitcast.16), channel_id=1, source_target_pairs={{0,192},{64,0},{128,64},{192,128},{1,193},{65,1},{129,65},{193,129... | collective-permute-start | bytes 1572872 | tf_op jit(solution)/shard_map/ppermute | solution.py:45
  38.4 1.9 collective-permute-start
  40.4 0.8 slice_bitcast_fusion.1
  41.1 4.8 %collective-permute-done.1.ahead = bf16[8,2,32,512]{3,2,1,0:T(8,128)(2,1)S(1)} collective-permute-done((bf16[8,2,32,512]{3,2,1,0:T(8,128)(2,1)S(1)}, bf16[8,2,32,512]{3,2,1,0:T(8,128)(2,1)S(1)}, u32[]{:S(2)}, u32[]{:S(2)}) %collective-permute-start.1) | collective-permute-done | bytes 524320 | tf_op jit(solution)/shard_map/ppermute | solution.py:45
  45.9 5.3 %collective-permute-start.3 = (bf16[4,2,32,512]{3,2,1,0:T(8,128)(2,1)S(1)}, bf16[4,2,32,512]{3,2,1,0:T(8,128)(2,1)S(1)}, u32[]{:S(2)}, u32[]{:S(2)}) collective-permute-start(bf16[4,2,32,512]{3,2,1,0:T(8,128)(2,1)S(1)} %slice.17), channel_id=1, source_target_pairs={{0,192},{64,0},{128,64},{192,128},{1,193},{65,1},{129,65},{193,129... | collective-permute-start | bytes 786440 | tf_op jit(solution)/shard_map/ppermute | solution.py:45
  51.3 1.9 collective-permute-start.2
  53.3 0.3 fusion
  53.5 0.6 stack.27.at.refs_0_
  54.1 0.8 pad_maximum_fusion.view
  55.0 4.7 %collective-permute-done.2.far_low = bf16[4,2,32,512]{3,2,1,0:T(8,128)(2,1)S(1)} collective-permute-done((bf16[4,2,32,512]{3,2,1,0:T(8,128)(2,1)S(1)}, bf16[4,2,32,512]{3,2,1,0:T(8,128)(2,1)S(1)}, u32[]{:S(2)}, u32[]{:S(2)}) %collective-permute-start.2) | collective-permute-done | bytes 262176 | tf_op jit(solution)/shard_map/ppermute | solution.py:45
  59.7 0.7 copy-done.10
  60.4 3.2 %project_b.1 = (bf16[2,4,8,32,512]{4,3,2,1,0:T(8,128)(2,1)}, bf16[64,512]{1,0:T(8,128)(2,1)}) custom-call(s32[6]{0:T(128)} %stack.27.at.refs_0_, bf16[128,2048]{1,0:T(8,128)(2,1)} %pad_maximum_fusion.view, bf16[8,2,32,512]{3,2,1,0:T(8,128)(2,1)} %bitcast.18, bf16[8,2,32,512]{3,2,1,0:T(8,128)(2,1)} %copy-done.4, bf16[8,2,32,512]{3,2,1,0:T(8,128)(2,1)} %copy-done.3, ...), custom_call_target="tpu_custom_call" | custom-call | tf_op jit(solution)/shard_map/project_b/pallas_call | solution.py:92
  63.6 8.1 %collective-permute-start.4 = (bf16[64,512]{1,0:T(8,128)(2,1)}, bf16[64,512]{1,0:T(8,128)(2,1)S(1)}, u32[]{:S(2)}, u32[]{:S(2)}) collective-permute-start(bf16[64,512]{1,0:T(8,128)(2,1)} %get-tuple-element.25), channel_id=1, source_target_pairs={{0,0},{1,8},{2,16},{3,24},{4,32},{5,40},{6,48},{7,56},{8,1},{9,9},... | collective-permute-start | bytes 196616 | tf_op jit(solution)/shard_map/ppermute | solution.py:398
  71.7 3.1 %project_a.1 = (bf16[8,64,512]{2,1,0:T(8,128)(2,1)}, bf16[64,512]{1,0:T(8,128)(2,1)}) custom-call(bf16[128,2048]{1,0:T(8,128)(2,1)} %pad_maximum_fusion.view, bf16[2,4,8,32,512]{4,3,2,1,0:T(8,128)(2,1)} %get-tuple-element.26.weight), custom_call_target="tpu_custom_call" | custom-call | tf_op jit(solution)/shard_map/project_a/pallas_call | solution.py:92
  74.8 7.8 %all-to-all-start.1 = ((bf16[8,64,512]{2,1,0:T(8,128)(2,1)}), bf16[8,64,512]{2,1,0:T(8,128)(2,1)S(1)}, u32[]{:S(2)}, u32[]{:S(2)}) async-start(bf16[8,64,512]{2,1,0:T(8,128)(2,1)} %get-tuple-element.28), calls=%async_computation.1 | async-start | bytes 1048576 | tf_op jit(solution)/shard_map/all_to_all | solution.py:406
  82.6 18.8 %all-gather = bf16[512,512]{1,0:T(8,128)(2,1)} all-gather(bf16[64,512]{1,0:T(8,128)(2,1)S(1)} %collective-permute-done.4.raw_b), channel_id=2, replica_groups=mesh['zh'=2,'x'=4,'y'=8,'zl'=4,'c'=2] {'zl','c'}, dimensions={0}, use_global_device_ids=true | all-gather | bytes 589824 | tf_op jit(solution)/shard_map/all_gather | solution.py:407
  101.4 0.8 copy-done
  102.2 3.0 %gram.1 = bf16[4,144,512]{2,1,0:T(8,128)(2,1)} custom-call(bf16[8,64,512]{2,1,0:T(8,128)(2,1)} %copy-done, bf16[8,64,512]{2,1,0:T(8,128)(2,1)} %bitcast.14), custom_call_target="tpu_custom_call" | custom-call | tf_op jit(solution)/shard_map/gram/pallas_call | solution.py:92
  105.2 14.4 %all_to_all.31.got = bf16[4,144,512]{2,1,0:T(8,128)(2,1)} all-to-all(bf16[4,144,512]{2,1,0:T(8,128)(2,1)} %gram.1), channel_id=1, replica_groups=mesh['zh'=2,'x'=4,'y'=8,'zl'=4,'c'=2] {'x'}, dimensions={0} | all-to-all | bytes 1179648 | tf_op jit(solution)/shard_map/all_to_all | solution.py:412
  119.6 1.8 merge.1.refs_1_
  121.4 6.9 %collective-permute-start.5 = (bf16[192,512]{1,0:T(8,128)(2,1)}, bf16[192,512]{1,0:T(8,128)(2,1)S(1)}, u32[]{:S(2)}, u32[]{:S(2)}) collective-permute-start(bf16[192,512]{1,0:T(8,128)(2,1)} %merge.1.refs_1_), channel_id=1, source_target_pairs={{0,256},{256,0},{1,257},{257,1},{2,258},{258,2},{3,259},{259,3},{4... | collective-permute-start | bytes 589832 | tf_op jit(solution)/shard_map/ppermute | solution.py:50
  128.3 4.5 %collective-permute-done.5.refs_2_ = bf16[192,512]{1,0:T(8,128)(2,1)S(1)} collective-permute-done((bf16[192,512]{1,0:T(8,128)(2,1)}, bf16[192,512]{1,0:T(8,128)(2,1)S(1)}, u32[]{:S(2)}, u32[]{:S(2)}) %collective-permute-start.5) | collective-permute-done | bytes 196640 | tf_op jit(solution)/shard_map/ppermute | solution.py:50
  132.8 0.7 copy-done.11
  133.5 2.9 %mix.1 = (bf16[128,512]{1,0:T(8,128)(2,1)}, f32[8,512]{1,0:T(8,128)}) custom-call(s32[6]{0:T(128)} %stack.27.at.refs_0_, bf16[192,512]{1,0:T(8,128)(2,1)} %merge.1.refs_1_, bf16[192,512]{1,0:T(8,128)(2,1)} %copy-done.11), custom_call_target="tpu_custom_call" | custom-call | tf_op jit(solution)/shard_map/mix/pallas_call | solution.py:92
  136.4 0.9 broadcast_in_dim.5
  137.3 10.0 %all_to_all.32.mix4 = bf16[4,128,512]{2,1,0:T(8,128)(2,1)} all-to-all(bf16[4,128,512]{2,1,0:T(8,128)(2,1)S(1)} %broadcast_in_dim.5), channel_id=1, replica_groups=mesh['zh'=2,'x'=4,'y'=8,'zl'=4,'c'=2] {'x'}, dimensions={0} | all-to-all | bytes 1048576 | tf_op jit(solution)/shard_map/all_to_all | solution.py:38
  147.3 2.9 %grad_b.1 = (bf16[264,512]{1,0:T(8,128)(2,1)}, f32[264,512]{1,0:T(8,128)}, f32[8,512]{1,0:T(8,128)}) custom-call(s32[6]{0:T(128)} %stack.27.at.refs_0_, bf16[4,128,512]{2,1,0:T(8,128)(2,1)} %all_to_all.32.mix4, bf16[8,64,512]{2,1,0:T(8,128)(2,1)} %copy-done, f32[8,512]{1,0:T(8,128)} %get-tuple-element.31.stats), custom_call_target="tpu_custom_call" | custom-call | tf_op jit(solution)/shard_map/grad_b/pallas_call | solution.py:92
  150.3 7.1 %collective-permute-start.6 = (bf16[264,512]{1,0:T(8,128)(2,1)}, bf16[264,512]{1,0:T(8,128)(2,1)S(1)}, u32[]{:S(2)}, u32[]{:S(2)}) collective-permute-start(bf16[264,512]{1,0:T(8,128)(2,1)} %get-tuple-element.32), channel_id=1, source_target_pairs={{0,1},{1,0},{2,3},{3,2},{4,5},{5,4},{6,7},{7,6},{8,9},{9,8},{10,11... | collective-permute-start | bytes 811016 | tf_op jit(solution)/shard_map/ppermute | solution.py:50
  157.4 3.3 %grad_a.1 = bf16[8,72,512]{2,1,0:T(8,128)(2,1)} custom-call(s32[6]{0:T(128)} %stack.27.at.refs_0_, bf16[4,128,512]{2,1,0:T(8,128)(2,1)} %all_to_all.32.mix4, bf16[8,64,512]{2,1,0:T(8,128)(2,1)} %bitcast.15, f32[8,512]{1,0:T(8,128)} %get-tuple-element.33.stats), custom_call_target="tpu_custom_call" | custom-call | tf_op jit(solution)/shard_map/grad_a/pallas_call | solution.py:92
  160.7 7.0 %all-to-all-start.4 = ((bf16[8,72,512]{2,1,0:T(8,128)(2,1)}), bf16[8,72,512]{2,1,0:T(8,128)(2,1)S(1)}, u32[]{:S(2)}, u32[]{:S(2)}) async-start(bf16[8,72,512]{2,1,0:T(8,128)(2,1)} %grad_a.1), calls=%async_computation.4 | async-start | bytes 1179648 | tf_op jit(solution)/shard_map/all_to_all | solution.py:436
  167.7 2.0 core.1
  169.6 3.7 %collective-permute-start.7 = (bf16[72,512]{1,0:T(8,128)(2,1)}, bf16[72,512]{1,0:T(8,128)(2,1)S(1)}, u32[]{:S(2)}, u32[]{:S(2)}) collective-permute-start(bf16[72,512]{1,0:T(8,128)(2,1)} %get-tuple-element.40), channel_id=1, source_target_pairs={{0,2},{2,0},{4,6},{6,4},{1,3},{3,1},{5,7},{7,5},{8,10},{10,8},{12,... | collective-permute-start | bytes 221192 | tf_op jit(solution)/shard_map/ppermute | solution.py:50
  173.4 2.5 %collective-permute-start.8 = (bf16[72,512]{1,0:T(8,128)(2,1)}, bf16[72,512]{1,0:T(8,128)(2,1)S(1)}, u32[]{:S(2)}, u32[]{:S(2)}) collective-permute-start(bf16[72,512]{1,0:T(8,128)(2,1)} %get-tuple-element.41), channel_id=1, source_target_pairs={{0,4},{2,6},{4,0},{6,2},{1,5},{3,7},{5,1},{7,3},{8,12},{10,14},{12... | collective-permute-start | bytes 221192 | tf_op jit(solution)/shard_map/ppermute | solution.py:50
  175.9 3.4 %collective-permute-start.9 = (bf16[72,512]{1,0:T(8,128)(2,1)}, bf16[72,512]{1,0:T(8,128)(2,1)S(1)}, u32[]{:S(2)}, u32[]{:S(2)}) collective-permute-start(bf16[72,512]{1,0:T(8,128)(2,1)} %get-tuple-element.42), channel_id=1, source_target_pairs={{0,6},{2,4},{4,2},{6,0},{1,7},{3,5},{5,3},{7,1},{8,14},{10,12},{12... | collective-permute-start | bytes 221192 | tf_op jit(solution)/shard_map/ppermute | solution.py:50
  179.3 2.6 %collective-permute-done.8.got2 = bf16[72,512]{1,0:T(8,128)(2,1)S(1)} collective-permute-done((bf16[72,512]{1,0:T(8,128)(2,1)}, bf16[72,512]{1,0:T(8,128)(2,1)S(1)}, u32[]{:S(2)}, u32[]{:S(2)}) %collective-permute-start.8) | collective-permute-done | bytes 73760 | tf_op jit(solution)/shard_map/ppermute | solution.py:50
  181.9 1.3 collective-permute-done.9.got3
  183.1 0.6 copy-done.14
  183.7 1.8 dz_b.1
  185.5 5.2 %collective-permute-start.10 = (bf16[64,512]{1,0:T(8,128)(2,1)}, bf16[64,512]{1,0:T(8,128)(2,1)S(1)}, u32[]{:S(2)}, u32[]{:S(2)}) collective-permute-start(bf16[64,512]{1,0:T(8,128)(2,1)} %dz_b.1), channel_id=1, source_target_pairs={{0,0},{1,8},{2,16},{3,24},{4,32},{5,40},{6,48},{7,56},{8,1},{9,9},... | collective-permute-start | bytes 196616 | tf_op jit(solution)/shard_map/ppermute | solution.py:446
  190.7 1.1 compare_convert_fusion
  191.8 0.8 copy-done.1
  192.6 3.6 %back_a.1 = (f32[64,2048]{1,0:T(8,128)}, f32[1,512]{1,0:T(1,128)}, f32[1,256]{1,0:T(1,128)}) custom-call(bf16[8,72,512]{2,1,0:T(8,128)(2,1)} %copy-done.1, bf16[64,512]{1,0:T(8,128)(2,1)} %get-tuple-element.35.raw_a, f32[8,512]{1,0:T(8,128)} %get-tuple-element.31.stats, f32[64,2048]{1,0:T(8,128)} %get-tuple-element.50.keep, ...), custom_call_target="tpu_custom_call" | custom-call | tf_op jit(solution)/shard_map/back_a/pallas_call | solution.py:92
  196.2 0.6 copy-done.15
  196.8 3.3 %back_b.1 = bf16[8,72,256]{2,1,0:T(8,128)(2,1)} custom-call(f32[64,2048]{1,0:T(8,128)} %get-tuple-element.36.part, bf16[64,512]{1,0:T(8,128)(2,1)} %copy-done.15, f32[64,2048]{1,0:T(8,128)} %get-tuple-element.49.keep, bf16[2,4,8,32,512]{4,3,2,1,0:T(8,128)(2,1)} %get-tuple-element.26.weight, f32[1,256]{1,0:T(1,128)} %get-tuple-element.43.power), custom_call_target="tpu_custom_call" | custom-call | tf_op jit(solution)/shard_map/back_b/pallas_call | solution.py:92
  200.2 17.9 %all_to_all.33.refs_0_ = bf16[8,72,256]{2,1,0:T(8,128)(2,1)} all-to-all(bf16[8,72,256]{2,1,0:T(8,128)(2,1)} %back_b.1), channel_id=1, replica_groups=mesh['zh'=2,'x'=4,'y'=8,'zl'=4,'c'=2] {'zl','c'}, dimensions={0} | all-to-all | bytes 589824 | tf_op jit(solution)/shard_map/all_to_all | solution.py:460
  218.1 1.6 end.1
  (38 shorter events, 0.1 us)
Async XLA Ops:
  0.6 52.6 %copy-start.7 = (bf16[64,2048]{1,0:T(8,128)(2,1)S(1)}, bf16[64,2048]{1,0:T(8,128)(2,1)}, u32[]{:S(2)}) copy-start(bf16[64,2048]{1,0:T(8,128)(2,1)} %param.5) | copy-start | bytes 786436
  0.6 52.6 %copy-start.6 = (bf16[64,2048]{1,0:T(8,128)(2,1)S(1)}, bf16[64,2048]{1,0:T(8,128)(2,1)}, u32[]{:S(2)}) copy-start(bf16[64,2048]{1,0:T(8,128)(2,1)} %param.4) | copy-start | bytes 786436
  34.0 25.6 %copy-start.2 = (bf16[8,64,512]{2,1,0:T(8,128)(2,1)}, bf16[8,64,512]{2,1,0:T(8,128)(2,1)S(1)}, u32[]{:S(2)}) copy-start(bf16[8,64,512]{2,1,0:T(8,128)(2,1)S(1)} %all_to_all.30) | copy-start | bytes 1572868
  34.0 11.9 %collective-permute-start.1 = (bf16[8,2,32,512]{3,2,1,0:T(8,128)(2,1)S(1)}, bf16[8,2,32,512]{3,2,1,0:T(8,128)(2,1)S(1)}, u32[]{:S(2)}, u32[]{:S(2)}) collective-permute-start(bf16[8,2,32,512]{3,2,1,0:T(8,128)(2,1)S(1)} %bitcast.16), channel_id=1, source_target_pairs={{0,192},{64,0},{128,64},{192,128},{1,193},{65,1},{129,65},{193,129... | collective-permute-start | bytes 1572872 | tf_op jit(solution)/shard_map/ppermute | solution.py:45
  38.4 12.9 %collective-permute-start = (bf16[8,2,32,512]{3,2,1,0:T(8,128)(2,1)S(1)}, bf16[8,2,32,512]{3,2,1,0:T(8,128)(2,1)S(1)}, u32[]{:S(2)}, u32[]{:S(2)}) collective-permute-start(bf16[8,2,32,512]{3,2,1,0:T(8,128)(2,1)S(1)} %bitcast.17), channel_id=1, source_target_pairs={{0,64},{64,128},{128,192},{192,0},{1,65},{65,129},{129,193},{193,1... | collective-permute-start | bytes 1572872 | tf_op jit(solution)/shard_map/ppermute | solution.py:45
  45.9 13.7 %copy-start.3 = (bf16[8,2,32,512]{3,2,1,0:T(8,128)(2,1)}, bf16[8,2,32,512]{3,2,1,0:T(8,128)(2,1)S(1)}, u32[]{:S(2)}) copy-start(bf16[8,2,32,512]{3,2,1,0:T(8,128)(2,1)S(1)} %collective-permute-done.1.ahead) | copy-start | bytes 1572868
  45.9 9.0 %collective-permute-start.3 = (bf16[4,2,32,512]{3,2,1,0:T(8,128)(2,1)S(1)}, bf16[4,2,32,512]{3,2,1,0:T(8,128)(2,1)S(1)}, u32[]{:S(2)}, u32[]{:S(2)}) collective-permute-start(bf16[4,2,32,512]{3,2,1,0:T(8,128)(2,1)S(1)} %slice.17), channel_id=1, source_target_pairs={{0,192},{64,0},{128,64},{192,128},{1,193},{65,1},{129,65},{193,129... | collective-permute-start | bytes 786440 | tf_op jit(solution)/shard_map/ppermute | solution.py:45
  51.3 8.4 %copy-start.4 = (bf16[8,2,32,512]{3,2,1,0:T(8,128)(2,1)}, bf16[8,2,32,512]{3,2,1,0:T(8,128)(2,1)S(1)}, u32[]{:S(2)}) copy-start(bf16[8,2,32,512]{3,2,1,0:T(8,128)(2,1)S(1)} %collective-permute-done.back) | copy-start | bytes 1572868
  51.3 8.3 %collective-permute-start.2 = (bf16[4,2,32,512]{3,2,1,0:T(8,128)(2,1)S(1)}, bf16[4,2,32,512]{3,2,1,0:T(8,128)(2,1)S(1)}, u32[]{:S(2)}, u32[]{:S(2)}) collective-permute-start(bf16[4,2,32,512]{3,2,1,0:T(8,128)(2,1)S(1)} %slice.16), channel_id=1, source_target_pairs={{0,64},{64,128},{128,192},{192,0},{1,65},{65,129},{129,193},{193,1... | collective-permute-start | bytes 786440 | tf_op jit(solution)/shard_map/ppermute | solution.py:45
  55.0 4.7 %copy-start.9 = (bf16[4,2,32,512]{3,2,1,0:T(8,128)(2,1)}, bf16[4,2,32,512]{3,2,1,0:T(8,128)(2,1)S(1)}, u32[]{:S(2)}) copy-start(bf16[4,2,32,512]{3,2,1,0:T(8,128)(2,1)S(1)} %collective-permute-done.3.far_high) | copy-start | bytes 786436
  59.7 0.7 copy-start.10
  63.6 11.2 %collective-permute-start.4 = (bf16[64,512]{1,0:T(8,128)(2,1)}, bf16[64,512]{1,0:T(8,128)(2,1)S(1)}, u32[]{:S(2)}, u32[]{:S(2)}) collective-permute-start(bf16[64,512]{1,0:T(8,128)(2,1)} %get-tuple-element.25), channel_id=1, source_target_pairs={{0,0},{1,8},{2,16},{3,24},{4,32},{5,40},{6,48},{7,56},{8,1},{9,9},... | collective-permute-start | bytes 196616 | tf_op jit(solution)/shard_map/ppermute | solution.py:398
  74.8 44.8 %copy-start.8 = (bf16[64,512]{1,0:T(8,128)(2,1)}, bf16[64,512]{1,0:T(8,128)(2,1)S(1)}, u32[]{:S(2)}) copy-start(bf16[64,512]{1,0:T(8,128)(2,1)S(1)} %collective-permute-done.4.raw_b) | copy-start | bytes 196612
  74.8 26.6 %all-to-all-start.1 = ((bf16[8,64,512]{2,1,0:T(8,128)(2,1)}), bf16[8,64,512]{2,1,0:T(8,128)(2,1)S(1)}, u32[]{:S(2)}, u32[]{:S(2)}) async-start(bf16[8,64,512]{2,1,0:T(8,128)(2,1)} %get-tuple-element.28), calls=%async_computation.1 | async-start | bytes 1048576 | tf_op jit(solution)/shard_map/all_to_all | solution.py:406
  101.4 0.8 copy-start
  121.4 11.4 %collective-permute-start.5 = (bf16[192,512]{1,0:T(8,128)(2,1)}, bf16[192,512]{1,0:T(8,128)(2,1)S(1)}, u32[]{:S(2)}, u32[]{:S(2)}) collective-permute-start(bf16[192,512]{1,0:T(8,128)(2,1)} %merge.1.refs_1_), channel_id=1, source_target_pairs={{0,256},{256,0},{1,257},{257,1},{2,258},{258,2},{3,259},{259,3},{4... | collective-permute-start | bytes 589832 | tf_op jit(solution)/shard_map/ppermute | solution.py:50
  132.8 0.7 copy-start.11
  150.3 10.4 %collective-permute-start.6 = (bf16[264,512]{1,0:T(8,128)(2,1)}, bf16[264,512]{1,0:T(8,128)(2,1)S(1)}, u32[]{:S(2)}, u32[]{:S(2)}) collective-permute-start(bf16[264,512]{1,0:T(8,128)(2,1)} %get-tuple-element.32), channel_id=1, source_target_pairs={{0,1},{1,0},{2,3},{3,2},{4,5},{5,4},{6,7},{7,6},{8,9},{9,8},{10,11... | collective-permute-start | bytes 811016 | tf_op jit(solution)/shard_map/ppermute | solution.py:50
  160.7 7.0 %copy-start.5 = (bf16[264,512]{1,0:T(8,128)(2,1)}, bf16[264,512]{1,0:T(8,128)(2,1)S(1)}, u32[]{:S(2)}) copy-start(bf16[264,512]{1,0:T(8,128)(2,1)S(1)} %collective-permute-done.6.got) | copy-start | bytes 811012
  160.7 31.1 %all-to-all-start.4 = ((bf16[8,72,512]{2,1,0:T(8,128)(2,1)}), bf16[8,72,512]{2,1,0:T(8,128)(2,1)S(1)}, u32[]{:S(2)}, u32[]{:S(2)}) async-start(bf16[8,72,512]{2,1,0:T(8,128)(2,1)} %grad_a.1), calls=%async_computation.4 | async-start | bytes 1179648 | tf_op jit(solution)/shard_map/all_to_all | solution.py:436
  169.6 9.6 %collective-permute-start.7 = (bf16[72,512]{1,0:T(8,128)(2,1)}, bf16[72,512]{1,0:T(8,128)(2,1)S(1)}, u32[]{:S(2)}, u32[]{:S(2)}) collective-permute-start(bf16[72,512]{1,0:T(8,128)(2,1)} %get-tuple-element.40), channel_id=1, source_target_pairs={{0,2},{2,0},{4,6},{6,4},{1,3},{3,1},{5,7},{7,5},{8,10},{10,8},{12,... | collective-permute-start | bytes 221192 | tf_op jit(solution)/shard_map/ppermute | solution.py:50
  173.4 8.5 %collective-permute-start.8 = (bf16[72,512]{1,0:T(8,128)(2,1)}, bf16[72,512]{1,0:T(8,128)(2,1)S(1)}, u32[]{:S(2)}, u32[]{:S(2)}) collective-permute-start(bf16[72,512]{1,0:T(8,128)(2,1)} %get-tuple-element.41), channel_id=1, source_target_pairs={{0,4},{2,6},{4,0},{6,2},{1,5},{3,7},{5,1},{7,3},{8,12},{10,14},{12... | collective-permute-start | bytes 221192 | tf_op jit(solution)/shard_map/ppermute | solution.py:50
  175.9 7.2 %collective-permute-start.9 = (bf16[72,512]{1,0:T(8,128)(2,1)}, bf16[72,512]{1,0:T(8,128)(2,1)S(1)}, u32[]{:S(2)}, u32[]{:S(2)}) collective-permute-start(bf16[72,512]{1,0:T(8,128)(2,1)} %get-tuple-element.42), channel_id=1, source_target_pairs={{0,6},{2,4},{4,2},{6,0},{1,7},{3,5},{5,3},{7,1},{8,14},{10,12},{12... | collective-permute-start | bytes 221192 | tf_op jit(solution)/shard_map/ppermute | solution.py:50
  179.3 3.8 %copy-start.12 = (bf16[72,512]{1,0:T(8,128)(2,1)}, bf16[72,512]{1,0:T(8,128)(2,1)S(1)}, u32[]{:S(2)}) copy-start(bf16[72,512]{1,0:T(8,128)(2,1)S(1)} %collective-permute-done.7.got1) | copy-start | bytes 221188
  181.9 1.3 copy-start.13
  183.1 0.6 copy-start.14
  185.5 10.7 %collective-permute-start.10 = (bf16[64,512]{1,0:T(8,128)(2,1)}, bf16[64,512]{1,0:T(8,128)(2,1)S(1)}, u32[]{:S(2)}, u32[]{:S(2)}) collective-permute-start(bf16[64,512]{1,0:T(8,128)(2,1)} %dz_b.1), channel_id=1, source_target_pairs={{0,0},{1,8},{2,16},{3,24},{4,32},{5,40},{6,48},{7,56},{8,1},{9,9},... | collective-permute-start | bytes 196616 | tf_op jit(solution)/shard_map/ppermute | solution.py:446
  191.8 0.8 copy-start.1
  196.2 0.6 copy-start.15

commit v11 on v10

--- a/solution.py
+++ b/solution.py
@@ -160,7 +160,7 @@
 
 
 def mix_body(at, mine, theirs, mix, stats, table, offs, *, block):
-    sub, kt = mix.shape
+    _, sub, kt = mix.shape
     each = (mine.shape[0] - sub) // 16
     sets = 2 * each
     total = block * sets
@@ -191,14 +191,15 @@
     coeff = -2.0 * (1.0 - diag) - 2.0 * LAMBDA_OFF * diag
     k_of = lax.broadcasted_iota(jnp.int32, (sub, kt), 0)
     l_of = lax.broadcasted_iota(jnp.int32, (sub, kt), 1)
-    chosen = exact((k_of + at[3] == l_of).astype(F32), table[...], 1, 1)
+    hot = (k_of + at[3] == l_of).astype(F32).astype(BF)
+    chosen = sum(dot(hot, p, 1, 1) for p in thirds(table[...]))
     corr = mine[:sub].astype(F32) + theirs[:sub].astype(F32)
     corr = corr + exact(chosen[:, :sets], offs[...], 1, 0)
     corr = corr * (chosen[:, sets : sets + 1] * (inv_b / total))
     here = k_of + (at[3] + at[4]) == l_of
-    mix[...] = jnp.where(
-        here, coeff + 2.0 * LAMBDA_OFF * diag, 2.0 * LAMBDA_OFF * corr
-    ).astype(BF)
+    out = jnp.where(here, coeff + 2.0 * LAMBDA_OFF * diag, 2.0 * LAMBDA_OFF * corr).astype(BF)
+    for i in range(mix.shape[0]):
+        mix[i] = out
     stats[0:1, :] = mean_a
     stats[1:2, :] = inv_a
     stats[2:3, :] = mean_b
@@ -414,11 +415,11 @@
     mix, stats = call(
         lambda *refs: mix_body(*refs, block=block),
         "mix",
-        [((sub, kt), BF), ((8, kt), F32)],
+        [((x_n, sub, kt), BF), ((8, kt), F32)],
         (at, got, flip(got, "zh", 1)),
         [((16, kt), F32), ((rows_n, kt), F32)],
     )
-    mix = spread(mix, "x")
+    mix = lax.all_to_all(mix, "x", 0, 0, tiled=True)
 
     line_rows = zl_n * rows + 8
     sent, kept, stats_a = call(

time: 221 us -> 221 us (level)
    all_to_all x0 -> x1, blocking collectives: none -> 11.1 us  [on_device(): mix = lax.all_to_all(mix, 'x', 0, 0, tiled=True)]
    all_to_all x2 -> x1, blocking collectives: 31.4 us -> 21.4 us  [spread(): lax.all_to_all(jnp.broadcast_to(value[None], (parts,) + value.shape), axe...]
where the time goes in v11:
time: 221 us; the launch traced here: 220 us
  blocking collectives  95.6 us (43%)
  starting transfers between devices  65.1 us (29%)
  Pallas kernels  32.4 us (15%)
  waiting for transfers between devices  17.8 us (8%)
  local copies, waits for them, and re-layouts  5.72 us (3%)
    pallas_call x12, Pallas kernels, call(): pl.pallas_call(body, name=name, out_shape=[jax.ShapeDtypeStruct(s, d) for...  32.4 us
    ppermute x5, starting transfers between devices, flip(): return lax.ppermute(value, axis, [(i, i ^ step) for i in range(n)])  23.6 us
    all_to_all x1, blocking collectives, spread(): lax.all_to_all(jnp.broadcast_to(value[None], (parts,) + value.shape), axe...  21.4 us
    all_gather x1, blocking collectives, on_device(): big_b = lax.all_gather(own_b, TILE, axis=0)  18.8 us
    all_to_all x1, blocking collectives, on_device(): got = lax.all_to_all(share, TILE, 0, 0, tiled=True)  17.9 us
    all_to_all x1, blocking collectives, on_device(): got = lax.all_to_all(gram, 'x', 0, 0, tiled=True)  14.4 us
    ppermute x4, starting transfers between devices, shift(): return lax.ppermute(value, axis, [(i, (i + step) % n) for i in range(n)])  13.5 us
    all_gather x1, blocking collectives, on_device(): own = lax.all_gather(weight, 'zh', axis=0, tiled=True)  12 us
  transfers between devices with their start and end apart: 13, of which 5 were waited for; matrix products, arithmetic and copies ran while one was open for 2% of the time, Pallas kernels for 6%

profile of v11, /device:TPU:1, one launch (start us, length us, event | category | flops | bytes accessed | tf_op | source)
XLA Modules:
  0.0 219.7 jit_solution(5656359732059811003)
XLA Ops:
  0.7 12.0 %all_gather.9 = bf16[64,512]{1,0:T(8,128)(2,1)S(1)} all-gather(bf16[32,512]{1,0:T(8,128)(2,1)} %param.7), channel_id=1, replica_groups=mesh['zh'=2,'x'=4,'y'=8,'zl'=4,'c'=2] {'zh'}, dimensions={0}, use_global_device_ids=true | all-gather | bytes 98304 | tf_op jit(solution)/shard_map/all_gather | solution.py:385
  12.7 21.4 %all_to_all.30 = bf16[8,64,512]{2,1,0:T(8,128)(2,1)S(1)} all-to-all(bf16[8,64,512]{2,1,0:T(8,128)(2,1)S(1)} %broadcast_in_dim.2), channel_id=1, replica_groups=mesh['zh'=2,'x'=4,'y'=8,'zl'=4,'c'=2] {'y'}, dimensions={0} | all-to-all | bytes 1048576 | tf_op jit(solution)/shard_map/all_to_all | solution.py:38
  34.0 4.4 %collective-permute-start.1 = (bf16[8,2,32,512]{3,2,1,0:T(8,128)(2,1)S(1)}, bf16[8,2,32,512]{3,2,1,0:T(8,128)(2,1)S(1)}, u32[]{:S(2)}, u32[]{:S(2)}) collective-permute-start(bf16[8,2,32,512]{3,2,1,0:T(8,128)(2,1)S(1)} %bitcast.16), channel_id=1, source_target_pairs={{0,192},{64,0},{128,64},{192,128},{1,193},{65,1},{129,65},{193,129... | collective-permute-start | bytes 1572872 | tf_op jit(solution)/shard_map/ppermute | solution.py:45
  38.4 1.9 collective-permute-start
  40.4 0.8 slice_bitcast_fusion.1
  41.1 4.8 %collective-permute-done.1.ahead = bf16[8,2,32,512]{3,2,1,0:T(8,128)(2,1)S(1)} collective-permute-done((bf16[8,2,32,512]{3,2,1,0:T(8,128)(2,1)S(1)}, bf16[8,2,32,512]{3,2,1,0:T(8,128)(2,1)S(1)}, u32[]{:S(2)}, u32[]{:S(2)}) %collective-permute-start.1) | collective-permute-done | bytes 524320 | tf_op jit(solution)/shard_map/ppermute | solution.py:45
  45.9 5.3 %collective-permute-start.3 = (bf16[4,2,32,512]{3,2,1,0:T(8,128)(2,1)S(1)}, bf16[4,2,32,512]{3,2,1,0:T(8,128)(2,1)S(1)}, u32[]{:S(2)}, u32[]{:S(2)}) collective-permute-start(bf16[4,2,32,512]{3,2,1,0:T(8,128)(2,1)S(1)} %slice.17), channel_id=1, source_target_pairs={{0,192},{64,0},{128,64},{192,128},{1,193},{65,1},{129,65},{193,129... | collective-permute-start | bytes 786440 | tf_op jit(solution)/shard_map/ppermute | solution.py:45
  51.3 0.0 collective-permute-done.back
  51.3 1.9 collective-permute-start.2
  53.3 0.3 fusion
  53.5 0.6 stack.27.at.refs_0_
  54.1 0.8 pad_maximum_fusion.view
  55.0 4.7 %collective-permute-done.2.far_low = bf16[4,2,32,512]{3,2,1,0:T(8,128)(2,1)S(1)} collective-permute-done((bf16[4,2,32,512]{3,2,1,0:T(8,128)(2,1)S(1)}, bf16[4,2,32,512]{3,2,1,0:T(8,128)(2,1)S(1)}, u32[]{:S(2)}, u32[]{:S(2)}) %collective-permute-start.2) | collective-permute-done | bytes 262176 | tf_op jit(solution)/shard_map/ppermute | solution.py:45
  59.7 0.7 copy-done.10
  60.4 3.2 %project_b.1 = (bf16[2,4,8,32,512]{4,3,2,1,0:T(8,128)(2,1)}, bf16[64,512]{1,0:T(8,128)(2,1)}) custom-call(s32[6]{0:T(128)} %stack.27.at.refs_0_, bf16[128,2048]{1,0:T(8,128)(2,1)} %pad_maximum_fusion.view, bf16[8,2,32,512]{3,2,1,0:T(8,128)(2,1)} %bitcast.18, bf16[8,2,32,512]{3,2,1,0:T(8,128)(2,1)} %copy-done.4, bf16[8,2,32,512]{3,2,1,0:T(8,128)(2,1)} %copy-done.3, ...), custom_call_target="tpu_custom_call" | custom-call | tf_op jit(solution)/shard_map/project_b/pallas_call | solution.py:92
  63.6 8.1 %collective-permute-start.4 = (bf16[64,512]{1,0:T(8,128)(2,1)}, bf16[64,512]{1,0:T(8,128)(2,1)S(1)}, u32[]{:S(2)}, u32[]{:S(2)}) collective-permute-start(bf16[64,512]{1,0:T(8,128)(2,1)} %get-tuple-element.25), channel_id=1, source_target_pairs={{0,0},{1,8},{2,16},{3,24},{4,32},{5,40},{6,48},{7,56},{8,1},{9,9},... | collective-permute-start | bytes 196616 | tf_op jit(solution)/shard_map/ppermute | solution.py:399
  71.7 3.1 %project_a.1 = (bf16[8,64,512]{2,1,0:T(8,128)(2,1)}, bf16[64,512]{1,0:T(8,128)(2,1)}) custom-call(bf16[128,2048]{1,0:T(8,128)(2,1)} %pad_maximum_fusion.view, bf16[2,4,8,32,512]{4,3,2,1,0:T(8,128)(2,1)} %get-tuple-element.26.weight), custom_call_target="tpu_custom_call" | custom-call | tf_op jit(solution)/shard_map/project_a/pallas_call | solution.py:92
  74.8 7.8 %all-to-all-start.1 = ((bf16[8,64,512]{2,1,0:T(8,128)(2,1)}), bf16[8,64,512]{2,1,0:T(8,128)(2,1)S(1)}, u32[]{:S(2)}, u32[]{:S(2)}) async-start(bf16[8,64,512]{2,1,0:T(8,128)(2,1)} %get-tuple-element.28), calls=%async_computation.1 | async-start | bytes 1048576 | tf_op jit(solution)/shard_map/all_to_all | solution.py:407
  82.6 18.8 %all-gather = bf16[512,512]{1,0:T(8,128)(2,1)} all-gather(bf16[64,512]{1,0:T(8,128)(2,1)S(1)} %collective-permute-done.4.raw_b), channel_id=2, replica_groups=mesh['zh'=2,'x'=4,'y'=8,'zl'=4,'c'=2] {'zl','c'}, dimensions={0}, use_global_device_ids=true | all-gather | bytes 589824 | tf_op jit(solution)/shard_map/all_gather | solution.py:408
  101.4 0.8 copy-done
  102.2 3.0 %gram.1 = bf16[4,144,512]{2,1,0:T(8,128)(2,1)} custom-call(bf16[8,64,512]{2,1,0:T(8,128)(2,1)} %copy-done, bf16[8,64,512]{2,1,0:T(8,128)(2,1)} %bitcast.14), custom_call_target="tpu_custom_call" | custom-call | tf_op jit(solution)/shard_map/gram/pallas_call | solution.py:92
  105.2 14.4 %all_to_all.31.got = bf16[4,144,512]{2,1,0:T(8,128)(2,1)} all-to-all(bf16[4,144,512]{2,1,0:T(8,128)(2,1)} %gram.1), channel_id=1, replica_groups=mesh['zh'=2,'x'=4,'y'=8,'zl'=4,'c'=2] {'x'}, dimensions={0} | all-to-all | bytes 1179648 | tf_op jit(solution)/shard_map/all_to_all | solution.py:413
  119.6 1.8 merge.1.refs_1_
  121.4 6.9 %collective-permute-start.5 = (bf16[192,512]{1,0:T(8,128)(2,1)}, bf16[192,512]{1,0:T(8,128)(2,1)S(1)}, u32[]{:S(2)}, u32[]{:S(2)}) collective-permute-start(bf16[192,512]{1,0:T(8,128)(2,1)} %merge.1.refs_1_), channel_id=1, source_target_pairs={{0,256},{256,0},{1,257},{257,1},{2,258},{258,2},{3,259},{259,3},{4... | collective-permute-start | bytes 589832 | tf_op jit(solution)/shard_map/ppermute | solution.py:50
  128.3 4.5 %collective-permute-done.5.refs_2_ = bf16[192,512]{1,0:T(8,128)(2,1)S(1)} collective-permute-done((bf16[192,512]{1,0:T(8,128)(2,1)}, bf16[192,512]{1,0:T(8,128)(2,1)S(1)}, u32[]{:S(2)}, u32[]{:S(2)}) %collective-permute-start.5) | collective-permute-done | bytes 196640 | tf_op jit(solution)/shard_map/ppermute | solution.py:50
  132.8 0.7 copy-done.11
  133.5 2.7 %mix.1 = (bf16[4,128,512]{2,1,0:T(8,128)(2,1)}, f32[8,512]{1,0:T(8,128)}) custom-call(s32[6]{0:T(128)} %stack.27.at.refs_0_, bf16[192,512]{1,0:T(8,128)(2,1)} %merge.1.refs_1_, bf16[192,512]{1,0:T(8,128)(2,1)} %copy-done.11), custom_call_target="tpu_custom_call" | custom-call | tf_op jit(solution)/shard_map/mix/pallas_call | solution.py:92
  136.2 11.1 %all_to_all.32.mix4 = bf16[4,128,512]{2,1,0:T(8,128)(2,1)} all-to-all(bf16[4,128,512]{2,1,0:T(8,128)(2,1)} %get-tuple-element.30), channel_id=1, replica_groups=mesh['zh'=2,'x'=4,'y'=8,'zl'=4,'c'=2] {'x'}, dimensions={0} | all-to-all | bytes 1048576 | tf_op jit(solution)/shard_map/all_to_all | solution.py:422
  147.4 2.9 %grad_b.1 = (bf16[264,512]{1,0:T(8,128)(2,1)}, f32[264,512]{1,0:T(8,128)}, f32[8,512]{1,0:T(8,128)}) custom-call(s32[6]{0:T(128)} %stack.27.at.refs_0_, bf16[4,128,512]{2,1,0:T(8,128)(2,1)} %all_to_all.32.mix4, bf16[8,64,512]{2,1,0:T(8,128)(2,1)} %copy-done, f32[8,512]{1,0:T(8,128)} %get-tuple-element.31.stats), custom_call_target="tpu_custom_call" | custom-call | tf_op jit(solution)/shard_map/grad_b/pallas_call | solution.py:92
  150.3 7.1 %collective-permute-start.6 = (bf16[264,512]{1,0:T(8,128)(2,1)}, bf16[264,512]{1,0:T(8,128)(2,1)S(1)}, u32[]{:S(2)}, u32[]{:S(2)}) collective-permute-start(bf16[264,512]{1,0:T(8,128)(2,1)} %get-tuple-element.32), channel_id=1, source_target_pairs={{0,1},{1,0},{2,3},{3,2},{4,5},{5,4},{6,7},{7,6},{8,9},{9,8},{10,11... | collective-permute-start | bytes 811016 | tf_op jit(solution)/shard_map/ppermute | solution.py:50
  157.4 3.3 %grad_a.1 = bf16[8,72,512]{2,1,0:T(8,128)(2,1)} custom-call(s32[6]{0:T(128)} %stack.27.at.refs_0_, bf16[4,128,512]{2,1,0:T(8,128)(2,1)} %all_to_all.32.mix4, bf16[8,64,512]{2,1,0:T(8,128)(2,1)} %bitcast.15, f32[8,512]{1,0:T(8,128)} %get-tuple-element.33.stats), custom_call_target="tpu_custom_call" | custom-call | tf_op jit(solution)/shard_map/grad_a/pallas_call | solution.py:92
  160.7 7.0 %all-to-all-start.4 = ((bf16[8,72,512]{2,1,0:T(8,128)(2,1)}), bf16[8,72,512]{2,1,0:T(8,128)(2,1)S(1)}, u32[]{:S(2)}, u32[]{:S(2)}) async-start(bf16[8,72,512]{2,1,0:T(8,128)(2,1)} %grad_a.1), calls=%async_computation.4 | async-start | bytes 1179648 | tf_op jit(solution)/shard_map/all_to_all | solution.py:437
  167.7 2.0 core.1
  169.7 3.7 %collective-permute-start.7 = (bf16[72,512]{1,0:T(8,128)(2,1)}, bf16[72,512]{1,0:T(8,128)(2,1)S(1)}, u32[]{:S(2)}, u32[]{:S(2)}) collective-permute-start(bf16[72,512]{1,0:T(8,128)(2,1)} %get-tuple-element.40), channel_id=1, source_target_pairs={{0,2},{2,0},{4,6},{6,4},{1,3},{3,1},{5,7},{7,5},{8,10},{10,8},{12,... | collective-permute-start | bytes 221192 | tf_op jit(solution)/shard_map/ppermute | solution.py:50
  173.4 2.5 %collective-permute-start.8 = (bf16[72,512]{1,0:T(8,128)(2,1)}, bf16[72,512]{1,0:T(8,128)(2,1)S(1)}, u32[]{:S(2)}, u32[]{:S(2)}) collective-permute-start(bf16[72,512]{1,0:T(8,128)(2,1)} %get-tuple-element.41), channel_id=1, source_target_pairs={{0,4},{2,6},{4,0},{6,2},{1,5},{3,7},{5,1},{7,3},{8,12},{10,14},{12... | collective-permute-start | bytes 221192 | tf_op jit(solution)/shard_map/ppermute | solution.py:50
  175.9 3.4 %collective-permute-start.9 = (bf16[72,512]{1,0:T(8,128)(2,1)}, bf16[72,512]{1,0:T(8,128)(2,1)S(1)}, u32[]{:S(2)}, u32[]{:S(2)}) collective-permute-start(bf16[72,512]{1,0:T(8,128)(2,1)} %get-tuple-element.42), channel_id=1, source_target_pairs={{0,6},{2,4},{4,2},{6,0},{1,7},{3,5},{5,3},{7,1},{8,14},{10,12},{12... | collective-permute-start | bytes 221192 | tf_op jit(solution)/shard_map/ppermute | solution.py:50
  179.3 2.6 %collective-permute-done.8.got2 = bf16[72,512]{1,0:T(8,128)(2,1)S(1)} collective-permute-done((bf16[72,512]{1,0:T(8,128)(2,1)}, bf16[72,512]{1,0:T(8,128)(2,1)S(1)}, u32[]{:S(2)}, u32[]{:S(2)}) %collective-permute-start.8) | collective-permute-done | bytes 73760 | tf_op jit(solution)/shard_map/ppermute | solution.py:50
  181.9 1.3 collective-permute-done.9.got3
  183.1 0.6 copy-done.14
  183.8 1.8 dz_b.1
  185.5 5.2 %collective-permute-start.10 = (bf16[64,512]{1,0:T(8,128)(2,1)}, bf16[64,512]{1,0:T(8,128)(2,1)S(1)}, u32[]{:S(2)}, u32[]{:S(2)}) collective-permute-start(bf16[64,512]{1,0:T(8,128)(2,1)} %dz_b.1), channel_id=1, source_target_pairs={{0,0},{1,8},{2,16},{3,24},{4,32},{5,40},{6,48},{7,56},{8,1},{9,9},... | collective-permute-start | bytes 196616 | tf_op jit(solution)/shard_map/ppermute | solution.py:447
  190.7 1.1 compare_convert_fusion
  191.8 0.8 copy-done.1
  192.7 3.6 %back_a.1 = (f32[64,2048]{1,0:T(8,128)}, f32[1,512]{1,0:T(1,128)}, f32[1,256]{1,0:T(1,128)}) custom-call(bf16[8,72,512]{2,1,0:T(8,128)(2,1)} %copy-done.1, bf16[64,512]{1,0:T(8,128)(2,1)} %get-tuple-element.35.raw_a, f32[8,512]{1,0:T(8,128)} %get-tuple-element.31.stats, f32[64,2048]{1,0:T(8,128)} %get-tuple-element.50.keep, ...), custom_call_target="tpu_custom_call" | custom-call | tf_op jit(solution)/shard_map/back_a/pallas_call | solution.py:92
  196.2 0.6 copy-done.15
  196.9 3.3 %back_b.1 = bf16[8,72,256]{2,1,0:T(8,128)(2,1)} custom-call(f32[64,2048]{1,0:T(8,128)} %get-tuple-element.36.part, bf16[64,512]{1,0:T(8,128)(2,1)} %copy-done.15, f32[64,2048]{1,0:T(8,128)} %get-tuple-element.49.keep, bf16[2,4,8,32,512]{4,3,2,1,0:T(8,128)(2,1)} %get-tuple-element.26.weight, f32[1,256]{1,0:T(1,128)} %get-tuple-element.43.power), custom_call_target="tpu_custom_call" | custom-call | tf_op jit(solution)/shard_map/back_b/pallas_call | solution.py:92
  200.2 17.9 %all_to_all.33.refs_0_ = bf16[8,72,256]{2,1,0:T(8,128)(2,1)} all-to-all(bf16[8,72,256]{2,1,0:T(8,128)(2,1)} %back_b.1), channel_id=1, replica_groups=mesh['zh'=2,'x'=4,'y'=8,'zl'=4,'c'=2] {'zl','c'}, dimensions={0} | all-to-all | bytes 589824 | tf_op jit(solution)/shard_map/all_to_all | solution.py:461
  218.1 1.6 end.1
  (37 shorter events, 0.1 us)
Async XLA Ops:
  0.6 52.6 %copy-start.7 = (bf16[64,2048]{1,0:T(8,128)(2,1)S(1)}, bf16[64,2048]{1,0:T(8,128)(2,1)}, u32[]{:S(2)}) copy-start(bf16[64,2048]{1,0:T(8,128)(2,1)} %param.5) | copy-start | bytes 786436
  0.6 52.6 %copy-start.6 = (bf16[64,2048]{1,0:T(8,128)(2,1)S(1)}, bf16[64,2048]{1,0:T(8,128)(2,1)}, u32[]{:S(2)}) copy-start(bf16[64,2048]{1,0:T(8,128)(2,1)} %param.4) | copy-start | bytes 786436
  34.0 25.6 %copy-start.2 = (bf16[8,64,512]{2,1,0:T(8,128)(2,1)}, bf16[8,64,512]{2,1,0:T(8,128)(2,1)S(1)}, u32[]{:S(2)}) copy-start(bf16[8,64,512]{2,1,0:T(8,128)(2,1)S(1)} %all_to_all.30) | copy-start | bytes 1572868
  34.0 11.9 %collective-permute-start.1 = (bf16[8,2,32,512]{3,2,1,0:T(8,128)(2,1)S(1)}, bf16[8,2,32,512]{3,2,1,0:T(8,128)(2,1)S(1)}, u32[]{:S(2)}, u32[]{:S(2)}) collective-permute-start(bf16[8,2,32,512]{3,2,1,0:T(8,128)(2,1)S(1)} %bitcast.16), channel_id=1, source_target_pairs={{0,192},{64,0},{128,64},{192,128},{1,193},{65,1},{129,65},{193,129... | collective-permute-start | bytes 1572872 | tf_op jit(solution)/shard_map/ppermute | solution.py:45
  38.4 12.9 %collective-permute-start = (bf16[8,2,32,512]{3,2,1,0:T(8,128)(2,1)S(1)}, bf16[8,2,32,512]{3,2,1,0:T(8,128)(2,1)S(1)}, u32[]{:S(2)}, u32[]{:S(2)}) collective-permute-start(bf16[8,2,32,512]{3,2,1,0:T(8,128)(2,1)S(1)} %bitcast.17), channel_id=1, source_target_pairs={{0,64},{64,128},{128,192},{192,0},{1,65},{65,129},{129,193},{193,1... | collective-permute-start | bytes 1572872 | tf_op jit(solution)/shard_map/ppermute | solution.py:45
  45.9 13.7 %copy-start.3 = (bf16[8,2,32,512]{3,2,1,0:T(8,128)(2,1)}, bf16[8,2,32,512]{3,2,1,0:T(8,128)(2,1)S(1)}, u32[]{:S(2)}) copy-start(bf16[8,2,32,512]{3,2,1,0:T(8,128)(2,1)S(1)} %collective-permute-done.1.ahead) | copy-start | bytes 1572868
  45.9 9.0 %collective-permute-start.3 = (bf16[4,2,32,512]{3,2,1,0:T(8,128)(2,1)S(1)}, bf16[4,2,32,512]{3,2,1,0:T(8,128)(2,1)S(1)}, u32[]{:S(2)}, u32[]{:S(2)}) collective-permute-start(bf16[4,2,32,512]{3,2,1,0:T(8,128)(2,1)S(1)} %slice.17), channel_id=1, source_target_pairs={{0,192},{64,0},{128,64},{192,128},{1,193},{65,1},{129,65},{193,129... | collective-permute-start | bytes 786440 | tf_op jit(solution)/shard_map/ppermute | solution.py:45
  51.3 8.4 %copy-start.4 = (bf16[8,2,32,512]{3,2,1,0:T(8,128)(2,1)}, bf16[8,2,32,512]{3,2,1,0:T(8,128)(2,1)S(1)}, u32[]{:S(2)}) copy-start(bf16[8,2,32,512]{3,2,1,0:T(8,128)(2,1)S(1)} %collective-permute-done.back) | copy-start | bytes 1572868
  51.3 8.3 %collective-permute-start.2 = (bf16[4,2,32,512]{3,2,1,0:T(8,128)(2,1)S(1)}, bf16[4,2,32,512]{3,2,1,0:T(8,128)(2,1)S(1)}, u32[]{:S(2)}, u32[]{:S(2)}) collective-permute-start(bf16[4,2,32,512]{3,2,1,0:T(8,128)(2,1)S(1)} %slice.16), channel_id=1, source_target_pairs={{0,64},{64,128},{128,192},{192,0},{1,65},{65,129},{129,193},{193,1... | collective-permute-start | bytes 786440 | tf_op jit(solution)/shard_map/ppermute | solution.py:45
  55.0 4.7 %copy-start.9 = (bf16[4,2,32,512]{3,2,1,0:T(8,128)(2,1)}, bf16[4,2,32,512]{3,2,1,0:T(8,128)(2,1)S(1)}, u32[]{:S(2)}) copy-start(bf16[4,2,32,512]{3,2,1,0:T(8,128)(2,1)S(1)} %collective-permute-done.3.far_high) | copy-start | bytes 786436
  59.7 0.7 copy-start.10
  63.6 11.2 %collective-permute-start.4 = (bf16[64,512]{1,0:T(8,128)(2,1)}, bf16[64,512]{1,0:T(8,128)(2,1)S(1)}, u32[]{:S(2)}, u32[]{:S(2)}) collective-permute-start(bf16[64,512]{1,0:T(8,128)(2,1)} %get-tuple-element.25), channel_id=1, source_target_pairs={{0,0},{1,8},{2,16},{3,24},{4,32},{5,40},{6,48},{7,56},{8,1},{9,9},... | collective-permute-start | bytes 196616 | tf_op jit(solution)/shard_map/ppermute | solution.py:399
  74.8 44.8 %copy-start.8 = (bf16[64,512]{1,0:T(8,128)(2,1)}, bf16[64,512]{1,0:T(8,128)(2,1)S(1)}, u32[]{:S(2)}) copy-start(bf16[64,512]{1,0:T(8,128)(2,1)S(1)} %collective-permute-done.4.raw_b) | copy-start | bytes 196612
  74.8 26.6 %all-to-all-start.1 = ((bf16[8,64,512]{2,1,0:T(8,128)(2,1)}), bf16[8,64,512]{2,1,0:T(8,128)(2,1)S(1)}, u32[]{:S(2)}, u32[]{:S(2)}) async-start(bf16[8,64,512]{2,1,0:T(8,128)(2,1)} %get-tuple-element.28), calls=%async_computation.1 | async-start | bytes 1048576 | tf_op jit(solution)/shard_map/all_to_all | solution.py:407
  101.4 0.8 copy-start
  121.4 11.4 %collective-permute-start.5 = (bf16[192,512]{1,0:T(8,128)(2,1)}, bf16[192,512]{1,0:T(8,128)(2,1)S(1)}, u32[]{:S(2)}, u32[]{:S(2)}) collective-permute-start(bf16[192,512]{1,0:T(8,128)(2,1)} %merge.1.refs_1_), channel_id=1, source_target_pairs={{0,256},{256,0},{1,257},{257,1},{2,258},{258,2},{3,259},{259,3},{4... | collective-permute-start | bytes 589832 | tf_op jit(solution)/shard_map/ppermute | solution.py:50
  132.8 0.7 copy-start.11
  150.3 10.4 %collective-permute-start.6 = (bf16[264,512]{1,0:T(8,128)(2,1)}, bf16[264,512]{1,0:T(8,128)(2,1)S(1)}, u32[]{:S(2)}, u32[]{:S(2)}) collective-permute-start(bf16[264,512]{1,0:T(8,128)(2,1)} %get-tuple-element.32), channel_id=1, source_target_pairs={{0,1},{1,0},{2,3},{3,2},{4,5},{5,4},{6,7},{7,6},{8,9},{9,8},{10,11... | collective-permute-start | bytes 811016 | tf_op jit(solution)/shard_map/ppermute | solution.py:50
  160.7 7.0 %copy-start.5 = (bf16[264,512]{1,0:T(8,128)(2,1)}, bf16[264,512]{1,0:T(8,128)(2,1)S(1)}, u32[]{:S(2)}) copy-start(bf16[264,512]{1,0:T(8,128)(2,1)S(1)} %collective-permute-done.6.got) | copy-start | bytes 811012
  160.7 31.1 %all-to-all-start.4 = ((bf16[8,72,512]{2,1,0:T(8,128)(2,1)}), bf16[8,72,512]{2,1,0:T(8,128)(2,1)S(1)}, u32[]{:S(2)}, u32[]{:S(2)}) async-start(bf16[8,72,512]{2,1,0:T(8,128)(2,1)} %grad_a.1), calls=%async_computation.4 | async-start | bytes 1179648 | tf_op jit(solution)/shard_map/all_to_all | solution.py:437
  169.7 9.6 %collective-permute-start.7 = (bf16[72,512]{1,0:T(8,128)(2,1)}, bf16[72,512]{1,0:T(8,128)(2,1)S(1)}, u32[]{:S(2)}, u32[]{:S(2)}) collective-permute-start(bf16[72,512]{1,0:T(8,128)(2,1)} %get-tuple-element.40), channel_id=1, source_target_pairs={{0,2},{2,0},{4,6},{6,4},{1,3},{3,1},{5,7},{7,5},{8,10},{10,8},{12,... | collective-permute-start | bytes 221192 | tf_op jit(solution)/shard_map/ppermute | solution.py:50
  173.4 8.5 %collective-permute-start.8 = (bf16[72,512]{1,0:T(8,128)(2,1)}, bf16[72,512]{1,0:T(8,128)(2,1)S(1)}, u32[]{:S(2)}, u32[]{:S(2)}) collective-permute-start(bf16[72,512]{1,0:T(8,128)(2,1)} %get-tuple-element.41), channel_id=1, source_target_pairs={{0,4},{2,6},{4,0},{6,2},{1,5},{3,7},{5,1},{7,3},{8,12},{10,14},{12... | collective-permute-start | bytes 221192 | tf_op jit(solution)/shard_map/ppermute | solution.py:50
  175.9 7.2 %collective-permute-start.9 = (bf16[72,512]{1,0:T(8,128)(2,1)}, bf16[72,512]{1,0:T(8,128)(2,1)S(1)}, u32[]{:S(2)}, u32[]{:S(2)}) collective-permute-start(bf16[72,512]{1,0:T(8,128)(2,1)} %get-tuple-element.42), channel_id=1, source_target_pairs={{0,6},{2,4},{4,2},{6,0},{1,7},{3,5},{5,3},{7,1},{8,14},{10,12},{12... | collective-permute-start | bytes 221192 | tf_op jit(solution)/shard_map/ppermute | solution.py:50
  179.3 3.8 %copy-start.12 = (bf16[72,512]{1,0:T(8,128)(2,1)}, bf16[72,512]{1,0:T(8,128)(2,1)S(1)}, u32[]{:S(2)}) copy-start(bf16[72,512]{1,0:T(8,128)(2,1)S(1)} %collective-permute-done.7.got1) | copy-start | bytes 221188
  181.9 1.3 copy-start.13
  183.1 0.6 copy-start.14
  185.5 10.7 %collective-permute-start.10 = (bf16[64,512]{1,0:T(8,128)(2,1)}, bf16[64,512]{1,0:T(8,128)(2,1)S(1)}, u32[]{:S(2)}, u32[]{:S(2)}) collective-permute-start(bf16[64,512]{1,0:T(8,128)(2,1)} %dz_b.1), channel_id=1, source_target_pairs={{0,0},{1,8},{2,16},{3,24},{4,32},{5,40},{6,48},{7,56},{8,1},{9,9},... | collective-permute-start | bytes 196616 | tf_op jit(solution)/shard_map/ppermute | solution.py:447
  191.8 0.8 copy-start.1
  196.2 0.6 copy-start.15
